TPU v7x, 32 devices: a whole 2x2x4 slice. The times are simulated.
32 devices in a mesh: dom: 8 (over z, x), mode: 4 (over y, core).
Axes of the slice: x: 2, y: 2, z: 4, core: 2. Of those that a mesh axis runs over, the one named last changes fastest.
Arguments:
- shapes: bfloat16 [3, 2048, 4096], P(None, 'dom', 'mode'), may hold values from -6 to 6
- masses: float32 [2048], P('dom'), may hold values from 0.1 to 30, as said below
- spectral: float32 [3, 4096], replicated, may hold values from 2 to 16, as said below
- frequencies: float32 [4096], replicated, may hold values from 2 to 300, as said below
- damping: float32 [4096], replicated, may hold values from 0.015 to 0.03, as said below
- recovery: bfloat16 [512, 8, 4, 3], P('dom'), may hold values from -1.75 to 1.75
- connectivity: int32 [512, 4], P('dom'), may hold values from 0 to 383
- node_count: int32 [512], P('dom'), may hold values from 2 to 4
- shared: int32 [2, 512], P(None, 'dom'), may hold values from 0 to 255
Outputs:
- response: float32 [4096], P('dom')
Inputs may be any that keep to these rules, and one draw needn't show every extreme that they name: Positive node masses. Positive spectral displacements. Positive circular frequencies. Positive damping ratios. `connectivity`: codes below 256 are own nodes; the next 64 codes name the lower neighbour's upper list, the last 64 the upper neighbour's lower list. `shared`: local node numbers; entries may repeat.
All inputs are finite; a program needn't handle non-finite values.
Results may differ from a plain program's by a relative error of at most 0.0025.
Values may be sent and summed in bfloat16 or wider, within the bound.
No kernel may reach another device: no remote copies, remote signals or barrier semaphores. Data moves between devices by JAX's collectives and lax.ppermute only.
A program may use at most 64 MiB of HBM per device.

v0:
```python
import jax
import jax.numpy as jnp
from jax import lax
from jax.sharding import PartitionSpec as P


def extended_2(block, sides, width):
    for axis, dim in sides:
        count = lax.axis_size(axis)
        forward = [(i, i + 1) for i in range(count - 1)]
        backward = [(target, source) for source, target in forward]
        low = lax.ppermute(
            lax.slice_in_dim(block, block.shape[dim] - width, None, axis=dim), axis, forward
        )
        high = lax.ppermute(lax.slice_in_dim(block, 0, width, axis=dim), axis, backward)
        block = jnp.concatenate([low, block, high], axis=dim)
    return block


def shifted(value, axis, steps):
    count = lax.axis_size(axis)
    pairs = [(source, (source + steps) % count) for source in range(count)]
    return lax.ppermute(value, axis, pairs)


def correlation_block(freq_rows, freq_cols, rate_rows, rate_cols):
    ratio = freq_cols[None, :] / freq_rows[:, None]
    ratio_sq = ratio * ratio
    rate_row = rate_rows[:, None]
    rate_col = rate_cols[None, :]
    top_part = (
        8.0
        * jnp.sqrt(rate_row * rate_col)
        * (rate_row + ratio * rate_col)
        * ratio
        * jnp.sqrt(ratio)
    )
    spread = 1.0 - ratio_sq
    bottom_part = (
        spread * spread
        + 4.0 * rate_row * rate_col * ratio * (1.0 + ratio_sq)
        + 4.0 * (rate_row * rate_row + rate_col * rate_col) * ratio_sq
    )
    return top_part / bottom_part


def block_terms(own_forces, own_start, far_forces, far_start, amplitudes, frequencies, damping):
    row_count = own_forces.shape[1]
    col_count = far_forces.shape[1]
    freq_rows = lax.dynamic_slice_in_dim(frequencies, own_start, row_count)
    freq_cols = lax.dynamic_slice_in_dim(frequencies, far_start, col_count)
    rate_rows = lax.dynamic_slice_in_dim(damping, own_start, row_count)
    rate_cols = lax.dynamic_slice_in_dim(damping, far_start, col_count)
    correlation = correlation_block(freq_rows, freq_cols, rate_rows, rate_cols)
    amp_rows = lax.dynamic_slice_in_dim(amplitudes, own_start, row_count, 1)
    amp_cols = lax.dynamic_slice_in_dim(amplitudes, far_start, col_count, 1)
    weights = (amp_rows.T[:, :, None] * correlation[:, None, :] * amp_cols[None, :, :]).astype(
        jnp.bfloat16
    )
    weights = weights.reshape(row_count, 3 * col_count)
    projected = jnp.dot(own_forces, weights, preferred_element_type=jnp.float32)
    projected = projected.reshape(own_forces.shape[0], 3, col_count)
    far_wide = far_forces.astype(jnp.float32)
    return jnp.sum(projected * far_wide[:, None, :], axis=(1, 2))


def per_device(
    shapes, masses, spectral, frequencies, damping, recovery, connectivity, node_count, shared
):
    rim_width = shared.shape[1]
    block_width = shapes.shape[2]
    elem_count = connectivity.shape[0]
    slot_count = connectivity.shape[1]
    mode_index = lax.axis_index("mode")
    own_start = mode_index * block_width
    shape_wide = shapes.astype(jnp.float32)
    weighted = masses[None, :, None] * shape_wide
    lever_arm = jnp.sum(weighted, axis=1)
    general = jnp.sum(weighted * shape_wide, axis=(0, 1))
    lever_sum, general_sum = lax.psum((lever_arm, general), "dom")
    own_spectral = lax.dynamic_slice_in_dim(spectral, own_start, block_width, 1)
    local_amps = lever_sum / general_sum[None, :] * own_spectral
    amplitudes = lax.all_gather(local_amps, "mode", axis=1, tiled=True)
    outgoing = jnp.concatenate(
        [jnp.take(shapes, shared[0], axis=1), jnp.take(shapes, shared[1], axis=1)], axis=1
    )
    extended = extended_2(outgoing, (("dom", 1),), rim_width)
    node_table = jnp.concatenate(
        [shapes, extended[:, :rim_width], extended[:, 3 * rim_width :]], axis=1
    )
    gathered = jnp.take(node_table, connectivity.reshape(-1), axis=1).reshape(
        3, elem_count, slot_count, block_width
    )
    slot_live = (jnp.arange(slot_count)[None, :] < node_count[:, None]).astype(jnp.bfloat16)
    masked = recovery * slot_live[:, None, :, None]
    forces = jnp.einsum("ekna,aenm->ekm", masked, gathered, preferred_element_type=jnp.float32)
    forces = forces.astype(jnp.bfloat16).reshape(elem_count * recovery.shape[1], block_width)
    groups = lax.axis_size("mode")
    half_count = groups // 2
    partial_value = block_terms(
        forces, own_start, forces, own_start, amplitudes, frequencies, damping
    )

    def advance(turn_index, carried):
        incoming, summed = carried
        incoming = shifted(incoming, "mode", 1)
        source = (mode_index - turn_index) % groups * block_width
        factor = jnp.where(turn_index == half_count, jnp.float32(1.0), jnp.float32(2.0))
        summed = summed + factor * block_terms(
            forces, own_start, incoming, source, amplitudes, frequencies, damping
        )
        return (incoming, summed)

    carried = lax.fori_loop(1, half_count + 1, advance, (forces, partial_value))
    partial_value = carried[1]
    return lax.psum(partial_value, "mode")


def solution(mesh):
    in_specs = (
        P(None, "dom", "mode"),
        P("dom"),
        P(),
        P(),
        P(),
        P("dom", None, None, None),
        P("dom", None),
        P("dom"),
        P(None, "dom"),
    )
    out_specs = P("dom")
    return jax.shard_map(
        per_device, mesh=mesh, in_specs=in_specs, out_specs=out_specs, check_vma=False
    )
```

profile of v0, /device:TPU:0, one launch (start us, length us, event | category | flops | bytes accessed | tf_op | source)
XLA Modules:
  0.0 167.8 jit_solution(11176786676996653308)
XLA Ops:
  0.0 0.0 copy-start
  0.0 0.8 compare_and_fusion.1
  0.8 0.0 copy-start.5
  0.8 2.4 %gather_fusion.1 = bf16[64,3,1024]{2,0,1:T(8,128)(2,1)S(1)} fusion(bf16[3,256,1024]{2,1,0:T(8,128)(2,1)} %param.13, s32[1024]{0:T(1024)S(1)} %pad_clamp_fusion.2), kind=kCustom, calls=%fused_computation.clone | custom fusion | bytes 786688 | tf_op jit(solution)/shard_map/jit(_take)/gather | solution.py:85
  3.3 0.0 copy-start.2
  3.3 0.0 copy-start.1
  3.3 0.0 copy-start.6
  3.3 0.1 select_bitcast_fusion.1
  3.4 4.9 %collective-permute-start.1 = (bf16[3,64,1024]{2,1,0:T(8,128)(2,1)S(1)}, bf16[3,64,1024]{2,1,0:T(8,128)(2,1)S(1)}, u32[]{:S(2)}, u32[]{:S(2)}) collective-permute-start(bf16[3,64,1024]{2,1,0:T(8,128)(2,1)S(1)} %select_bitcast_fusion.1), channel_id=1, source_target_pairs={{0,4},{4,8},{8,12},{12,16},{16,20},{20,24},{24,28},{1,5},{5,9},{9,... | collective-permute-start | bytes 1179656 | tf_op jit(solution)/shard_map/ppermute | solution.py:12
  8.3 0.0 copy-done
  8.3 1.8 %gather_fusion.2 = bf16[64,3,1024]{2,0,1:T(8,128)(2,1)S(1)} fusion(bf16[3,256,1024]{2,1,0:T(8,128)(2,1)S(1)} %copy-done, s32[1024]{0:T(1024)S(1)} %pad_clamp_fusion.1), kind=kCustom, calls=%fused_computation.1.clone | custom fusion | bytes 786688 | tf_op jit(solution)/shard_map/jit(_take)/gather | solution.py:85
  10.1 0.1 select_bitcast_fusion
  10.2 1.3 collective-permute-start.2
  11.5 0.0 copy-done.5
  11.5 0.7 fusion.3
  12.2 42.8 %all-reduce = (f32[3,1024]{1,0:T(4,128)S(1)}, f32[1024]{0:T(1024)S(1)}) all-reduce(f32[3,1024]{1,0:T(4,128)S(1)} %get-tuple-element.276, f32[1024]{0:T(1024)S(1)} %get-tuple-element.275), channel_id=1, replica_groups=mesh['dom'=8,'mode'=4] {'dom'}, use_global_device_ids=true, to_apply=%region_1.3 | all-reduce | flops 4096 | bytes 32768 | tf_op jit(solution)/shard_map/psum | solution.py:80
  55.0 0.7 divide_multiply_fusion
  55.7 5.4 %all_gather.3 = f32[3,4096]{1,0:T(4,128)S(1)} all-gather(f32[3,1024]{1,0:T(4,128)S(1)} %divide_multiply_fusion), channel_id=1, replica_groups=mesh['dom'=8,'mode'=4] {'mode'}, dimensions={1}, use_global_device_ids=true | all-gather | bytes 61440 | tf_op jit(solution)/shard_map/all_gather | solution.py:83
  61.2 0.0 copy-done.2
  61.2 0.0 copy-done.1
  61.3 0.0 copy-done.6
  61.3 4.9 %add_divide_fusion.1 = f32[1024,1024]{0,1:T(8,128)S(1)} fusion(f32[1024]{0:T(1024)S(1)} %mul.574, f32[1024]{0:T(1024)S(1)} %get-tuple-element.305, f32[1024]{0:T(1024)S(1)} %dynamic_slice.69, f32[1024]{0:T(1024)S(1)} %get-tuple-element.399), kind=kLoop, calls=%fused_computation.18 | loop fusion | flops 22020096 | bytes 4210688 | tf_op jit(solution)/shard_map/div | solution.py:44
  66.2 6.2 %broadcast_multiply_fusion.2 = f32[1024,3,1024]{0,2,1:T(8,128)} fusion(f32[1024,1024]{0,1:T(8,128)S(1)} %add_divide_fusion.1, f32[1024,3]{0,1:T(4,128)S(1)} %fusion.14), kind=kLoop, calls=%fused_computation.15 | loop fusion | flops 3145728 | bytes 16789504 | tf_op jit(solution)/shard_map/mul | solution.py:57
  72.4 0.0 copy-start.3
  72.4 0.0 copy-start.4
  72.4 7.9 %fusion.2 = bf16[1024,3072]{0,1:T(8,128)(2,1)} fusion(f32[1024,3,1024]{0,2,1:T(8,128)} %broadcast_multiply_fusion.2, f32[3072]{0:T(1024)S(1)} %mul.580), kind=kLoop, calls=%fused_computation.13 | loop fusion | flops 6291456 | bytes 18886656 | tf_op jit(solution)/shard_map/convert_element_type | solution.py:57
  80.4 0.0 copy-done.3
  80.4 0.0 copy-done.4
  80.4 2.7 %copy.16 = bf16[3,256,1024]{2,0,1:T(4,128)(2,1)} copy(bf16[3,256,1024]{2,1,0:T(8,128)(2,1)S(1)} %copy-done) | data formatting | bytes 3145728 | tf_op args[0]
  83.1 0.1 copy.19
  83.2 0.1 reshape.381
  83.3 0.2 copy.21
  83.5 0.1 copy.15
  83.6 0.0 collective-permute-done.1
  83.6 0.3 copy.17
  84.0 0.0 collective-permute-done.2
  84.0 0.3 copy.18
  84.3 6.5 %pad_maximum_fusion = bf16[3,384,1024]{2,0,1:T(4,128)(2,1)S(1)} fusion(bf16[3,64,1024]{2,0,1:T(4,128)(2,1)S(1)} %copy.18, bf16[3,64,1024]{2,0,1:T(4,128)(2,1)S(1)} %copy.17, bf16[3,256,1024]{2,0,1:T(4,128)(2,1)} %copy.16), kind=kLoop, calls=%fused_computation.20 | loop fusion | flops 2359296 | bytes 4718592 | tf_op jit(solution)/shard_map/concatenate | solution.py:88
  90.9 3.6 %gather_fusion = bf16[256,3,1024]{2,1,0:T(4,128)(2,1)} fusion(bf16[3,384,1024]{2,0,1:T(4,128)(2,1)S(1)} %pad_maximum_fusion, s32[1024]{0:T(1024)S(1)} %pad_clamp_fusion), kind=kCustom, calls=%fused_computation.2 | custom fusion | bytes 3146752 | tf_op jit(solution)/shard_map/jit(_take)/gather | solution.py:91
  94.4 4.7 %bitcast_convert_fusion.1 = (f32[512,1024]{1,0:T(8,128)}, bf16[64,8,1024]{2,1,0:T(8,128)(2,1)S(1)}) fusion(bf16[64,8,4,3]{1,2,3,0:T(4,128)(2,1)S(1)} %copy.21, bf16[3,64,4,1024]{3,0,2,1:T(4,128)(2,1)} %bitcast.60, pred[64,4]{1,0:T(8,128)(4,1)S(1)} %copy.15), kind=kOutput, calls=%fused_computation.44 | convolution fusion | flops 14417920 | bytes 4731136 | tf_op jit(solution)/shard_map/ekna,aenm->ekm/dot_general | solution.py:96
  99.1 0.5 copy.22
  99.7 7.0 %multiply_reduce_fusion = f32[512]{0:T(512)S(1)} fusion(f32[512,1024]{1,0:T(8,128)} %get-tuple-element.314, bf16[3,1024,1024]{2,1,0:T(8,128)(2,1)} %bitcast.59, bf16[64,8,1024]{2,1,0:T(8,128)(2,1)S(1)} %get-tuple-element.315), kind=kOutput, calls=%fused_computation.14 | convolution fusion | flops 3224370688 | bytes 9439232 | tf_op jit(solution)/shard_map/dot_general | solution.py:61
  106.6 54.5 %while.17 = (s32[]{:T(128)}, bf16[512,1024]{0,1:T(8,128)(2,1)S(1)}, f32[512]{0:T(512)S(1)}, f32[3,1024]{1,0:T(4,128)S(1)}, f32[1024]{0:T(1024)S(1)}, /*index=5*/...) while((s32[]{:T(128)}, bf16[512,1024]{0,1:T(8,128)(2,1)S(1)}, ...), condition=%wide.region_7.9_spmd, body=%wide.region_5.8_spmd.sunk | while | flops 3256355328 | bytes 58859952 | solution.py:114
  106.9 0.4 collective-permute-start
  107.3 4.9 %add_divide_fusion.3 = f32[1024,1024]{0,1:T(8,128)S(1)} fusion(f32[1024]{0:T(1024)S(1)} %get-tuple-element.392, f32[1024]{0:T(1024)S(1)} %get-tuple-element.446, f32[1024]{0:T(1024)S(1)} %get-tuple-element.393, f32[1024]{0:T(1024)S(1)} %get-tuple-element.445, f32[1024]{0:T(1024)S(1)} %dynamic_slice.82, f32[1024]{0:T(1024)S(1)} %get-tuple-element.394, ...), kind=kLoop, calls=%fused_computation.8.clone.1 | loop fusion | flops 22020096 | bytes 4222976 | tf_op jit(solution)/shard_map/while/body/eval_jaxpr/div | solution.py:44
  112.3 6.2 %broadcast_multiply_fusion.6 = f32[1024,3,1024]{0,2,1:T(8,128)} fusion(f32[1024,1024]{0,1:T(8,128)S(1)} %add_divide_fusion.3, f32[1024,3]{0,1:T(4,128)S(1)} %bitcast.63), kind=kLoop, calls=%fused_computation.7.clone.1 | loop fusion | flops 3145728 | bytes 16789504 | tf_op jit(solution)/shard_map/while/body/eval_jaxpr/mul | solution.py:57
  118.5 7.9 %fusion.23 = bf16[1024,3072]{0,1:T(8,128)(2,1)} fusion(f32[1024,3,1024]{0,2,1:T(8,128)} %broadcast_multiply_fusion.6, f32[3072]{0:T(1024)S(1)} %mul.709), kind=kLoop, calls=%fused_computation.4.clone.1 | loop fusion | flops 6291456 | bytes 18886656 | tf_op jit(solution)/shard_map/while/body/eval_jaxpr/convert_element_type | solution.py:57
  126.4 0.0 collective-permute-done
  126.4 0.3 convert_element_type.62
  126.7 6.8 %fusion.24 = f32[512]{0:T(512)S(1)} fusion(f32[512,1024]{0,1:T(8,128)S(1)} %convert_element_type.62, bf16[1024,3072]{0,1:T(8,128)(2,1)} %fusion.23, bf16[512,1024]{1,0:T(8,128)(2,1)S(1)} %get-tuple-element.448), kind=kOutput, calls=%fused_computation.6.clone.1 | convolution fusion | flops 3224370688 | bytes 9439232 | tf_op jit(solution)/shard_map/while/body/eval_jaxpr/dot_general | solution.py:61
  133.5 0.1 copy.35
  133.6 1.3 collective-permute-start
  134.9 4.9 %add_divide_fusion.3 = f32[1024,1024]{0,1:T(8,128)S(1)} fusion(f32[1024]{0:T(1024)S(1)} %get-tuple-element.392, f32[1024]{0:T(1024)S(1)} %get-tuple-element.446, f32[1024]{0:T(1024)S(1)} %get-tuple-element.393, f32[1024]{0:T(1024)S(1)} %get-tuple-element.445, f32[1024]{0:T(1024)S(1)} %dynamic_slice.82, f32[1024]{0:T(1024)S(1)} %get-tuple-element.394, ...), kind=kLoop, calls=%fused_computation.8.clone.1 | loop fusion | flops 22020096 | bytes 4222976 | tf_op jit(solution)/shard_map/while/body/eval_jaxpr/div | solution.py:44
  139.9 6.2 %broadcast_multiply_fusion.6 = f32[1024,3,1024]{0,2,1:T(8,128)} fusion(f32[1024,1024]{0,1:T(8,128)S(1)} %add_divide_fusion.3, f32[1024,3]{0,1:T(4,128)S(1)} %bitcast.63), kind=kLoop, calls=%fused_computation.7.clone.1 | loop fusion | flops 3145728 | bytes 16789504 | tf_op jit(solution)/shard_map/while/body/eval_jaxpr/mul | solution.py:57
  146.1 7.9 %fusion.23 = bf16[1024,3072]{0,1:T(8,128)(2,1)} fusion(f32[1024,3,1024]{0,2,1:T(8,128)} %broadcast_multiply_fusion.6, f32[3072]{0:T(1024)S(1)} %mul.709), kind=kLoop, calls=%fused_computation.4.clone.1 | loop fusion | flops 6291456 | bytes 18886656 | tf_op jit(solution)/shard_map/while/body/eval_jaxpr/convert_element_type | solution.py:57
  154.0 0.0 collective-permute-done
  154.0 0.3 convert_element_type.62
  154.3 6.8 %fusion.24 = f32[512]{0:T(512)S(1)} fusion(f32[512,1024]{0,1:T(8,128)S(1)} %convert_element_type.62, bf16[1024,3072]{0,1:T(8,128)(2,1)} %fusion.23, bf16[512,1024]{1,0:T(8,128)(2,1)S(1)} %get-tuple-element.448), kind=kOutput, calls=%fused_computation.6.clone.1 | convolution fusion | flops 3224370688 | bytes 9439232 | tf_op jit(solution)/shard_map/while/body/eval_jaxpr/dot_general | solution.py:61
  161.1 0.1 copy.35
  161.1 6.7 %psum.23 = f32[512]{0:T(512)} all-reduce(f32[512]{0:T(512)S(1)} %get-tuple-element.250), channel_id=1, replica_groups=mesh['dom'=8,'mode'=4] {'mode'}, use_global_device_ids=true, to_apply=%region_8.10 | all-reduce | flops 512 | bytes 4096 | tf_op jit(solution)/shard_map/psum | solution.py:116
  (23 shorter events, 0.2 us)
Async XLA Ops:
  0.0 8.3 %copy-start = (bf16[3,256,1024]{2,1,0:T(8,128)(2,1)S(1)}, bf16[3,256,1024]{2,1,0:T(8,128)(2,1)}, u32[]{:S(2)}) copy-start(bf16[3,256,1024]{2,1,0:T(8,128)(2,1)} %param.13) | copy-start | bytes 4718596
  0.8 10.7 %copy-start.5 = (f32[256]{0:T(256)S(1)}, f32[256]{0:T(256)}, u32[]{:S(2)}) copy-start(f32[256]{0:T(256)} %param.14) | copy-start | bytes 3076
  3.3 57.9 %copy-start.2 = (f32[4096]{0:T(1024)S(1)}, f32[4096]{0:T(1024)}, u32[]{:S(2)}) copy-start(f32[4096]{0:T(1024)} %param.17) | copy-start | bytes 49156
  3.3 57.9 %copy-start.1 = (f32[4096]{0:T(1024)S(1)}, f32[4096]{0:T(1024)}, u32[]{:S(2)}) copy-start(f32[4096]{0:T(1024)} %param.16) | copy-start | bytes 49156
  3.3 58.0 %copy-start.6 = (s32[64]{0:T(128)S(1)}, s32[64]{0:T(128)}, u32[]{:S(2)}) copy-start(s32[64]{0:T(128)} %param.20) | copy-start | bytes 772
  3.4 80.2 %collective-permute-start.1 = (bf16[3,64,1024]{2,1,0:T(8,128)(2,1)S(1)}, bf16[3,64,1024]{2,1,0:T(8,128)(2,1)S(1)}, u32[]{:S(2)}, u32[]{:S(2)}) collective-permute-start(bf16[3,64,1024]{2,1,0:T(8,128)(2,1)S(1)} %select_bitcast_fusion.1), channel_id=1, source_target_pairs={{0,4},{4,8},{8,12},{12,16},{16,20},{20,24},{24,28},{1,5},{5,9},{9,... | collective-permute-start | bytes 1179656 | tf_op jit(solution)/shard_map/ppermute | solution.py:12
  10.2 73.8 %collective-permute-start.2 = (bf16[3,64,1024]{2,1,0:T(8,128)(2,1)S(1)}, bf16[3,64,1024]{2,1,0:T(8,128)(2,1)S(1)}, u32[]{:S(2)}, u32[]{:S(2)}) collective-permute-start(bf16[3,64,1024]{2,1,0:T(8,128)(2,1)S(1)} %select_bitcast_fusion), channel_id=1, source_target_pairs={{4,0},{8,4},{12,8},{16,12},{20,16},{24,20},{28,24},{5,1},{9,5},{13... | collective-permute-start | bytes 1179656 | tf_op jit(solution)/shard_map/ppermute | solution.py:15
  72.4 7.9 %copy-start.3 = (bf16[64,8,4,3]{0,2,3,1:T(4,128)(2,1)S(1)}, bf16[64,8,4,3]{0,2,3,1:T(4,128)(2,1)}, u32[]{:S(2)}) copy-start(bf16[64,8,4,3]{0,2,3,1:T(4,128)(2,1)} %param.18) | copy-start | bytes 36868
  72.4 8.0 %copy-start.4 = (s32[64,4]{0,1:T(4,128)S(1)}, s32[64,4]{0,1:T(4,128)}, u32[]{:S(2)}) copy-start(s32[64,4]{0,1:T(4,128)} %param.19) | copy-start | bytes 3076
  106.9 19.5 %collective-permute-start = (bf16[512,1024]{0,1:T(8,128)(2,1)S(1)}, bf16[512,1024]{0,1:T(8,128)(2,1)S(1)}, u32[]{:S(2)}, u32[]{:S(2)}) collective-permute-start(bf16[512,1024]{0,1:T(8,128)(2,1)S(1)} %get-tuple-element.417), channel_id=1, source_target_pairs={{0,1},{1,2},{2,3},{3,0},{4,5},{5,6},{6,7},{7,4},{8,9},{9,10},{10,1... | collective-permute-start | bytes 3145736 | tf_op jit(solution)/shard_map/while/body/eval_jaxpr/ppermute | solution.py:23
  133.6 20.4 %collective-permute-start = (bf16[512,1024]{0,1:T(8,128)(2,1)S(1)}, bf16[512,1024]{0,1:T(8,128)(2,1)S(1)}, u32[]{:S(2)}, u32[]{:S(2)}) collective-permute-start(bf16[512,1024]{0,1:T(8,128)(2,1)S(1)} %get-tuple-element.417), channel_id=1, source_target_pairs={{0,1},{1,2},{2,3},{3,0},{4,5},{5,6},{6,7},{7,4},{8,9},{9,10},{10,1... | collective-permute-start | bytes 3145736 | tf_op jit(solution)/shard_map/while/body/eval_jaxpr/ppermute | solution.py:23
where the time goes:
time: 168 us
  other arithmetic  66.8 us (40%)
  blocking collectives  54.9 us (33%)
  matrix products  25.2 us (15%)
  local copies, waits for them, and re-layouts  12.4 us (7%)
  starting transfers between devices  7.93 us (5%)
    psum x1, blocking collectives, per_device(): lever_sum, general_sum = lax.psum((lever_arm, general), 'dom')  42.8 us
    convert_element_type x3, other arithmetic, block_terms(): (amp_rows.T[:, :, None] * correlation[:, None, :] * amp_cols[None, :, :])...  23.8 us
    dot_general x3, matrix products, block_terms(): projected = jnp.dot(own_forces, weights, preferred_element_type=jnp.float32)  20.5 us
    mul x3, other arithmetic, block_terms(): amp_rows.T[:, :, None] * correlation[:, None, :] * amp_cols[None, :, :]  18.5 us
    div x3, other arithmetic, correlation_block(): return top_part / bottom_part  14.8 us
    psum x1, blocking collectives, per_device(): return lax.psum(partial_value, 'mode')  6.68 us
    concatenate x1, other arithmetic, per_device(): jnp.concatenate([shapes, extended[:, :rim_width], extended[:, 3 * rim_wid...  6.53 us
    all_gather x1, blocking collectives, per_device(): amplitudes = lax.all_gather(local_amps, 'mode', axis=1, tiled=True)  5.42 us
  transfers between devices with their start and end apart: 4, of which 0 were waited for; matrix products, arithmetic and copies ran while one was open for 38% of the time, Pallas kernels for 0%

commit v1 on v0

--- a/solution.py
+++ b/solution.py
@@ -1,7 +1,374 @@
+import functools
 import jax
 import jax.numpy as jnp
 from jax import lax
+from jax.experimental import pallas as pl
+from jax.experimental.pallas import tpu as pltpu
 from jax.sharding import PartitionSpec as P
+
+F32 = jnp.float32
+BF16 = jnp.bfloat16
+VMEM = pl.BlockSpec(memory_space=pltpu.VMEM)
+SMEM = pl.BlockSpec(memory_space=pltpu.SMEM)
+AMP_ROWS = 16
+
+
+def call(kernel, out_shape, args, flops, nbytes, smem=(), scratch=(), vmem=None):
+    specs = [SMEM if i in smem else VMEM for i in range(len(args))]
+    many = isinstance(out_shape, (tuple, list))
+    return pl.pallas_call(
+        kernel,
+        out_shape=out_shape,
+        in_specs=specs,
+        out_specs=[VMEM] * len(out_shape) if many else VMEM,
+        scratch_shapes=list(scratch),
+        cost_estimate=pl.CostEstimate(flops=flops, bytes_accessed=nbytes, transcendentals=0),
+        compiler_params=pltpu.CompilerParams(vmem_limit_bytes=vmem),
+    )(*args)
+
+
+def gather_kernel(rows_ref, shapes_ref, up_ref, down_ref):
+    dims, nodes, _ = shapes_ref.shape
+    width = up_ref.shape[0] // dims
+    count = rows_ref.shape[1]
+    node = lax.broadcasted_iota(jnp.int32, (nodes, count), 0)
+    pick = jnp.where(node == rows_ref[...], 1.0, 0.0).astype(F32).T.astype(BF16)
+    for d in range(dims):
+        got = jnp.dot(pick, shapes_ref[d], preferred_element_type=F32).astype(BF16)
+        up_ref[d * width : (d + 1) * width, :] = got[:width]
+        down_ref[d * width : (d + 1) * width, :] = got[width:]
+
+
+def stats_kernel(mass_ref, shapes_ref, out_ref, mass_scr):
+    dims, nodes, block = shapes_ref.shape
+    column = jnp.broadcast_to(mass_ref[...], (8, nodes)).T
+    mass_scr[...] = jnp.broadcast_to(column[:, 0:1], (nodes, 128))
+
+    @pl.loop(0, block // 128)
+    def _(t):
+        lanes = pl.ds(pl.multiple_of(t * 128, 128), 128)
+        general = jnp.zeros((8, 128), F32)
+        for d in range(dims):
+            lever = jnp.zeros((8, 128), F32)
+            for r in range(0, nodes, 16):
+                wide = shapes_ref[d, r : r + 16, lanes].astype(F32)
+                weighted = wide * mass_scr[r : r + 16, :]
+                square = weighted * wide
+                lever += weighted[:8] + weighted[8:]
+                general += square[:8] + square[8:]
+            out_ref[d : d + 1, lanes] = jnp.sum(lever, axis=0, keepdims=True)
+        out_ref[dims : dims + 1, lanes] = jnp.sum(general, axis=0, keepdims=True)
+
+
+def local_kernel(table_ref, shapes_ref, local_ref, rim_ref, own_scr):
+    dims, nodes, block = shapes_ref.shape
+    comps = table_ref.shape[0]
+    slots = table_ref.shape[1] // (dims + 1)
+    rim = rim_ref.shape[1] // (2 * dims)
+    span = nodes + rim
+    step = 32
+
+    @pl.loop(0, comps // step)
+    def _(t):
+        rows = pl.ds(pl.multiple_of(t * step, step), step)
+        table = table_ref[rows, :]
+        code = lax.broadcasted_iota(jnp.int32, (step, span), 1).astype(F32)
+        total = [jnp.zeros((step, span), F32) for _ in range(dims)]
+        for s in range(slots):
+            hit = table[:, slots * dims + s : slots * dims + s + 1] == code
+            for d in range(dims):
+                value = table[:, s * dims + d : s * dims + d + 1]
+                total[d] = total[d] + jnp.where(hit, value, 0.0)
+        for d in range(dims):
+            high = total[d].astype(BF16)
+            low = (total[d] - high.astype(F32)).astype(BF16)
+            own_scr[rows, d * nodes : (d + 1) * nodes] = high[:, :nodes]
+            own_scr[rows, (dims + d) * nodes : (dims + d + 1) * nodes] = low[:, :nodes]
+            rim_ref[rows, d * rim : (d + 1) * rim] = high[:, nodes:]
+            rim_ref[rows, (dims + d) * rim : (dims + d + 1) * rim] = low[:, nodes:]
+
+    wide = 256
+
+    @pl.loop(0, block // wide)
+    def _(t):
+        lanes = pl.ds(pl.multiple_of(t * wide, wide), wide)
+        total = jnp.zeros((comps, wide), F32)
+        for half in range(2):
+            for d in range(dims):
+                at = (half * dims + d) * nodes
+                total += jnp.dot(
+                    own_scr[:, at : at + nodes], shapes_ref[d, :, lanes], preferred_element_type=F32
+                )
+        local_ref[:, lanes] = total
+
+
+def mode_rows(freq, rate):
+    alpha = rate * freq
+    inverse = 1.0 / jnp.sqrt(alpha)
+    return (freq * freq * inverse, inverse, 2.0 * alpha, 2.0 * (freq / rate))
+
+
+def rho_kernel(place_ref, freq_ref, rate_ref, diag_ref, mate_ref, far_ref, col_scr, row_scr):
+    block = diag_ref.shape[0]
+    half = block // 2
+    tile = block // 4
+    own, mate, far, parity = place_ref[0], place_ref[1], place_ref[2], place_ref[3]
+    pad = jnp.zeros((4, block), F32)
+    for which, group in enumerate((own, mate, far)):
+        lanes = pl.ds(pl.multiple_of(group * block, block), block)
+        rows = jnp.concatenate(list(mode_rows(freq_ref[:, lanes], rate_ref[:, lanes])) + [pad], axis=0)
+        row_scr[which * 8 : which * 8 + 8, :] = rows
+        if which < 2:
+            col_scr[which * block : (which + 1) * block, 0:8] = rows.T
+
+    def fill(out_ref, lead, out_row, out_col, side_row, count, cols_at, col_off, width):
+        cols = [
+            jnp.broadcast_to(row_scr[cols_at + q : cols_at + q + 1, pl.ds(col_off, width)], (8, width))
+            for q in range(4)
+        ]
+
+        @pl.loop(0, count // 8, unroll=2)
+        def _(t):
+            at = pl.multiple_of(t * 8, 8)
+            side = col_scr[pl.ds(side_row + at, 8), 0:8]
+            high, low, alpha, zeta = (side[:, q : q + 1] for q in range(4))
+            spread = high * cols[1] - low * cols[0]
+            pair = alpha + cols[2]
+            bottom = spread * spread + pair * (zeta + cols[3])
+            value = pair / bottom
+            spot = pl.ds(out_row + at, 8)
+            if lead is None:
+                out_ref[spot, pl.ds(out_col, width)] = value
+            else:
+                out_ref[lead, spot, pl.ds(out_col, width)] = value
+
+    for j in range(4):
+        fill(diag_ref, None, 0, j * tile, 0, (j + 1) * tile, 0, j * tile, tile)
+    for i in range(2):
+        off = pl.multiple_of((i ^ parity) * half, half)
+        fill(mate_ref, i, 0, 0, i * half, half, 8, off, half)
+    for c in range(0, block, half):
+        fill(far_ref, None, 0, c, 0, 2 * block, 16, c, half)
+
+
+def forces_kernel(
+    place_ref, rim_ref, low_ref, high_ref, local_ref, stats_ref, spectral_ref, freq_ref, rate_ref,
+    all_ref, part_ref, rim_scr,
+):
+    comps, block = local_ref.shape
+    dims = spectral_ref.shape[0]
+    width = low_ref.shape[0] // dims
+    part = comps // 2
+    own, other = place_ref[0], place_ref[5]
+    lanes = pl.ds(pl.multiple_of(own * block, block), block)
+    scale = 2.0 * jnp.sqrt(freq_ref[:, lanes] / rate_ref[:, lanes])
+    amps = stats_ref[:dims, :] / stats_ref[dims : dims + 1, :] * spectral_ref[:, lanes] * scale
+    top = amps.astype(BF16)
+    rest = amps - top.astype(F32)
+    middle = rest.astype(BF16)
+    last = (rest - middle.astype(F32)).astype(BF16)
+    fill = jnp.zeros((AMP_ROWS - 3 * dims, block), F32)
+    stacked = jnp.concatenate(
+        [top.astype(F32), middle.astype(F32), last.astype(F32), fill], axis=0
+    ).astype(BF16)
+    all_ref[comps:, :] = stacked
+    part_ref[part:, :] = stacked
+    for d in range(dims):
+        for copy in range(2):
+            at = (copy * dims + d) * 2 * width
+            rim_scr[at : at + width, :] = low_ref[d * width : (d + 1) * width, :]
+            rim_scr[at + width : at + 2 * width, :] = high_ref[d * width : (d + 1) * width, :]
+    wide = 256
+
+    @pl.loop(0, block // wide)
+    def _(t):
+        spot = pl.ds(pl.multiple_of(t * wide, wide), wide)
+        total = local_ref[:, spot] + jnp.dot(rim_ref[...], rim_scr[:, spot], preferred_element_type=F32)
+        all_ref[:comps, spot] = total.astype(BF16)
+
+    part_ref[:part, :] = all_ref[pl.ds(pl.multiple_of(other * part, part), part), :]
+
+
+def read_amps(ref, base, dims):
+    rows = ref[base : base + AMP_ROWS, :].astype(F32)
+    amps = rows[:dims] + rows[dims : 2 * dims] + rows[2 * dims : 3 * dims]
+    return jnp.concatenate([amps, jnp.zeros((8 - dims, amps.shape[1]), F32)], axis=0)
+
+
+def fold(value):
+    total = value[:, :128]
+    for c in range(128, value.shape[1], 128):
+        total = total + value[:, c : c + 128]
+    return total
+
+
+def to_row(total):
+    ones = jnp.ones((8, total.shape[1]), F32)
+    return lax.dot_general(
+        ones, total, (((1,), (1,)), ((), ())),
+        precision=lax.Precision.HIGHEST, preferred_element_type=F32,
+    )[0:1]
+
+
+def weigh(rho, side, cols, dims):
+    pair = side[:, 0:1] * cols[0:1]
+    for d in range(1, dims):
+        pair = pair + side[:, d : d + 1] * cols[d : d + 1]
+    return (rho * pair).astype(BF16)
+
+
+def near_kernel(dims, place_ref, own_ref, mate_ref, diag_ref, cross_ref, out_ref, acc, side_scr, row_scr, w_scr):
+    comps, block = out_ref.shape[1], own_ref.shape[1]
+    tile = block // 4
+    half = block // 2
+    parity = place_ref[3]
+    own = read_amps(own_ref, comps, dims)
+    row_scr[0:8, :] = own
+    row_scr[8:16, :] = read_amps(mate_ref, comps, dims)
+    side_scr[:, 0:8] = own.T
+    turn = 0
+    for j in range(4):
+        cols = row_scr[0:8, j * tile : (j + 1) * tile]
+        for i in range(j + 1):
+            side = side_scr[i * tile : (i + 1) * tile, 0:8]
+            side = side * 2.0 if i < j else side
+            rho = diag_ref[i * tile : (i + 1) * tile, j * tile : (j + 1) * tile]
+            w_scr[turn, i * tile : (i + 1) * tile, :] = weigh(rho, side, cols, dims)
+        depth = (j + 1) * tile
+        got = jnp.dot(own_ref[:comps, :depth], w_scr[turn, :depth, :], preferred_element_type=F32)
+        got = fold(got * own_ref[:comps, j * tile : (j + 1) * tile].astype(F32))
+        acc[...] = got if j == 0 else acc[...] + got
+        turn = 1 - turn
+    for i in range(2):
+        for j in range(half // tile):
+            at = pl.multiple_of((i ^ parity) * half + j * tile, tile)
+            cols = row_scr[8:16, pl.ds(at, tile)]
+            side = side_scr[i * half : (i + 1) * half, 0:8] * 2.0
+            rho = cross_ref[i, :, j * tile : (j + 1) * tile]
+            w_scr[turn, :half, :] = weigh(rho, side, cols, dims)
+            got = jnp.dot(
+                own_ref[:comps, i * half : (i + 1) * half], w_scr[turn, :half, :], preferred_element_type=F32
+            )
+            acc[...] += fold(got * mate_ref[:comps, pl.ds(at, tile)].astype(F32))
+            turn = 1 - turn
+    out_ref[...] = to_row(acc[...])
+
+
+def far_kernel(dims, place_ref, own_ref, mate_ref, far_ref, rho_ref, near_ref, out_ref, acc, side_scr, w_scr):
+    comps, block = out_ref.shape[1], own_ref.shape[1]
+    part = comps // 2
+    tile = block // 4
+    here = place_ref[4]
+    rows = pl.ds(pl.multiple_of(here * part, part), part)
+    side_scr[:block, 0:8] = read_amps(own_ref, comps, dims).T * 2.0
+    side_scr[block:, 0:8] = read_amps(mate_ref, comps, dims).T * 2.0
+    far = read_amps(far_ref, part, dims)
+    for j in range(4):
+        turn = j % 2
+        spot = slice(j * tile, (j + 1) * tile)
+        cols = far[:, spot]
+        for i in range(2 * block // tile):
+            side = side_scr[i * tile : (i + 1) * tile, 0:8]
+            w_scr[turn, i * tile : (i + 1) * tile, :] = weigh(
+                rho_ref[i * tile : (i + 1) * tile, spot], side, cols, dims
+            )
+        got = jnp.dot(own_ref[rows, :], w_scr[turn, :block, :], preferred_element_type=F32)
+        got = got + jnp.dot(mate_ref[rows, :], w_scr[turn, block:, :], preferred_element_type=F32)
+        got = fold(got * far_ref[:part, spot].astype(F32))
+        acc[...] = got if j == 0 else acc[...] + got
+    cross = to_row(acc[...])
+    out_ref[...] = near_ref[...]
+    lanes = pl.ds(pl.multiple_of(here * part, part), part)
+    out_ref[:, lanes] = near_ref[:, lanes] + cross
+
+
+def four_groups(
+    shapes, masses, spectral, frequencies, damping, recovery, connectivity, node_count, shared
+):
+    dims, nodes, block = shapes.shape
+    elems, slots = connectivity.shape
+    per_elem = recovery.shape[1]
+    comps = elems * per_elem
+    part = comps // 2
+    width = shared.shape[1]
+    parts = lax.axis_size("dom")
+    group = lax.axis_index("mode").astype(jnp.int32)
+    place = jnp.stack(
+        [group, group ^ 1, group ^ 2, group & 1, group >> 1, 1 - (group >> 1)]
+    ).astype(jnp.int32)
+    sds = jax.ShapeDtypeStruct
+
+    picked = jnp.concatenate([shared[1], shared[0]]).reshape(1, 2 * width)
+    up, down = call(
+        gather_kernel,
+        (sds((dims * width, block), BF16), sds((dims * width, block), BF16)),
+        (picked, shapes), 2 * 2 * width * nodes * dims * block, 2 * dims * nodes * block,
+    )
+    ahead = [(i, i + 1) for i in range(parts - 1)]
+    back = [(i + 1, i) for i in range(parts - 1)]
+    low = lax.ppermute(up, "dom", ahead)
+    high = lax.ppermute(down, "dom", back)
+
+    stats = call(
+        stats_kernel, sds((dims + 1, block), F32), (masses.reshape(1, nodes), shapes),
+        5 * dims * nodes * block, 2 * dims * nodes * block,
+        scratch=[pltpu.VMEM((nodes, 128), F32)],
+    )
+    if parts & (parts - 1):
+        stats = lax.psum(stats, "dom")
+    else:
+        reach = 1
+        while reach < parts:
+            stats = stats + lax.ppermute(stats, "dom", [(i, i ^ reach) for i in range(parts)])
+            reach *= 2
+
+    used = jnp.where(jnp.arange(slots)[None, :] < node_count[:, None], connectivity, -1)
+    used = jnp.broadcast_to(used[:, None, :], (elems, per_elem, slots)).astype(F32)
+    table = jnp.concatenate(
+        [recovery.reshape(elems, per_elem, slots * dims).astype(F32), used], axis=-1
+    ).reshape(comps, slots * (dims + 1))
+    local, rim = call(
+        local_kernel,
+        (sds((comps, block), F32), sds((comps, 2 * dims * 2 * width), BF16)),
+        (table, shapes), 4 * comps * dims * nodes * block, 6 * dims * nodes * block,
+        scratch=[pltpu.VMEM((comps, 2 * dims * nodes), BF16)],
+    )
+    freq = frequencies.reshape(1, -1)
+    rate = damping.reshape(1, -1)
+    rho_diag, rho_mate, rho_far = call(
+        rho_kernel,
+        (sds((block, block), F32), sds((2, block // 2, block // 2), F32), sds((2 * block, block), F32)),
+        (place, freq, rate), 60 * block * block, 14 * block * block, smem=(0,),
+        scratch=[pltpu.VMEM((2 * block, 128), F32), pltpu.VMEM((24, block), F32)],
+    )
+    forces, sent = call(
+        forces_kernel,
+        (sds((comps + AMP_ROWS, block), BF16), sds((part + AMP_ROWS, block), BF16)),
+        (place, rim, low, high, local, stats, spectral, freq, rate),
+        8 * comps * dims * width * block, 8 * comps * block, smem=(0,),
+        scratch=[pltpu.VMEM((2 * dims * 2 * width, block), BF16)],
+    )
+    far = lax.ppermute(sent, "mode", [(i, i ^ 2) for i in range(4)])
+    mate = lax.ppermute(forces, "mode", [(i, i ^ 1) for i in range(4)])
+    near = call(
+        functools.partial(near_kernel, dims), sds((1, comps), F32),
+        (place, forces, mate, rho_diag, rho_mate), 2 * comps * block * block, 6 * block * block,
+        smem=(0,),
+        scratch=[
+            pltpu.VMEM((comps, 128), F32), pltpu.VMEM((block, 128), F32),
+            pltpu.VMEM((16, block), F32), pltpu.VMEM((2, block, block // 4), BF16),
+        ],
+    )
+    value = call(
+        functools.partial(far_kernel, dims), sds((1, comps), F32),
+        (place, forces, mate, far, rho_far, near), 2 * comps * block * block, 8 * block * block,
+        smem=(0,),
+        scratch=[
+            pltpu.VMEM((part, 128), F32), pltpu.VMEM((2 * block, 128), F32),
+            pltpu.VMEM((2, 2 * block, block // 4), BF16),
+        ],
+    )
+    return lax.psum(value.reshape(comps), "mode")
 
 
 def extended_2(block, sides, width):
@@ -64,7 +431,7 @@
     return jnp.sum(projected * far_wide[:, None, :], axis=(1, 2))
 
 
-def per_device(
+def any_groups(
     shapes, masses, spectral, frequencies, damping, recovery, connectivity, node_count, shared
 ):
     rim_width = shared.shape[1]
@@ -129,6 +496,7 @@
         P(None, "dom"),
     )
     out_specs = P("dom")
+    step = four_groups if mesh.shape["mode"] == 4 else any_groups
     return jax.shard_map(
-        per_device, mesh=mesh, in_specs=in_specs, out_specs=out_specs, check_vma=False
-    )
+        step, mesh=mesh, in_specs=in_specs, out_specs=out_specs, check_vma=False
+    )

time: 168 us -> 122 us (0.73)
  Pallas kernels: 0 us -> 85.6 us
  other arithmetic: 66.8 us -> 1.22 us
  blocking collectives: 54.9 us -> 6.66 us
  matrix products: 25.2 us -> 0 us
  starting transfers between devices: 7.93 us -> 15.6 us
  waiting for transfers between devices: 0.01 us -> 7.31 us
  local copies, waits for them, and re-layouts: 12.4 us -> 5.53 us
    pallas_call x0 -> x7, Pallas kernels: none -> 85.6 us  [call(): pl.pallas_call(kernel, out_shape=out_shape, in_specs=specs, out_specs=[VM...]
    psum x2 -> x1, blocking collectives: 49.5 us -> 6.66 us  [four_groups(): return lax.psum(value.reshape(comps), 'mode')]
    dot_general x4 -> x0, matrix products: 25.2 us -> none  [the longest x3 20.5 us: block_terms(): projected = jnp.dot(own_forces, weights, preferred_element_type=jnp.float32)]
    convert_element_type x6 -> x1, other arithmetic: 24.3 us -> 0.01 us  [four_groups(): jnp.broadcast_to(used[:, None, :], (elems, per_elem, slots)).astype(F32)]
    mul x9 -> x0, other arithmetic: 19.3 us -> none  [the longest x3 18.5 us: block_terms(): amp_rows.T[:, :, None] * correlation[:, None, :] * amp_cols[None, :, :]]
    div x3 -> x0, other arithmetic: 14.8 us -> none  [correlation_block(): return top_part / bottom_part]
    gather x3 -> x0, local copies, waits for them, and re-layouts: 7.73 us -> none  [the longest x1 3.55 us: per_device(): jnp.take(node_table, connectivity.reshape(-1), axis=1)]
    ppermute x4 -> x7, starting transfers between devices: 7.93 us -> 15.6 us  [the longest x3 10.9 us: four_groups(): lax.ppermute(stats, 'dom', [(i, i ^ reach) for i in range(parts)])]
  transfers between devices with their start and end apart: 4 -> 7, of which waited for: 0 -> 1; matrix products, arithmetic and copies ran while one was open for 38% -> 3% of each run, Pallas kernels for 0% -> 56%
where the time goes in v1:
time: 122 us
  Pallas kernels  85.6 us (70%)
  starting transfers between devices  15.6 us (13%)
  waiting for transfers between devices  7.31 us (6%)
  blocking collectives  6.66 us (5%)
  local copies, waits for them, and re-layouts  5.53 us (5%)
  other arithmetic  1.22 us (1%)
    pallas_call x7, Pallas kernels, call(): pl.pallas_call(kernel, out_shape=out_shape, in_specs=specs, out_specs=[VM...  85.6 us
    ppermute x3, starting transfers between devices, four_groups(): lax.ppermute(stats, 'dom', [(i, i ^ reach) for i in range(parts)])  10.9 us
    ppermute x3, waiting for transfers between devices, four_groups(): lax.ppermute(stats, 'dom', [(i, i ^ reach) for i in range(parts)])  7.3 us
    psum x1, blocking collectives, four_groups(): return lax.psum(value.reshape(comps), 'mode')  6.66 us
    unnamed x16, local copies, waits for them, and re-layouts  2.72 us
  transfers between devices with their start and end apart: 7, of which 1 were waited for; matrix products, arithmetic and copies ran while one was open for 3% of the time, Pallas kernels for 56%

profile of v1, /device:TPU:0, one launch (start us, length us, event | category | flops | bytes accessed | tf_op | source)
XLA Modules:
  0.0 122.1 jit_solution(15140144773922231317)
XLA Ops:
  0.0 0.0 copy-start.7
  0.0 0.0 copy-start.6
  0.0 0.0 copy-start.5
  0.0 3.0 %shard_map.93 = f32[4,1024]{1,0:T(4,128)} custom-call(f32[1,256]{1,0:T(1,128)} %bitcast.27, bf16[3,256,1024]{2,1,0:T(8,128)(2,1)} %shapes_ref.5), custom_call_target="tpu_custom_call" | custom-call | flops 3932160 | bytes 1572864 | tf_op jit(solution)/shard_map/pallas_call | solution.py:19
  3.0 0.0 copy-start.4
  3.0 3.0 %collective-permute-start.2 = (f32[4,1024]{1,0:T(4,128)}, f32[4,1024]{1,0:T(4,128)S(1)}, u32[]{:S(2)}, u32[]{:S(2)}) collective-permute-start(f32[4,1024]{1,0:T(4,128)} %shard_map.93), channel_id=1, source_target_pairs={{0,4},{4,0},{8,12},{12,8},{16,20},{20,16},{24,28},{28,24},{1,5},{5... | collective-permute-start | bytes 49160 | tf_op jit(solution)/shard_map/ppermute | solution.py:322
  6.0 0.8 slice_bitcast_fusion.1
  6.7 0.6 add_bitcast_fusion.rows_ref
  7.3 2.7 %shard_map.92 = (bf16[192,1024]{1,0:T(8,128)(2,1)}, bf16[192,1024]{1,0:T(8,128)(2,1)}) custom-call(s32[1,128]{1,0:T(1,128)} %add_bitcast_fusion.rows_ref, bf16[3,256,1024]{2,1,0:T(8,128)(2,1)} %shapes_ref.5), custom_call_target="tpu_custom_call" | custom-call | flops 201326592 | bytes 1572864 | tf_op jit(solution)/shard_map/pallas_call | solution.py:19
  10.0 1.9 %collective-permute-start = (bf16[192,1024]{1,0:T(8,128)(2,1)}, bf16[192,1024]{1,0:T(8,128)(2,1)S(1)}, u32[]{:S(2)}, u32[]{:S(2)}) collective-permute-start(bf16[192,1024]{1,0:T(8,128)(2,1)} %get-tuple-element.15), channel_id=1, source_target_pairs={{0,4},{4,8},{8,12},{12,16},{16,20},{20,24},{24,28},{1,5},{5,9},{9,... | collective-permute-start | bytes 1179656 | tf_op jit(solution)/shard_map/ppermute | solution.py:309
  11.9 1.3 %collective-permute-start.1 = (bf16[192,1024]{1,0:T(8,128)(2,1)}, bf16[192,1024]{1,0:T(8,128)(2,1)S(1)}, u32[]{:S(2)}, u32[]{:S(2)}) collective-permute-start(bf16[192,1024]{1,0:T(8,128)(2,1)} %get-tuple-element.16), channel_id=1, source_target_pairs={{4,0},{8,4},{12,8},{16,12},{20,16},{24,20},{28,24},{5,1},{9,5},{13... | collective-permute-start | bytes 1179656 | tf_op jit(solution)/shard_map/ppermute | solution.py:310
  13.2 0.0 copy-done.7
  13.2 0.0 copy-done.6
  13.3 0.1 broadcast_in_dim.7
  13.4 0.1 concatenate.9
  13.5 0.0 copy-done.5
  13.5 0.1 copy.17
  13.6 0.2 reshape.29
  13.8 0.0 collective-permute-done.2
  13.9 0.0 copy-done.4
  13.9 5.2 %collective-permute-start.3 = (f32[4,1024]{1,0:T(4,128)S(1)}, f32[4,1024]{1,0:T(4,128)S(1)}, u32[]{:S(2)}, u32[]{:S(2)}) collective-permute-start(f32[4,1024]{1,0:T(4,128)S(1)} %add.11), channel_id=1, source_target_pairs={{0,8},{4,12},{8,0},{12,4},{16,24},{20,28},{24,16},{28,20},{1,9},{5... | collective-permute-start | bytes 49160 | tf_op jit(solution)/shard_map/ppermute | solution.py:322
  19.0 0.8 copy.18.table_ref
  19.9 7.3 %collective-permute-done.3 = f32[4,1024]{1,0:T(4,128)S(1)} collective-permute-done((f32[4,1024]{1,0:T(4,128)S(1)}, f32[4,1024]{1,0:T(4,128)S(1)}, u32[]{:S(2)}, u32[]{:S(2)}) %collective-permute-start.3) | collective-permute-done | bytes 16416 | tf_op jit(solution)/shard_map/ppermute | solution.py:322
  27.2 2.8 %collective-permute-start.4 = (f32[4,1024]{1,0:T(4,128)S(1)}, f32[4,1024]{1,0:T(4,128)S(1)}, u32[]{:S(2)}, u32[]{:S(2)}) collective-permute-start(f32[4,1024]{1,0:T(4,128)S(1)} %add.12), channel_id=1, source_target_pairs={{0,16},{4,20},{8,24},{12,28},{16,0},{20,4},{24,8},{28,12},{1,17},{... | collective-permute-start | bytes 49160 | tf_op jit(solution)/shard_map/ppermute | solution.py:322
  30.0 7.9 %shard_map.91 = (f32[512,1024]{1,0:T(8,128)}, bf16[512,768]{1,0:T(8,128)(2,1)}) custom-call(f32[512,16]{1,0:T(8,128)} %copy.18.table_ref, bf16[3,256,1024]{2,1,0:T(8,128)(2,1)} %shapes_ref.5), custom_call_target="tpu_custom_call" | custom-call | flops 1610612736 | bytes 4718592 | tf_op jit(solution)/shard_map/pallas_call | solution.py:19
  37.8 0.7 stack.27.place_ref
  38.5 0.0 collective-permute-done.4
  38.5 0.6 add.13.stats_ref
  39.1 0.0 collective-permute-done.low_ref
  39.1 0.0 copy-start.2
  39.1 0.0 collective-permute-done.1.high_ref
  39.1 0.0 copy-start.3
  39.1 0.8 copy-done.2
  39.9 0.1 copy-done.3
  40.0 4.9 %shard_map.94 = (bf16[528,1024]{1,0:T(8,128)(2,1)}, bf16[272,1024]{1,0:T(8,128)(2,1)}) custom-call(s32[6]{0:T(128)} %stack.27.place_ref, bf16[512,768]{1,0:T(8,128)(2,1)} %get-tuple-element.14.rim_ref, bf16[192,1024]{1,0:T(8,128)(2,1)} %copy-done.2, bf16[192,1024]{1,0:T(8,128)(2,1)} %copy-done.3, f32[512,1024]{1,0:T(8,128)} %get-tuple-element.17.local_ref, ...), custom_call_target="tpu_custom_call" | custom-call | flops 805306368 | bytes 4194304 | tf_op jit(solution)/shard_map/pallas_call | solution.py:19
  44.9 0.0 collective-permute-start.5
  44.9 1.5 %collective-permute-start.6 = (bf16[272,1024]{1,0:T(8,128)(2,1)}, bf16[272,1024]{1,0:T(8,128)(2,1)S(1)}, u32[]{:S(2)}, u32[]{:S(2)}) collective-permute-start(bf16[272,1024]{1,0:T(8,128)(2,1)} %get-tuple-element.19), channel_id=1, source_target_pairs={{0,2},{1,3},{2,0},{3,1},{4,6},{5,7},{6,4},{7,5},{8,10},{9,11},{10,... | collective-permute-start | bytes 1671176 | tf_op jit(solution)/shard_map/ppermute | solution.py:351
  46.4 49.7 %shard_map.95 = (f32[1024,1024]{1,0:T(8,128)}, f32[2,512,512]{2,1,0:T(8,128)}, f32[2048,1024]{1,0:T(8,128)}) custom-call(s32[6]{0:T(128)} %stack.27.place_ref, f32[1,4096]{1,0:T(1,128)} %bitcast.23, f32[1,4096]{1,0:T(1,128)} %bitcast.25), custom_call_target="tpu_custom_call" | custom-call | flops 62914560 | bytes 14680064 | tf_op jit(solution)/shard_map/pallas_call | solution.py:19
  96.1 0.0 collective-permute-done.5.mate_ref
  96.1 0.0 copy-start
  96.1 1.0 copy-done
  97.0 7.7 %shard_map.96.near_ref = f32[1,512]{1,0:T(1,128)} custom-call(s32[6]{0:T(128)} %stack.27.place_ref, bf16[528,1024]{1,0:T(8,128)(2,1)} %get-tuple-element.18.own_ref, bf16[528,1024]{1,0:T(8,128)(2,1)} %copy-done, f32[1024,1024]{1,0:T(8,128)} %get-tuple-element.21.diag_ref, f32[2,512,512]{2,1,0:T(8,128)} %get-tuple-element.22.cross_ref), custom_call_target="tpu_custom_call" | custom-call | flops 1073741824 | bytes 6291456 | tf_op jit(solution)/shard_map/pallas_call | solution.py:19
  104.7 0.0 collective-permute-done.6.far_ref
  104.7 0.0 copy-start.1
  104.7 0.8 copy-done.1
  105.6 9.8 %shard_map.97 = f32[1,512]{1,0:T(1,128)} custom-call(s32[6]{0:T(128)} %stack.27.place_ref, bf16[528,1024]{1,0:T(8,128)(2,1)} %get-tuple-element.18.own_ref, bf16[528,1024]{1,0:T(8,128)(2,1)} %copy-done, bf16[272,1024]{1,0:T(8,128)(2,1)} %copy-done.1, f32[2048,1024]{1,0:T(8,128)} %get-tuple-element.20.rho_ref, f32[1,512]{1,0:T(1,128)} %shard_map.96.near_ref), custom_call_target="tpu_custom_call" | custom-call | flops 1073741824 | bytes 8388608 | tf_op jit(solution)/shard_map/pallas_call | solution.py:19
  115.4 6.7 %psum.7 = f32[512]{0:T(512)} all-reduce(f32[512]{0:T(512)} %bitcast.26), channel_id=1, replica_groups=mesh['dom'=8,'mode'=4] {'mode'}, use_global_device_ids=true, to_apply=%region_0.1 | all-reduce | flops 512 | bytes 4096 | tf_op jit(solution)/shard_map/psum | solution.py:371
  (4 shorter events, 0.0 us)
Async XLA Ops:
  0.0 13.2 %copy-start.7 = (s32[64]{0:T(128)S(1)}, s32[64]{0:T(128)}, u32[]{:S(2)}) copy-start(s32[64]{0:T(128)} %param.16) | copy-start | bytes 772
  0.0 13.2 %copy-start.6 = (s32[64,4]{0,1:T(4,128)S(1)}, s32[64,4]{0,1:T(4,128)}, u32[]{:S(2)}) copy-start(s32[64,4]{0,1:T(4,128)} %param.15) | copy-start | bytes 3076
  0.0 13.5 %copy-start.5 = (bf16[64,8,4,3]{0,2,3,1:T(4,128)(2,1)S(1)}, bf16[64,8,4,3]{0,2,3,1:T(4,128)(2,1)}, u32[]{:S(2)}) copy-start(bf16[64,8,4,3]{0,2,3,1:T(4,128)(2,1)} %param.14) | copy-start | bytes 36868
  3.0 10.9 %copy-start.4 = (f32[4,1024]{1,0:T(4,128)S(1)}, f32[4,1024]{1,0:T(4,128)}, u32[]{:S(2)}) copy-start(f32[4,1024]{1,0:T(4,128)} %shard_map.93) | copy-start | bytes 49156
  3.0 10.9 %collective-permute-start.2 = (f32[4,1024]{1,0:T(4,128)}, f32[4,1024]{1,0:T(4,128)S(1)}, u32[]{:S(2)}, u32[]{:S(2)}) collective-permute-start(f32[4,1024]{1,0:T(4,128)} %shard_map.93), channel_id=1, source_target_pairs={{0,4},{4,0},{8,12},{12,8},{16,20},{20,16},{24,28},{28,24},{1,5},{5... | collective-permute-start | bytes 49160 | tf_op jit(solution)/shard_map/ppermute | solution.py:322
  10.0 29.1 %collective-permute-start = (bf16[192,1024]{1,0:T(8,128)(2,1)}, bf16[192,1024]{1,0:T(8,128)(2,1)S(1)}, u32[]{:S(2)}, u32[]{:S(2)}) collective-permute-start(bf16[192,1024]{1,0:T(8,128)(2,1)} %get-tuple-element.15), channel_id=1, source_target_pairs={{0,4},{4,8},{8,12},{12,16},{16,20},{20,24},{24,28},{1,5},{5,9},{9,... | collective-permute-start | bytes 1179656 | tf_op jit(solution)/shard_map/ppermute | solution.py:309
  11.9 27.2 %collective-permute-start.1 = (bf16[192,1024]{1,0:T(8,128)(2,1)}, bf16[192,1024]{1,0:T(8,128)(2,1)S(1)}, u32[]{:S(2)}, u32[]{:S(2)}) collective-permute-start(bf16[192,1024]{1,0:T(8,128)(2,1)} %get-tuple-element.16), channel_id=1, source_target_pairs={{4,0},{8,4},{12,8},{16,12},{20,16},{24,20},{28,24},{5,1},{9,5},{13... | collective-permute-start | bytes 1179656 | tf_op jit(solution)/shard_map/ppermute | solution.py:310
  13.9 13.3 %collective-permute-start.3 = (f32[4,1024]{1,0:T(4,128)S(1)}, f32[4,1024]{1,0:T(4,128)S(1)}, u32[]{:S(2)}, u32[]{:S(2)}) collective-permute-start(f32[4,1024]{1,0:T(4,128)S(1)} %add.11), channel_id=1, source_target_pairs={{0,8},{4,12},{8,0},{12,4},{16,24},{20,28},{24,16},{28,20},{1,9},{5... | collective-permute-start | bytes 49160 | tf_op jit(solution)/shard_map/ppermute | solution.py:322
  27.2 11.3 %collective-permute-start.4 = (f32[4,1024]{1,0:T(4,128)S(1)}, f32[4,1024]{1,0:T(4,128)S(1)}, u32[]{:S(2)}, u32[]{:S(2)}) collective-permute-start(f32[4,1024]{1,0:T(4,128)S(1)} %add.12), channel_id=1, source_target_pairs={{0,16},{4,20},{8,24},{12,28},{16,0},{20,4},{24,8},{28,12},{1,17},{... | collective-permute-start | bytes 49160 | tf_op jit(solution)/shard_map/ppermute | solution.py:322
  39.1 0.8 copy-start.2
  39.1 0.9 copy-start.3
  44.9 51.2 %collective-permute-start.5 = (bf16[528,1024]{1,0:T(8,128)(2,1)}, bf16[528,1024]{1,0:T(8,128)(2,1)S(1)}, u32[]{:S(2)}, u32[]{:S(2)}) collective-permute-start(bf16[528,1024]{1,0:T(8,128)(2,1)} %get-tuple-element.18.own_ref), channel_id=1, source_target_pairs={{0,1},{1,0},{2,3},{3,2},{4,5},{5,4},{6,7},{7,6},{8,9},{9,8},{10,11... | collective-permute-start | bytes 3244040 | tf_op jit(solution)/shard_map/ppermute | solution.py:352
  44.9 59.8 %collective-permute-start.6 = (bf16[272,1024]{1,0:T(8,128)(2,1)}, bf16[272,1024]{1,0:T(8,128)(2,1)S(1)}, u32[]{:S(2)}, u32[]{:S(2)}) collective-permute-start(bf16[272,1024]{1,0:T(8,128)(2,1)} %get-tuple-element.19), channel_id=1, source_target_pairs={{0,2},{1,3},{2,0},{3,1},{4,6},{5,7},{6,4},{7,5},{8,10},{9,11},{10,... | collective-permute-start | bytes 1671176 | tf_op jit(solution)/shard_map/ppermute | solution.py:351
  96.1 1.0 copy-start
  104.7 0.9 copy-start.1

commit v2 on v1

--- a/solution.py
+++ b/solution.py
@@ -13,18 +13,25 @@
 AMP_ROWS = 16
 
 
-def call(kernel, out_shape, args, flops, nbytes, smem=(), scratch=(), vmem=None):
-    specs = [SMEM if i in smem else VMEM for i in range(len(args))]
+def call(kernel, out_shape, args, flops, nbytes, smem=(), scratch=(), vmem=24 << 20, after=()):
+    count = len(args)
+    specs = [SMEM if i in smem else VMEM for i in range(count)]
+    specs += [pl.BlockSpec(memory_space=pl.ANY)] * len(after)
     many = isinstance(out_shape, (tuple, list))
+
+    def body(*refs):
+        kernel(*refs[:count], *refs[count + len(after) :])
+
     return pl.pallas_call(
-        kernel,
+        body,
         out_shape=out_shape,
         in_specs=specs,
         out_specs=[VMEM] * len(out_shape) if many else VMEM,
         scratch_shapes=list(scratch),
         cost_estimate=pl.CostEstimate(flops=flops, bytes_accessed=nbytes, transcendentals=0),
         compiler_params=pltpu.CompilerParams(vmem_limit_bytes=vmem),
-    )(*args)
+        name=getattr(kernel, "func", kernel).__name__,
+    )(*args, *after)
 
 
 def gather_kernel(rows_ref, shapes_ref, up_ref, down_ref):
@@ -60,15 +67,15 @@
         out_ref[dims : dims + 1, lanes] = jnp.sum(general, axis=0, keepdims=True)
 
 
-def local_kernel(table_ref, shapes_ref, local_ref, rim_ref, own_scr):
-    dims, nodes, block = shapes_ref.shape
+def local_kernel(dims, table_ref, shapes_ref, local_ref, rim_ref, own_scr):
+    nodes, block = shapes_ref.shape[0] // dims, shapes_ref.shape[1]
     comps = table_ref.shape[0]
     slots = table_ref.shape[1] // (dims + 1)
     rim = rim_ref.shape[1] // (2 * dims)
     span = nodes + rim
     step = 32
 
-    @pl.loop(0, comps // step)
+    @pl.loop(0, comps // step, unroll=2)
     def _(t):
         rows = pl.ds(pl.multiple_of(t * step, step), step)
         table = table_ref[rows, :]
@@ -82,24 +89,16 @@
         for d in range(dims):
             high = total[d].astype(BF16)
             low = (total[d] - high.astype(F32)).astype(BF16)
-            own_scr[rows, d * nodes : (d + 1) * nodes] = high[:, :nodes]
-            own_scr[rows, (dims + d) * nodes : (dims + d + 1) * nodes] = low[:, :nodes]
+            own_scr[0, rows, d * nodes : (d + 1) * nodes] = high[:, :nodes]
+            own_scr[1, rows, d * nodes : (d + 1) * nodes] = low[:, :nodes]
             rim_ref[rows, d * rim : (d + 1) * rim] = high[:, nodes:]
             rim_ref[rows, (dims + d) * rim : (dims + d + 1) * rim] = low[:, nodes:]
 
     wide = 256
-
-    @pl.loop(0, block // wide)
-    def _(t):
-        lanes = pl.ds(pl.multiple_of(t * wide, wide), wide)
-        total = jnp.zeros((comps, wide), F32)
-        for half in range(2):
-            for d in range(dims):
-                at = (half * dims + d) * nodes
-                total += jnp.dot(
-                    own_scr[:, at : at + nodes], shapes_ref[d, :, lanes], preferred_element_type=F32
-                )
-        local_ref[:, lanes] = total
+    for c in range(0, block, wide):
+        total = jnp.dot(own_scr[0], shapes_ref[:, c : c + wide], preferred_element_type=F32)
+        total = total + jnp.dot(own_scr[1], shapes_ref[:, c : c + wide], preferred_element_type=F32)
+        local_ref[:, c : c + wide] = total
 
 
 def mode_rows(freq, rate):
@@ -108,47 +107,60 @@
     return (freq * freq * inverse, inverse, 2.0 * alpha, 2.0 * (freq / rate))
 
 
-def rho_kernel(place_ref, freq_ref, rate_ref, diag_ref, mate_ref, far_ref, col_scr, row_scr):
+def place_modes(freq_ref, rate_ref, row_scr, col_scr, groups, sides, block):
+    for which, group in enumerate(groups):
+        lanes = pl.ds(pl.multiple_of(group * block, block), block)
+        rows = jnp.concatenate(list(mode_rows(freq_ref[:, lanes], rate_ref[:, lanes])) * 2, axis=0)
+        row_scr[which * 8 : which * 8 + 8, :] = rows
+        if which < sides:
+            turned = rows.T
+            for q in range(4):
+                col_scr[q, which * block : (which + 1) * block, :] = jnp.broadcast_to(
+                    turned[:, q : q + 1], (block, 128)
+                )
+
+
+def fill_rho(row_scr, col_scr, out_ref, out_col, side_row, count, cols_at, col_off, tile):
+    step = 64
+    cols = [
+        jnp.broadcast_to(row_scr[cols_at + q : cols_at + q + 1, pl.ds(col_off, tile)], (8, tile))
+        for q in range(4)
+    ]
+
+    @pl.loop(0, count // step)
+    def _(t):
+        for k in range(0, step, 8):
+            at = pl.multiple_of(t * step, step) + k
+            high, low, alpha, zeta = (col_scr[q, pl.ds(side_row + at, 8), :] for q in range(4))
+            for c in range(0, tile, 128):
+                col = [value[:, c : c + 128] for value in cols]
+                spread = high * col[1] - low * col[0]
+                pair = alpha + col[2]
+                bottom = spread * spread + pair * (zeta + col[3])
+                out_ref[pl.ds(at, 8), out_col + c : out_col + c + 128] = pair / bottom
+
+
+def rho_near_kernel(place_ref, freq_ref, rate_ref, diag_ref, mate_ref, col_scr, row_scr):
     block = diag_ref.shape[0]
     half = block // 2
     tile = block // 4
-    own, mate, far, parity = place_ref[0], place_ref[1], place_ref[2], place_ref[3]
-    pad = jnp.zeros((4, block), F32)
-    for which, group in enumerate((own, mate, far)):
-        lanes = pl.ds(pl.multiple_of(group * block, block), block)
-        rows = jnp.concatenate(list(mode_rows(freq_ref[:, lanes], rate_ref[:, lanes])) + [pad], axis=0)
-        row_scr[which * 8 : which * 8 + 8, :] = rows
-        if which < 2:
-            col_scr[which * block : (which + 1) * block, 0:8] = rows.T
-
-    def fill(out_ref, lead, out_row, out_col, side_row, count, cols_at, col_off, width):
-        cols = [
-            jnp.broadcast_to(row_scr[cols_at + q : cols_at + q + 1, pl.ds(col_off, width)], (8, width))
-            for q in range(4)
-        ]
-
-        @pl.loop(0, count // 8, unroll=2)
-        def _(t):
-            at = pl.multiple_of(t * 8, 8)
-            side = col_scr[pl.ds(side_row + at, 8), 0:8]
-            high, low, alpha, zeta = (side[:, q : q + 1] for q in range(4))
-            spread = high * cols[1] - low * cols[0]
-            pair = alpha + cols[2]
-            bottom = spread * spread + pair * (zeta + cols[3])
-            value = pair / bottom
-            spot = pl.ds(out_row + at, 8)
-            if lead is None:
-                out_ref[spot, pl.ds(out_col, width)] = value
-            else:
-                out_ref[lead, spot, pl.ds(out_col, width)] = value
-
+    own, mate, parity = place_ref[0], place_ref[1], place_ref[3]
+    place_modes(freq_ref, rate_ref, row_scr, col_scr, (own, mate), 1, block)
     for j in range(4):
-        fill(diag_ref, None, 0, j * tile, 0, (j + 1) * tile, 0, j * tile, tile)
+        fill_rho(row_scr, col_scr, diag_ref, j * tile, 0, (j + 1) * tile, 0, j * tile, tile)
     for i in range(2):
-        off = pl.multiple_of((i ^ parity) * half, half)
-        fill(mate_ref, i, 0, 0, i * half, half, 8, off, half)
-    for c in range(0, block, half):
-        fill(far_ref, None, 0, c, 0, 2 * block, 16, c, half)
+        for j in range(2):
+            off = pl.multiple_of((i ^ parity) * half + j * tile, tile)
+            fill_rho(row_scr, col_scr, mate_ref.at[i], j * tile, i * half, half, 8, off, tile)
+
+
+def rho_far_kernel(place_ref, freq_ref, rate_ref, far_ref, col_scr, row_scr):
+    block = far_ref.shape[1]
+    tile = block // 4
+    own, mate, far = place_ref[0], place_ref[1], place_ref[2]
+    place_modes(freq_ref, rate_ref, row_scr, col_scr, (own, mate, far), 2, block)
+    for j in range(4):
+        fill_rho(row_scr, col_scr, far_ref, j * tile, 0, 2 * block, 16, j * tile, tile)
 
 
 def forces_kernel(
@@ -179,10 +191,8 @@
             rim_scr[at : at + width, :] = low_ref[d * width : (d + 1) * width, :]
             rim_scr[at + width : at + 2 * width, :] = high_ref[d * width : (d + 1) * width, :]
     wide = 256
-
-    @pl.loop(0, block // wide)
-    def _(t):
-        spot = pl.ds(pl.multiple_of(t * wide, wide), wide)
+    for c in range(0, block, wide):
+        spot = slice(c, c + wide)
         total = local_ref[:, spot] + jnp.dot(rim_ref[...], rim_scr[:, spot], preferred_element_type=F32)
         all_ref[:comps, spot] = total.astype(BF16)
 
@@ -210,11 +220,20 @@
     )[0:1]
 
 
-def weigh(rho, side, cols, dims):
-    pair = side[:, 0:1] * cols[0:1]
-    for d in range(1, dims):
-        pair = pair + side[:, d : d + 1] * cols[d : d + 1]
-    return (rho * pair).astype(BF16)
+def spread_sides(side_scr, at, amps, dims):
+    sides = amps.T
+    for d in range(dims):
+        side_scr[d, at : at + amps.shape[1], :] = jnp.broadcast_to(sides[:, d : d + 1], (amps.shape[1], 128))
+
+
+def weigh(w_scr, turn, at, rho, side_scr, side_at, cols, dims, factor):
+    for c in range(0, rho.shape[1], 128):
+        col = [jnp.broadcast_to(cols[d : d + 1, c : c + 128] * factor, (16, 128)) for d in range(dims)]
+        for r in range(0, rho.shape[0], 16):
+            pair = side_scr[0, side_at + r : side_at + r + 16, :] * col[0]
+            for d in range(1, dims):
+                pair = pair + side_scr[d, side_at + r : side_at + r + 16, :] * col[d]
+            w_scr[turn, at + r : at + r + 16, c : c + 128] = (rho[r : r + 16, c : c + 128] * pair).astype(BF16)
 
 
 def near_kernel(dims, place_ref, own_ref, mate_ref, diag_ref, cross_ref, out_ref, acc, side_scr, row_scr, w_scr):
@@ -225,15 +244,13 @@
     own = read_amps(own_ref, comps, dims)
     row_scr[0:8, :] = own
     row_scr[8:16, :] = read_amps(mate_ref, comps, dims)
-    side_scr[:, 0:8] = own.T
+    spread_sides(side_scr, 0, own, dims)
     turn = 0
     for j in range(4):
         cols = row_scr[0:8, j * tile : (j + 1) * tile]
         for i in range(j + 1):
-            side = side_scr[i * tile : (i + 1) * tile, 0:8]
-            side = side * 2.0 if i < j else side
-            rho = diag_ref[i * tile : (i + 1) * tile, j * tile : (j + 1) * tile]
-            w_scr[turn, i * tile : (i + 1) * tile, :] = weigh(rho, side, cols, dims)
+            rho = diag_ref.at[i * tile : (i + 1) * tile, j * tile : (j + 1) * tile]
+            weigh(w_scr, turn, i * tile, rho, side_scr, i * tile, cols, dims, 2.0 if i < j else 1.0)
         depth = (j + 1) * tile
         got = jnp.dot(own_ref[:comps, :depth], w_scr[turn, :depth, :], preferred_element_type=F32)
         got = fold(got * own_ref[:comps, j * tile : (j + 1) * tile].astype(F32))
@@ -243,9 +260,8 @@
         for j in range(half // tile):
             at = pl.multiple_of((i ^ parity) * half + j * tile, tile)
             cols = row_scr[8:16, pl.ds(at, tile)]
-            side = side_scr[i * half : (i + 1) * half, 0:8] * 2.0
-            rho = cross_ref[i, :, j * tile : (j + 1) * tile]
-            w_scr[turn, :half, :] = weigh(rho, side, cols, dims)
+            rho = cross_ref.at[i, :, j * tile : (j + 1) * tile]
+            weigh(w_scr, turn, 0, rho, side_scr, i * half, cols, dims, 2.0)
             got = jnp.dot(
                 own_ref[:comps, i * half : (i + 1) * half], w_scr[turn, :half, :], preferred_element_type=F32
             )
@@ -260,18 +276,14 @@
     tile = block // 4
     here = place_ref[4]
     rows = pl.ds(pl.multiple_of(here * part, part), part)
-    side_scr[:block, 0:8] = read_amps(own_ref, comps, dims).T * 2.0
-    side_scr[block:, 0:8] = read_amps(mate_ref, comps, dims).T * 2.0
+    spread_sides(side_scr, 0, read_amps(own_ref, comps, dims), dims)
+    spread_sides(side_scr, block, read_amps(mate_ref, comps, dims), dims)
     far = read_amps(far_ref, part, dims)
     for j in range(4):
         turn = j % 2
         spot = slice(j * tile, (j + 1) * tile)
         cols = far[:, spot]
-        for i in range(2 * block // tile):
-            side = side_scr[i * tile : (i + 1) * tile, 0:8]
-            w_scr[turn, i * tile : (i + 1) * tile, :] = weigh(
-                rho_ref[i * tile : (i + 1) * tile, spot], side, cols, dims
-            )
+        weigh(w_scr, turn, 0, rho_ref.at[:, spot], side_scr, 0, cols, dims, 2.0)
         got = jnp.dot(own_ref[rows, :], w_scr[turn, :block, :], preferred_element_type=F32)
         got = got + jnp.dot(mate_ref[rows, :], w_scr[turn, block:, :], preferred_element_type=F32)
         got = fold(got * far_ref[:part, spot].astype(F32))
@@ -312,15 +324,19 @@
     stats = call(
         stats_kernel, sds((dims + 1, block), F32), (masses.reshape(1, nodes), shapes),
         5 * dims * nodes * block, 2 * dims * nodes * block,
-        scratch=[pltpu.VMEM((nodes, 128), F32)],
-    )
+        scratch=[pltpu.VMEM((nodes, 128), F32)], after=(up,),
+    )
+    steps = [stats]
     if parts & (parts - 1):
         stats = lax.psum(stats, "dom")
+        steps += [stats, stats]
     else:
         reach = 1
         while reach < parts:
             stats = stats + lax.ppermute(stats, "dom", [(i, i ^ reach) for i in range(parts)])
+            steps.append(stats)
             reach *= 2
+    steps += [stats] * 2
 
     used = jnp.where(jnp.arange(slots)[None, :] < node_count[:, None], connectivity, -1)
     used = jnp.broadcast_to(used[:, None, :], (elems, per_elem, slots)).astype(F32)
@@ -328,25 +344,32 @@
         [recovery.reshape(elems, per_elem, slots * dims).astype(F32), used], axis=-1
     ).reshape(comps, slots * (dims + 1))
     local, rim = call(
-        local_kernel,
+        functools.partial(local_kernel, dims),
         (sds((comps, block), F32), sds((comps, 2 * dims * 2 * width), BF16)),
-        (table, shapes), 4 * comps * dims * nodes * block, 6 * dims * nodes * block,
-        scratch=[pltpu.VMEM((comps, 2 * dims * nodes), BF16)],
+        (table, shapes.reshape(dims * nodes, block)), 4 * comps * dims * nodes * block, 6 * dims * nodes * block,
+        scratch=[pltpu.VMEM((2, comps, dims * nodes), BF16)],
     )
     freq = frequencies.reshape(1, -1)
     rate = damping.reshape(1, -1)
-    rho_diag, rho_mate, rho_far = call(
-        rho_kernel,
-        (sds((block, block), F32), sds((2, block // 2, block // 2), F32), sds((2 * block, block), F32)),
-        (place, freq, rate), 60 * block * block, 14 * block * block, smem=(0,),
-        scratch=[pltpu.VMEM((2 * block, 128), F32), pltpu.VMEM((24, block), F32)],
+    rho_diag, rho_mate = call(
+        rho_near_kernel,
+        (sds((block, block), F32), sds((2, block // 2, block // 2), F32)),
+        (place, freq, rate), 20 * block * block, 5 * block * block, smem=(0,),
+        scratch=[pltpu.VMEM((4, block, 128), F32), pltpu.VMEM((16, block), F32)],
+        after=(steps[1],),
+    )
+    rho_far = call(
+        rho_far_kernel, sds((2 * block, block), F32), (place, freq, rate),
+        40 * block * block, 8 * block * block, smem=(0,),
+        scratch=[pltpu.VMEM((4, 2 * block, 128), F32), pltpu.VMEM((24, block), F32)],
+        after=(steps[2],),
     )
     forces, sent = call(
         forces_kernel,
         (sds((comps + AMP_ROWS, block), BF16), sds((part + AMP_ROWS, block), BF16)),
         (place, rim, low, high, local, stats, spectral, freq, rate),
         8 * comps * dims * width * block, 8 * comps * block, smem=(0,),
-        scratch=[pltpu.VMEM((2 * dims * 2 * width, block), BF16)],
+        scratch=[pltpu.VMEM((2 * dims * 2 * width, block), BF16)], after=(rho_diag, rho_far),
     )
     far = lax.ppermute(sent, "mode", [(i, i ^ 2) for i in range(4)])
     mate = lax.ppermute(forces, "mode", [(i, i ^ 1) for i in range(4)])
@@ -355,7 +378,7 @@
         (place, forces, mate, rho_diag, rho_mate), 2 * comps * block * block, 6 * block * block,
         smem=(0,),
         scratch=[
-            pltpu.VMEM((comps, 128), F32), pltpu.VMEM((block, 128), F32),
+            pltpu.VMEM((comps, 128), F32), pltpu.VMEM((dims, block, 128), F32),
             pltpu.VMEM((16, block), F32), pltpu.VMEM((2, block, block // 4), BF16),
         ],
     )
@@ -364,7 +387,7 @@
         (place, forces, mate, far, rho_far, near), 2 * comps * block * block, 8 * block * block,
         smem=(0,),
         scratch=[
-            pltpu.VMEM((part, 128), F32), pltpu.VMEM((2 * block, 128), F32),
+            pltpu.VMEM((part, 128), F32), pltpu.VMEM((dims, 2 * block, 128), F32),
             pltpu.VMEM((2, 2 * block, block // 4), BF16),
         ],
     )

time: 122 us -> 80.1 us (0.66)
  Pallas kernels: 85.6 us -> 26.3 us
  waiting for transfers between devices: 7.31 us -> 22.8 us
  local copies, waits for them, and re-layouts: 5.53 us -> 8.76 us
  starting transfers between devices: 15.6 us -> 13.8 us
    pallas_call x7 -> x8, Pallas kernels: 85.6 us -> 26.3 us  [call(): pl.pallas_call(body, out_shape=out_shape, in_specs=specs, out_specs=[VMEM...]
    ppermute x1, waiting for transfers between devices: 0.01 us -> 8.33 us  [four_groups(): far = lax.ppermute(sent, 'mode', [(i, i ^ 2) for i in range(4)])]
    ppermute x3, waiting for transfers between devices: 7.3 us -> 13.3 us  [four_groups(): lax.ppermute(stats, 'dom', [(i, i ^ reach) for i in range(parts)])]
    ppermute x3, starting transfers between devices: 10.9 us -> 5.82 us  [four_groups(): lax.ppermute(stats, 'dom', [(i, i ^ reach) for i in range(parts)])]
    unnamed x16 -> x28, local copies, waits for them, and re-layouts: 2.72 us -> 6.53 us
    ppermute x1, starting transfers between devices: 1.92 us -> 5.01 us  [four_groups(): low = lax.ppermute(up, 'dom', ahead)]
  transfers between devices with their start and end apart: 7 -> 7, of which waited for: 1 -> 4; matrix products, arithmetic and copies ran while one was open for 3% -> 3% of each run, Pallas kernels for 56% -> 23%
where the time goes in v2:
time: 80.1 us; the launch traced here: 79.5 us
  Pallas kernels  26.3 us (33%)
  waiting for transfers between devices  22.8 us (28%)
  starting transfers between devices  13.8 us (17%)
  local copies, waits for them, and re-layouts  8.76 us (11%)
  blocking collectives  6.92 us (9%)
  other arithmetic  0.83 us (1%)
    pallas_call x8, Pallas kernels, call(): pl.pallas_call(body, out_shape=out_shape, in_specs=specs, out_specs=[VMEM...  26.3 us
    ppermute x3, waiting for transfers between devices, four_groups(): lax.ppermute(stats, 'dom', [(i, i ^ reach) for i in range(parts)])  13.3 us
    ppermute x1, waiting for transfers between devices, four_groups(): far = lax.ppermute(sent, 'mode', [(i, i ^ 2) for i in range(4)])  8.33 us
    psum x1, blocking collectives, four_groups(): return lax.psum(value.reshape(comps), 'mode')  6.92 us
    unnamed x28, local copies, waits for them, and re-layouts  6.53 us
    ppermute x3, starting transfers between devices, four_groups(): lax.ppermute(stats, 'dom', [(i, i ^ reach) for i in range(parts)])  5.82 us
    ppermute x1, starting transfers between devices, four_groups(): low = lax.ppermute(up, 'dom', ahead)  5.01 us
  transfers between devices with their start and end apart: 7, of which 4 were waited for; matrix products, arithmetic and copies ran while one was open for 3% of the time, Pallas kernels for 23%

profile of v2, /device:TPU:0, one launch (start us, length us, event | category | flops | bytes accessed | tf_op | source)
XLA Modules:
  0.0 79.5 jit_solution(3584587804350537459)
XLA Ops:
  0.0 0.0 copy-start.13
  0.0 0.0 copy-start.12
  0.0 0.8 slice_bitcast_fusion.1
  0.8 0.1 add_bitcast_fusion.refs_0_
  0.8 0.0 copy-start
  0.8 1.4 %copy-done = bf16[3,256,1024]{2,1,0:T(8,128)(2,1)S(1)} copy-done((bf16[3,256,1024]{2,1,0:T(8,128)(2,1)S(1)}, bf16[3,256,1024]{2,1,0:T(8,128)(2,1)}, u32[]{:S(2)}) %copy-start) | copy-done | bytes 1572888
  2.2 0.0 copy-start.11
  2.2 1.2 %gather_kernel.1 = (bf16[192,1024]{1,0:T(8,128)(2,1)S(1)}, bf16[192,1024]{1,0:T(8,128)(2,1)}) custom-call(s32[1,128]{1,0:T(1,128)S(1)} %add_bitcast_fusion.refs_0_, bf16[3,256,1024]{2,1,0:T(8,128)(2,1)S(1)} %copy-done), custom_call_target="tpu_custom_call" | custom-call | flops 201326592 | bytes 1572864 | tf_op jit(solution)/shard_map/gather_kernel/pallas_call | solution.py:25
  3.4 0.0 copy-start.1
  3.4 5.0 %collective-permute-start = (bf16[192,1024]{1,0:T(8,128)(2,1)S(1)}, bf16[192,1024]{1,0:T(8,128)(2,1)S(1)}, u32[]{:S(2)}, u32[]{:S(2)}) collective-permute-start(bf16[192,1024]{1,0:T(8,128)(2,1)S(1)} %get-tuple-element.14.refs_2_), channel_id=1, source_target_pairs={{0,4},{4,8},{8,12},{12,16},{16,20},{20,24},{24,28},{1,5},{5,9},{9,... | collective-permute-start | bytes 1179656 | tf_op jit(solution)/shard_map/ppermute | solution.py:321
  8.4 0.0 copy-start.10
  8.5 0.7 copy-done.10
  9.1 0.9 %stats_kernel.1 = f32[4,1024]{1,0:T(4,128)S(1)} custom-call(f32[1,256]{1,0:T(1,128)S(1)} %bitcast.31, bf16[3,256,1024]{2,1,0:T(8,128)(2,1)S(1)} %copy-done, bf16[192,1024]{1,0:T(8,128)(2,1)S(1)} %get-tuple-element.14.refs_2_), custom_call_target="tpu_custom_call" | custom-call | flops 3932160 | bytes 1572864 | tf_op jit(solution)/shard_map/stats_kernel/pallas_call | solution.py:25
  10.0 1.6 %collective-permute-start.2 = (f32[4,1024]{1,0:T(4,128)S(1)}, f32[4,1024]{1,0:T(4,128)S(1)}, u32[]{:S(2)}, u32[]{:S(2)}) collective-permute-start(f32[4,1024]{1,0:T(4,128)S(1)} %stats_kernel.1), channel_id=1, source_target_pairs={{0,4},{4,0},{8,12},{12,8},{16,20},{20,16},{24,28},{28,24},{1,5},{5... | collective-permute-start | bytes 49160 | tf_op jit(solution)/shard_map/ppermute | solution.py:336
  11.6 1.3 %collective-permute-start.1 = (bf16[192,1024]{1,0:T(8,128)(2,1)}, bf16[192,1024]{1,0:T(8,128)(2,1)S(1)}, u32[]{:S(2)}, u32[]{:S(2)}) collective-permute-start(bf16[192,1024]{1,0:T(8,128)(2,1)} %get-tuple-element.15), channel_id=1, source_target_pairs={{4,0},{8,4},{12,8},{16,12},{20,16},{24,20},{28,24},{5,1},{9,5},{13... | collective-permute-start | bytes 1179656 | tf_op jit(solution)/shard_map/ppermute | solution.py:322
  12.9 0.0 copy-done.13
  12.9 0.0 copy-done.12
  13.0 0.1 broadcast_in_dim.7
  13.1 0.1 concatenate.9
  13.2 0.0 copy-done.11
  13.2 0.1 copy.17
  13.3 0.2 reshape.33
  13.5 12.0 %collective-permute-done.2 = f32[4,1024]{1,0:T(4,128)S(1)} collective-permute-done((f32[4,1024]{1,0:T(4,128)S(1)}, f32[4,1024]{1,0:T(4,128)S(1)}, u32[]{:S(2)}, u32[]{:S(2)}) %collective-permute-start.2) | collective-permute-done | bytes 16416 | tf_op jit(solution)/shard_map/ppermute | solution.py:336
  25.6 0.0 copy-start.6
  25.6 1.6 %collective-permute-start.3 = (f32[4,1024]{1,0:T(4,128)S(1)}, f32[4,1024]{1,0:T(4,128)S(1)}, u32[]{:S(2)}, u32[]{:S(2)}) collective-permute-start(f32[4,1024]{1,0:T(4,128)S(1)} %add.11.refs_3_), channel_id=1, source_target_pairs={{0,8},{4,12},{8,0},{12,4},{16,24},{20,28},{24,16},{28,20},{1,9},{5... | collective-permute-start | bytes 49160 | tf_op jit(solution)/shard_map/ppermute | solution.py:336
  27.2 0.8 %copy.18.refs_0_ = f32[512,16]{1,0:T(8,128)} copy(f32[512,16]{0,1:T(8,128)S(1)} %pad_maximum_fusion) | data formatting | bytes 65536 | tf_op jit(solution)/shard_map/concatenate | solution.py:343
  28.0 1.3 %collective-permute-done.3 = f32[4,1024]{1,0:T(4,128)S(1)} collective-permute-done((f32[4,1024]{1,0:T(4,128)S(1)}, f32[4,1024]{1,0:T(4,128)S(1)}, u32[]{:S(2)}, u32[]{:S(2)}) %collective-permute-start.3) | collective-permute-done | bytes 16416 | tf_op jit(solution)/shard_map/ppermute | solution.py:336
  29.4 2.6 %collective-permute-start.4 = (f32[4,1024]{1,0:T(4,128)S(1)}, f32[4,1024]{1,0:T(4,128)}, u32[]{:S(2)}, u32[]{:S(2)}) collective-permute-start(f32[4,1024]{1,0:T(4,128)S(1)} %add.12.refs_3_), channel_id=1, source_target_pairs={{0,16},{4,20},{8,24},{12,28},{16,0},{20,4},{24,8},{28,12},{1,17},{... | collective-permute-start | bytes 49160 | tf_op jit(solution)/shard_map/ppermute | solution.py:336
  32.0 0.0 copy-done.6
  32.0 0.0 copy-done.1
  32.0 0.0 copy-start.4
  32.0 0.9 %copy-done.4 = f32[512,16]{1,0:T(8,128)S(1)} copy-done((f32[512,16]{1,0:T(8,128)S(1)}, f32[512,16]{1,0:T(8,128)}, u32[]{:S(2)}) %copy-start.4) | copy-done | bytes 32792
  32.9 3.9 %local_kernel.1 = (f32[512,1024]{1,0:T(8,128)S(1)}, bf16[512,768]{1,0:T(8,128)(2,1)S(1)}) custom-call(f32[512,16]{1,0:T(8,128)S(1)} %copy-done.4, bf16[768,1024]{1,0:T(8,128)(2,1)S(1)} %bitcast.23), custom_call_target="tpu_custom_call" | custom-call | flops 1610612736 | bytes 4718592 | tf_op jit(solution)/shard_map/local_kernel/pallas_call | solution.py:25
  36.8 0.0 copy-start.2
  36.8 1.3 %copy-done.2 = f32[512,1024]{1,0:T(8,128)} copy-done((f32[512,1024]{1,0:T(8,128)}, f32[512,1024]{1,0:T(8,128)S(1)}, u32[]{:S(2)}) %copy-start.2) | copy-done | bytes 2097176
  38.1 0.1 stack.27.refs_0_
  38.2 0.0 copy-start.7
  38.2 0.7 copy-done.7
  38.9 0.0 copy-start.8
  38.9 0.7 copy-done.8
  39.7 0.0 copy-start.9
  39.7 0.7 copy-done.9
  40.4 3.7 %rho_near_kernel.1 = (f32[1024,1024]{1,0:T(8,128)S(1)}, f32[2,512,512]{2,1,0:T(8,128)S(1)}) custom-call(s32[6]{0:T(128)S(1)} %stack.27.refs_0_, f32[1,4096]{1,0:T(1,128)S(1)} %bitcast.24, f32[1,4096]{1,0:T(1,128)S(1)} %bitcast.27, f32[4,1024]{1,0:T(4,128)S(1)} %copy-done.7), custom_call_target="tpu_custom_call" | custom-call | flops 20971520 | bytes 5242880 | tf_op jit(solution)/shard_map/rho_near_kernel/pallas_call | solution.py:25
  44.1 0.0 copy-start.3
  44.1 0.0 copy-start.5
  44.1 6.1 %rho_far_kernel.1.refs_10_.refs_4_ = f32[2048,1024]{1,0:T(8,128)S(1)} custom-call(s32[6]{0:T(128)S(1)} %stack.27.refs_0_, f32[1,4096]{1,0:T(1,128)S(1)} %bitcast.25, f32[1,4096]{1,0:T(1,128)S(1)} %bitcast.28, f32[4,1024]{1,0:T(4,128)S(1)} %add.12.refs_3_), custom_call_target="tpu_custom_call" | custom-call | flops 41943040 | bytes 8388608 | tf_op jit(solution)/shard_map/rho_far_kernel/pallas_call | solution.py:25
  50.2 0.0 collective-permute-done.4
  50.2 0.7 add.13.refs_5_
  50.9 0.0 collective-permute-done.1.refs_3_
  50.9 0.0 collective-permute-done.refs_2_
  51.0 0.0 copy-done.3
  51.0 0.0 copy-done.5
  51.0 1.6 %forces_kernel.1 = (bf16[528,1024]{1,0:T(8,128)(2,1)S(1)}, bf16[272,1024]{1,0:T(8,128)(2,1)S(1)}) custom-call(s32[6]{0:T(128)S(1)} %stack.27.refs_0_, bf16[512,768]{1,0:T(8,128)(2,1)S(1)} %get-tuple-element.13.refs_1_, bf16[192,1024]{1,0:T(8,128)(2,1)S(1)} %collective-permute-done.refs_2_, bf16[192,1024]{1,0:T(8,128)(2,1)S(1)} %collective-permute-done.1.refs_3_, ...), custom_call_target="tpu_custom_call" | custom-call | flops 805306368 | bytes 4194304 | tf_op jit(solution)/shard_map/forces_kernel/pallas_call | solution.py:25
  52.6 0.1 collective-permute-start.5
  52.6 1.6 %collective-permute-start.6 = (bf16[272,1024]{1,0:T(8,128)(2,1)S(1)}, bf16[272,1024]{1,0:T(8,128)(2,1)S(1)}, u32[]{:S(2)}, u32[]{:S(2)}) collective-permute-start(bf16[272,1024]{1,0:T(8,128)(2,1)S(1)} %get-tuple-element.19), channel_id=1, source_target_pairs={{0,2},{1,3},{2,0},{3,1},{4,6},{5,7},{6,4},{7,5},{8,10},{9,11},{10,... | collective-permute-start | bytes 1671176 | tf_op jit(solution)/shard_map/ppermute | solution.py:374
  54.2 1.1 %collective-permute-done.5.refs_2_ = bf16[528,1024]{1,0:T(8,128)(2,1)S(1)} collective-permute-done((bf16[528,1024]{1,0:T(8,128)(2,1)S(1)}, bf16[528,1024]{1,0:T(8,128)(2,1)S(1)}, u32[]{:S(2)}, u32[]{:S(2)}) %collective-permute-start.5) | collective-permute-done | bytes 1081376 | tf_op jit(solution)/shard_map/ppermute | solution.py:375
  55.3 4.0 %near_kernel.1.refs_5_ = f32[1,512]{1,0:T(1,128)S(1)} custom-call(s32[6]{0:T(128)S(1)} %stack.27.refs_0_, bf16[528,1024]{1,0:T(8,128)(2,1)S(1)} %get-tuple-element.18.refs_1_, bf16[528,1024]{1,0:T(8,128)(2,1)S(1)} %collective-permute-done.5.refs_2_, f32[1024,1024]{1,0:T(8,128)S(1)} %get-tuple-element.17.refs_9_.refs_3_, ...), custom_call_target="tpu_custom_call" | custom-call | flops 1073741824 | bytes 6291456 | tf_op jit(solution)/shard_map/near_kernel/pallas_call | solution.py:25
  59.3 8.3 %collective-permute-done.6.refs_3_ = bf16[272,1024]{1,0:T(8,128)(2,1)S(1)} collective-permute-done((bf16[272,1024]{1,0:T(8,128)(2,1)S(1)}, bf16[272,1024]{1,0:T(8,128)(2,1)S(1)}, u32[]{:S(2)}, u32[]{:S(2)}) %collective-permute-start.6) | collective-permute-done | bytes 557088 | tf_op jit(solution)/shard_map/ppermute | solution.py:374
  67.7 4.9 %far_kernel.1 = f32[1,512]{1,0:T(1,128)S(1)} custom-call(s32[6]{0:T(128)S(1)} %stack.27.refs_0_, bf16[528,1024]{1,0:T(8,128)(2,1)S(1)} %get-tuple-element.18.refs_1_, bf16[528,1024]{1,0:T(8,128)(2,1)S(1)} %collective-permute-done.5.refs_2_, bf16[272,1024]{1,0:T(8,128)(2,1)S(1)} %collective-permute-done.6.refs_3_, ...), custom_call_target="tpu_custom_call" | custom-call | flops 1073741824 | bytes 8388608 | tf_op jit(solution)/shard_map/far_kernel/pallas_call | solution.py:25
  72.6 6.9 %psum.7 = f32[512]{0:T(512)} all-reduce(f32[512]{0:T(512)S(1)} %bitcast.30), channel_id=1, replica_groups=mesh['dom'=8,'mode'=4] {'mode'}, use_global_device_ids=true, to_apply=%region_0.1 | all-reduce | flops 512 | bytes 4096 | tf_op jit(solution)/shard_map/psum | solution.py:394
  (4 shorter events, 0.0 us)
Async XLA Ops:
  0.0 12.9 %copy-start.13 = (s32[64]{0:T(128)S(1)}, s32[64]{0:T(128)}, u32[]{:S(2)}) copy-start(s32[64]{0:T(128)} %param.16) | copy-start | bytes 772
  0.0 12.9 %copy-start.12 = (s32[64,4]{0,1:T(4,128)S(1)}, s32[64,4]{0,1:T(4,128)}, u32[]{:S(2)}) copy-start(s32[64,4]{0,1:T(4,128)} %param.15) | copy-start | bytes 3076
  0.8 1.4 %copy-start = (bf16[3,256,1024]{2,1,0:T(8,128)(2,1)S(1)}, bf16[3,256,1024]{2,1,0:T(8,128)(2,1)}, u32[]{:S(2)}) copy-start(bf16[3,256,1024]{2,1,0:T(8,128)(2,1)} %refs_1_.3) | copy-start | bytes 4718596
  2.2 10.9 %copy-start.11 = (bf16[64,8,4,3]{0,2,3,1:T(4,128)(2,1)S(1)}, bf16[64,8,4,3]{0,2,3,1:T(4,128)(2,1)}, u32[]{:S(2)}) copy-start(bf16[64,8,4,3]{0,2,3,1:T(4,128)(2,1)} %param.14) | copy-start | bytes 36868
  3.4 28.5 %copy-start.1 = (bf16[3,256,1024]{2,1,0:T(8,128)(2,1)S(1)}, bf16[3,256,1024]{2,1,0:T(8,128)(2,1)}, u32[]{:S(2)}) copy-start(bf16[3,256,1024]{2,1,0:T(8,128)(2,1)} %refs_1_.3) | copy-start | bytes 4718596
  3.4 47.5 %collective-permute-start = (bf16[192,1024]{1,0:T(8,128)(2,1)S(1)}, bf16[192,1024]{1,0:T(8,128)(2,1)S(1)}, u32[]{:S(2)}, u32[]{:S(2)}) collective-permute-start(bf16[192,1024]{1,0:T(8,128)(2,1)S(1)} %get-tuple-element.14.refs_2_), channel_id=1, source_target_pairs={{0,4},{4,8},{8,12},{12,16},{16,20},{20,24},{24,28},{1,5},{5,9},{9,... | collective-permute-start | bytes 1179656 | tf_op jit(solution)/shard_map/ppermute | solution.py:321
  8.4 0.7 copy-start.10
  10.0 15.5 %collective-permute-start.2 = (f32[4,1024]{1,0:T(4,128)S(1)}, f32[4,1024]{1,0:T(4,128)S(1)}, u32[]{:S(2)}, u32[]{:S(2)}) collective-permute-start(f32[4,1024]{1,0:T(4,128)S(1)} %stats_kernel.1), channel_id=1, source_target_pairs={{0,4},{4,0},{8,12},{12,8},{16,20},{20,16},{24,28},{28,24},{1,5},{5... | collective-permute-start | bytes 49160 | tf_op jit(solution)/shard_map/ppermute | solution.py:336
  11.6 39.3 %collective-permute-start.1 = (bf16[192,1024]{1,0:T(8,128)(2,1)}, bf16[192,1024]{1,0:T(8,128)(2,1)S(1)}, u32[]{:S(2)}, u32[]{:S(2)}) collective-permute-start(bf16[192,1024]{1,0:T(8,128)(2,1)} %get-tuple-element.15), channel_id=1, source_target_pairs={{4,0},{8,4},{12,8},{16,12},{20,16},{24,20},{28,24},{5,1},{9,5},{13... | collective-permute-start | bytes 1179656 | tf_op jit(solution)/shard_map/ppermute | solution.py:322
  25.6 6.4 %copy-start.6 = (f32[4,1024]{1,0:T(4,128)}, f32[4,1024]{1,0:T(4,128)S(1)}, u32[]{:S(2)}) copy-start(f32[4,1024]{1,0:T(4,128)S(1)} %add.11.refs_3_) | copy-start | bytes 49156
  25.6 3.8 %collective-permute-start.3 = (f32[4,1024]{1,0:T(4,128)S(1)}, f32[4,1024]{1,0:T(4,128)S(1)}, u32[]{:S(2)}, u32[]{:S(2)}) collective-permute-start(f32[4,1024]{1,0:T(4,128)S(1)} %add.11.refs_3_), channel_id=1, source_target_pairs={{0,8},{4,12},{8,0},{12,4},{16,24},{20,28},{24,16},{28,20},{1,9},{5... | collective-permute-start | bytes 49160 | tf_op jit(solution)/shard_map/ppermute | solution.py:336
  29.4 20.8 %collective-permute-start.4 = (f32[4,1024]{1,0:T(4,128)S(1)}, f32[4,1024]{1,0:T(4,128)}, u32[]{:S(2)}, u32[]{:S(2)}) collective-permute-start(f32[4,1024]{1,0:T(4,128)S(1)} %add.12.refs_3_), channel_id=1, source_target_pairs={{0,16},{4,20},{8,24},{12,28},{16,0},{20,4},{24,8},{28,12},{1,17},{... | collective-permute-start | bytes 49160 | tf_op jit(solution)/shard_map/ppermute | solution.py:336
  32.0 1.0 %copy-start.4 = (f32[512,16]{1,0:T(8,128)S(1)}, f32[512,16]{1,0:T(8,128)}, u32[]{:S(2)}) copy-start(f32[512,16]{1,0:T(8,128)} %copy.18.refs_0_) | copy-start | bytes 98308
  36.8 1.3 %copy-start.2 = (f32[512,1024]{1,0:T(8,128)}, f32[512,1024]{1,0:T(8,128)S(1)}, u32[]{:S(2)}) copy-start(f32[512,1024]{1,0:T(8,128)S(1)} %get-tuple-element.16.refs_4_) | copy-start | bytes 6291460
  38.2 0.7 copy-start.7
  38.9 0.7 copy-start.8
  39.7 0.7 copy-start.9
  44.1 6.9 %copy-start.3 = (f32[512,1024]{1,0:T(8,128)S(1)}, f32[512,1024]{1,0:T(8,128)}, u32[]{:S(2)}) copy-start(f32[512,1024]{1,0:T(8,128)} %copy-done.2) | copy-start | bytes 6291460
  44.1 6.9 %copy-start.5 = (f32[3,4096]{1,0:T(4,128)S(1)}, f32[3,4096]{1,0:T(4,128)}, u32[]{:S(2)}) copy-start(f32[3,4096]{1,0:T(4,128)} %refs_6_.1) | copy-start | bytes 147460
  52.6 2.8 %collective-permute-start.5 = (bf16[528,1024]{1,0:T(8,128)(2,1)S(1)}, bf16[528,1024]{1,0:T(8,128)(2,1)S(1)}, u32[]{:S(2)}, u32[]{:S(2)}) collective-permute-start(bf16[528,1024]{1,0:T(8,128)(2,1)S(1)} %get-tuple-element.18.refs_1_), channel_id=1, source_target_pairs={{0,1},{1,0},{2,3},{3,2},{4,5},{5,4},{6,7},{7,6},{8,9},{9,8},{10,11... | collective-permute-start | bytes 3244040 | tf_op jit(solution)/shard_map/ppermute | solution.py:375
  52.6 15.0 %collective-permute-start.6 = (bf16[272,1024]{1,0:T(8,128)(2,1)S(1)}, bf16[272,1024]{1,0:T(8,128)(2,1)S(1)}, u32[]{:S(2)}, u32[]{:S(2)}) collective-permute-start(bf16[272,1024]{1,0:T(8,128)(2,1)S(1)} %get-tuple-element.19), channel_id=1, source_target_pairs={{0,2},{1,3},{2,0},{3,1},{4,6},{5,7},{6,4},{7,5},{8,10},{9,11},{10,... | collective-permute-start | bytes 1671176 | tf_op jit(solution)/shard_map/ppermute | solution.py:374

commit v3 on v0

--- a/solution.py
+++ b/solution.py
@@ -1,7 +1,461 @@
+import functools
 import jax
 import jax.numpy as jnp
 from jax import lax
+from jax.experimental import pallas as pl
+from jax.experimental.pallas import tpu as pltpu
 from jax.sharding import PartitionSpec as P
+
+F32 = jnp.float32
+BF16 = jnp.bfloat16
+VMEM = pl.BlockSpec(memory_space=pltpu.VMEM)
+HBM = pl.BlockSpec(memory_space=pltpu.HBM)
+ANY = pl.BlockSpec(memory_space=pl.ANY)
+SMEM = pl.BlockSpec(memory_space=pltpu.SMEM)
+
+
+def call(kernel, out_shape, args, flops, nbytes, smem=(), hbm=(), scratch=(), vmem=24 << 20, after=()):
+    count = len(args)
+    specs = [SMEM if i in smem else HBM if i in hbm else VMEM for i in range(count)]
+    specs += [ANY] * len(after)
+    many = isinstance(out_shape, (tuple, list))
+
+    def body(*refs):
+        kernel(*refs[:count], *refs[count + len(after) :])
+
+    return pl.pallas_call(
+        body,
+        out_shape=out_shape,
+        in_specs=specs,
+        out_specs=[VMEM] * len(out_shape) if many else VMEM,
+        scratch_shapes=list(scratch),
+        cost_estimate=pl.CostEstimate(flops=flops, bytes_accessed=nbytes, transcendentals=0),
+        compiler_params=pltpu.CompilerParams(vmem_limit_bytes=vmem),
+        name=getattr(kernel, "func", kernel).__name__,
+    )(*args, *after)
+
+
+def add_kernel(left_ref, right_ref, out_ref):
+    out_ref[...] = left_ref[...] + right_ref[...]
+
+
+def gather_kernel(at, shared_ref, shapes_ref, up_ref, down_ref, buf, sem):
+    dims, nodes, chunk = buf.shape
+    width = shared_ref.shape[1]
+    load = pltpu.make_async_copy(shapes_ref.at[:, :, at : at + chunk], buf, sem)
+    load.start()
+    node = lax.broadcasted_iota(jnp.int32, (nodes, 2 * width), 0)
+    wanted = jnp.concatenate([shared_ref[1:2, :], shared_ref[0:1, :]], axis=1)
+    pick = jnp.where(node == wanted, 1.0, 0.0).astype(F32).T.astype(BF16)
+    load.wait()
+    for d in range(dims):
+        got = jnp.dot(pick, buf[d], preferred_element_type=F32).astype(BF16)
+        up_ref[d * width : (d + 1) * width, :] = got[:width]
+        down_ref[d * width : (d + 1) * width, :] = got[width:]
+
+
+def stats_kernel(chunks, mass_ref, *refs):
+    shapes_refs, (out_ref, mass_scr) = refs[:chunks], refs[chunks:]
+    dims, nodes, chunk = shapes_refs[0].shape
+    column = jnp.broadcast_to(mass_ref[...], (8, nodes)).T
+    mass_scr[...] = jnp.broadcast_to(column[:, 0:1], (nodes, 128))
+    for c, shapes_ref in enumerate(shapes_refs):
+        for at in range(0, chunk, 128):
+            lanes = slice(c * chunk + at, c * chunk + at + 128)
+            general = jnp.zeros((8, 128), F32)
+            for d in range(dims):
+                lever = jnp.zeros((8, 128), F32)
+                for r in range(0, nodes, 16):
+                    wide = shapes_ref[d, r : r + 16, at : at + 128].astype(F32)
+                    weighted = wide * mass_scr[r : r + 16, :]
+                    square = weighted * wide
+                    lever += weighted[:8] + weighted[8:]
+                    general += square[:8] + square[8:]
+                out_ref[d : d + 1, lanes] = jnp.sum(lever, axis=0, keepdims=True)
+            out_ref[dims : dims + 1, lanes] = jnp.sum(general, axis=0, keepdims=True)
+
+
+def table_kernel(codes_ref, count_ref, recovery_ref, pick_ref, force_ref):
+    slots, elems = codes_ref.shape
+    per_elem, dims = recovery_ref.shape[0], recovery_ref.shape[1]
+    span = pick_ref.shape[1]
+    node = lax.broadcasted_iota(jnp.int32, (span, elems), 0)
+    for s in range(0, slots, 2):
+        picks = []
+        for q in range(s, min(s + 2, slots)):
+            code = jnp.where(q < count_ref[...], codes_ref[q : q + 1, :], -1)
+            picks.append(jnp.where(node == code, 1.0, 0.0).astype(F32))
+        pick_ref[s * elems : s * elems + len(picks) * elems, :] = (
+            jnp.concatenate(picks, axis=1).T.astype(BF16)
+        )
+    row = lax.broadcasted_iota(jnp.int32, (elems, 2 * elems), 0)
+    column = lax.broadcasted_iota(jnp.int32, (elems, 2 * elems), 1)
+    same = (column == row) | (column == row + elems)
+    for k in range(per_elem):
+        for d in range(dims):
+            value = recovery_ref[k, d].astype(F32)
+            for s in range(0, slots, 2):
+                pair = jnp.concatenate([value[s : s + 1], value[s + 1 : s + 2]], axis=1)
+                at = (d * slots + s) * elems
+                force_ref[k * elems : (k + 1) * elems, at : at + 2 * elems] = jnp.where(
+                    same, pair, 0.0
+                ).astype(BF16)
+
+
+def mode_rows(freq, rate):
+    alpha = rate * freq
+    inverse = 1.0 / jnp.sqrt(alpha)
+    return (freq * freq * inverse, inverse, 2.0 * alpha, 2.0 * (freq / rate))
+
+
+def place_modes(freq_ref, rate_ref, row_scr, col_scr, groups, sides, block):
+    for which, group in enumerate(groups):
+        lanes = pl.ds(pl.multiple_of(group * block, block), block)
+        rows = jnp.concatenate(list(mode_rows(freq_ref[:, lanes], rate_ref[:, lanes])) * 2, axis=0)
+        row_scr[which * 8 : which * 8 + 8, :] = rows
+        if which < sides:
+            turned = rows.T
+            for q in range(4):
+                col_scr[q, which * block : (which + 1) * block, :] = jnp.broadcast_to(
+                    turned[:, q : q + 1], (block, 128)
+                )
+
+
+def fill_rho(row_scr, col_scr, out_ref, out_col, side_row, count, cols_at, col_off, tile):
+    step = min(count, 256)
+    cols = [
+        jnp.broadcast_to(row_scr[cols_at + q : cols_at + q + 1, pl.ds(col_off, tile)], (8, tile))
+        for q in range(4)
+    ]
+
+    @pl.loop(0, count // step)
+    def _(t):
+        for k in range(0, step, 8):
+            at = pl.multiple_of(t * step, step) + k
+            high, low, alpha, zeta = (col_scr[q, pl.ds(side_row + at, 8), :] for q in range(4))
+            for c in range(0, tile, 128):
+                col = [value[:, c : c + 128] for value in cols]
+                spread = high * col[1] - low * col[0]
+                pair = alpha + col[2]
+                bottom = spread * spread + pair * (zeta + col[3])
+                out_ref[pl.ds(at, 8), out_col + c : out_col + c + 128] = pair / bottom
+
+
+def rho_near_kernel(place_ref, freq_ref, rate_ref, diag_ref, mate_ref, col_scr, row_scr):
+    block = diag_ref.shape[0]
+    half = block // 2
+    tile = block // 4
+    own, mate, parity = place_ref[0], place_ref[1], place_ref[3]
+    place_modes(freq_ref, rate_ref, row_scr, col_scr, (own, mate), 1, block)
+    for j in range(4):
+        fill_rho(row_scr, col_scr, diag_ref, j * tile, 0, (j + 1) * tile, 0, j * tile, tile)
+    for i in range(2):
+        for j in range(2):
+            off = pl.multiple_of((i ^ parity) * half + j * tile, tile)
+            fill_rho(row_scr, col_scr, mate_ref.at[i], j * tile, i * half, half, 8, off, tile)
+
+
+def rho_far_kernel(place_ref, freq_ref, rate_ref, far_ref, col_scr, row_scr):
+    block = far_ref.shape[1]
+    tile = block // 4
+    own, mate, far = place_ref[0], place_ref[1], place_ref[2]
+    place_modes(freq_ref, rate_ref, row_scr, col_scr, (own, mate, far), 2, block)
+    for j in range(4):
+        fill_rho(row_scr, col_scr, far_ref, j * tile, 0, 2 * block, 16, j * tile, tile)
+
+
+def forces_kernel(
+    place_ref, pick_ref, force_ref, shapes_ref, low_ref, high_ref, all_ref, part_ref, rim_scr, got_scr
+):
+    dims, nodes, _ = shapes_ref.shape
+    comps, chunk = all_ref.shape
+    width = low_ref.shape[0] // dims
+    taken = pick_ref.shape[0]
+    part = comps // 2
+    other = place_ref[5]
+    for d in range(dims):
+        rim_scr[d, :width, :] = low_ref[d * width : (d + 1) * width, :]
+        rim_scr[d, width:, :] = high_ref[d * width : (d + 1) * width, :]
+    wide = 256
+    for c in range(0, chunk, wide):
+        for d in range(dims):
+            got = jnp.dot(
+                pick_ref[:, :nodes], shapes_ref[d, :, c : c + wide], preferred_element_type=F32
+            )
+            got = got + jnp.dot(
+                pick_ref[:, nodes:], rim_scr[d, :, c : c + wide], preferred_element_type=F32
+            )
+            got_scr[d * taken : (d + 1) * taken, c : c + wide] = got.astype(BF16)
+        total = jnp.dot(force_ref[...], got_scr[:, c : c + wide], preferred_element_type=F32)
+        all_ref[:, c : c + wide] = total.astype(BF16)
+    part_ref[...] = all_ref[pl.ds(pl.multiple_of(other * part, part), part), :]
+
+
+def amps_kernel(place_ref, stats_ref, extra_ref, spectral_ref, freq_ref, rate_ref, out_ref):
+    dims, block = spectral_ref.shape[0], stats_ref.shape[1]
+    lanes = pl.ds(pl.multiple_of(place_ref[0] * block, block), block)
+    total = stats_ref[...] + extra_ref[...]
+    scale = 2.0 * jnp.sqrt(freq_ref[:, lanes] / rate_ref[:, lanes])
+    amps = total[:dims] / total[dims : dims + 1] * spectral_ref[:, lanes] * scale
+    out_ref[...] = jnp.concatenate([amps, jnp.zeros((8 - dims, block), F32)], axis=0)
+
+
+def fold(value):
+    total = value[:, :128]
+    for c in range(128, value.shape[1], 128):
+        total = total + value[:, c : c + 128]
+    return total
+
+
+def to_row(acc, turned, per_elem):
+    elems = acc.shape[0] // per_elem
+    for k in range(per_elem):
+        turned[pl.ds(k, elems, stride=per_elem), :] = acc[k * elems : (k + 1) * elems, :]
+    ones = jnp.ones((8, acc.shape[1]), F32)
+    return lax.dot_general(
+        ones, turned[...], (((1,), (1,)), ((), ())),
+        precision=lax.Precision.HIGHEST, preferred_element_type=F32,
+    )[0:1]
+
+
+def spread_sides(side_scr, at, amps, dims):
+    sides = amps.T
+    for d in range(dims):
+        side_scr[d, at : at + amps.shape[1], :] = jnp.broadcast_to(sides[:, d : d + 1], (amps.shape[1], 128))
+
+
+def weigh(out, rho, side_scr, side_at, cols, dims, factor):
+    for c in range(0, rho.shape[1], 128):
+        col = [jnp.broadcast_to(cols[d : d + 1, c : c + 128] * factor, (16, 128)) for d in range(dims)]
+        for r in range(0, rho.shape[0], 16):
+            pair = side_scr[0, side_at + r : side_at + r + 16, :] * col[0]
+            for d in range(1, dims):
+                pair = pair + side_scr[d, side_at + r : side_at + r + 16, :] * col[d]
+            out[r : r + 16, c : c + 128] = (rho[r : r + 16, c : c + 128] * pair).astype(BF16)
+
+
+def near_kernel(dims, chunks, *refs):
+    place_ref, own_amps_ref, mate_amps_ref, diag_ref, cross_ref = refs[:5]
+    own_refs, mate_refs = refs[5 : 5 + chunks], refs[5 + chunks : 5 + 2 * chunks]
+    acc, side_scr, w_scr = refs[5 + 2 * chunks :]
+    comps, chunk = own_refs[0].shape
+    block = diag_ref.shape[0]
+    tile = block // 4
+    half = block // 2
+    parity = place_ref[3]
+
+    def part(parts, at, size):
+        return parts[at // chunk][:, at % chunk : at % chunk + size]
+
+    def product(w, at, depth):
+        total = None
+        for c in range(at, at + depth, min(chunk, depth)):
+            size = min(chunk, at + depth - c)
+            got = jnp.dot(part(own_refs, c, size), w[c - at : c - at + size, :], preferred_element_type=F32)
+            total = got if total is None else total + got
+        return total
+
+    spread_sides(side_scr, 0, own_amps_ref[...], dims)
+    turn = 0
+    for j in range(4):
+        cols = own_amps_ref[:, j * tile : (j + 1) * tile]
+        for i in range(j + 1):
+            rho = diag_ref.at[i * tile : (i + 1) * tile, j * tile : (j + 1) * tile]
+            out = w_scr.at[turn, i * tile : (i + 1) * tile, :]
+            weigh(out, rho, side_scr, i * tile, cols, dims, 2.0 if i < j else 1.0)
+        got = product(w_scr.at[turn], 0, (j + 1) * tile)
+        got = fold(got * part(own_refs, j * tile, tile).astype(F32))
+        acc[...] = got if j == 0 else acc[...] + got
+        turn = 1 - turn
+    for i in range(2):
+        for j in range(half // tile):
+            here, there = i * half + j * tile, (1 - i) * half + j * tile
+            straight = parity == 0
+            cols = jnp.where(
+                straight, mate_amps_ref[:, here : here + tile], mate_amps_ref[:, there : there + tile]
+            )
+            rho = cross_ref.at[i, :, j * tile : (j + 1) * tile]
+            weigh(w_scr.at[turn, :half, :], rho, side_scr, i * half, cols, dims, 2.0)
+            got = product(w_scr.at[turn], i * half, half)
+            other = jnp.where(
+                straight, part(mate_refs, here, tile).astype(F32), part(mate_refs, there, tile).astype(F32)
+            )
+            acc[...] += fold(got * other)
+            turn = 1 - turn
+
+
+def weights_kernel(dims, own_amps_ref, mate_amps_ref, far_amps_ref, rho_ref, out_ref, side_scr):
+    block = rho_ref.shape[1]
+    tile = block // 4
+    spread_sides(side_scr, 0, own_amps_ref[...], dims)
+    spread_sides(side_scr, block, mate_amps_ref[...], dims)
+
+    @pl.loop(0, 2 * block // tile)
+    def _(t):
+        rows = pl.ds(pl.multiple_of(t * tile, tile), tile)
+        sides = side_scr.at[:, rows, :]
+        weigh(out_ref.at[rows, :], rho_ref.at[rows, :], sides, 0, far_amps_ref[...], dims, 2.0)
+
+
+def far_kernel(at, chunks, per_elem, place_ref, near_ref, w_ref, far_ref, *refs):
+    own_refs, mate_refs = refs[:chunks], refs[chunks : 2 * chunks]
+    if len(refs) == 2 * chunks + 1:
+        acc, last = refs[-1], False
+    else:
+        (out_ref, acc, turned), last = refs[2 * chunks :], True
+    comps, chunk = own_refs[0].shape
+    block = w_ref.shape[1]
+    part = comps // 2
+    tile = min(256, chunk)
+    here = pl.multiple_of(place_ref[4] * part, part)
+    rows = pl.ds(here, part)
+    total = near_ref[rows, :]
+    for c in range(0, chunk, tile):
+        spot = slice(at + c, at + c + tile)
+        got = None
+        for which, parts in enumerate((own_refs, mate_refs)):
+            for q in range(chunks):
+                base = which * block + q * chunk
+                piece = jnp.dot(
+                    parts[q][rows, :], w_ref[base : base + chunk, spot], preferred_element_type=F32
+                )
+                got = piece if got is None else got + piece
+        total = total + fold(got * far_ref[:, c : c + tile].astype(F32))
+    acc[...] = near_ref[...]
+    acc[rows, :] = total
+    if last:
+        out_ref[...] = to_row(acc, turned, per_elem)
+
+
+CHUNKS = 1
+
+
+def four_groups(
+    shapes, masses, spectral, frequencies, damping, recovery, connectivity, node_count, shared
+):
+    dims, nodes, block = shapes.shape
+    elems, slots = connectivity.shape
+    per_elem = recovery.shape[1]
+    comps = elems * per_elem
+    part = comps // 2
+    width = shared.shape[1]
+    parts = lax.axis_size("dom")
+    group = lax.axis_index("mode").astype(jnp.int32)
+    place = jnp.stack(
+        [group, group ^ 1, group ^ 2, group & 1, group >> 1, 1 - (group >> 1)]
+    ).astype(jnp.int32)
+    sds = jax.ShapeDtypeStruct
+    chunk = block // CHUNKS
+    ahead = [(i, i + 1) for i in range(parts - 1)]
+    back = [(i + 1, i) for i in range(parts - 1)]
+    freq = frequencies.reshape(1, -1)
+    rate = damping.reshape(1, -1)
+
+    def moved(name, value, axis, pairs):
+        with jax.named_scope(name):
+            return lax.ppermute(value, axis, pairs)
+
+    def gathered(c, after):
+        return call(
+            functools.partial(gather_kernel, c * chunk),
+            (sds((dims * width, chunk), BF16), sds((dims * width, chunk), BF16), sds((dims, nodes, chunk), BF16)),
+            (shared, shapes), 4 * width * nodes * dims * chunk, 2 * dims * nodes * chunk, hbm=(1,),
+            scratch=[pltpu.SemaphoreType.DMA], after=after,
+        )
+
+    halos, held = [], []
+    after = ()
+    for c in range(CHUNKS):
+        up, down, kept = gathered(c, after)
+        held.append(kept)
+        after = (up,)
+        halos.append((moved("up%d" % c, up, "dom", ahead), moved("down%d" % c, down, "dom", back)))
+
+    stats = call(
+        functools.partial(stats_kernel, CHUNKS), sds((dims + 1, block), F32), (masses.reshape(1, nodes), *held),
+        5 * dims * nodes * block, 2 * dims * nodes * block,
+        scratch=[pltpu.VMEM((nodes, 128), F32)], after=after,
+    )
+    pick, force = call(
+        table_kernel, (sds((slots * elems, nodes + 2 * width), BF16), sds((comps, dims * slots * elems), BF16)),
+        (connectivity.T, node_count.reshape(1, elems), recovery.transpose(1, 3, 2, 0)),
+        4 * comps * slots * elems, 4 * comps * slots * elems, after=(stats,),
+    )
+    rho_diag, rho_mate = call(
+        rho_near_kernel,
+        (sds((block, block), F32), sds((2, block // 2, block // 2), F32)),
+        (place, freq, rate), 20 * block * block, 5 * block * block, smem=(0,),
+        scratch=[pltpu.VMEM((4, block, 128), F32), pltpu.VMEM((16, block), F32)], after=(pick,),
+    )
+    rho_far = call(
+        rho_far_kernel, sds((2 * block, block), F32), (place, freq, rate),
+        40 * block * block, 8 * block * block, smem=(0,),
+        scratch=[pltpu.VMEM((4, 2 * block, 128), F32), pltpu.VMEM((24, block), F32)],
+        after=(rho_diag,),
+    )
+    first = ()
+    if parts & (parts - 1) or parts == 1:
+        stats = lax.psum(stats, "dom")
+        extra = jnp.zeros_like(stats)
+    else:
+        reach = 1
+        waits = (rho_far,)
+        while True:
+            extra = moved("stage%d" % reach, stats, "dom", [(i, i ^ reach) for i in range(parts)])
+            reach *= 2
+            if reach == parts:
+                break
+            stats = call(
+                add_kernel, sds(stats.shape, F32), (stats, extra), stats.size, 12 * stats.size, after=waits
+            )
+            waits = ()
+            first = first or (stats,)
+    amps = call(
+        amps_kernel, sds((8, block), F32), (place, stats, extra, spectral, freq, rate),
+        20 * block, 60 * block, smem=(0,),
+    )
+    mate_amps = moved("amps_mate", amps, "mode", [(i, i ^ 1) for i in range(4)])
+    far_amps = moved("amps_far", amps, "mode", [(i, i ^ 2) for i in range(4)])
+
+    own, mate, far = [], [], []
+    for c in range(CHUNKS):
+        forces, sent = call(
+            forces_kernel,
+            (sds((comps, chunk), BF16), sds((part, chunk), BF16)),
+            (place, pick, force, held[c]) + halos[c],
+            4 * comps * dims * nodes * chunk, 8 * comps * chunk, smem=(0,),
+            scratch=[
+                pltpu.VMEM((dims, 2 * width, chunk), BF16), pltpu.VMEM((dims * slots * elems, chunk), BF16)
+            ],
+            after=first,
+        )
+        own.append(forces)
+        far.append(moved("far%d" % c, sent, "mode", [(i, i ^ 2) for i in range(4)]))
+        mate.append(moved("mate%d" % c, forces, "mode", [(i, i ^ 1) for i in range(4)]))
+    near = call(
+        functools.partial(near_kernel, dims, CHUNKS), sds((comps, 128), F32),
+        (place, amps, mate_amps, rho_diag, rho_mate, *own, *mate),
+        2 * comps * block * block, 6 * block * block, smem=(0,),
+        scratch=[pltpu.VMEM((dims, block, 128), F32), pltpu.VMEM((2, block, block // 4), BF16)],
+    )
+    weights = call(
+        functools.partial(weights_kernel, dims), sds((2 * block, block), BF16),
+        (amps, mate_amps, far_amps, rho_far), 14 * block * block, 12 * block * block,
+        scratch=[pltpu.VMEM((dims, 2 * block, 128), F32)],
+    )
+    value = near
+    for c in range(CHUNKS):
+        last = c == CHUNKS - 1
+        value = call(
+            functools.partial(far_kernel, c * chunk, CHUNKS, per_elem),
+            sds((1, comps) if last else (comps, 128), F32),
+            (place, value, weights, far[c], *own, *mate), 2 * comps * block * chunk, 8 * block * chunk,
+            smem=(0,), scratch=[pltpu.VMEM((comps, 128), F32)] * 2 if last else (),
+        )
+    value = value.reshape(comps)
+    for reach in (1, 2):
+        value = value + moved("sum%d" % reach, value, "mode", [(i, i ^ reach) for i in range(4)])
+    return value
 
 
 def extended_2(block, sides, width):
@@ -64,7 +518,7 @@
     return jnp.sum(projected * far_wide[:, None, :], axis=(1, 2))
 
 
-def per_device(
+def any_groups(
     shapes, masses, spectral, frequencies, damping, recovery, connectivity, node_count, shared
 ):
     rim_width = shared.shape[1]
@@ -129,6 +583,7 @@
         P(None, "dom"),
     )
     out_specs = P("dom")
+    step = four_groups if mesh.shape["mode"] == 4 else any_groups
     return jax.shard_map(
-        per_device, mesh=mesh, in_specs=in_specs, out_specs=out_specs, check_vma=False
-    )
+        step, mesh=mesh, in_specs=in_specs, out_specs=out_specs, check_vma=False
+    )

time: 168 us -> 58.7 us (0.35)
  other arithmetic: 66.8 us -> 0.58 us
  blocking collectives: 54.9 us -> 0 us
  matrix products: 25.2 us -> 0 us
  Pallas kernels: 0 us -> 22.1 us
  waiting for transfers between devices: 0.01 us -> 10.2 us
  starting transfers between devices: 7.93 us -> 18 us
  local copies, waits for them, and re-layouts: 12.4 us -> 7.07 us
    psum x2 -> x0, blocking collectives: 49.5 us -> none  [the longest x1 42.8 us: per_device(): lever_sum, general_sum = lax.psum((lever_arm, general), 'dom')]
    dot_general x4 -> x0, matrix products: 25.2 us -> none  [the longest x3 20.5 us: block_terms(): projected = jnp.dot(own_forces, weights, preferred_element_type=jnp.float32)]
    convert_element_type x6 -> x0, other arithmetic: 24.3 us -> none  [the longest x3 23.8 us: block_terms(): (amp_rows.T[:, :, None] * correlation[:, None, :] * amp_cols[None, :, :])...]
    pallas_call x0 -> x12, Pallas kernels: none -> 22.1 us  [call(): pl.pallas_call(body, out_shape=out_shape, in_specs=specs, out_specs=[VMEM...]
    mul x9 -> x0, other arithmetic: 19.3 us -> none  [the longest x3 18.5 us: block_terms(): amp_rows.T[:, :, None] * correlation[:, None, :] * amp_cols[None, :, :]]
    div x3 -> x0, other arithmetic: 14.8 us -> none  [correlation_block(): return top_part / bottom_part]
    ppermute x4 -> x11, waiting for transfers between devices: 0.01 us -> 10.2 us  [moved(): return lax.ppermute(value, axis, pairs)]
    ppermute x4 -> x11, starting transfers between devices: 7.93 us -> 18 us  [moved(): return lax.ppermute(value, axis, pairs)]
  transfers between devices with their start and end apart: 4 -> 11, of which waited for: 0 -> 6; matrix products, arithmetic and copies ran while one was open for 38% -> 0% of each run, Pallas kernels for 0% -> 29%
where the time goes in v3:
time: 58.7 us; the launch traced here: 58.2 us
  Pallas kernels  22.1 us (38%)
  starting transfers between devices  18 us (31%)
  waiting for transfers between devices  10.2 us (17%)
  local copies, waits for them, and re-layouts  7.07 us (12%)
    pallas_call x12, Pallas kernels, call(): pl.pallas_call(body, out_shape=out_shape, in_specs=specs, out_specs=[VMEM...  22.1 us
    ppermute x11, starting transfers between devices, moved(): return lax.ppermute(value, axis, pairs)  18 us
    ppermute x11, waiting for transfers between devices, moved(): return lax.ppermute(value, axis, pairs)  10.2 us
    unnamed x22, local copies, waits for them, and re-layouts  6.99 us
  transfers between devices with their start and end apart: 11, of which 6 were waited for; matrix products, arithmetic and copies ran while one was open for 0% of the time, Pallas kernels for 29%

profile of v3, /device:TPU:0, one launch (start us, length us, event | category | flops | bytes accessed | tf_op | source)
XLA Modules:
  0.0 58.2 jit_solution(6327753119013368478)
XLA Ops:
  0.0 0.0 copy-start
  0.0 1.4 %copy-done = bf16[3,256,1024]{2,1,0:T(8,128)(2,1)S(1)} copy-done((bf16[3,256,1024]{2,1,0:T(8,128)(2,1)S(1)}, bf16[3,256,1024]{2,1,0:T(8,128)(2,1)}, u32[]{:S(2)}) %copy-start) | copy-done | bytes 1572888
  1.4 0.0 copy-start.9
  1.4 0.7 %copy-done.9 = s32[2,64]{1,0:T(2,128)S(1)} copy-done((s32[2,64]{1,0:T(2,128)S(1)}, s32[2,64]{1,0:T(2,128)}, u32[]{:S(2)}) %copy-start.9) | copy-done | bytes 536
  2.1 0.7 %gather_kernel.1 = (bf16[192,1024]{1,0:T(8,128)(2,1)S(1)}, bf16[192,1024]{1,0:T(8,128)(2,1)S(1)}, bf16[3,256,1024]{2,1,0:T(8,128)(2,1)S(1)}) custom-call(s32[2,64]{1,0:T(2,128)S(1)} %copy-done.9, bf16[3,256,1024]{2,1,0:T(8,128)(2,1)S(1)} %copy-done), custom_call_target="tpu_custom_call" | custom-call | flops 201326592 | bytes 1572864 | tf_op jit(solution)/shard_map/gather_kernel/pallas_call | solution.py:26
  2.8 4.9 %collective-permute-start.4 = (bf16[192,1024]{1,0:T(8,128)(2,1)S(1)}, bf16[192,1024]{1,0:T(8,128)(2,1)S(1)}, u32[]{:S(2)}, u32[]{:S(2)}) collective-permute-start(bf16[192,1024]{1,0:T(8,128)(2,1)S(1)} %get-tuple-element.15.refs_2_), channel_id=1, source_target_pairs={{0,4},{4,8},{8,12},{12,16},{16,20},{20,24},{24,28},{1,5},{5,9},{9,... | collective-permute-start | bytes 1179656 | tf_op jit(solution)/shard_map/up0/ppermute | solution.py:356
  7.7 1.3 %collective-permute-start.5 = (bf16[192,1024]{1,0:T(8,128)(2,1)S(1)}, bf16[192,1024]{1,0:T(8,128)(2,1)S(1)}, u32[]{:S(2)}, u32[]{:S(2)}) collective-permute-start(bf16[192,1024]{1,0:T(8,128)(2,1)S(1)} %get-tuple-element.20), channel_id=1, source_target_pairs={{4,0},{8,4},{12,8},{16,12},{20,16},{24,20},{28,24},{5,1},{9,5},{13... | collective-permute-start | bytes 1179656 | tf_op jit(solution)/shard_map/down0/ppermute | solution.py:356
  9.0 0.0 copy-start.8
  9.0 0.7 %copy-done.8 = f32[256]{0:T(256)S(1)} copy-done((f32[256]{0:T(256)S(1)}, f32[256]{0:T(256)}, u32[]{:S(2)}) %copy-start.8) | copy-done | bytes 1048
  9.6 0.8 %stats_kernel.1.refs_3_.refs_0_ = f32[4,1024]{1,0:T(4,128)S(1)} custom-call(f32[1,256]{1,0:T(1,128)S(1)} %bitcast.23, bf16[3,256,1024]{2,1,0:T(8,128)(2,1)S(1)} %get-tuple-element.14.refs_1_.refs_3_, bf16[192,1024]{1,0:T(8,128)(2,1)S(1)} %get-tuple-element.15.refs_2_), custom_call_target="tpu_custom_call" | custom-call | flops 3932160 | bytes 1572864 | tf_op jit(solution)/shard_map/stats_kernel/pallas_call | solution.py:26
  10.5 2.7 %collective-permute-start = (f32[4,1024]{1,0:T(4,128)S(1)}, f32[4,1024]{1,0:T(4,128)S(1)}, u32[]{:S(2)}, u32[]{:S(2)}) collective-permute-start(f32[4,1024]{1,0:T(4,128)S(1)} %stats_kernel.1.refs_3_.refs_0_), channel_id=1, source_target_pairs={{0,4},{4,0},{8,12},{12,8},{16,20},{20,16},{24,28},{28,24},{1,5},{5... | collective-permute-start | bytes 49160 | tf_op jit(solution)/shard_map/stage1/ppermute | solution.py:356
  13.2 0.1 stack.27.refs_0_
  13.3 0.0 copy-start.6
  13.3 0.7 %copy-done.6 = bf16[64,8,4,3]{0,2,3,1:T(4,128)(2,1)S(1)} copy-done((bf16[64,8,4,3]{0,2,3,1:T(4,128)(2,1)S(1)}, bf16[64,8,4,3]{0,2,3,1:T(4,128)(2,1)}, u32[]{:S(2)}) %copy-start.6) | copy-done | bytes 12312
  14.0 0.0 copy-start.7
  14.0 0.7 %copy-done.7 = s32[64,4]{0,1:T(4,128)S(1)} copy-done((s32[64,4]{0,1:T(4,128)S(1)}, s32[64,4]{0,1:T(4,128)}, u32[]{:S(2)}) %copy-start.7) | copy-done | bytes 1048
  14.7 0.0 copy-start.10
  14.7 0.7 %copy-done.10 = s32[64]{0:T(128)S(1)} copy-done((s32[64]{0:T(128)S(1)}, s32[64]{0:T(128)}, u32[]{:S(2)}) %copy-start.10) | copy-done | bytes 280
  15.3 0.4 table_kernel.1
  15.8 0.0 copy-start.1
  15.8 0.7 %copy-done.1 = f32[4096]{0:T(1024)S(1)} copy-done((f32[4096]{0:T(1024)S(1)}, f32[4096]{0:T(1024)}, u32[]{:S(2)}) %copy-start.1) | copy-done | bytes 16408
  16.5 0.0 copy-start.2
  16.5 0.7 %copy-done.2 = f32[4096]{0:T(1024)S(1)} copy-done((f32[4096]{0:T(1024)S(1)}, f32[4096]{0:T(1024)}, u32[]{:S(2)}) %copy-start.2) | copy-done | bytes 16408
  17.2 3.0 %rho_near_kernel.1 = (f32[1024,1024]{1,0:T(8,128)S(1)}, f32[2,512,512]{2,1,0:T(8,128)S(1)}) custom-call(s32[6]{0:T(128)S(1)} %stack.27.refs_0_, f32[1,4096]{1,0:T(1,128)S(1)} %bitcast.13, f32[1,4096]{1,0:T(1,128)S(1)} %bitcast.16, bf16[256,384]{1,0:T(8,128)(2,1)S(1)} %get-tuple-element.16.refs_3_.refs_1_), custom_call_target="tpu_custom_call" | custom-call | flops 20971520 | bytes 5242880 | tf_op jit(solution)/shard_map/rho_near_kernel/pallas_call | solution.py:26
  20.2 0.0 copy-start.3
  20.2 0.7 %copy-done.3 = f32[4096]{0:T(1024)S(1)} copy-done((f32[4096]{0:T(1024)S(1)}, f32[4096]{0:T(1024)}, u32[]{:S(2)}) %copy-start.3) | copy-done | bytes 16408
  20.9 5.1 %rho_far_kernel.1.refs_2_.refs_3_ = f32[2048,1024]{1,0:T(8,128)S(1)} custom-call(s32[6]{0:T(128)S(1)} %stack.27.refs_0_, f32[1,4096]{1,0:T(1,128)S(1)} %bitcast.14, f32[1,4096]{1,0:T(1,128)S(1)} %bitcast.17, f32[1024,1024]{1,0:T(8,128)S(1)} %get-tuple-element.17.refs_3_), custom_call_target="tpu_custom_call" | custom-call | flops 41943040 | bytes 8388608 | tf_op jit(solution)/shard_map/rho_far_kernel/pallas_call | solution.py:26
  26.0 0.0 collective-permute-done.refs_1_
  26.0 0.0 copy-start.4
  26.0 0.0 copy-start.5
  26.0 0.0 collective-permute-done.4.refs_4_
  26.0 0.0 collective-permute-done.5.refs_5_
  26.1 2.6 %forces_kernel.1 = (bf16[512,1024]{1,0:T(8,128)(2,1)S(1)}, bf16[256,1024]{1,0:T(8,128)(2,1)S(1)}) custom-call(s32[6]{0:T(128)S(1)} %stack.27.refs_0_, bf16[256,384]{1,0:T(8,128)(2,1)S(1)} %get-tuple-element.16.refs_3_.refs_1_, bf16[512,768]{1,0:T(8,128)(2,1)S(1)} %get-tuple-element.19.refs_2_, bf16[3,256,1024]{2,1,0:T(8,128)(2,1)S(1)} %get-tuple-element.14.refs_1_.refs_3_, ...), custom_call_target="tpu_custom_call" | custom-call | flops 1610612736 | bytes 4194304 | tf_op jit(solution)/shard_map/forces_kernel/pallas_call | solution.py:26
  28.7 0.1 collective-permute-start.6
  28.8 1.6 %collective-permute-start.8 = (bf16[256,1024]{1,0:T(8,128)(2,1)S(1)}, bf16[256,1024]{1,0:T(8,128)(2,1)S(1)}, u32[]{:S(2)}, u32[]{:S(2)}) collective-permute-start(bf16[256,1024]{1,0:T(8,128)(2,1)S(1)} %get-tuple-element.22), channel_id=1, source_target_pairs={{0,2},{1,3},{2,0},{3,1},{4,6},{5,7},{6,4},{7,5},{8,10},{9,11},{10,... | collective-permute-start | bytes 1572872 | tf_op jit(solution)/shard_map/far0/ppermute | solution.py:356
  30.4 2.2 %collective-permute-start.1 = (f32[4,1024]{1,0:T(4,128)S(1)}, f32[4,1024]{1,0:T(4,128)S(1)}, u32[]{:S(2)}, u32[]{:S(2)}) collective-permute-start(f32[4,1024]{1,0:T(4,128)S(1)} %add_kernel.2.refs_0_.refs_6_), channel_id=1, source_target_pairs={{0,8},{4,12},{8,0},{12,4},{16,24},{20,28},{24,16},{28,20},{1,9},{5... | collective-permute-start | bytes 49160 | tf_op jit(solution)/shard_map/stage2/ppermute | solution.py:356
  32.6 1.7 %collective-permute-done.1.refs_1_ = f32[4,1024]{1,0:T(4,128)S(1)} collective-permute-done((f32[4,1024]{1,0:T(4,128)S(1)}, f32[4,1024]{1,0:T(4,128)S(1)}, u32[]{:S(2)}, u32[]{:S(2)}) %collective-permute-start.1) | collective-permute-done | bytes 16416 | tf_op jit(solution)/shard_map/stage2/ppermute | solution.py:356
  34.3 3.0 %collective-permute-start.2 = (f32[4,1024]{1,0:T(4,128)S(1)}, f32[4,1024]{1,0:T(4,128)S(1)}, u32[]{:S(2)}, u32[]{:S(2)}) collective-permute-start(f32[4,1024]{1,0:T(4,128)S(1)} %add_kernel.3.refs_1_), channel_id=1, source_target_pairs={{0,16},{4,20},{8,24},{12,28},{16,0},{20,4},{24,8},{28,12},{1,17},{... | collective-permute-start | bytes 49160 | tf_op jit(solution)/shard_map/stage4/ppermute | solution.py:356
  37.3 1.7 %collective-permute-done.2.refs_2_ = f32[4,1024]{1,0:T(4,128)S(1)} collective-permute-done((f32[4,1024]{1,0:T(4,128)S(1)}, f32[4,1024]{1,0:T(4,128)S(1)}, u32[]{:S(2)}, u32[]{:S(2)}) %collective-permute-start.2) | collective-permute-done | bytes 16416 | tf_op jit(solution)/shard_map/stage4/ppermute | solution.py:356
  39.1 0.0 copy-done.4
  39.1 0.0 copy-done.5
  39.1 0.6 amps_kernel.1.refs_1_.refs_0_
  39.6 0.1 collective-permute-start.3
  39.7 0.6 collective-permute-start.7
  40.3 0.6 %collective-permute-done.3.refs_2_.refs_1_ = f32[8,1024]{1,0:T(8,128)S(1)} collective-permute-done((f32[8,1024]{1,0:T(8,128)S(1)}, f32[8,1024]{1,0:T(8,128)S(1)}, u32[]{:S(2)}, u32[]{:S(2)}) %collective-permute-start.3) | collective-permute-done | bytes 32800 | tf_op jit(solution)/shard_map/amps_mate/ppermute | solution.py:356
  40.9 2.9 %collective-permute-done.7.refs_2_ = f32[8,1024]{1,0:T(8,128)S(1)} collective-permute-done((f32[8,1024]{1,0:T(8,128)S(1)}, f32[8,1024]{1,0:T(8,128)S(1)}, u32[]{:S(2)}, u32[]{:S(2)}) %collective-permute-start.7) | collective-permute-done | bytes 32800 | tf_op jit(solution)/shard_map/amps_far/ppermute | solution.py:356
  43.8 3.3 %weights_kernel.1.refs_2_ = bf16[2048,1024]{1,0:T(8,128)(2,1)S(1)} custom-call(f32[8,1024]{1,0:T(8,128)S(1)} %amps_kernel.1.refs_1_.refs_0_, f32[8,1024]{1,0:T(8,128)S(1)} %collective-permute-done.3.refs_2_.refs_1_, f32[8,1024]{1,0:T(8,128)S(1)} %collective-permute-done.7.refs_2_, f32[2048,1024]{1,0:T(8,128)S(1)} %rho_far_kernel.1.refs_2_.refs_3_), custom_call_target="tpu_custom_call" | custom-call | flops 14680064 | bytes 12582912 | tf_op jit(solution)/shard_map/weights_kernel/pallas_call | solution.py:26
  47.2 0.0 collective-permute-done.6.refs_6_.refs_5_
  47.2 3.5 %near_kernel.1.refs_1_ = f32[512,128]{1,0:T(8,128)S(1)} custom-call(s32[6]{0:T(128)S(1)} %stack.27.refs_0_, f32[8,1024]{1,0:T(8,128)S(1)} %amps_kernel.1.refs_1_.refs_0_, f32[8,1024]{1,0:T(8,128)S(1)} %collective-permute-done.3.refs_2_.refs_1_, f32[1024,1024]{1,0:T(8,128)S(1)} %get-tuple-element.17.refs_3_, f32[2,512,512]{2,1,0:T(8,128)S(1)} %get-tuple-element.18.refs_4_, ...), custom_call_target="tpu_custom_call" | custom-call | flops 1073741824 | bytes 6291456 | tf_op jit(solution)/shard_map/near_kernel/pallas_call | solution.py:26
  50.6 0.0 collective-permute-done.8.refs_3_
  50.6 2.2 %far_kernel.1 = f32[1,512]{1,0:T(1,128)S(1)} custom-call(s32[6]{0:T(128)S(1)} %stack.27.refs_0_, f32[512,128]{1,0:T(8,128)S(1)} %near_kernel.1.refs_1_, bf16[2048,1024]{1,0:T(8,128)(2,1)S(1)} %weights_kernel.1.refs_2_, bf16[256,1024]{1,0:T(8,128)(2,1)S(1)} %collective-permute-done.8.refs_3_, bf16[512,1024]{1,0:T(8,128)(2,1)S(1)} %get-tuple-element.21.refs_5_.refs_4_, ...), custom_call_target="tpu_custom_call" | custom-call | flops 1073741824 | bytes 8388608 | tf_op jit(solution)/shard_map/far_kernel/pallas_call | solution.py:26
  52.8 0.0 collective-permute-start.9
  52.8 1.2 %collective-permute-done.9 = f32[512]{0:T(512)S(1)} collective-permute-done((f32[512]{0:T(512)S(1)}, f32[512]{0:T(512)S(1)}, u32[]{:S(2)}, u32[]{:S(2)}) %collective-permute-start.9) | collective-permute-done | bytes 2080 | tf_op jit(solution)/shard_map/sum1/ppermute | solution.py:356
  54.0 1.5 %collective-permute-start.10 = (f32[512]{0:T(512)S(1)}, f32[512]{0:T(512)S(1)}, u32[]{:S(2)}, u32[]{:S(2)}) collective-permute-start(f32[512]{0:T(512)S(1)} %add.6), channel_id=1, source_target_pairs={{0,2},{1,3},{2,0},{3,1},{4,6},{5,7},{6,4},{7,5},{8,10},{9,11},{10,... | collective-permute-start | bytes 6152 | tf_op jit(solution)/shard_map/sum2/ppermute | solution.py:356
  55.5 2.1 %collective-permute-done.10 = f32[512]{0:T(512)S(1)} collective-permute-done((f32[512]{0:T(512)S(1)}, f32[512]{0:T(512)S(1)}, u32[]{:S(2)}, u32[]{:S(2)}) %collective-permute-start.10) | collective-permute-done | bytes 2080 | tf_op jit(solution)/shard_map/sum2/ppermute | solution.py:356
  57.6 0.6 add.7
  (3 shorter events, 0.0 us)
Async XLA Ops:
  0.0 1.4 %copy-start = (bf16[3,256,1024]{2,1,0:T(8,128)(2,1)S(1)}, bf16[3,256,1024]{2,1,0:T(8,128)(2,1)}, u32[]{:S(2)}) copy-start(bf16[3,256,1024]{2,1,0:T(8,128)(2,1)} %refs_1_.1) | copy-start | bytes 4718596
  1.4 0.7 %copy-start.9 = (s32[2,64]{1,0:T(2,128)S(1)}, s32[2,64]{1,0:T(2,128)}, u32[]{:S(2)}) copy-start(s32[2,64]{1,0:T(2,128)} %refs_0_.1) | copy-start | bytes 1540
  2.8 23.3 %collective-permute-start.4 = (bf16[192,1024]{1,0:T(8,128)(2,1)S(1)}, bf16[192,1024]{1,0:T(8,128)(2,1)S(1)}, u32[]{:S(2)}, u32[]{:S(2)}) collective-permute-start(bf16[192,1024]{1,0:T(8,128)(2,1)S(1)} %get-tuple-element.15.refs_2_), channel_id=1, source_target_pairs={{0,4},{4,8},{8,12},{12,16},{16,20},{20,24},{24,28},{1,5},{5,9},{9,... | collective-permute-start | bytes 1179656 | tf_op jit(solution)/shard_map/up0/ppermute | solution.py:356
  7.7 18.4 %collective-permute-start.5 = (bf16[192,1024]{1,0:T(8,128)(2,1)S(1)}, bf16[192,1024]{1,0:T(8,128)(2,1)S(1)}, u32[]{:S(2)}, u32[]{:S(2)}) collective-permute-start(bf16[192,1024]{1,0:T(8,128)(2,1)S(1)} %get-tuple-element.20), channel_id=1, source_target_pairs={{4,0},{8,4},{12,8},{16,12},{20,16},{24,20},{28,24},{5,1},{9,5},{13... | collective-permute-start | bytes 1179656 | tf_op jit(solution)/shard_map/down0/ppermute | solution.py:356
  9.0 0.7 %copy-start.8 = (f32[256]{0:T(256)S(1)}, f32[256]{0:T(256)}, u32[]{:S(2)}) copy-start(f32[256]{0:T(256)} %param.10) | copy-start | bytes 3076
  10.5 15.5 %collective-permute-start = (f32[4,1024]{1,0:T(4,128)S(1)}, f32[4,1024]{1,0:T(4,128)S(1)}, u32[]{:S(2)}, u32[]{:S(2)}) collective-permute-start(f32[4,1024]{1,0:T(4,128)S(1)} %stats_kernel.1.refs_3_.refs_0_), channel_id=1, source_target_pairs={{0,4},{4,0},{8,12},{12,8},{16,20},{20,16},{24,28},{28,24},{1,5},{5... | collective-permute-start | bytes 49160 | tf_op jit(solution)/shard_map/stage1/ppermute | solution.py:356
  13.3 0.7 %copy-start.6 = (bf16[64,8,4,3]{0,2,3,1:T(4,128)(2,1)S(1)}, bf16[64,8,4,3]{0,2,3,1:T(4,128)(2,1)}, u32[]{:S(2)}) copy-start(bf16[64,8,4,3]{0,2,3,1:T(4,128)(2,1)} %param.14) | copy-start | bytes 36868
  14.0 0.7 %copy-start.7 = (s32[64,4]{0,1:T(4,128)S(1)}, s32[64,4]{0,1:T(4,128)}, u32[]{:S(2)}) copy-start(s32[64,4]{0,1:T(4,128)} %param.15) | copy-start | bytes 3076
  14.7 0.7 %copy-start.10 = (s32[64]{0:T(128)S(1)}, s32[64]{0:T(128)}, u32[]{:S(2)}) copy-start(s32[64]{0:T(128)} %param.16) | copy-start | bytes 772
  15.8 0.7 %copy-start.1 = (f32[4096]{0:T(1024)S(1)}, f32[4096]{0:T(1024)}, u32[]{:S(2)}) copy-start(f32[4096]{0:T(1024)} %param.12) | copy-start | bytes 49156
  16.5 0.7 %copy-start.2 = (f32[4096]{0:T(1024)S(1)}, f32[4096]{0:T(1024)}, u32[]{:S(2)}) copy-start(f32[4096]{0:T(1024)} %param.13) | copy-start | bytes 49156
  20.2 0.7 %copy-start.3 = (f32[4096]{0:T(1024)S(1)}, f32[4096]{0:T(1024)}, u32[]{:S(2)}) copy-start(f32[4096]{0:T(1024)} %param.13) | copy-start | bytes 49156
  26.0 13.1 %copy-start.4 = (f32[4096]{0:T(1024)S(1)}, f32[4096]{0:T(1024)}, u32[]{:S(2)}) copy-start(f32[4096]{0:T(1024)} %param.13) | copy-start | bytes 49156
  26.0 13.0 %copy-start.5 = (f32[3,4096]{1,0:T(4,128)S(1)}, f32[3,4096]{1,0:T(4,128)}, u32[]{:S(2)}) copy-start(f32[3,4096]{1,0:T(4,128)} %refs_3_.1) | copy-start | bytes 147460
  28.7 18.5 %collective-permute-start.6 = (bf16[512,1024]{1,0:T(8,128)(2,1)S(1)}, bf16[512,1024]{1,0:T(8,128)(2,1)S(1)}, u32[]{:S(2)}, u32[]{:S(2)}) collective-permute-start(bf16[512,1024]{1,0:T(8,128)(2,1)S(1)} %get-tuple-element.21.refs_5_.refs_4_), channel_id=1, source_target_pairs={{0,1},{1,0},{2,3},{3,2},{4,5},{5,4},{6,7},{7,6},{8,9},{9,8},{10,11... | collective-permute-start | bytes 3145736 | tf_op jit(solution)/shard_map/mate0/ppermute | solution.py:356
  28.8 21.9 %collective-permute-start.8 = (bf16[256,1024]{1,0:T(8,128)(2,1)S(1)}, bf16[256,1024]{1,0:T(8,128)(2,1)S(1)}, u32[]{:S(2)}, u32[]{:S(2)}) collective-permute-start(bf16[256,1024]{1,0:T(8,128)(2,1)S(1)} %get-tuple-element.22), channel_id=1, source_target_pairs={{0,2},{1,3},{2,0},{3,1},{4,6},{5,7},{6,4},{7,5},{8,10},{9,11},{10,... | collective-permute-start | bytes 1572872 | tf_op jit(solution)/shard_map/far0/ppermute | solution.py:356
  30.4 3.9 %collective-permute-start.1 = (f32[4,1024]{1,0:T(4,128)S(1)}, f32[4,1024]{1,0:T(4,128)S(1)}, u32[]{:S(2)}, u32[]{:S(2)}) collective-permute-start(f32[4,1024]{1,0:T(4,128)S(1)} %add_kernel.2.refs_0_.refs_6_), channel_id=1, source_target_pairs={{0,8},{4,12},{8,0},{12,4},{16,24},{20,28},{24,16},{28,20},{1,9},{5... | collective-permute-start | bytes 49160 | tf_op jit(solution)/shard_map/stage2/ppermute | solution.py:356
  34.3 4.8 %collective-permute-start.2 = (f32[4,1024]{1,0:T(4,128)S(1)}, f32[4,1024]{1,0:T(4,128)S(1)}, u32[]{:S(2)}, u32[]{:S(2)}) collective-permute-start(f32[4,1024]{1,0:T(4,128)S(1)} %add_kernel.3.refs_1_), channel_id=1, source_target_pairs={{0,16},{4,20},{8,24},{12,28},{16,0},{20,4},{24,8},{28,12},{1,17},{... | collective-permute-start | bytes 49160 | tf_op jit(solution)/shard_map/stage4/ppermute | solution.py:356
  39.6 1.3 %collective-permute-start.3 = (f32[8,1024]{1,0:T(8,128)S(1)}, f32[8,1024]{1,0:T(8,128)S(1)}, u32[]{:S(2)}, u32[]{:S(2)}) collective-permute-start(f32[8,1024]{1,0:T(8,128)S(1)} %amps_kernel.1.refs_1_.refs_0_), channel_id=1, source_target_pairs={{0,1},{1,0},{2,3},{3,2},{4,5},{5,4},{6,7},{7,6},{8,9},{9,8},{10,11... | collective-permute-start | bytes 98312 | tf_op jit(solution)/shard_map/amps_mate/ppermute | solution.py:356
  39.7 4.1 %collective-permute-start.7 = (f32[8,1024]{1,0:T(8,128)S(1)}, f32[8,1024]{1,0:T(8,128)S(1)}, u32[]{:S(2)}, u32[]{:S(2)}) collective-permute-start(f32[8,1024]{1,0:T(8,128)S(1)} %amps_kernel.1.refs_1_.refs_0_), channel_id=1, source_target_pairs={{0,2},{1,3},{2,0},{3,1},{4,6},{5,7},{6,4},{7,5},{8,10},{9,11},{10,... | collective-permute-start | bytes 98312 | tf_op jit(solution)/shard_map/amps_far/ppermute | solution.py:356
  52.8 1.2 %collective-permute-start.9 = (f32[512]{0:T(512)S(1)}, f32[512]{0:T(512)S(1)}, u32[]{:S(2)}, u32[]{:S(2)}) collective-permute-start(f32[512]{0:T(512)S(1)} %bitcast.20), channel_id=1, source_target_pairs={{0,1},{1,0},{2,3},{3,2},{4,5},{5,4},{6,7},{7,6},{8,9},{9,8},{10,11... | collective-permute-start | bytes 6152 | tf_op jit(solution)/shard_map/sum1/ppermute | solution.py:356
  54.0 3.6 %collective-permute-start.10 = (f32[512]{0:T(512)S(1)}, f32[512]{0:T(512)S(1)}, u32[]{:S(2)}, u32[]{:S(2)}) collective-permute-start(f32[512]{0:T(512)S(1)} %add.6), channel_id=1, source_target_pairs={{0,2},{1,3},{2,0},{3,1},{4,6},{5,7},{6,4},{7,5},{8,10},{9,11},{10,... | collective-permute-start | bytes 6152 | tf_op jit(solution)/shard_map/sum2/ppermute | solution.py:356

commit v4 on v3

--- a/solution.py
+++ b/solution.py
@@ -6,6 +6,7 @@
 from jax.experimental.pallas import tpu as pltpu
 from jax.sharding import PartitionSpec as P
 
+
 F32 = jnp.float32
 BF16 = jnp.bfloat16
 VMEM = pl.BlockSpec(memory_space=pltpu.VMEM)
@@ -14,7 +15,7 @@
 SMEM = pl.BlockSpec(memory_space=pltpu.SMEM)
 
 
-def call(kernel, out_shape, args, flops, nbytes, smem=(), hbm=(), scratch=(), vmem=24 << 20, after=()):
+def call(kernel, out_shape, args, cost, smem=(), hbm=(), scratch=(), vmem=14 << 20, after=()):
     count = len(args)
     specs = [SMEM if i in smem else HBM if i in hbm else VMEM for i in range(count)]
     specs += [ANY] * len(after)
@@ -29,9 +30,8 @@
         in_specs=specs,
         out_specs=[VMEM] * len(out_shape) if many else VMEM,
         scratch_shapes=list(scratch),
-        cost_estimate=pl.CostEstimate(flops=flops, bytes_accessed=nbytes, transcendentals=0),
+        cost_estimate=pl.CostEstimate(flops=int(1.1e9 * cost), bytes_accessed=0, transcendentals=0),
         compiler_params=pltpu.CompilerParams(vmem_limit_bytes=vmem),
-        name=getattr(kernel, "func", kernel).__name__,
     )(*args, *after)
 
 
@@ -238,7 +238,7 @@
     place_ref, own_amps_ref, mate_amps_ref, diag_ref, cross_ref = refs[:5]
     own_refs, mate_refs = refs[5 : 5 + chunks], refs[5 + chunks : 5 + 2 * chunks]
     acc, side_scr, w_scr = refs[5 + 2 * chunks :]
-    comps, chunk = own_refs[0].shape
+    _, chunk = own_refs[0].shape
     block = diag_ref.shape[0]
     tile = block // 4
     half = block // 2
@@ -330,7 +330,11 @@
 CHUNKS = 1
 
 
-def four_groups(
+def four_groups(*args):
+    return combined(*args)
+
+
+def combined(
     shapes, masses, spectral, frequencies, damping, recovery, connectivity, node_count, shared
 ):
     dims, nodes, block = shapes.shape
@@ -351,15 +355,11 @@
     freq = frequencies.reshape(1, -1)
     rate = damping.reshape(1, -1)
 
-    def moved(name, value, axis, pairs):
-        with jax.named_scope(name):
-            return lax.ppermute(value, axis, pairs)
-
     def gathered(c, after):
         return call(
             functools.partial(gather_kernel, c * chunk),
             (sds((dims * width, chunk), BF16), sds((dims * width, chunk), BF16), sds((dims, nodes, chunk), BF16)),
-            (shared, shapes), 4 * width * nodes * dims * chunk, 2 * dims * nodes * chunk, hbm=(1,),
+            (shared, shapes), 2.0 / CHUNKS, hbm=(1,),
             scratch=[pltpu.SemaphoreType.DMA], after=after,
         )
 
@@ -369,53 +369,44 @@
         up, down, kept = gathered(c, after)
         held.append(kept)
         after = (up,)
-        halos.append((moved("up%d" % c, up, "dom", ahead), moved("down%d" % c, down, "dom", back)))
+        halos.append((lax.ppermute(up, "dom", ahead), lax.ppermute(down, "dom", back)))
 
     stats = call(
-        functools.partial(stats_kernel, CHUNKS), sds((dims + 1, block), F32), (masses.reshape(1, nodes), *held),
-        5 * dims * nodes * block, 2 * dims * nodes * block,
+        functools.partial(stats_kernel, CHUNKS), sds((dims + 1, block), F32), (masses.reshape(1, nodes), *held), 0.8,
         scratch=[pltpu.VMEM((nodes, 128), F32)], after=after,
     )
     pick, force = call(
         table_kernel, (sds((slots * elems, nodes + 2 * width), BF16), sds((comps, dims * slots * elems), BF16)),
         (connectivity.T, node_count.reshape(1, elems), recovery.transpose(1, 3, 2, 0)),
-        4 * comps * slots * elems, 4 * comps * slots * elems, after=(stats,),
-    )
+        0.5, after=(stats,),
+    )
+    order = [1 << q for q in range(1, parts.bit_length() - 1)] + [1]
+    if parts & (parts - 1) or parts == 1:
+        stats = lax.psum(stats, "dom")
+        order = []
+    extra = jnp.zeros_like(stats)
+    for q, reach in enumerate(order):
+        if q:
+            stats = call(add_kernel, sds(stats.shape, F32), (stats, extra), 0.5)
+        extra = lax.ppermute(stats, "dom", [(i, i ^ reach) for i in range(parts)])
     rho_diag, rho_mate = call(
         rho_near_kernel,
         (sds((block, block), F32), sds((2, block // 2, block // 2), F32)),
-        (place, freq, rate), 20 * block * block, 5 * block * block, smem=(0,),
+        (place, freq, rate), 3.0, smem=(0,),
         scratch=[pltpu.VMEM((4, block, 128), F32), pltpu.VMEM((16, block), F32)], after=(pick,),
     )
     rho_far = call(
         rho_far_kernel, sds((2 * block, block), F32), (place, freq, rate),
-        40 * block * block, 8 * block * block, smem=(0,),
+        5.0, smem=(0,),
         scratch=[pltpu.VMEM((4, 2 * block, 128), F32), pltpu.VMEM((24, block), F32)],
         after=(rho_diag,),
     )
-    first = ()
-    if parts & (parts - 1) or parts == 1:
-        stats = lax.psum(stats, "dom")
-        extra = jnp.zeros_like(stats)
-    else:
-        reach = 1
-        waits = (rho_far,)
-        while True:
-            extra = moved("stage%d" % reach, stats, "dom", [(i, i ^ reach) for i in range(parts)])
-            reach *= 2
-            if reach == parts:
-                break
-            stats = call(
-                add_kernel, sds(stats.shape, F32), (stats, extra), stats.size, 12 * stats.size, after=waits
-            )
-            waits = ()
-            first = first or (stats,)
     amps = call(
         amps_kernel, sds((8, block), F32), (place, stats, extra, spectral, freq, rate),
-        20 * block, 60 * block, smem=(0,),
-    )
-    mate_amps = moved("amps_mate", amps, "mode", [(i, i ^ 1) for i in range(4)])
-    far_amps = moved("amps_far", amps, "mode", [(i, i ^ 2) for i in range(4)])
+        0.6, smem=(0,), after=(rho_far,),
+    )
+    mate_amps = lax.ppermute(amps, "mode", [(i, i ^ 1) for i in range(4)])
+    far_amps = lax.ppermute(amps, "mode", [(i, i ^ 2) for i in range(4)])
 
     own, mate, far = [], [], []
     for c in range(CHUNKS):
@@ -423,24 +414,24 @@
             forces_kernel,
             (sds((comps, chunk), BF16), sds((part, chunk), BF16)),
             (place, pick, force, held[c]) + halos[c],
-            4 * comps * dims * nodes * chunk, 8 * comps * chunk, smem=(0,),
+            2.6 / CHUNKS, smem=(0,),
             scratch=[
                 pltpu.VMEM((dims, 2 * width, chunk), BF16), pltpu.VMEM((dims * slots * elems, chunk), BF16)
             ],
-            after=first,
+            after=(amps,),
         )
         own.append(forces)
-        far.append(moved("far%d" % c, sent, "mode", [(i, i ^ 2) for i in range(4)]))
-        mate.append(moved("mate%d" % c, forces, "mode", [(i, i ^ 1) for i in range(4)]))
+        far.append(lax.ppermute(sent, "mode", [(i, i ^ 2) for i in range(4)]))
+        mate.append(lax.ppermute(forces, "mode", [(i, i ^ 1) for i in range(4)]))
     near = call(
         functools.partial(near_kernel, dims, CHUNKS), sds((comps, 128), F32),
         (place, amps, mate_amps, rho_diag, rho_mate, *own, *mate),
-        2 * comps * block * block, 6 * block * block, smem=(0,),
+        3.4, smem=(0,),
         scratch=[pltpu.VMEM((dims, block, 128), F32), pltpu.VMEM((2, block, block // 4), BF16)],
     )
     weights = call(
         functools.partial(weights_kernel, dims), sds((2 * block, block), BF16),
-        (amps, mate_amps, far_amps, rho_far), 14 * block * block, 12 * block * block,
+        (amps, mate_amps, far_amps, rho_far), 3.3,
         scratch=[pltpu.VMEM((dims, 2 * block, 128), F32)],
     )
     value = near
@@ -449,12 +440,12 @@
         value = call(
             functools.partial(far_kernel, c * chunk, CHUNKS, per_elem),
             sds((1, comps) if last else (comps, 128), F32),
-            (place, value, weights, far[c], *own, *mate), 2 * comps * block * chunk, 8 * block * chunk,
+            (place, value, weights, far[c], *own, *mate), 2.1 / CHUNKS,
             smem=(0,), scratch=[pltpu.VMEM((comps, 128), F32)] * 2 if last else (),
         )
     value = value.reshape(comps)
     for reach in (1, 2):
-        value = value + moved("sum%d" % reach, value, "mode", [(i, i ^ reach) for i in range(4)])
+        value = value + lax.ppermute(value, "mode", [(i, i ^ reach) for i in range(4)])
     return value
 
 
@@ -583,7 +574,9 @@
         P(None, "dom"),
     )
     out_specs = P("dom")
-    step = four_groups if mesh.shape["mode"] == 4 else any_groups
-    return jax.shard_map(
+    special = mesh.shape["mode"] == 4
+    step = four_groups if special else any_groups
+    step = jax.shard_map(
         step, mesh=mesh, in_specs=in_specs, out_specs=out_specs, check_vma=False
     )
+    return step

time: 58.7 us -> 56.2 us (0.957)
  waiting for transfers between devices: 10.2 us -> 14.5 us
  local copies, waits for them, and re-layouts: 7.07 us -> 3.58 us
  starting transfers between devices: 18 us -> 14.9 us
    ppermute x11, waiting for transfers between devices: 10.2 us -> 14.5 us  [the longest x1 4.47 us: combined(): far.append(lax.ppermute(sent, 'mode', [(i, i ^ 2) for i in range(4)]))]
    unnamed x22, local copies, waits for them, and re-layouts: 6.99 us -> 3.5 us
    ppermute x11, starting transfers between devices: 18 us -> 14.9 us  [the longest x3 5.2 us: combined(): extra = lax.ppermute(stats, 'dom', [(i, i ^ reach) for i in range(parts)])]
  transfers between devices with their start and end apart: 11 -> 11, of which waited for: 6 -> 6; matrix products, arithmetic and copies ran while one was open for 0% -> 0% of each run, Pallas kernels for 29% -> 30%
where the time goes in v4:
time: 56.2 us; the launch traced here: 55.9 us
  Pallas kernels  22.1 us (39%)
  starting transfers between devices  14.9 us (27%)
  waiting for transfers between devices  14.5 us (26%)
  local copies, waits for them, and re-layouts  3.58 us (6%)
  other arithmetic  0.58 us (1%)
    pallas_call x12, Pallas kernels, call(): pl.pallas_call(body, out_shape=out_shape, in_specs=specs, out_specs=[VMEM...  22.1 us
    ppermute x3, starting transfers between devices, combined(): extra = lax.ppermute(stats, 'dom', [(i, i ^ reach) for i in range(parts)])  5.2 us
    ppermute x1, starting transfers between devices, combined(): lax.ppermute(up, 'dom', ahead)  4.89 us
    ppermute x1, waiting for transfers between devices, combined(): far.append(lax.ppermute(sent, 'mode', [(i, i ^ 2) for i in range(4)]))  4.47 us
    ppermute x3, waiting for transfers between devices, combined(): extra = lax.ppermute(stats, 'dom', [(i, i ^ reach) for i in range(parts)])  4.34 us
    ppermute x2, waiting for transfers between devices, combined(): lax.ppermute(value, 'mode', [(i, i ^ reach) for i in range(4)])  3.79 us
    unnamed x22, local copies, waits for them, and re-layouts  3.5 us
    ppermute x1, waiting for transfers between devices, combined(): far_amps = lax.ppermute(amps, 'mode', [(i, i ^ 2) for i in range(4)])  1.73 us
  transfers between devices with their start and end apart: 11, of which 6 were waited for; matrix products, arithmetic and copies ran while one was open for 0% of the time, Pallas kernels for 30%

profile of v4, /device:TPU:0, one launch (start us, length us, event | category | flops | bytes accessed | tf_op | source)
XLA Modules:
  0.0 55.9 jit_solution(15105453791758765696)
XLA Ops:
  0.0 0.0 copy-start.3
  0.0 1.4 %copy-done.3 = bf16[3,256,1024]{2,1,0:T(8,128)(2,1)S(1)} copy-done((bf16[3,256,1024]{2,1,0:T(8,128)(2,1)S(1)}, bf16[3,256,1024]{2,1,0:T(8,128)(2,1)}, u32[]{:S(2)}) %copy-start.3) | copy-done | bytes 1572888
  1.4 0.0 copy-start.6
  1.4 0.7 %copy-done.6 = s32[2,64]{1,0:T(2,128)S(1)} copy-done((s32[2,64]{1,0:T(2,128)S(1)}, s32[2,64]{1,0:T(2,128)}, u32[]{:S(2)}) %copy-start.6) | copy-done | bytes 536
  2.1 0.0 copy-start.7
  2.1 0.0 copy-start.4
  2.1 0.0 copy-start.5
  2.1 0.0 copy-start.8
  2.1 0.7 %shard_map.91 = (bf16[192,1024]{1,0:T(8,128)(2,1)S(1)}, bf16[192,1024]{1,0:T(8,128)(2,1)S(1)}, bf16[3,256,1024]{2,1,0:T(8,128)(2,1)S(1)}) custom-call(s32[2,64]{1,0:T(2,128)S(1)} %copy-done.6, bf16[3,256,1024]{2,1,0:T(8,128)(2,1)S(1)} %copy-done.3), custom_call_target="tpu_custom_call" | custom-call | flops 2200000000 | tf_op jit(solution)/shard_map/pallas_call | solution.py:27
  2.8 0.0 copy-start.1
  2.8 0.0 copy-start.2
  2.8 4.9 %collective-permute-start.4 = (bf16[192,1024]{1,0:T(8,128)(2,1)S(1)}, bf16[192,1024]{1,0:T(8,128)(2,1)S(1)}, u32[]{:S(2)}, u32[]{:S(2)}) collective-permute-start(bf16[192,1024]{1,0:T(8,128)(2,1)S(1)} %get-tuple-element.15.refs_2_), channel_id=1, source_target_pairs={{0,4},{4,8},{8,12},{12,16},{16,20},{20,24},{24,28},{1,5},{5,9},{9,... | collective-permute-start | bytes 1179656 | tf_op jit(solution)/shard_map/ppermute | solution.py:372
  7.7 0.0 copy-done.7
  7.7 0.8 %shard_map.92.refs_0_.refs_3_ = f32[4,1024]{1,0:T(4,128)S(1)} custom-call(f32[1,256]{1,0:T(1,128)S(1)} %bitcast.23, bf16[3,256,1024]{2,1,0:T(8,128)(2,1)S(1)} %get-tuple-element.14.refs_1_.refs_3_, bf16[192,1024]{1,0:T(8,128)(2,1)S(1)} %get-tuple-element.15.refs_2_), custom_call_target="tpu_custom_call" | custom-call | flops 880000000 | tf_op jit(solution)/shard_map/pallas_call | solution.py:27
  8.6 1.6 %collective-permute-start = (f32[4,1024]{1,0:T(4,128)S(1)}, f32[4,1024]{1,0:T(4,128)S(1)}, u32[]{:S(2)}, u32[]{:S(2)}) collective-permute-start(f32[4,1024]{1,0:T(4,128)S(1)} %shard_map.92.refs_0_.refs_3_), channel_id=1, source_target_pairs={{0,8},{4,12},{8,0},{12,4},{16,24},{20,28},{24,16},{28,20},{1,9},{5... | collective-permute-start | bytes 49160 | tf_op jit(solution)/shard_map/ppermute | solution.py:391
  10.2 1.3 %collective-permute-start.5 = (bf16[192,1024]{1,0:T(8,128)(2,1)S(1)}, bf16[192,1024]{1,0:T(8,128)(2,1)S(1)}, u32[]{:S(2)}, u32[]{:S(2)}) collective-permute-start(bf16[192,1024]{1,0:T(8,128)(2,1)S(1)} %get-tuple-element.20), channel_id=1, source_target_pairs={{4,0},{8,4},{12,8},{16,12},{20,16},{24,20},{28,24},{5,1},{9,5},{13... | collective-permute-start | bytes 1179656 | tf_op jit(solution)/shard_map/ppermute | solution.py:372
  11.5 0.0 copy-done.4
  11.5 0.0 copy-done.5
  11.5 0.0 copy-done.8
  11.5 0.4 shard_map.95
  11.9 0.0 copy-start.9
  11.9 0.9 %copy-done.9 = bf16[512,768]{1,0:T(8,128)(2,1)} copy-done((bf16[512,768]{1,0:T(8,128)(2,1)}, bf16[512,768]{1,0:T(8,128)(2,1)S(1)}, u32[]{:S(2)}) %copy-start.9) | copy-done | bytes 786456
  12.8 0.1 stack.27.refs_0_
  12.9 0.0 collective-permute-done.refs_1_
  12.9 3.6 %collective-permute-start.1 = (f32[4,1024]{1,0:T(4,128)S(1)}, f32[4,1024]{1,0:T(4,128)S(1)}, u32[]{:S(2)}, u32[]{:S(2)}) collective-permute-start(f32[4,1024]{1,0:T(4,128)S(1)} %shard_map.93.refs_0_), channel_id=1, source_target_pairs={{0,16},{4,20},{8,24},{12,28},{16,0},{20,4},{24,8},{28,12},{1,17},{... | collective-permute-start | bytes 49160 | tf_op jit(solution)/shard_map/ppermute | solution.py:391
  16.5 0.0 copy-done.1
  16.5 0.0 copy-done.2
  16.5 3.0 %shard_map.96 = (f32[1024,1024]{1,0:T(8,128)S(1)}, f32[2,512,512]{2,1,0:T(8,128)S(1)}) custom-call(s32[6]{0:T(128)S(1)} %stack.27.refs_0_, f32[1,4096]{1,0:T(1,128)S(1)} %bitcast.13, f32[1,4096]{1,0:T(1,128)S(1)} %bitcast.16, bf16[256,384]{1,0:T(8,128)(2,1)S(1)} %get-tuple-element.16.refs_3_.refs_1_), custom_call_target="tpu_custom_call" | custom-call | flops 3300000000 | tf_op jit(solution)/shard_map/pallas_call | solution.py:27
  19.5 4.3 %collective-permute-done.1.refs_1_ = f32[4,1024]{1,0:T(4,128)S(1)} collective-permute-done((f32[4,1024]{1,0:T(4,128)S(1)}, f32[4,1024]{1,0:T(4,128)S(1)}, u32[]{:S(2)}, u32[]{:S(2)}) %collective-permute-start.1) | collective-permute-done | bytes 16416 | tf_op jit(solution)/shard_map/ppermute | solution.py:391
  23.8 0.0 collective-permute-start.2
  23.8 0.0 copy-start
  23.8 5.1 %shard_map.97.refs_6_.refs_3_ = f32[2048,1024]{1,0:T(8,128)S(1)} custom-call(s32[6]{0:T(128)S(1)} %stack.27.refs_0_, f32[1,4096]{1,0:T(1,128)S(1)} %bitcast.14, f32[1,4096]{1,0:T(1,128)S(1)} %bitcast.17, f32[1024,1024]{1,0:T(8,128)S(1)} %get-tuple-element.17.refs_3_), custom_call_target="tpu_custom_call" | custom-call | flops 5500000256 | tf_op jit(solution)/shard_map/pallas_call | solution.py:27
  28.9 0.0 copy-start.10
  28.9 0.0 collective-permute-done.2.refs_2_
  28.9 0.0 copy-done
  28.9 0.6 %shard_map.98.refs_6_.refs_1_.refs_0_ = f32[8,1024]{1,0:T(8,128)S(1)} custom-call(s32[6]{0:T(128)S(1)} %stack.27.refs_0_, f32[4,1024]{1,0:T(4,128)S(1)} %shard_map.94.refs_1_, f32[4,1024]{1,0:T(4,128)S(1)} %collective-permute-done.2.refs_2_, f32[3,4096]{1,0:T(4,128)S(1)} %copy-done, f32[1,4096]{1,0:T(1,128)S(1)} %bitcast.15, f32[1,4096]{1,0:T(1,128)S(1)} %bitcast.18, ...), custom_call_target="tpu_custom_call" | custom-call | flops 660000000 | tf_op jit(solution)/shard_map/pallas_call | solution.py:27
  29.5 0.0 collective-permute-done.4.refs_4_
  29.5 0.0 collective-permute-done.5.refs_5_
  29.5 0.5 copy-done.10
  30.0 2.6 %shard_map.99 = (bf16[512,1024]{1,0:T(8,128)(2,1)S(1)}, bf16[256,1024]{1,0:T(8,128)(2,1)S(1)}) custom-call(s32[6]{0:T(128)S(1)} %stack.27.refs_0_, bf16[256,384]{1,0:T(8,128)(2,1)S(1)} %get-tuple-element.16.refs_3_.refs_1_, bf16[512,768]{1,0:T(8,128)(2,1)S(1)} %copy-done.10, bf16[3,256,1024]{2,1,0:T(8,128)(2,1)S(1)} %get-tuple-element.14.refs_1_.refs_3_, ...), custom_call_target="tpu_custom_call" | custom-call | flops 2860000000 | tf_op jit(solution)/shard_map/pallas_call | solution.py:27
  32.7 0.1 collective-permute-start.6
  32.7 0.5 collective-permute-start.3
  33.2 1.5 %collective-permute-start.7 = (f32[8,1024]{1,0:T(8,128)S(1)}, f32[8,1024]{1,0:T(8,128)S(1)}, u32[]{:S(2)}, u32[]{:S(2)}) collective-permute-start(f32[8,1024]{1,0:T(8,128)S(1)} %shard_map.98.refs_6_.refs_1_.refs_0_), channel_id=1, source_target_pairs={{0,2},{1,3},{2,0},{3,1},{4,6},{5,7},{6,4},{7,5},{8,10},{9,11},{10,... | collective-permute-start | bytes 98312 | tf_op jit(solution)/shard_map/ppermute | solution.py:409
  34.8 0.5 collective-permute-start.8
  35.3 0.2 collective-permute-done.3.refs_2_.refs_1_
  35.4 1.7 %collective-permute-done.7.refs_2_ = f32[8,1024]{1,0:T(8,128)S(1)} collective-permute-done((f32[8,1024]{1,0:T(8,128)S(1)}, f32[8,1024]{1,0:T(8,128)S(1)}, u32[]{:S(2)}, u32[]{:S(2)}) %collective-permute-start.7) | collective-permute-done | bytes 32800 | tf_op jit(solution)/shard_map/ppermute | solution.py:409
  37.2 3.3 %shard_map.101.refs_2_ = bf16[2048,1024]{1,0:T(8,128)(2,1)S(1)} custom-call(f32[8,1024]{1,0:T(8,128)S(1)} %shard_map.98.refs_6_.refs_1_.refs_0_, f32[8,1024]{1,0:T(8,128)S(1)} %collective-permute-done.3.refs_2_.refs_1_, f32[8,1024]{1,0:T(8,128)S(1)} %collective-permute-done.7.refs_2_, f32[2048,1024]{1,0:T(8,128)S(1)} %shard_map.97.refs_6_.refs_3_), custom_call_target="tpu_custom_call" | custom-call | flops 3630000128 | tf_op jit(solution)/shard_map/pallas_call | solution.py:27
  40.5 0.0 collective-permute-done.6.refs_6_.refs_5_
  40.5 3.4 %shard_map.100.refs_1_ = f32[512,128]{1,0:T(8,128)S(1)} custom-call(s32[6]{0:T(128)S(1)} %stack.27.refs_0_, f32[8,1024]{1,0:T(8,128)S(1)} %shard_map.98.refs_6_.refs_1_.refs_0_, f32[8,1024]{1,0:T(8,128)S(1)} %collective-permute-done.3.refs_2_.refs_1_, f32[1024,1024]{1,0:T(8,128)S(1)} %get-tuple-element.17.refs_3_, ...), custom_call_target="tpu_custom_call" | custom-call | flops 3740000000 | tf_op jit(solution)/shard_map/pallas_call | solution.py:27
  43.9 4.5 %collective-permute-done.8.refs_3_ = bf16[256,1024]{1,0:T(8,128)(2,1)S(1)} collective-permute-done((bf16[256,1024]{1,0:T(8,128)(2,1)S(1)}, bf16[256,1024]{1,0:T(8,128)(2,1)S(1)}, u32[]{:S(2)}, u32[]{:S(2)}) %collective-permute-start.8) | collective-permute-done | bytes 524320 | tf_op jit(solution)/shard_map/ppermute | solution.py:424
  48.4 2.2 %shard_map.102 = f32[1,512]{1,0:T(1,128)S(1)} custom-call(s32[6]{0:T(128)S(1)} %stack.27.refs_0_, f32[512,128]{1,0:T(8,128)S(1)} %shard_map.100.refs_1_, bf16[2048,1024]{1,0:T(8,128)(2,1)S(1)} %shard_map.101.refs_2_, bf16[256,1024]{1,0:T(8,128)(2,1)S(1)} %collective-permute-done.8.refs_3_, bf16[512,1024]{1,0:T(8,128)(2,1)S(1)} %get-tuple-element.21.refs_5_.refs_4_, ...), custom_call_target="tpu_custom_call" | custom-call | flops 2310000128 | tf_op jit(solution)/shard_map/pallas_call | solution.py:27
  50.5 0.0 collective-permute-start.9
  50.5 1.2 %collective-permute-done.9 = f32[512]{0:T(512)S(1)} collective-permute-done((f32[512]{0:T(512)S(1)}, f32[512]{0:T(512)S(1)}, u32[]{:S(2)}, u32[]{:S(2)}) %collective-permute-start.9) | collective-permute-done | bytes 2080 | tf_op jit(solution)/shard_map/ppermute | solution.py:448
  51.7 1.0 %collective-permute-start.10 = (f32[512]{0:T(512)S(1)}, f32[512]{0:T(512)S(1)}, u32[]{:S(2)}, u32[]{:S(2)}) collective-permute-start(f32[512]{0:T(512)S(1)} %add.6), channel_id=1, source_target_pairs={{0,2},{1,3},{2,0},{3,1},{4,6},{5,7},{6,4},{7,5},{8,10},{9,11},{10,... | collective-permute-start | bytes 6152 | tf_op jit(solution)/shard_map/ppermute | solution.py:448
  52.7 2.6 %collective-permute-done.10 = f32[512]{0:T(512)S(1)} collective-permute-done((f32[512]{0:T(512)S(1)}, f32[512]{0:T(512)S(1)}, u32[]{:S(2)}, u32[]{:S(2)}) %collective-permute-start.10) | collective-permute-done | bytes 2080 | tf_op jit(solution)/shard_map/ppermute | solution.py:448
  55.3 0.6 %add.7 = f32[512]{0:T(512)} add(f32[512]{0:T(512)S(1)} %add.6, f32[512]{0:T(512)S(1)} %collective-permute-done.10) | non-fusion elementwise | flops 512 | bytes 6144 | tf_op jit(solution)/shard_map/add | solution.py:448
  (3 shorter events, 0.0 us)
Async XLA Ops:
  0.0 1.4 %copy-start.3 = (bf16[3,256,1024]{2,1,0:T(8,128)(2,1)S(1)}, bf16[3,256,1024]{2,1,0:T(8,128)(2,1)}, u32[]{:S(2)}) copy-start(bf16[3,256,1024]{2,1,0:T(8,128)(2,1)} %refs_1_.1) | copy-start | bytes 4718596
  1.4 0.7 %copy-start.6 = (s32[2,64]{1,0:T(2,128)S(1)}, s32[2,64]{1,0:T(2,128)}, u32[]{:S(2)}) copy-start(s32[2,64]{1,0:T(2,128)} %refs_0_.1) | copy-start | bytes 1540
  2.1 5.6 %copy-start.7 = (f32[256]{0:T(256)S(1)}, f32[256]{0:T(256)}, u32[]{:S(2)}) copy-start(f32[256]{0:T(256)} %param.10) | copy-start | bytes 3076
  2.1 9.4 %copy-start.4 = (bf16[64,8,4,3]{0,2,3,1:T(4,128)(2,1)S(1)}, bf16[64,8,4,3]{0,2,3,1:T(4,128)(2,1)}, u32[]{:S(2)}) copy-start(bf16[64,8,4,3]{0,2,3,1:T(4,128)(2,1)} %param.14) | copy-start | bytes 36868
  2.1 9.4 %copy-start.5 = (s32[64,4]{0,1:T(4,128)S(1)}, s32[64,4]{0,1:T(4,128)}, u32[]{:S(2)}) copy-start(s32[64,4]{0,1:T(4,128)} %param.15) | copy-start | bytes 3076
  2.1 9.4 %copy-start.8 = (s32[64]{0:T(128)S(1)}, s32[64]{0:T(128)}, u32[]{:S(2)}) copy-start(s32[64]{0:T(128)} %param.16) | copy-start | bytes 772
  2.8 13.7 %copy-start.1 = (f32[4096]{0:T(1024)S(1)}, f32[4096]{0:T(1024)}, u32[]{:S(2)}) copy-start(f32[4096]{0:T(1024)} %param.12) | copy-start | bytes 49156
  2.8 13.7 %copy-start.2 = (f32[4096]{0:T(1024)S(1)}, f32[4096]{0:T(1024)}, u32[]{:S(2)}) copy-start(f32[4096]{0:T(1024)} %param.13) | copy-start | bytes 49156
  2.8 26.7 %collective-permute-start.4 = (bf16[192,1024]{1,0:T(8,128)(2,1)S(1)}, bf16[192,1024]{1,0:T(8,128)(2,1)S(1)}, u32[]{:S(2)}, u32[]{:S(2)}) collective-permute-start(bf16[192,1024]{1,0:T(8,128)(2,1)S(1)} %get-tuple-element.15.refs_2_), channel_id=1, source_target_pairs={{0,4},{4,8},{8,12},{12,16},{16,20},{20,24},{24,28},{1,5},{5,9},{9,... | collective-permute-start | bytes 1179656 | tf_op jit(solution)/shard_map/ppermute | solution.py:372
  8.6 4.3 %collective-permute-start = (f32[4,1024]{1,0:T(4,128)S(1)}, f32[4,1024]{1,0:T(4,128)S(1)}, u32[]{:S(2)}, u32[]{:S(2)}) collective-permute-start(f32[4,1024]{1,0:T(4,128)S(1)} %shard_map.92.refs_0_.refs_3_), channel_id=1, source_target_pairs={{0,8},{4,12},{8,0},{12,4},{16,24},{20,28},{24,16},{28,20},{1,9},{5... | collective-permute-start | bytes 49160 | tf_op jit(solution)/shard_map/ppermute | solution.py:391
  10.2 19.3 %collective-permute-start.5 = (bf16[192,1024]{1,0:T(8,128)(2,1)S(1)}, bf16[192,1024]{1,0:T(8,128)(2,1)S(1)}, u32[]{:S(2)}, u32[]{:S(2)}) collective-permute-start(bf16[192,1024]{1,0:T(8,128)(2,1)S(1)} %get-tuple-element.20), channel_id=1, source_target_pairs={{4,0},{8,4},{12,8},{16,12},{20,16},{24,20},{28,24},{5,1},{9,5},{13... | collective-permute-start | bytes 1179656 | tf_op jit(solution)/shard_map/ppermute | solution.py:372
  11.9 0.9 %copy-start.9 = (bf16[512,768]{1,0:T(8,128)(2,1)}, bf16[512,768]{1,0:T(8,128)(2,1)S(1)}, u32[]{:S(2)}) copy-start(bf16[512,768]{1,0:T(8,128)(2,1)S(1)} %get-tuple-element.19.refs_2_) | copy-start | bytes 2359300
  12.9 10.9 %collective-permute-start.1 = (f32[4,1024]{1,0:T(4,128)S(1)}, f32[4,1024]{1,0:T(4,128)S(1)}, u32[]{:S(2)}, u32[]{:S(2)}) collective-permute-start(f32[4,1024]{1,0:T(4,128)S(1)} %shard_map.93.refs_0_), channel_id=1, source_target_pairs={{0,16},{4,20},{8,24},{12,28},{16,0},{20,4},{24,8},{28,12},{1,17},{... | collective-permute-start | bytes 49160 | tf_op jit(solution)/shard_map/ppermute | solution.py:391
  23.8 5.1 %collective-permute-start.2 = (f32[4,1024]{1,0:T(4,128)S(1)}, f32[4,1024]{1,0:T(4,128)S(1)}, u32[]{:S(2)}, u32[]{:S(2)}) collective-permute-start(f32[4,1024]{1,0:T(4,128)S(1)} %shard_map.94.refs_1_), channel_id=1, source_target_pairs={{0,4},{4,0},{8,12},{12,8},{16,20},{20,16},{24,28},{28,24},{1,5},{5... | collective-permute-start | bytes 49160 | tf_op jit(solution)/shard_map/ppermute | solution.py:391
  23.8 5.1 %copy-start = (f32[3,4096]{1,0:T(4,128)S(1)}, f32[3,4096]{1,0:T(4,128)}, u32[]{:S(2)}) copy-start(f32[3,4096]{1,0:T(4,128)} %refs_3_.1) | copy-start | bytes 147460
  28.9 1.1 %copy-start.10 = (bf16[512,768]{1,0:T(8,128)(2,1)S(1)}, bf16[512,768]{1,0:T(8,128)(2,1)}, u32[]{:S(2)}) copy-start(bf16[512,768]{1,0:T(8,128)(2,1)} %copy-done.9) | copy-start | bytes 2359300
  32.7 7.9 %collective-permute-start.6 = (bf16[512,1024]{1,0:T(8,128)(2,1)S(1)}, bf16[512,1024]{1,0:T(8,128)(2,1)S(1)}, u32[]{:S(2)}, u32[]{:S(2)}) collective-permute-start(bf16[512,1024]{1,0:T(8,128)(2,1)S(1)} %get-tuple-element.21.refs_5_.refs_4_), channel_id=1, source_target_pairs={{0,1},{1,0},{2,3},{3,2},{4,5},{5,4},{6,7},{7,6},{8,9},{9,8},{10,11... | collective-permute-start | bytes 3145736 | tf_op jit(solution)/shard_map/ppermute | solution.py:425
  32.7 2.7 %collective-permute-start.3 = (f32[8,1024]{1,0:T(8,128)S(1)}, f32[8,1024]{1,0:T(8,128)S(1)}, u32[]{:S(2)}, u32[]{:S(2)}) collective-permute-start(f32[8,1024]{1,0:T(8,128)S(1)} %shard_map.98.refs_6_.refs_1_.refs_0_), channel_id=1, source_target_pairs={{0,1},{1,0},{2,3},{3,2},{4,5},{5,4},{6,7},{7,6},{8,9},{9,8},{10,11... | collective-permute-start | bytes 98312 | tf_op jit(solution)/shard_map/ppermute | solution.py:408
  33.2 3.9 %collective-permute-start.7 = (f32[8,1024]{1,0:T(8,128)S(1)}, f32[8,1024]{1,0:T(8,128)S(1)}, u32[]{:S(2)}, u32[]{:S(2)}) collective-permute-start(f32[8,1024]{1,0:T(8,128)S(1)} %shard_map.98.refs_6_.refs_1_.refs_0_), channel_id=1, source_target_pairs={{0,2},{1,3},{2,0},{3,1},{4,6},{5,7},{6,4},{7,5},{8,10},{9,11},{10,... | collective-permute-start | bytes 98312 | tf_op jit(solution)/shard_map/ppermute | solution.py:409
  34.8 13.6 %collective-permute-start.8 = (bf16[256,1024]{1,0:T(8,128)(2,1)S(1)}, bf16[256,1024]{1,0:T(8,128)(2,1)S(1)}, u32[]{:S(2)}, u32[]{:S(2)}) collective-permute-start(bf16[256,1024]{1,0:T(8,128)(2,1)S(1)} %get-tuple-element.22), channel_id=1, source_target_pairs={{0,2},{1,3},{2,0},{3,1},{4,6},{5,7},{6,4},{7,5},{8,10},{9,11},{10,... | collective-permute-start | bytes 1572872 | tf_op jit(solution)/shard_map/ppermute | solution.py:424
  50.5 1.2 %collective-permute-start.9 = (f32[512]{0:T(512)S(1)}, f32[512]{0:T(512)S(1)}, u32[]{:S(2)}, u32[]{:S(2)}) collective-permute-start(f32[512]{0:T(512)S(1)} %bitcast.19), channel_id=1, source_target_pairs={{0,1},{1,0},{2,3},{3,2},{4,5},{5,4},{6,7},{7,6},{8,9},{9,8},{10,11... | collective-permute-start | bytes 6152 | tf_op jit(solution)/shard_map/ppermute | solution.py:448
  51.7 3.6 %collective-permute-start.10 = (f32[512]{0:T(512)S(1)}, f32[512]{0:T(512)S(1)}, u32[]{:S(2)}, u32[]{:S(2)}) collective-permute-start(f32[512]{0:T(512)S(1)} %add.6), channel_id=1, source_target_pairs={{0,2},{1,3},{2,0},{3,1},{4,6},{5,7},{6,4},{7,5},{8,10},{9,11},{10,... | collective-permute-start | bytes 6152 | tf_op jit(solution)/shard_map/ppermute | solution.py:448

commit v5 on v4

--- a/solution.py
+++ b/solution.py
@@ -191,13 +191,22 @@
     part_ref[...] = all_ref[pl.ds(pl.multiple_of(other * part, part), part), :]
 
 
-def amps_kernel(place_ref, stats_ref, extra_ref, spectral_ref, freq_ref, rate_ref, out_ref):
+def join_kernel(*refs):
+    out_ref = refs[-1]
+    size = refs[0].shape[0]
+    for q, ref in enumerate(refs[:-1]):
+        out_ref[q * size : (q + 1) * size, :] = ref[...]
+
+
+def amps_kernel(place_ref, stats_ref, extra_ref, spectral_ref, freq_ref, rate_ref, *out_refs):
     dims, block = spectral_ref.shape[0], stats_ref.shape[1]
-    lanes = pl.ds(pl.multiple_of(place_ref[0] * block, block), block)
-    total = stats_ref[...] + extra_ref[...]
-    scale = 2.0 * jnp.sqrt(freq_ref[:, lanes] / rate_ref[:, lanes])
-    amps = total[:dims] / total[dims : dims + 1] * spectral_ref[:, lanes] * scale
-    out_ref[...] = jnp.concatenate([amps, jnp.zeros((8 - dims, block), F32)], axis=0)
+    for q, out_ref in enumerate(out_refs):
+        lanes = pl.ds(pl.multiple_of(place_ref[q] * block, block), block)
+        rows = slice(q * (dims + 1), (q + 1) * (dims + 1))
+        total = stats_ref[rows, :] + extra_ref[rows, :]
+        scale = 2.0 * jnp.sqrt(freq_ref[:, lanes] / rate_ref[:, lanes])
+        amps = total[:dims] / total[dims : dims + 1] * spectral_ref[:, lanes] * scale
+        out_ref[...] = jnp.concatenate([amps, jnp.zeros((8 - dims, block), F32)], axis=0)
 
 
 def fold(value):
@@ -225,13 +234,20 @@
 
 
 def weigh(out, rho, side_scr, side_at, cols, dims, factor):
-    for c in range(0, rho.shape[1], 128):
-        col = [jnp.broadcast_to(cols[d : d + 1, c : c + 128] * factor, (16, 128)) for d in range(dims)]
+    span = min(512, rho.shape[1])
+    for base in range(0, rho.shape[1], span):
+        lanes = range(base, base + span, 128)
+        col = [
+            [jnp.broadcast_to(cols[d : d + 1, c : c + 128] * factor, (16, 128)) for d in range(dims)]
+            for c in lanes
+        ]
         for r in range(0, rho.shape[0], 16):
-            pair = side_scr[0, side_at + r : side_at + r + 16, :] * col[0]
-            for d in range(1, dims):
-                pair = pair + side_scr[d, side_at + r : side_at + r + 16, :] * col[d]
-            out[r : r + 16, c : c + 128] = (rho[r : r + 16, c : c + 128] * pair).astype(BF16)
+            side = [side_scr[d, side_at + r : side_at + r + 16, :] for d in range(dims)]
+            for c, own in zip(lanes, col):
+                pair = side[0] * own[0]
+                for d in range(1, dims):
+                    pair = pair + side[d] * own[d]
+                out[r : r + 16, c : c + 128] = (rho[r : r + 16, c : c + 128] * pair).astype(BF16)
 
 
 def near_kernel(dims, chunks, *refs):
@@ -380,6 +396,21 @@
         (connectivity.T, node_count.reshape(1, elems), recovery.transpose(1, 3, 2, 0)),
         0.5, after=(stats,),
     )
+    rho_diag, rho_mate = call(
+        rho_near_kernel,
+        (sds((block, block), F32), sds((2, block // 2, block // 2), F32)),
+        (place, freq, rate), 3.0, smem=(0,),
+        scratch=[pltpu.VMEM((4, block, 128), F32), pltpu.VMEM((16, block), F32)], after=(pick,),
+    )
+    rho_far = call(
+        rho_far_kernel, sds((2 * block, block), F32), (place, freq, rate),
+        5.0, smem=(0,),
+        scratch=[pltpu.VMEM((4, 2 * block, 128), F32), pltpu.VMEM((24, block), F32)],
+        after=(rho_diag,),
+    )
+    given = [stats] + [lax.ppermute(stats, "mode", [(i, i ^ q) for i in range(4)]) for q in (1, 2)]
+    stats = call(join_kernel, sds((3 * (dims + 1), block), F32), given, 0.5, after=(pick,))
+    first = stats
     order = [1 << q for q in range(1, parts.bit_length() - 1)] + [1]
     if parts & (parts - 1) or parts == 1:
         stats = lax.psum(stats, "dom")
@@ -387,26 +418,14 @@
     extra = jnp.zeros_like(stats)
     for q, reach in enumerate(order):
         if q:
-            stats = call(add_kernel, sds(stats.shape, F32), (stats, extra), 0.5)
+            stats = call(
+                add_kernel, sds(stats.shape, F32), (stats, extra), 0.5, after=(rho_far,) if q == 1 else ()
+            )
+            first = stats if q == 1 else first
         extra = lax.ppermute(stats, "dom", [(i, i ^ reach) for i in range(parts)])
-    rho_diag, rho_mate = call(
-        rho_near_kernel,
-        (sds((block, block), F32), sds((2, block // 2, block // 2), F32)),
-        (place, freq, rate), 3.0, smem=(0,),
-        scratch=[pltpu.VMEM((4, block, 128), F32), pltpu.VMEM((16, block), F32)], after=(pick,),
-    )
-    rho_far = call(
-        rho_far_kernel, sds((2 * block, block), F32), (place, freq, rate),
-        5.0, smem=(0,),
-        scratch=[pltpu.VMEM((4, 2 * block, 128), F32), pltpu.VMEM((24, block), F32)],
-        after=(rho_diag,),
-    )
-    amps = call(
-        amps_kernel, sds((8, block), F32), (place, stats, extra, spectral, freq, rate),
-        0.6, smem=(0,), after=(rho_far,),
-    )
-    mate_amps = lax.ppermute(amps, "mode", [(i, i ^ 1) for i in range(4)])
-    far_amps = lax.ppermute(amps, "mode", [(i, i ^ 2) for i in range(4)])
+    amps, mate_amps, far_amps = call(
+        amps_kernel, [sds((8, block), F32)] * 3, (place, stats, extra, spectral, freq, rate), 0.8, smem=(0,)
+    )
 
     own, mate, far = [], [], []
     for c in range(CHUNKS):
@@ -418,7 +437,7 @@
             scratch=[
                 pltpu.VMEM((dims, 2 * width, chunk), BF16), pltpu.VMEM((dims * slots * elems, chunk), BF16)
             ],
-            after=(amps,),
+            after=(first,),
         )
         own.append(forces)
         far.append(lax.ppermute(sent, "mode", [(i, i ^ 2) for i in range(4)]))

time: 56.2 us -> 62.6 us (1.11)
  waiting for transfers between devices: 14.5 us -> 18.6 us
  starting transfers between devices: 14.9 us -> 17.9 us
    ppermute x3, waiting for transfers between devices: 4.34 us -> 8.37 us  [combined(): extra = lax.ppermute(stats, 'dom', [(i, i ^ reach) for i in range(parts)])]
    ppermute x3, starting transfers between devices: 5.2 us -> 8.93 us  [combined(): extra = lax.ppermute(stats, 'dom', [(i, i ^ reach) for i in range(parts)])]
    ppermute x2, waiting for transfers between devices: 1.9 us -> 0.01 us  [combined(): lax.ppermute(stats, 'mode', [(i, i ^ q) for i in range(4)])]
    ppermute x1, waiting for transfers between devices: 0.01 us -> 1.86 us  [combined(): lax.ppermute(up, 'dom', ahead)]
    ppermute x1, starting transfers between devices: 4.89 us -> 3.41 us  [combined(): lax.ppermute(up, 'dom', ahead)]
    ppermute x2, starting transfers between devices: 2.01 us -> 3.13 us  [combined(): lax.ppermute(stats, 'mode', [(i, i ^ q) for i in range(4)])]
    pallas_call x12 -> x13, Pallas kernels: 22.1 us -> 21.9 us  [call(): pl.pallas_call(body, out_shape=out_shape, in_specs=specs, out_specs=[VMEM...]
  transfers between devices with their start and end apart: 11 -> 11, of which waited for: 6 -> 7; matrix products, arithmetic and copies ran while one was open for 0% -> 0% of each run, Pallas kernels for 30% -> 25%
where the time goes in v5:
time: 62.6 us; the launch traced here: 62.3 us
  Pallas kernels  21.9 us (35%)
  waiting for transfers between devices  18.6 us (30%)
  starting transfers between devices  17.9 us (29%)
  local copies, waits for them, and re-layouts  3.09 us (5%)
    pallas_call x13, Pallas kernels, call(): pl.pallas_call(body, out_shape=out_shape, in_specs=specs, out_specs=[VMEM...  21.9 us
    ppermute x3, starting transfers between devices, combined(): extra = lax.ppermute(stats, 'dom', [(i, i ^ reach) for i in range(parts)])  8.93 us
    ppermute x3, waiting for transfers between devices, combined(): extra = lax.ppermute(stats, 'dom', [(i, i ^ reach) for i in range(parts)])  8.37 us
    ppermute x2, waiting for transfers between devices, combined(): lax.ppermute(value, 'mode', [(i, i ^ reach) for i in range(4)])  4.25 us
    ppermute x1, waiting for transfers between devices, combined(): far.append(lax.ppermute(sent, 'mode', [(i, i ^ 2) for i in range(4)]))  4.09 us
    ppermute x1, starting transfers between devices, combined(): lax.ppermute(up, 'dom', ahead)  3.41 us
    ppermute x2, starting transfers between devices, combined(): lax.ppermute(stats, 'mode', [(i, i ^ q) for i in range(4)])  3.13 us
    unnamed x22, local copies, waits for them, and re-layouts  3 us
  transfers between devices with their start and end apart: 11, of which 7 were waited for; matrix products, arithmetic and copies ran while one was open for 0% of the time, Pallas kernels for 25%

profile of v5, /device:TPU:0, one launch (start us, length us, event | category | flops | bytes accessed | tf_op | source)
XLA Modules:
  0.0 62.3 jit_solution(5910693756510783597)
XLA Ops:
  0.0 0.0 copy-start
  0.0 1.4 %copy-done = bf16[3,256,1024]{2,1,0:T(8,128)(2,1)S(1)} copy-done((bf16[3,256,1024]{2,1,0:T(8,128)(2,1)S(1)}, bf16[3,256,1024]{2,1,0:T(8,128)(2,1)}, u32[]{:S(2)}) %copy-start) | copy-done | bytes 1572888
  1.4 0.0 copy-start.6
  1.4 0.7 %copy-done.6 = s32[2,64]{1,0:T(2,128)S(1)} copy-done((s32[2,64]{1,0:T(2,128)S(1)}, s32[2,64]{1,0:T(2,128)}, u32[]{:S(2)}) %copy-start.6) | copy-done | bytes 536
  2.1 0.0 copy-start.7
  2.1 0.0 copy-start.2
  2.1 0.0 copy-start.5
  2.1 0.0 copy-start.8
  2.1 0.7 %shard_map.91 = (bf16[192,1024]{1,0:T(8,128)(2,1)S(1)}, bf16[192,1024]{1,0:T(8,128)(2,1)S(1)}, bf16[3,256,1024]{2,1,0:T(8,128)(2,1)S(1)}) custom-call(s32[2,64]{1,0:T(2,128)S(1)} %copy-done.6, bf16[3,256,1024]{2,1,0:T(8,128)(2,1)S(1)} %copy-done), custom_call_target="tpu_custom_call" | custom-call | flops 2200000000 | tf_op jit(solution)/shard_map/pallas_call | solution.py:27
  2.8 0.0 copy-start.3
  2.8 0.0 copy-start.4
  2.8 0.0 copy-done.7
  2.8 0.8 %shard_map.92.refs_3_.refs_0_ = f32[4,1024]{1,0:T(4,128)S(1)} custom-call(f32[1,256]{1,0:T(1,128)S(1)} %bitcast.23, bf16[3,256,1024]{2,1,0:T(8,128)(2,1)S(1)} %get-tuple-element.17.refs_1_.refs_3_, bf16[192,1024]{1,0:T(8,128)(2,1)S(1)} %get-tuple-element.18.refs_2_), custom_call_target="tpu_custom_call" | custom-call | flops 880000000 | tf_op jit(solution)/shard_map/pallas_call | solution.py:27
  3.6 0.6 collective-permute-start
  4.2 2.6 %collective-permute-start.1 = (f32[4,1024]{1,0:T(4,128)S(1)}, f32[4,1024]{1,0:T(4,128)S(1)}, u32[]{:S(2)}, u32[]{:S(2)}) collective-permute-start(f32[4,1024]{1,0:T(4,128)S(1)} %shard_map.92.refs_3_.refs_0_), channel_id=1, source_target_pairs={{0,2},{1,3},{2,0},{3,1},{4,6},{5,7},{6,4},{7,5},{8,10},{9,11},{10,... | collective-permute-start | bytes 49160 | tf_op jit(solution)/shard_map/ppermute | solution.py:411
  6.8 3.4 %collective-permute-start.5 = (bf16[192,1024]{1,0:T(8,128)(2,1)S(1)}, bf16[192,1024]{1,0:T(8,128)(2,1)S(1)}, u32[]{:S(2)}, u32[]{:S(2)}) collective-permute-start(bf16[192,1024]{1,0:T(8,128)(2,1)S(1)} %get-tuple-element.18.refs_2_), channel_id=1, source_target_pairs={{0,4},{4,8},{8,12},{12,16},{16,20},{20,24},{24,28},{1,5},{5,9},{9,... | collective-permute-start | bytes 1179656 | tf_op jit(solution)/shard_map/ppermute | solution.py:388
  10.2 1.3 %collective-permute-start.6 = (bf16[192,1024]{1,0:T(8,128)(2,1)S(1)}, bf16[192,1024]{1,0:T(8,128)(2,1)S(1)}, u32[]{:S(2)}, u32[]{:S(2)}) collective-permute-start(bf16[192,1024]{1,0:T(8,128)(2,1)S(1)} %get-tuple-element.25), channel_id=1, source_target_pairs={{4,0},{8,4},{12,8},{16,12},{20,16},{24,20},{28,24},{5,1},{9,5},{13... | collective-permute-start | bytes 1179656 | tf_op jit(solution)/shard_map/ppermute | solution.py:388
  11.5 0.0 copy-done.2
  11.5 0.0 copy-done.5
  11.5 0.0 copy-done.8
  11.5 0.4 shard_map.93
  11.9 0.0 copy-start.9
  12.0 0.9 %copy-done.9 = bf16[512,768]{1,0:T(8,128)(2,1)} copy-done((bf16[512,768]{1,0:T(8,128)(2,1)}, bf16[512,768]{1,0:T(8,128)(2,1)S(1)}, u32[]{:S(2)}) %copy-start.9) | copy-done | bytes 786456
  12.8 0.1 stack.27.refs_0_
  12.9 0.0 copy-done.3
  12.9 0.0 copy-done.4
  12.9 3.0 %shard_map.95 = (f32[1024,1024]{1,0:T(8,128)S(1)}, f32[2,512,512]{2,1,0:T(8,128)S(1)}) custom-call(s32[6]{0:T(128)S(1)} %stack.27.refs_0_, f32[1,4096]{1,0:T(1,128)S(1)} %bitcast.16, f32[1,4096]{1,0:T(1,128)S(1)} %bitcast.19, bf16[256,384]{1,0:T(8,128)(2,1)S(1)} %get-tuple-element.19.refs_3_.refs_1_), custom_call_target="tpu_custom_call" | custom-call | flops 3300000000 | tf_op jit(solution)/shard_map/pallas_call | solution.py:27
  15.9 0.0 collective-permute-done.refs_1_
  15.9 0.0 collective-permute-done.1.refs_2_
  16.0 3.7 %collective-permute-start.2 = (f32[12,1024]{1,0:T(8,128)S(1)}, f32[12,1024]{1,0:T(8,128)S(1)}, u32[]{:S(2)}, u32[]{:S(2)}) collective-permute-start(f32[12,1024]{1,0:T(8,128)S(1)} %shard_map.94.refs_0_), channel_id=1, source_target_pairs={{0,8},{4,12},{8,0},{12,4},{16,24},{20,28},{24,16},{28,20},{1,9},{5... | collective-permute-start | bytes 147464 | tf_op jit(solution)/shard_map/ppermute | solution.py:425
  19.6 5.1 %shard_map.96.refs_2_.refs_3_ = f32[2048,1024]{1,0:T(8,128)S(1)} custom-call(s32[6]{0:T(128)S(1)} %stack.27.refs_0_, f32[1,4096]{1,0:T(1,128)S(1)} %bitcast.17, f32[1,4096]{1,0:T(1,128)S(1)} %bitcast.20, f32[1024,1024]{1,0:T(8,128)S(1)} %get-tuple-element.20.refs_3_), custom_call_target="tpu_custom_call" | custom-call | flops 5500000256 | tf_op jit(solution)/shard_map/pallas_call | solution.py:27
  24.7 0.0 copy-start.10
  24.7 0.7 %collective-permute-done.2.refs_1_ = f32[12,1024]{1,0:T(8,128)S(1)} collective-permute-done((f32[12,1024]{1,0:T(8,128)S(1)}, f32[12,1024]{1,0:T(8,128)S(1)}, u32[]{:S(2)}, u32[]{:S(2)}) %collective-permute-start.2) | collective-permute-done | bytes 49184 | tf_op jit(solution)/shard_map/ppermute | solution.py:425
  25.4 1.9 %collective-permute-done.5.refs_4_ = bf16[192,1024]{1,0:T(8,128)(2,1)S(1)} collective-permute-done((bf16[192,1024]{1,0:T(8,128)(2,1)S(1)}, bf16[192,1024]{1,0:T(8,128)(2,1)S(1)}, u32[]{:S(2)}, u32[]{:S(2)}) %collective-permute-start.5) | collective-permute-done | bytes 393248 | tf_op jit(solution)/shard_map/ppermute | solution.py:388
  27.3 0.0 collective-permute-done.6.refs_5_
  27.3 0.0 copy-done.10
  27.3 0.0 copy-start.1
  27.3 2.6 %shard_map.100 = (bf16[512,1024]{1,0:T(8,128)(2,1)S(1)}, bf16[256,1024]{1,0:T(8,128)(2,1)S(1)}) custom-call(s32[6]{0:T(128)S(1)} %stack.27.refs_0_, bf16[256,384]{1,0:T(8,128)(2,1)S(1)} %get-tuple-element.19.refs_3_.refs_1_, bf16[512,768]{1,0:T(8,128)(2,1)S(1)} %copy-done.10, bf16[3,256,1024]{2,1,0:T(8,128)(2,1)S(1)} %get-tuple-element.17.refs_1_.refs_3_, ...), custom_call_target="tpu_custom_call" | custom-call | flops 2860000000 | tf_op jit(solution)/shard_map/pallas_call | solution.py:27
  29.9 0.1 collective-permute-start.7
  30.0 4.5 %collective-permute-start.3 = (f32[12,1024]{1,0:T(8,128)S(1)}, f32[12,1024]{1,0:T(8,128)S(1)}, u32[]{:S(2)}, u32[]{:S(2)}) collective-permute-start(f32[12,1024]{1,0:T(8,128)S(1)} %shard_map.97.refs_0_.refs_6_), channel_id=1, source_target_pairs={{0,16},{4,20},{8,24},{12,28},{16,0},{20,4},{24,8},{28,12},{1,17},{... | collective-permute-start | bytes 147464 | tf_op jit(solution)/shard_map/ppermute | solution.py:425
  34.5 4.1 %collective-permute-done.3.refs_1_ = f32[12,1024]{1,0:T(8,128)S(1)} collective-permute-done((f32[12,1024]{1,0:T(8,128)S(1)}, f32[12,1024]{1,0:T(8,128)S(1)}, u32[]{:S(2)}, u32[]{:S(2)}) %collective-permute-start.3) | collective-permute-done | bytes 49184 | tf_op jit(solution)/shard_map/ppermute | solution.py:425
  38.6 0.7 %collective-permute-start.4 = (f32[12,1024]{1,0:T(8,128)S(1)}, f32[12,1024]{1,0:T(8,128)S(1)}, u32[]{:S(2)}, u32[]{:S(2)}) collective-permute-start(f32[12,1024]{1,0:T(8,128)S(1)} %shard_map.98.refs_1_), channel_id=1, source_target_pairs={{0,4},{4,0},{8,12},{12,8},{16,20},{20,16},{24,28},{28,24},{1,5},{5... | collective-permute-start | bytes 147464 | tf_op jit(solution)/shard_map/ppermute | solution.py:425
  39.3 3.6 %collective-permute-done.4.refs_2_ = f32[12,1024]{1,0:T(8,128)S(1)} collective-permute-done((f32[12,1024]{1,0:T(8,128)S(1)}, f32[12,1024]{1,0:T(8,128)S(1)}, u32[]{:S(2)}, u32[]{:S(2)}) %collective-permute-start.4) | collective-permute-done | bytes 49184 | tf_op jit(solution)/shard_map/ppermute | solution.py:425
  42.9 0.0 copy-done.1
  43.0 0.6 shard_map.99
  43.5 0.6 collective-permute-start.8
  44.1 3.2 %shard_map.102.refs_2_ = bf16[2048,1024]{1,0:T(8,128)(2,1)S(1)} custom-call(f32[8,1024]{1,0:T(8,128)S(1)} %get-tuple-element.21.refs_1_.refs_0_, f32[8,1024]{1,0:T(8,128)S(1)} %get-tuple-element.22.refs_2_.refs_1_, f32[8,1024]{1,0:T(8,128)S(1)} %get-tuple-element.27.refs_2_, f32[2048,1024]{1,0:T(8,128)S(1)} %shard_map.96.refs_2_.refs_3_), custom_call_target="tpu_custom_call" | custom-call | flops 3630000128 | tf_op jit(solution)/shard_map/pallas_call | solution.py:27
  47.3 0.0 collective-permute-done.7.refs_6_.refs_5_
  47.3 3.4 %shard_map.101.refs_1_ = f32[512,128]{1,0:T(8,128)S(1)} custom-call(s32[6]{0:T(128)S(1)} %stack.27.refs_0_, f32[8,1024]{1,0:T(8,128)S(1)} %get-tuple-element.21.refs_1_.refs_0_, f32[8,1024]{1,0:T(8,128)S(1)} %get-tuple-element.22.refs_2_.refs_1_, f32[1024,1024]{1,0:T(8,128)S(1)} %get-tuple-element.20.refs_3_, f32[2,512,512]{2,1,0:T(8,128)S(1)} %get-tuple-element.23.refs_4_, ...), custom_call_target="tpu_custom_call" | custom-call | flops 3740000000 | tf_op jit(solution)/shard_map/pallas_call | solution.py:27
  50.7 4.1 %collective-permute-done.8.refs_3_ = bf16[256,1024]{1,0:T(8,128)(2,1)S(1)} collective-permute-done((bf16[256,1024]{1,0:T(8,128)(2,1)S(1)}, bf16[256,1024]{1,0:T(8,128)(2,1)S(1)}, u32[]{:S(2)}, u32[]{:S(2)}) %collective-permute-start.8) | collective-permute-done | bytes 524320 | tf_op jit(solution)/shard_map/ppermute | solution.py:443
  54.7 2.2 %shard_map.103 = f32[1,512]{1,0:T(1,128)S(1)} custom-call(s32[6]{0:T(128)S(1)} %stack.27.refs_0_, f32[512,128]{1,0:T(8,128)S(1)} %shard_map.101.refs_1_, bf16[2048,1024]{1,0:T(8,128)(2,1)S(1)} %shard_map.102.refs_2_, bf16[256,1024]{1,0:T(8,128)(2,1)S(1)} %collective-permute-done.8.refs_3_, bf16[512,1024]{1,0:T(8,128)(2,1)S(1)} %get-tuple-element.26.refs_5_.refs_4_, ...), custom_call_target="tpu_custom_call" | custom-call | flops 2310000128 | tf_op jit(solution)/shard_map/pallas_call | solution.py:27
  56.9 0.0 collective-permute-start.9
  56.9 1.2 %collective-permute-done.9 = f32[512]{0:T(512)S(1)} collective-permute-done((f32[512]{0:T(512)S(1)}, f32[512]{0:T(512)S(1)}, u32[]{:S(2)}, u32[]{:S(2)}) %collective-permute-start.9) | collective-permute-done | bytes 2080 | tf_op jit(solution)/shard_map/ppermute | solution.py:467
  58.1 0.5 collective-permute-start.10
  58.6 3.1 %collective-permute-done.10 = f32[512]{0:T(512)S(1)} collective-permute-done((f32[512]{0:T(512)S(1)}, f32[512]{0:T(512)S(1)}, u32[]{:S(2)}, u32[]{:S(2)}) %collective-permute-start.10) | collective-permute-done | bytes 2080 | tf_op jit(solution)/shard_map/ppermute | solution.py:467
  61.7 0.6 add.7
  (4 shorter events, 0.0 us)
Async XLA Ops:
  0.0 1.4 %copy-start = (bf16[3,256,1024]{2,1,0:T(8,128)(2,1)S(1)}, bf16[3,256,1024]{2,1,0:T(8,128)(2,1)}, u32[]{:S(2)}) copy-start(bf16[3,256,1024]{2,1,0:T(8,128)(2,1)} %refs_1_.1) | copy-start | bytes 4718596
  1.4 0.7 %copy-start.6 = (s32[2,64]{1,0:T(2,128)S(1)}, s32[2,64]{1,0:T(2,128)}, u32[]{:S(2)}) copy-start(s32[2,64]{1,0:T(2,128)} %refs_0_.1) | copy-start | bytes 1540
  2.1 0.7 %copy-start.7 = (f32[256]{0:T(256)S(1)}, f32[256]{0:T(256)}, u32[]{:S(2)}) copy-start(f32[256]{0:T(256)} %param.10) | copy-start | bytes 3076
  2.1 9.4 %copy-start.2 = (bf16[64,8,4,3]{0,2,3,1:T(4,128)(2,1)S(1)}, bf16[64,8,4,3]{0,2,3,1:T(4,128)(2,1)}, u32[]{:S(2)}) copy-start(bf16[64,8,4,3]{0,2,3,1:T(4,128)(2,1)} %param.14) | copy-start | bytes 36868
  2.1 9.4 %copy-start.5 = (s32[64,4]{0,1:T(4,128)S(1)}, s32[64,4]{0,1:T(4,128)}, u32[]{:S(2)}) copy-start(s32[64,4]{0,1:T(4,128)} %param.15) | copy-start | bytes 3076
  2.1 9.4 %copy-start.8 = (s32[64]{0:T(128)S(1)}, s32[64]{0:T(128)}, u32[]{:S(2)}) copy-start(s32[64]{0:T(128)} %param.16) | copy-start | bytes 772
  2.8 10.1 %copy-start.3 = (f32[4096]{0:T(1024)S(1)}, f32[4096]{0:T(1024)}, u32[]{:S(2)}) copy-start(f32[4096]{0:T(1024)} %param.12) | copy-start | bytes 49156
  2.8 10.1 %copy-start.4 = (f32[4096]{0:T(1024)S(1)}, f32[4096]{0:T(1024)}, u32[]{:S(2)}) copy-start(f32[4096]{0:T(1024)} %param.13) | copy-start | bytes 49156
  3.6 12.3 %collective-permute-start = (f32[4,1024]{1,0:T(4,128)S(1)}, f32[4,1024]{1,0:T(4,128)S(1)}, u32[]{:S(2)}, u32[]{:S(2)}) collective-permute-start(f32[4,1024]{1,0:T(4,128)S(1)} %shard_map.92.refs_3_.refs_0_), channel_id=1, source_target_pairs={{0,1},{1,0},{2,3},{3,2},{4,5},{5,4},{6,7},{7,6},{8,9},{9,8},{10,11... | collective-permute-start | bytes 49160 | tf_op jit(solution)/shard_map/ppermute | solution.py:411
  4.2 11.7 %collective-permute-start.1 = (f32[4,1024]{1,0:T(4,128)S(1)}, f32[4,1024]{1,0:T(4,128)S(1)}, u32[]{:S(2)}, u32[]{:S(2)}) collective-permute-start(f32[4,1024]{1,0:T(4,128)S(1)} %shard_map.92.refs_3_.refs_0_), channel_id=1, source_target_pairs={{0,2},{1,3},{2,0},{3,1},{4,6},{5,7},{6,4},{7,5},{8,10},{9,11},{10,... | collective-permute-start | bytes 49160 | tf_op jit(solution)/shard_map/ppermute | solution.py:411
  6.8 20.5 %collective-permute-start.5 = (bf16[192,1024]{1,0:T(8,128)(2,1)S(1)}, bf16[192,1024]{1,0:T(8,128)(2,1)S(1)}, u32[]{:S(2)}, u32[]{:S(2)}) collective-permute-start(bf16[192,1024]{1,0:T(8,128)(2,1)S(1)} %get-tuple-element.18.refs_2_), channel_id=1, source_target_pairs={{0,4},{4,8},{8,12},{12,16},{16,20},{20,24},{24,28},{1,5},{5,9},{9,... | collective-permute-start | bytes 1179656 | tf_op jit(solution)/shard_map/ppermute | solution.py:388
  10.2 17.1 %collective-permute-start.6 = (bf16[192,1024]{1,0:T(8,128)(2,1)S(1)}, bf16[192,1024]{1,0:T(8,128)(2,1)S(1)}, u32[]{:S(2)}, u32[]{:S(2)}) collective-permute-start(bf16[192,1024]{1,0:T(8,128)(2,1)S(1)} %get-tuple-element.25), channel_id=1, source_target_pairs={{4,0},{8,4},{12,8},{16,12},{20,16},{24,20},{28,24},{5,1},{9,5},{13... | collective-permute-start | bytes 1179656 | tf_op jit(solution)/shard_map/ppermute | solution.py:388
  11.9 0.9 %copy-start.9 = (bf16[512,768]{1,0:T(8,128)(2,1)}, bf16[512,768]{1,0:T(8,128)(2,1)S(1)}, u32[]{:S(2)}) copy-start(bf16[512,768]{1,0:T(8,128)(2,1)S(1)} %get-tuple-element.24.refs_2_) | copy-start | bytes 2359300
  16.0 9.4 %collective-permute-start.2 = (f32[12,1024]{1,0:T(8,128)S(1)}, f32[12,1024]{1,0:T(8,128)S(1)}, u32[]{:S(2)}, u32[]{:S(2)}) collective-permute-start(f32[12,1024]{1,0:T(8,128)S(1)} %shard_map.94.refs_0_), channel_id=1, source_target_pairs={{0,8},{4,12},{8,0},{12,4},{16,24},{20,28},{24,16},{28,20},{1,9},{5... | collective-permute-start | bytes 147464 | tf_op jit(solution)/shard_map/ppermute | solution.py:425
  24.7 2.6 %copy-start.10 = (bf16[512,768]{1,0:T(8,128)(2,1)S(1)}, bf16[512,768]{1,0:T(8,128)(2,1)}, u32[]{:S(2)}) copy-start(bf16[512,768]{1,0:T(8,128)(2,1)} %copy-done.9) | copy-start | bytes 2359300
  27.3 15.7 %copy-start.1 = (f32[3,4096]{1,0:T(4,128)S(1)}, f32[3,4096]{1,0:T(4,128)}, u32[]{:S(2)}) copy-start(f32[3,4096]{1,0:T(4,128)} %refs_3_.1) | copy-start | bytes 147460
  29.9 17.4 %collective-permute-start.7 = (bf16[512,1024]{1,0:T(8,128)(2,1)S(1)}, bf16[512,1024]{1,0:T(8,128)(2,1)S(1)}, u32[]{:S(2)}, u32[]{:S(2)}) collective-permute-start(bf16[512,1024]{1,0:T(8,128)(2,1)S(1)} %get-tuple-element.26.refs_5_.refs_4_), channel_id=1, source_target_pairs={{0,1},{1,0},{2,3},{3,2},{4,5},{5,4},{6,7},{7,6},{8,9},{9,8},{10,11... | collective-permute-start | bytes 3145736 | tf_op jit(solution)/shard_map/ppermute | solution.py:444
  30.0 8.6 %collective-permute-start.3 = (f32[12,1024]{1,0:T(8,128)S(1)}, f32[12,1024]{1,0:T(8,128)S(1)}, u32[]{:S(2)}, u32[]{:S(2)}) collective-permute-start(f32[12,1024]{1,0:T(8,128)S(1)} %shard_map.97.refs_0_.refs_6_), channel_id=1, source_target_pairs={{0,16},{4,20},{8,24},{12,28},{16,0},{20,4},{24,8},{28,12},{1,17},{... | collective-permute-start | bytes 147464 | tf_op jit(solution)/shard_map/ppermute | solution.py:425
  38.6 4.3 %collective-permute-start.4 = (f32[12,1024]{1,0:T(8,128)S(1)}, f32[12,1024]{1,0:T(8,128)S(1)}, u32[]{:S(2)}, u32[]{:S(2)}) collective-permute-start(f32[12,1024]{1,0:T(8,128)S(1)} %shard_map.98.refs_1_), channel_id=1, source_target_pairs={{0,4},{4,0},{8,12},{12,8},{16,20},{20,16},{24,28},{28,24},{1,5},{5... | collective-permute-start | bytes 147464 | tf_op jit(solution)/shard_map/ppermute | solution.py:425
  43.5 11.2 %collective-permute-start.8 = (bf16[256,1024]{1,0:T(8,128)(2,1)S(1)}, bf16[256,1024]{1,0:T(8,128)(2,1)S(1)}, u32[]{:S(2)}, u32[]{:S(2)}) collective-permute-start(bf16[256,1024]{1,0:T(8,128)(2,1)S(1)} %get-tuple-element.28), channel_id=1, source_target_pairs={{0,2},{1,3},{2,0},{3,1},{4,6},{5,7},{6,4},{7,5},{8,10},{9,11},{10,... | collective-permute-start | bytes 1572872 | tf_op jit(solution)/shard_map/ppermute | solution.py:443
  56.9 1.2 %collective-permute-start.9 = (f32[512]{0:T(512)S(1)}, f32[512]{0:T(512)S(1)}, u32[]{:S(2)}, u32[]{:S(2)}) collective-permute-start(f32[512]{0:T(512)S(1)} %bitcast.13), channel_id=1, source_target_pairs={{0,1},{1,0},{2,3},{3,2},{4,5},{5,4},{6,7},{7,6},{8,9},{9,8},{10,11... | collective-permute-start | bytes 6152 | tf_op jit(solution)/shard_map/ppermute | solution.py:467
  58.1 3.6 %collective-permute-start.10 = (f32[512]{0:T(512)S(1)}, f32[512]{0:T(512)S(1)}, u32[]{:S(2)}, u32[]{:S(2)}) collective-permute-start(f32[512]{0:T(512)S(1)} %add.6), channel_id=1, source_target_pairs={{0,2},{1,3},{2,0},{3,1},{4,6},{5,7},{6,4},{7,5},{8,10},{9,11},{10,... | collective-permute-start | bytes 6152 | tf_op jit(solution)/shard_map/ppermute | solution.py:467

commit v6 on v5

--- a/solution.py
+++ b/solution.py
@@ -108,17 +108,28 @@
     return (freq * freq * inverse, inverse, 2.0 * alpha, 2.0 * (freq / rate))
 
 
+def turn_rows(rows):
+    pieces = [rows[:, c : c + 128] for c in range(0, rows.shape[1], 128)]
+    while len(pieces) * 8 % 128:
+        pieces.append(jnp.zeros((8, 128), F32))
+    return [jnp.concatenate(pieces[c : c + 16], axis=0).T for c in range(0, len(pieces), 16)]
+
+
 def place_modes(freq_ref, rate_ref, row_scr, col_scr, groups, sides, block):
+    side_rows = []
     for which, group in enumerate(groups):
         lanes = pl.ds(pl.multiple_of(group * block, block), block)
         rows = jnp.concatenate(list(mode_rows(freq_ref[:, lanes], rate_ref[:, lanes])) * 2, axis=0)
         row_scr[which * 8 : which * 8 + 8, :] = rows
         if which < sides:
-            turned = rows.T
-            for q in range(4):
-                col_scr[q, which * block : (which + 1) * block, :] = jnp.broadcast_to(
-                    turned[:, q : q + 1], (block, 128)
-                )
+            side_rows.append(rows)
+    turned = turn_rows(jnp.concatenate(side_rows, axis=1))
+    for t in range(sides * block // 128):
+        for q in range(4):
+            lane = t % 16 * 8 + q
+            col_scr[q, t * 128 : (t + 1) * 128, :] = jnp.broadcast_to(
+                turned[t // 16][:, lane : lane + 1], (128, 128)
+            )
 
 
 def fill_rho(row_scr, col_scr, out_ref, out_col, side_row, count, cols_at, col_off, tile):
@@ -227,27 +238,33 @@
     )[0:1]
 
 
-def spread_sides(side_scr, at, amps, dims):
-    sides = amps.T
-    for d in range(dims):
-        side_scr[d, at : at + amps.shape[1], :] = jnp.broadcast_to(sides[:, d : d + 1], (amps.shape[1], 128))
-
-
-def weigh(out, rho, side_scr, side_at, cols, dims, factor):
-    span = min(512, rho.shape[1])
-    for base in range(0, rho.shape[1], span):
-        lanes = range(base, base + span, 128)
-        col = [
-            [jnp.broadcast_to(cols[d : d + 1, c : c + 128] * factor, (16, 128)) for d in range(dims)]
-            for c in lanes
-        ]
-        for r in range(0, rho.shape[0], 16):
-            side = [side_scr[d, side_at + r : side_at + r + 16, :] for d in range(dims)]
-            for c, own in zip(lanes, col):
-                pair = side[0] * own[0]
-                for d in range(1, dims):
-                    pair = pair + side[d] * own[d]
-                out[r : r + 16, c : c + 128] = (rho[r : r + 16, c : c + 128] * pair).astype(BF16)
+def split(value):
+    top = value.astype(BF16).astype(F32)
+    rest = value - top
+    middle = rest.astype(BF16).astype(F32)
+    return top, middle, rest - middle
+
+
+def side_terms(out_scr, at, amps, dims):
+    top, middle, last = split(amps[:dims])
+    rows = jnp.concatenate([top, top, middle, middle, top, last], axis=0)
+    rows = jnp.concatenate([rows, jnp.zeros((32 - rows.shape[0], rows.shape[1]), F32)], axis=0)
+    for c in range(0, amps.shape[1], 512):
+        stack = [rows[:, c + q : c + q + 128] for q in range(0, 512, 128)]
+        turned = jnp.concatenate(stack, axis=0).T
+        for q in range(4):
+            out_scr[at + c + q * 128 : at + c + (q + 1) * 128, :] = turned[:, q * 32 : (q + 1) * 32].astype(BF16)
+
+
+def col_terms(amps, dims, factor):
+    top, middle, last = split(amps[:dims] * factor)
+    rows = jnp.concatenate([top, middle, top, middle, last, top], axis=0)
+    rows = jnp.concatenate([rows, jnp.zeros((32 - rows.shape[0], rows.shape[1]), F32)], axis=0)
+    return rows.astype(BF16)
+
+
+def weigh(rho, side, cols):
+    return (rho * jnp.dot(side, cols, preferred_element_type=F32)).astype(BF16)
 
 
 def near_kernel(dims, chunks, *refs):
@@ -271,14 +288,16 @@
             total = got if total is None else total + got
         return total
 
-    spread_sides(side_scr, 0, own_amps_ref[...], dims)
+    side_terms(side_scr, 0, own_amps_ref[...], dims)
+    once, twice = (col_terms(own_amps_ref[...], dims, factor) for factor in (1.0, 2.0))
+    straight = parity == 0
     turn = 0
     for j in range(4):
-        cols = own_amps_ref[:, j * tile : (j + 1) * tile]
+        spot = slice(j * tile, (j + 1) * tile)
         for i in range(j + 1):
-            rho = diag_ref.at[i * tile : (i + 1) * tile, j * tile : (j + 1) * tile]
-            out = w_scr.at[turn, i * tile : (i + 1) * tile, :]
-            weigh(out, rho, side_scr, i * tile, cols, dims, 2.0 if i < j else 1.0)
+            rows = slice(i * tile, (i + 1) * tile)
+            cols = twice if i < j else once
+            w_scr[turn, rows, :] = weigh(diag_ref[rows, spot], side_scr[rows, :], cols[:, spot])
         got = product(w_scr.at[turn], 0, (j + 1) * tile)
         got = fold(got * part(own_refs, j * tile, tile).astype(F32))
         acc[...] = got if j == 0 else acc[...] + got
@@ -286,12 +305,13 @@
     for i in range(2):
         for j in range(half // tile):
             here, there = i * half + j * tile, (1 - i) * half + j * tile
-            straight = parity == 0
             cols = jnp.where(
                 straight, mate_amps_ref[:, here : here + tile], mate_amps_ref[:, there : there + tile]
             )
-            rho = cross_ref.at[i, :, j * tile : (j + 1) * tile]
-            weigh(w_scr.at[turn, :half, :], rho, side_scr, i * half, cols, dims, 2.0)
+            w_scr[turn, :half, :] = weigh(
+                cross_ref[i, :, j * tile : (j + 1) * tile],
+                side_scr[i * half : (i + 1) * half, :], col_terms(cols, dims, 2.0),
+            )
             got = product(w_scr.at[turn], i * half, half)
             other = jnp.where(
                 straight, part(mate_refs, here, tile).astype(F32), part(mate_refs, there, tile).astype(F32)
@@ -303,14 +323,14 @@
 def weights_kernel(dims, own_amps_ref, mate_amps_ref, far_amps_ref, rho_ref, out_ref, side_scr):
     block = rho_ref.shape[1]
     tile = block // 4
-    spread_sides(side_scr, 0, own_amps_ref[...], dims)
-    spread_sides(side_scr, block, mate_amps_ref[...], dims)
-
-    @pl.loop(0, 2 * block // tile)
-    def _(t):
-        rows = pl.ds(pl.multiple_of(t * tile, tile), tile)
-        sides = side_scr.at[:, rows, :]
-        weigh(out_ref.at[rows, :], rho_ref.at[rows, :], sides, 0, far_amps_ref[...], dims, 2.0)
+    side_terms(side_scr, 0, own_amps_ref[...], dims)
+    side_terms(side_scr, block, mate_amps_ref[...], dims)
+    cols = col_terms(far_amps_ref[...], dims, 2.0)
+    for at in range(0, 2 * block, tile):
+        rows = slice(at, at + tile)
+        for c in range(0, block, tile):
+            spot = slice(c, c + tile)
+            out_ref[rows, spot] = weigh(rho_ref[rows, spot], side_scr[rows, :], cols[:, spot])
 
 
 def far_kernel(at, chunks, per_elem, place_ref, near_ref, w_ref, far_ref, *refs):
@@ -375,7 +395,7 @@
         return call(
             functools.partial(gather_kernel, c * chunk),
             (sds((dims * width, chunk), BF16), sds((dims * width, chunk), BF16), sds((dims, nodes, chunk), BF16)),
-            (shared, shapes), 2.0 / CHUNKS, hbm=(1,),
+            (shared, shapes), 2.0 / CHUNKS, hbm=(1,), vmem=60 << 20,
             scratch=[pltpu.SemaphoreType.DMA], after=after,
         )
 
@@ -389,18 +409,18 @@
 
     stats = call(
         functools.partial(stats_kernel, CHUNKS), sds((dims + 1, block), F32), (masses.reshape(1, nodes), *held), 0.8,
-        scratch=[pltpu.VMEM((nodes, 128), F32)], after=after,
-    )
-    pick, force = call(
-        table_kernel, (sds((slots * elems, nodes + 2 * width), BF16), sds((comps, dims * slots * elems), BF16)),
-        (connectivity.T, node_count.reshape(1, elems), recovery.transpose(1, 3, 2, 0)),
-        0.5, after=(stats,),
+        scratch=[pltpu.VMEM((nodes, 128), F32)],
     )
     rho_diag, rho_mate = call(
         rho_near_kernel,
         (sds((block, block), F32), sds((2, block // 2, block // 2), F32)),
         (place, freq, rate), 3.0, smem=(0,),
-        scratch=[pltpu.VMEM((4, block, 128), F32), pltpu.VMEM((16, block), F32)], after=(pick,),
+        scratch=[pltpu.VMEM((4, block, 128), F32), pltpu.VMEM((16, block), F32)], after=(stats,),
+    )
+    pick, force = call(
+        table_kernel, (sds((slots * elems, nodes + 2 * width), BF16), sds((comps, dims * slots * elems), BF16)),
+        (connectivity.T, node_count.reshape(1, elems), recovery.transpose(1, 3, 2, 0)),
+        0.5, after=(rho_diag,),
     )
     rho_far = call(
         rho_far_kernel, sds((2 * block, block), F32), (place, freq, rate),
@@ -409,7 +429,7 @@
         after=(rho_diag,),
     )
     given = [stats] + [lax.ppermute(stats, "mode", [(i, i ^ q) for i in range(4)]) for q in (1, 2)]
-    stats = call(join_kernel, sds((3 * (dims + 1), block), F32), given, 0.5, after=(pick,))
+    stats = call(join_kernel, sds((3 * (dims + 1), block), F32), given, 0.5)
     first = stats
     order = [1 << q for q in range(1, parts.bit_length() - 1)] + [1]
     if parts & (parts - 1) or parts == 1:
@@ -419,7 +439,7 @@
     for q, reach in enumerate(order):
         if q:
             stats = call(
-                add_kernel, sds(stats.shape, F32), (stats, extra), 0.5, after=(rho_far,) if q == 1 else ()
+                add_kernel, sds(stats.shape, F32), (stats, extra), 0.5, after=(rho_diag,) if q == 1 else ()
             )
             first = stats if q == 1 else first
         extra = lax.ppermute(stats, "dom", [(i, i ^ reach) for i in range(parts)])
@@ -446,12 +466,12 @@
         functools.partial(near_kernel, dims, CHUNKS), sds((comps, 128), F32),
         (place, amps, mate_amps, rho_diag, rho_mate, *own, *mate),
         3.4, smem=(0,),
-        scratch=[pltpu.VMEM((dims, block, 128), F32), pltpu.VMEM((2, block, block // 4), BF16)],
+        scratch=[pltpu.VMEM((block, 32), BF16), pltpu.VMEM((2, block, block // 4), BF16)],
     )
     weights = call(
         functools.partial(weights_kernel, dims), sds((2 * block, block), BF16),
         (amps, mate_amps, far_amps, rho_far), 3.3,
-        scratch=[pltpu.VMEM((dims, 2 * block, 128), F32)],
+        scratch=[pltpu.VMEM((2 * block, 32), BF16)],
     )
     value = near
     for c in range(CHUNKS):

time: 62.6 us -> 67.7 us (1.081)
  waiting for transfers between devices: 18.6 us -> 24.1 us
  local copies, waits for them, and re-layouts: 3.09 us -> 1.52 us
  Pallas kernels: 21.9 us -> 23 us
    ppermute x3, waiting for transfers between devices: 8.37 us -> 11.3 us  [combined(): extra = lax.ppermute(stats, 'dom', [(i, i ^ reach) for i in range(parts)])]
    ppermute x1, waiting for transfers between devices: 4.09 us -> 6.59 us  [combined(): far.append(lax.ppermute(sent, 'mode', [(i, i ^ 2) for i in range(4)]))]
    unnamed x22 -> x18, local copies, waits for them, and re-layouts: 3 us -> 1.44 us
    pallas_call x13, Pallas kernels: 21.9 us -> 23 us  [call(): pl.pallas_call(body, out_shape=out_shape, in_specs=specs, out_specs=[VMEM...]
  transfers between devices with their start and end apart: 11 -> 11, of which waited for: 7 -> 6; matrix products, arithmetic and copies ran while one was open for 0% -> 0% of each run, Pallas kernels for 25% -> 20%
where the time goes in v6:
time: 67.7 us; the launch traced here: 67.2 us
  waiting for transfers between devices  24.1 us (36%)
  Pallas kernels  23 us (34%)
  starting transfers between devices  17.7 us (26%)
  local copies, waits for them, and re-layouts  1.52 us (2%)
    pallas_call x13, Pallas kernels, call(): pl.pallas_call(body, out_shape=out_shape, in_specs=specs, out_specs=[VMEM...  23 us
    ppermute x3, waiting for transfers between devices, combined(): extra = lax.ppermute(stats, 'dom', [(i, i ^ reach) for i in range(parts)])  11.3 us
    ppermute x3, starting transfers between devices, combined(): extra = lax.ppermute(stats, 'dom', [(i, i ^ reach) for i in range(parts)])  8.83 us
    ppermute x1, waiting for transfers between devices, combined(): far.append(lax.ppermute(sent, 'mode', [(i, i ^ 2) for i in range(4)]))  6.59 us
    ppermute x2, waiting for transfers between devices, combined(): lax.ppermute(value, 'mode', [(i, i ^ reach) for i in range(4)])  4.25 us
    ppermute x1, starting transfers between devices, combined(): lax.ppermute(up, 'dom', ahead)  3.41 us
    ppermute x2, starting transfers between devices, combined(): lax.ppermute(stats, 'mode', [(i, i ^ q) for i in range(4)])  3.06 us
    ppermute x1, waiting for transfers between devices, combined(): lax.ppermute(up, 'dom', ahead)  1.96 us
  transfers between devices with their start and end apart: 11, of which 6 were waited for; matrix products, arithmetic and copies ran while one was open for 0% of the time, Pallas kernels for 20%

profile of v6, /device:TPU:0, one launch (start us, length us, event | category | flops | bytes accessed | tf_op | source)
XLA Modules:
  0.0 67.2 jit_solution(10350608554217591876)
XLA Ops:
  0.0 0.0 copy-start.6
  0.0 0.0 copy-start.5
  0.0 0.0 copy-start.4
  0.0 3.9 %shard_map.91 = (bf16[192,1024]{1,0:T(8,128)(2,1)}, bf16[192,1024]{1,0:T(8,128)(2,1)}, bf16[3,256,1024]{2,1,0:T(8,128)(2,1)}) custom-call(s32[2,64]{1,0:T(2,128)} %refs_0_.1, bf16[3,256,1024]{2,1,0:T(8,128)(2,1)} %refs_1_.1), custom_call_target="tpu_custom_call" | custom-call | flops 2200000000 | tf_op jit(solution)/shard_map/pallas_call | solution.py:27
  3.9 0.0 copy-done.6
  3.9 0.0 copy-start.7
  3.9 1.4 %copy-done.7 = bf16[3,256,1024]{2,1,0:T(8,128)(2,1)S(1)} copy-done((bf16[3,256,1024]{2,1,0:T(8,128)(2,1)S(1)}, bf16[3,256,1024]{2,1,0:T(8,128)(2,1)}, u32[]{:S(2)}) %copy-start.7) | copy-done | bytes 1572888
  5.3 0.8 %shard_map.92.refs_0_.refs_3_ = f32[4,1024]{1,0:T(4,128)S(1)} custom-call(f32[1,256]{1,0:T(1,128)S(1)} %bitcast.24, bf16[3,256,1024]{2,1,0:T(8,128)(2,1)S(1)} %copy-done.7), custom_call_target="tpu_custom_call" | custom-call | flops 880000000 | tf_op jit(solution)/shard_map/pallas_call | solution.py:27
  6.1 3.1 %collective-permute-start.1 = (f32[4,1024]{1,0:T(4,128)S(1)}, f32[4,1024]{1,0:T(4,128)S(1)}, u32[]{:S(2)}, u32[]{:S(2)}) collective-permute-start(f32[4,1024]{1,0:T(4,128)S(1)} %shard_map.92.refs_0_.refs_3_), channel_id=1, source_target_pairs={{0,2},{1,3},{2,0},{3,1},{4,6},{5,7},{6,4},{7,5},{8,10},{9,11},{10,... | collective-permute-start | bytes 49160 | tf_op jit(solution)/shard_map/ppermute | solution.py:431
  9.2 0.0 collective-permute-start
  9.2 3.4 %collective-permute-start.5 = (bf16[192,1024]{1,0:T(8,128)(2,1)}, bf16[192,1024]{1,0:T(8,128)(2,1)S(1)}, u32[]{:S(2)}, u32[]{:S(2)}) collective-permute-start(bf16[192,1024]{1,0:T(8,128)(2,1)} %get-tuple-element.24), channel_id=1, source_target_pairs={{0,4},{4,8},{8,12},{12,16},{16,20},{20,24},{24,28},{1,5},{5,9},{9,... | collective-permute-start | bytes 1179656 | tf_op jit(solution)/shard_map/ppermute | solution.py:408
  12.6 1.3 %collective-permute-start.6 = (bf16[192,1024]{1,0:T(8,128)(2,1)}, bf16[192,1024]{1,0:T(8,128)(2,1)S(1)}, u32[]{:S(2)}, u32[]{:S(2)}) collective-permute-start(bf16[192,1024]{1,0:T(8,128)(2,1)} %get-tuple-element.25), channel_id=1, source_target_pairs={{4,0},{8,4},{12,8},{16,12},{20,16},{24,20},{28,24},{5,1},{9,5},{13... | collective-permute-start | bytes 1179656 | tf_op jit(solution)/shard_map/ppermute | solution.py:408
  13.9 0.1 stack.27.refs_0_
  14.0 0.0 copy-done.5
  14.0 0.0 copy-done.4
  14.0 0.0 copy-start
  14.0 0.0 copy-start.1
  14.1 0.0 copy-start.2
  14.1 3.0 %shard_map.94 = (f32[1024,1024]{1,0:T(8,128)S(1)}, f32[2,512,512]{2,1,0:T(8,128)S(1)}) custom-call(s32[6]{0:T(128)S(1)} %stack.27.refs_0_, f32[1,4096]{1,0:T(1,128)S(1)} %bitcast.18, f32[1,4096]{1,0:T(1,128)S(1)} %bitcast.21, f32[4,1024]{1,0:T(4,128)S(1)} %shard_map.92.refs_0_.refs_3_), custom_call_target="tpu_custom_call" | custom-call | flops 3300000000 | tf_op jit(solution)/shard_map/pallas_call | solution.py:27
  17.0 0.0 collective-permute-done.1.refs_2_
  17.0 0.0 collective-permute-done.refs_1_
  17.1 3.7 %collective-permute-start.2 = (f32[12,1024]{1,0:T(8,128)S(1)}, f32[12,1024]{1,0:T(8,128)S(1)}, u32[]{:S(2)}, u32[]{:S(2)}) collective-permute-start(f32[12,1024]{1,0:T(8,128)S(1)} %shard_map.93.refs_0_), channel_id=1, source_target_pairs={{0,8},{4,12},{8,0},{12,4},{16,24},{20,28},{24,16},{28,20},{1,9},{5... | collective-permute-start | bytes 147464 | tf_op jit(solution)/shard_map/ppermute | solution.py:445
  20.7 0.0 copy-done
  20.7 0.0 copy-done.1
  20.7 0.0 copy-done.2
  20.8 0.0 copy-start.8
  20.8 0.4 shard_map.98
  21.2 7.2 %collective-permute-done.2.refs_1_ = f32[12,1024]{1,0:T(8,128)S(1)} collective-permute-done((f32[12,1024]{1,0:T(8,128)S(1)}, f32[12,1024]{1,0:T(8,128)S(1)}, u32[]{:S(2)}, u32[]{:S(2)}) %collective-permute-start.2) | collective-permute-done | bytes 49184 | tf_op jit(solution)/shard_map/ppermute | solution.py:445
  28.4 2.0 %collective-permute-done.5.refs_4_ = bf16[192,1024]{1,0:T(8,128)(2,1)S(1)} collective-permute-done((bf16[192,1024]{1,0:T(8,128)(2,1)}, bf16[192,1024]{1,0:T(8,128)(2,1)S(1)}, u32[]{:S(2)}, u32[]{:S(2)}) %collective-permute-start.5) | collective-permute-done | bytes 393248 | tf_op jit(solution)/shard_map/ppermute | solution.py:408
  30.4 0.0 collective-permute-done.6.refs_5_
  30.4 0.0 copy-done.8
  30.4 2.6 %shard_map.99 = (bf16[512,1024]{1,0:T(8,128)(2,1)S(1)}, bf16[256,1024]{1,0:T(8,128)(2,1)S(1)}) custom-call(s32[6]{0:T(128)S(1)} %stack.27.refs_0_, bf16[256,384]{1,0:T(8,128)(2,1)S(1)} %get-tuple-element.22.refs_1_, bf16[512,768]{1,0:T(8,128)(2,1)S(1)} %get-tuple-element.23.refs_2_, bf16[3,256,1024]{2,1,0:T(8,128)(2,1)S(1)} %copy-done.8, ...), custom_call_target="tpu_custom_call" | custom-call | flops 2860000000 | tf_op jit(solution)/shard_map/pallas_call | solution.py:27
  33.0 0.1 collective-permute-start.7
  33.1 4.4 %collective-permute-start.3 = (f32[12,1024]{1,0:T(8,128)S(1)}, f32[12,1024]{1,0:T(8,128)S(1)}, u32[]{:S(2)}, u32[]{:S(2)}) collective-permute-start(f32[12,1024]{1,0:T(8,128)S(1)} %shard_map.95.refs_0_.refs_6_), channel_id=1, source_target_pairs={{0,16},{4,20},{8,24},{12,28},{16,0},{20,4},{24,8},{28,12},{1,17},{... | collective-permute-start | bytes 147464 | tf_op jit(solution)/shard_map/ppermute | solution.py:445
  37.5 4.1 %collective-permute-done.3.refs_1_ = f32[12,1024]{1,0:T(8,128)S(1)} collective-permute-done((f32[12,1024]{1,0:T(8,128)S(1)}, f32[12,1024]{1,0:T(8,128)S(1)}, u32[]{:S(2)}, u32[]{:S(2)}) %collective-permute-start.3) | collective-permute-done | bytes 49184 | tf_op jit(solution)/shard_map/ppermute | solution.py:445
  41.6 0.0 copy-start.3
  41.6 0.7 %collective-permute-start.4 = (f32[12,1024]{1,0:T(8,128)S(1)}, f32[12,1024]{1,0:T(8,128)S(1)}, u32[]{:S(2)}, u32[]{:S(2)}) collective-permute-start(f32[12,1024]{1,0:T(8,128)S(1)} %shard_map.96.refs_1_), channel_id=1, source_target_pairs={{0,4},{4,0},{8,12},{12,8},{16,20},{20,16},{24,28},{28,24},{1,5},{5... | collective-permute-start | bytes 147464 | tf_op jit(solution)/shard_map/ppermute | solution.py:445
  42.4 5.0 %shard_map.101.refs_3_ = f32[2048,1024]{1,0:T(8,128)S(1)} custom-call(s32[6]{0:T(128)S(1)} %stack.27.refs_0_, f32[1,4096]{1,0:T(1,128)S(1)} %bitcast.19, f32[1,4096]{1,0:T(1,128)S(1)} %bitcast.22, f32[1024,1024]{1,0:T(8,128)S(1)} %get-tuple-element.18.refs_2_.refs_3_), custom_call_target="tpu_custom_call" | custom-call | flops 5500000256 | tf_op jit(solution)/shard_map/pallas_call | solution.py:27
  47.3 0.0 collective-permute-done.4.refs_2_
  47.3 0.0 copy-done.3
  47.3 0.6 shard_map.97
  47.9 0.6 collective-permute-start.8
  48.5 1.4 %shard_map.102.refs_2_ = bf16[2048,1024]{1,0:T(8,128)(2,1)S(1)} custom-call(f32[8,1024]{1,0:T(8,128)S(1)} %get-tuple-element.19.refs_1_.refs_0_, f32[8,1024]{1,0:T(8,128)S(1)} %get-tuple-element.20.refs_2_.refs_1_, f32[8,1024]{1,0:T(8,128)S(1)} %get-tuple-element.27.refs_2_, f32[2048,1024]{1,0:T(8,128)S(1)} %shard_map.101.refs_3_), custom_call_target="tpu_custom_call" | custom-call | flops 3630000128 | tf_op jit(solution)/shard_map/pallas_call | solution.py:27
  49.9 0.0 collective-permute-done.7.refs_6_.refs_5_
  49.9 3.2 %shard_map.100.refs_1_ = f32[512,128]{1,0:T(8,128)S(1)} custom-call(s32[6]{0:T(128)S(1)} %stack.27.refs_0_, f32[8,1024]{1,0:T(8,128)S(1)} %get-tuple-element.19.refs_1_.refs_0_, f32[8,1024]{1,0:T(8,128)S(1)} %get-tuple-element.20.refs_2_.refs_1_, f32[1024,1024]{1,0:T(8,128)S(1)} %get-tuple-element.18.refs_2_.refs_3_, ...), custom_call_target="tpu_custom_call" | custom-call | flops 3740000000 | tf_op jit(solution)/shard_map/pallas_call | solution.py:27
  53.1 6.6 %collective-permute-done.8.refs_3_ = bf16[256,1024]{1,0:T(8,128)(2,1)S(1)} collective-permute-done((bf16[256,1024]{1,0:T(8,128)(2,1)S(1)}, bf16[256,1024]{1,0:T(8,128)(2,1)S(1)}, u32[]{:S(2)}, u32[]{:S(2)}) %collective-permute-start.8) | collective-permute-done | bytes 524320 | tf_op jit(solution)/shard_map/ppermute | solution.py:463
  59.7 2.2 %shard_map.103 = f32[1,512]{1,0:T(1,128)S(1)} custom-call(s32[6]{0:T(128)S(1)} %stack.27.refs_0_, f32[512,128]{1,0:T(8,128)S(1)} %shard_map.100.refs_1_, bf16[2048,1024]{1,0:T(8,128)(2,1)S(1)} %shard_map.102.refs_2_, bf16[256,1024]{1,0:T(8,128)(2,1)S(1)} %collective-permute-done.8.refs_3_, bf16[512,1024]{1,0:T(8,128)(2,1)S(1)} %get-tuple-element.26.refs_5_.refs_4_, ...), custom_call_target="tpu_custom_call" | custom-call | flops 2310000128 | tf_op jit(solution)/shard_map/pallas_call | solution.py:27
  61.9 0.0 collective-permute-start.9
  61.9 1.2 %collective-permute-done.9 = f32[512]{0:T(512)S(1)} collective-permute-done((f32[512]{0:T(512)S(1)}, f32[512]{0:T(512)S(1)}, u32[]{:S(2)}, u32[]{:S(2)}) %collective-permute-start.9) | collective-permute-done | bytes 2080 | tf_op jit(solution)/shard_map/ppermute | solution.py:487
  63.1 0.5 collective-permute-start.10
  63.6 3.1 %collective-permute-done.10 = f32[512]{0:T(512)S(1)} collective-permute-done((f32[512]{0:T(512)S(1)}, f32[512]{0:T(512)S(1)}, u32[]{:S(2)}, u32[]{:S(2)}) %collective-permute-start.10) | collective-permute-done | bytes 2080 | tf_op jit(solution)/shard_map/ppermute | solution.py:487
  66.6 0.6 add.7
  (4 shorter events, 0.0 us)
Async XLA Ops:
  0.0 3.9 %copy-start.6 = (f32[256]{0:T(256)S(1)}, f32[256]{0:T(256)}, u32[]{:S(2)}) copy-start(f32[256]{0:T(256)} %param.10) | copy-start | bytes 3076
  0.0 14.0 %copy-start.5 = (f32[4096]{0:T(1024)S(1)}, f32[4096]{0:T(1024)}, u32[]{:S(2)}) copy-start(f32[4096]{0:T(1024)} %param.13) | copy-start | bytes 49156
  0.0 14.0 %copy-start.4 = (f32[4096]{0:T(1024)S(1)}, f32[4096]{0:T(1024)}, u32[]{:S(2)}) copy-start(f32[4096]{0:T(1024)} %param.12) | copy-start | bytes 49156
  3.9 1.4 %copy-start.7 = (bf16[3,256,1024]{2,1,0:T(8,128)(2,1)S(1)}, bf16[3,256,1024]{2,1,0:T(8,128)(2,1)}, u32[]{:S(2)}) copy-start(bf16[3,256,1024]{2,1,0:T(8,128)(2,1)} %get-tuple-element.17.refs_1_.refs_3_) | copy-start | bytes 4718596
  6.1 10.9 %collective-permute-start.1 = (f32[4,1024]{1,0:T(4,128)S(1)}, f32[4,1024]{1,0:T(4,128)S(1)}, u32[]{:S(2)}, u32[]{:S(2)}) collective-permute-start(f32[4,1024]{1,0:T(4,128)S(1)} %shard_map.92.refs_0_.refs_3_), channel_id=1, source_target_pairs={{0,2},{1,3},{2,0},{3,1},{4,6},{5,7},{6,4},{7,5},{8,10},{9,11},{10,... | collective-permute-start | bytes 49160 | tf_op jit(solution)/shard_map/ppermute | solution.py:431
  9.2 7.8 %collective-permute-start = (f32[4,1024]{1,0:T(4,128)S(1)}, f32[4,1024]{1,0:T(4,128)S(1)}, u32[]{:S(2)}, u32[]{:S(2)}) collective-permute-start(f32[4,1024]{1,0:T(4,128)S(1)} %shard_map.92.refs_0_.refs_3_), channel_id=1, source_target_pairs={{0,1},{1,0},{2,3},{3,2},{4,5},{5,4},{6,7},{7,6},{8,9},{9,8},{10,11... | collective-permute-start | bytes 49160 | tf_op jit(solution)/shard_map/ppermute | solution.py:431
  9.2 21.2 %collective-permute-start.5 = (bf16[192,1024]{1,0:T(8,128)(2,1)}, bf16[192,1024]{1,0:T(8,128)(2,1)S(1)}, u32[]{:S(2)}, u32[]{:S(2)}) collective-permute-start(bf16[192,1024]{1,0:T(8,128)(2,1)} %get-tuple-element.24), channel_id=1, source_target_pairs={{0,4},{4,8},{8,12},{12,16},{16,20},{20,24},{24,28},{1,5},{5,9},{9,... | collective-permute-start | bytes 1179656 | tf_op jit(solution)/shard_map/ppermute | solution.py:408
  12.6 17.7 %collective-permute-start.6 = (bf16[192,1024]{1,0:T(8,128)(2,1)}, bf16[192,1024]{1,0:T(8,128)(2,1)S(1)}, u32[]{:S(2)}, u32[]{:S(2)}) collective-permute-start(bf16[192,1024]{1,0:T(8,128)(2,1)} %get-tuple-element.25), channel_id=1, source_target_pairs={{4,0},{8,4},{12,8},{16,12},{20,16},{24,20},{28,24},{5,1},{9,5},{13... | collective-permute-start | bytes 1179656 | tf_op jit(solution)/shard_map/ppermute | solution.py:408
  14.0 6.7 %copy-start = (bf16[64,8,4,3]{0,2,3,1:T(4,128)(2,1)S(1)}, bf16[64,8,4,3]{0,2,3,1:T(4,128)(2,1)}, u32[]{:S(2)}) copy-start(bf16[64,8,4,3]{0,2,3,1:T(4,128)(2,1)} %param.14) | copy-start | bytes 36868
  14.0 6.7 %copy-start.1 = (s32[64,4]{0,1:T(4,128)S(1)}, s32[64,4]{0,1:T(4,128)}, u32[]{:S(2)}) copy-start(s32[64,4]{0,1:T(4,128)} %param.15) | copy-start | bytes 3076
  14.1 6.7 %copy-start.2 = (s32[64]{0:T(128)S(1)}, s32[64]{0:T(128)}, u32[]{:S(2)}) copy-start(s32[64]{0:T(128)} %param.16) | copy-start | bytes 772
  17.1 11.3 %collective-permute-start.2 = (f32[12,1024]{1,0:T(8,128)S(1)}, f32[12,1024]{1,0:T(8,128)S(1)}, u32[]{:S(2)}, u32[]{:S(2)}) collective-permute-start(f32[12,1024]{1,0:T(8,128)S(1)} %shard_map.93.refs_0_), channel_id=1, source_target_pairs={{0,8},{4,12},{8,0},{12,4},{16,24},{20,28},{24,16},{28,20},{1,9},{5... | collective-permute-start | bytes 147464 | tf_op jit(solution)/shard_map/ppermute | solution.py:445
  20.8 9.6 %copy-start.8 = (bf16[3,256,1024]{2,1,0:T(8,128)(2,1)S(1)}, bf16[3,256,1024]{2,1,0:T(8,128)(2,1)}, u32[]{:S(2)}) copy-start(bf16[3,256,1024]{2,1,0:T(8,128)(2,1)} %get-tuple-element.17.refs_1_.refs_3_) | copy-start | bytes 4718596
  33.0 16.9 %collective-permute-start.7 = (bf16[512,1024]{1,0:T(8,128)(2,1)S(1)}, bf16[512,1024]{1,0:T(8,128)(2,1)S(1)}, u32[]{:S(2)}, u32[]{:S(2)}) collective-permute-start(bf16[512,1024]{1,0:T(8,128)(2,1)S(1)} %get-tuple-element.26.refs_5_.refs_4_), channel_id=1, source_target_pairs={{0,1},{1,0},{2,3},{3,2},{4,5},{5,4},{6,7},{7,6},{8,9},{9,8},{10,11... | collective-permute-start | bytes 3145736 | tf_op jit(solution)/shard_map/ppermute | solution.py:464
  33.1 8.5 %collective-permute-start.3 = (f32[12,1024]{1,0:T(8,128)S(1)}, f32[12,1024]{1,0:T(8,128)S(1)}, u32[]{:S(2)}, u32[]{:S(2)}) collective-permute-start(f32[12,1024]{1,0:T(8,128)S(1)} %shard_map.95.refs_0_.refs_6_), channel_id=1, source_target_pairs={{0,16},{4,20},{8,24},{12,28},{16,0},{20,4},{24,8},{28,12},{1,17},{... | collective-permute-start | bytes 147464 | tf_op jit(solution)/shard_map/ppermute | solution.py:445
  41.6 5.7 %copy-start.3 = (f32[3,4096]{1,0:T(4,128)S(1)}, f32[3,4096]{1,0:T(4,128)}, u32[]{:S(2)}) copy-start(f32[3,4096]{1,0:T(4,128)} %refs_3_.1) | copy-start | bytes 147460
  41.6 5.7 %collective-permute-start.4 = (f32[12,1024]{1,0:T(8,128)S(1)}, f32[12,1024]{1,0:T(8,128)S(1)}, u32[]{:S(2)}, u32[]{:S(2)}) collective-permute-start(f32[12,1024]{1,0:T(8,128)S(1)} %shard_map.96.refs_1_), channel_id=1, source_target_pairs={{0,4},{4,0},{8,12},{12,8},{16,20},{20,16},{24,28},{28,24},{1,5},{5... | collective-permute-start | bytes 147464 | tf_op jit(solution)/shard_map/ppermute | solution.py:445
  47.9 11.8 %collective-permute-start.8 = (bf16[256,1024]{1,0:T(8,128)(2,1)S(1)}, bf16[256,1024]{1,0:T(8,128)(2,1)S(1)}, u32[]{:S(2)}, u32[]{:S(2)}) collective-permute-start(bf16[256,1024]{1,0:T(8,128)(2,1)S(1)} %get-tuple-element.28), channel_id=1, source_target_pairs={{0,2},{1,3},{2,0},{3,1},{4,6},{5,7},{6,4},{7,5},{8,10},{9,11},{10,... | collective-permute-start | bytes 1572872 | tf_op jit(solution)/shard_map/ppermute | solution.py:463
  61.9 1.2 %collective-permute-start.9 = (f32[512]{0:T(512)S(1)}, f32[512]{0:T(512)S(1)}, u32[]{:S(2)}, u32[]{:S(2)}) collective-permute-start(f32[512]{0:T(512)S(1)} %bitcast.15), channel_id=1, source_target_pairs={{0,1},{1,0},{2,3},{3,2},{4,5},{5,4},{6,7},{7,6},{8,9},{9,8},{10,11... | collective-permute-start | bytes 6152 | tf_op jit(solution)/shard_map/ppermute | solution.py:487
  63.1 3.6 %collective-permute-start.10 = (f32[512]{0:T(512)S(1)}, f32[512]{0:T(512)S(1)}, u32[]{:S(2)}, u32[]{:S(2)}) collective-permute-start(f32[512]{0:T(512)S(1)} %add.6), channel_id=1, source_target_pairs={{0,2},{1,3},{2,0},{3,1},{4,6},{5,7},{6,4},{7,5},{8,10},{9,11},{10,... | collective-permute-start | bytes 6152 | tf_op jit(solution)/shard_map/ppermute | solution.py:487

commit v7 on v6

--- a/solution.py
+++ b/solution.py
@@ -39,45 +39,54 @@
     out_ref[...] = left_ref[...] + right_ref[...]
 
 
-def gather_kernel(at, shared_ref, shapes_ref, up_ref, down_ref, buf, sem):
-    dims, nodes, chunk = buf.shape
+def gather_kernel(shared_ref, shapes_ref, up_ref, down_ref, ids, buf, sems):
+    dims, nodes, _ = buf.shape
     width = shared_ref.shape[1]
-    load = pltpu.make_async_copy(shapes_ref.at[:, :, at : at + chunk], buf, sem)
-    load.start()
+    listed = pltpu.make_async_copy(shared_ref, ids, sems.at[dims])
+    listed.start()
+    loads = [pltpu.make_async_copy(shapes_ref.at[d], buf.at[d], sems.at[d]) for d in range(dims)]
+    for load in loads:
+        load.start()
+    listed.wait()
     node = lax.broadcasted_iota(jnp.int32, (nodes, 2 * width), 0)
-    wanted = jnp.concatenate([shared_ref[1:2, :], shared_ref[0:1, :]], axis=1)
+    wanted = jnp.concatenate([ids[1:2, :], ids[0:1, :]], axis=1)
     pick = jnp.where(node == wanted, 1.0, 0.0).astype(F32).T.astype(BF16)
-    load.wait()
     for d in range(dims):
+        loads[d].wait()
         got = jnp.dot(pick, buf[d], preferred_element_type=F32).astype(BF16)
         up_ref[d * width : (d + 1) * width, :] = got[:width]
         down_ref[d * width : (d + 1) * width, :] = got[width:]
 
 
-def stats_kernel(chunks, mass_ref, *refs):
-    shapes_refs, (out_ref, mass_scr) = refs[:chunks], refs[chunks:]
-    dims, nodes, chunk = shapes_refs[0].shape
+def stats_kernel(mass_ref, shapes_ref, out_ref, mass_scr, total_scr, buf, sems):
+    dims, nodes, block = buf.shape
+    loads = [pltpu.make_async_copy(shapes_ref.at[d], buf.at[d], sems.at[d]) for d in range(dims)]
+    for load in loads:
+        load.start()
     column = jnp.broadcast_to(mass_ref[...], (8, nodes)).T
     mass_scr[...] = jnp.broadcast_to(column[:, 0:1], (nodes, 128))
-    for c, shapes_ref in enumerate(shapes_refs):
-        for at in range(0, chunk, 128):
-            lanes = slice(c * chunk + at, c * chunk + at + 128)
-            general = jnp.zeros((8, 128), F32)
-            for d in range(dims):
-                lever = jnp.zeros((8, 128), F32)
-                for r in range(0, nodes, 16):
-                    wide = shapes_ref[d, r : r + 16, at : at + 128].astype(F32)
-                    weighted = wide * mass_scr[r : r + 16, :]
-                    square = weighted * wide
-                    lever += weighted[:8] + weighted[8:]
-                    general += square[:8] + square[8:]
-                out_ref[d : d + 1, lanes] = jnp.sum(lever, axis=0, keepdims=True)
-            out_ref[dims : dims + 1, lanes] = jnp.sum(general, axis=0, keepdims=True)
-
-
-def table_kernel(codes_ref, count_ref, recovery_ref, pick_ref, force_ref):
+    for d in range(dims):
+        loads[d].wait()
+        for at in range(0, block, 128):
+            lanes = slice(at, at + 128)
+            lever = jnp.zeros((8, 128), F32)
+            general = jnp.zeros((8, 128), F32) if d == 0 else total_scr[:, lanes]
+            for r in range(0, nodes, 16):
+                wide = buf[d, r : r + 16, lanes].astype(F32)
+                weighted = wide * mass_scr[r : r + 16, :]
+                square = weighted * wide
+                lever += weighted[:8] + weighted[8:]
+                general += square[:8] + square[8:]
+            out_ref[d : d + 1, lanes] = jnp.sum(lever, axis=0, keepdims=True)
+            total_scr[:, lanes] = general
+    out_ref[dims : dims + 1, :] = jnp.sum(total_scr[...], axis=0, keepdims=True)
+
+
+def local_kernel(codes_ref, count_ref, recovery_ref, shapes_ref, local_ref, rim_ref, pick_ref, force_ref, got_scr):
     slots, elems = codes_ref.shape
     per_elem, dims = recovery_ref.shape[0], recovery_ref.shape[1]
+    nodes, block = shapes_ref.shape[1], shapes_ref.shape[2]
+    taken = slots * elems
     span = pick_ref.shape[1]
     node = lax.broadcasted_iota(jnp.int32, (span, elems), 0)
     for s in range(0, slots, 2):
@@ -100,6 +109,19 @@
                 force_ref[k * elems : (k + 1) * elems, at : at + 2 * elems] = jnp.where(
                     same, pair, 0.0
                 ).astype(BF16)
+    rim = span - nodes
+    for d in range(dims):
+        rows = slice(d * taken, (d + 1) * taken)
+        value = jnp.dot(force_ref[:, rows], pick_ref[:, nodes:], preferred_element_type=F32)
+        high = value.astype(BF16)
+        rim_ref[:, d * rim : (d + 1) * rim] = high
+        rim_ref[:, (dims + d) * rim : (dims + d + 1) * rim] = (value - high.astype(F32)).astype(BF16)
+        got = jnp.dot(pick_ref[:, :nodes], shapes_ref[d], preferred_element_type=F32)
+        got_scr[rows, :] = got.astype(BF16)
+    for c in range(0, block, 256):
+        local_ref[:, c : c + 256] = jnp.dot(
+            force_ref[...], got_scr[:, c : c + 256], preferred_element_type=F32
+        )
 
 
 def mode_rows(freq, rate):
@@ -115,16 +137,16 @@
     return [jnp.concatenate(pieces[c : c + 16], axis=0).T for c in range(0, len(pieces), 16)]
 
 
-def place_modes(freq_ref, rate_ref, row_scr, col_scr, groups, sides, block):
+def place_modes(freq_ref, rate_ref, row_scr, col_scr, groups, side, block):
     side_rows = []
     for which, group in enumerate(groups):
         lanes = pl.ds(pl.multiple_of(group * block, block), block)
         rows = jnp.concatenate(list(mode_rows(freq_ref[:, lanes], rate_ref[:, lanes])) * 2, axis=0)
         row_scr[which * 8 : which * 8 + 8, :] = rows
-        if which < sides:
+        if which == side:
             side_rows.append(rows)
     turned = turn_rows(jnp.concatenate(side_rows, axis=1))
-    for t in range(sides * block // 128):
+    for t in range(block // 128):
         for q in range(4):
             lane = t % 16 * 8 + q
             col_scr[q, t * 128 : (t + 1) * 128, :] = jnp.broadcast_to(
@@ -157,7 +179,7 @@
     half = block // 2
     tile = block // 4
     own, mate, parity = place_ref[0], place_ref[1], place_ref[3]
-    place_modes(freq_ref, rate_ref, row_scr, col_scr, (own, mate), 1, block)
+    place_modes(freq_ref, rate_ref, row_scr, col_scr, (own, mate), 0, block)
     for j in range(4):
         fill_rho(row_scr, col_scr, diag_ref, j * tile, 0, (j + 1) * tile, 0, j * tile, tile)
     for i in range(2):
@@ -166,39 +188,31 @@
             fill_rho(row_scr, col_scr, mate_ref.at[i], j * tile, i * half, half, 8, off, tile)
 
 
-def rho_far_kernel(place_ref, freq_ref, rate_ref, far_ref, col_scr, row_scr):
+def rho_far_kernel(place_ref, freq_ref, rate_ref, own_side_ref, far_ref, col_scr, row_scr):
     block = far_ref.shape[1]
     tile = block // 4
-    own, mate, far = place_ref[0], place_ref[1], place_ref[2]
-    place_modes(freq_ref, rate_ref, row_scr, col_scr, (own, mate, far), 2, block)
-    for j in range(4):
-        fill_rho(row_scr, col_scr, far_ref, j * tile, 0, 2 * block, 16, j * tile, tile)
-
-
-def forces_kernel(
-    place_ref, pick_ref, force_ref, shapes_ref, low_ref, high_ref, all_ref, part_ref, rim_scr, got_scr
-):
-    dims, nodes, _ = shapes_ref.shape
+    mate, far = place_ref[1], place_ref[2]
+    place_modes(freq_ref, rate_ref, row_scr, col_scr, (mate, far), 0, block)
+    for q, side_ref in enumerate((own_side_ref, col_scr)):
+        rows = far_ref.at[q * block : (q + 1) * block, :]
+        for j in range(4):
+            fill_rho(row_scr, side_ref, rows, j * tile, 0, block, 8, j * tile, tile)
+
+
+def forces_kernel(at, dims, place_ref, rim_ref, low_ref, high_ref, local_ref, all_ref, part_ref, rim_scr):
     comps, chunk = all_ref.shape
     width = low_ref.shape[0] // dims
-    taken = pick_ref.shape[0]
     part = comps // 2
     other = place_ref[5]
-    for d in range(dims):
-        rim_scr[d, :width, :] = low_ref[d * width : (d + 1) * width, :]
-        rim_scr[d, width:, :] = high_ref[d * width : (d + 1) * width, :]
-    wide = 256
-    for c in range(0, chunk, wide):
+    lanes = slice(at, at + chunk)
+    for copy in range(2):
         for d in range(dims):
-            got = jnp.dot(
-                pick_ref[:, :nodes], shapes_ref[d, :, c : c + wide], preferred_element_type=F32
-            )
-            got = got + jnp.dot(
-                pick_ref[:, nodes:], rim_scr[d, :, c : c + wide], preferred_element_type=F32
-            )
-            got_scr[d * taken : (d + 1) * taken, c : c + wide] = got.astype(BF16)
-        total = jnp.dot(force_ref[...], got_scr[:, c : c + wide], preferred_element_type=F32)
-        all_ref[:, c : c + wide] = total.astype(BF16)
+            base = (copy * dims + d) * 2 * width
+            rim_scr[base : base + width, :] = low_ref[d * width : (d + 1) * width, lanes]
+            rim_scr[base + width : base + 2 * width, :] = high_ref[d * width : (d + 1) * width, lanes]
+    for c in range(0, chunk, 256):
+        total = jnp.dot(rim_ref[...], rim_scr[:, c : c + 256], preferred_element_type=F32)
+        all_ref[:, c : c + 256] = (local_ref[:, at + c : at + c + 256] + total).astype(BF16)
     part_ref[...] = all_ref[pl.ds(pl.multiple_of(other * part, part), part), :]
 
 
@@ -363,7 +377,7 @@
         out_ref[...] = to_row(acc, turned, per_elem)
 
 
-CHUNKS = 1
+CHUNKS = 2
 
 
 def four_groups(*args):
@@ -391,42 +405,43 @@
     freq = frequencies.reshape(1, -1)
     rate = damping.reshape(1, -1)
 
-    def gathered(c, after):
-        return call(
-            functools.partial(gather_kernel, c * chunk),
-            (sds((dims * width, chunk), BF16), sds((dims * width, chunk), BF16), sds((dims, nodes, chunk), BF16)),
-            (shared, shapes), 2.0 / CHUNKS, hbm=(1,), vmem=60 << 20,
-            scratch=[pltpu.SemaphoreType.DMA], after=after,
-        )
-
-    halos, held = [], []
-    after = ()
-    for c in range(CHUNKS):
-        up, down, kept = gathered(c, after)
-        held.append(kept)
-        after = (up,)
-        halos.append((lax.ppermute(up, "dom", ahead), lax.ppermute(down, "dom", back)))
-
+    up, down = call(
+        gather_kernel, [sds((dims * width, block), BF16)] * 2, (shared, shapes), 2.0, hbm=(0, 1),
+        scratch=[
+            pltpu.VMEM(shared.shape, jnp.int32), pltpu.VMEM(shapes.shape, BF16),
+            pltpu.SemaphoreType.DMA((dims + 1,)),
+        ],
+        vmem=60 << 20,
+    )
+    low, high = lax.ppermute(up, "dom", ahead), lax.ppermute(down, "dom", back)
     stats = call(
-        functools.partial(stats_kernel, CHUNKS), sds((dims + 1, block), F32), (masses.reshape(1, nodes), *held), 0.8,
-        scratch=[pltpu.VMEM((nodes, 128), F32)],
-    )
-    rho_diag, rho_mate = call(
+        stats_kernel, sds((dims + 1, block), F32), (masses.reshape(1, nodes), shapes), 1.5, hbm=(1,),
+        scratch=[
+            pltpu.VMEM((nodes, 128), F32), pltpu.VMEM((8, block), F32),
+            pltpu.VMEM(shapes.shape, BF16), pltpu.SemaphoreType.DMA((dims,)),
+        ],
+        vmem=60 << 20, after=(up,),
+    )
+    taken = slots * elems
+    local, rim = call(
+        local_kernel, (sds((comps, block), F32), sds((comps, 4 * dims * width), BF16)),
+        (connectivity.T, node_count.reshape(1, elems), recovery.transpose(1, 3, 2, 0), shapes),
+        2.3,
+        scratch=[
+            pltpu.VMEM((taken, nodes + 2 * width), BF16), pltpu.VMEM((comps, dims * taken), BF16),
+            pltpu.VMEM((dims * taken, block), BF16),
+        ],
+    )
+    rho_diag, rho_mate, sides = call(
         rho_near_kernel,
-        (sds((block, block), F32), sds((2, block // 2, block // 2), F32)),
+        (sds((block, block), F32), sds((2, block // 2, block // 2), F32), sds((4, block, 128), F32)),
         (place, freq, rate), 3.0, smem=(0,),
-        scratch=[pltpu.VMEM((4, block, 128), F32), pltpu.VMEM((16, block), F32)], after=(stats,),
-    )
-    pick, force = call(
-        table_kernel, (sds((slots * elems, nodes + 2 * width), BF16), sds((comps, dims * slots * elems), BF16)),
-        (connectivity.T, node_count.reshape(1, elems), recovery.transpose(1, 3, 2, 0)),
-        0.5, after=(rho_diag,),
+        scratch=[pltpu.VMEM((16, block), F32)], after=(rim,),
     )
     rho_far = call(
-        rho_far_kernel, sds((2 * block, block), F32), (place, freq, rate),
-        5.0, smem=(0,),
-        scratch=[pltpu.VMEM((4, 2 * block, 128), F32), pltpu.VMEM((24, block), F32)],
-        after=(rho_diag,),
+        rho_far_kernel, sds((2 * block, block), F32), (place, freq, rate, sides),
+        4.5, smem=(0,),
+        scratch=[pltpu.VMEM((4, block, 128), F32), pltpu.VMEM((16, block), F32)],
     )
     given = [stats] + [lax.ppermute(stats, "mode", [(i, i ^ q) for i in range(4)]) for q in (1, 2)]
     stats = call(join_kernel, sds((3 * (dims + 1), block), F32), given, 0.5)
@@ -450,14 +465,10 @@
     own, mate, far = [], [], []
     for c in range(CHUNKS):
         forces, sent = call(
-            forces_kernel,
+            functools.partial(forces_kernel, c * chunk, dims),
             (sds((comps, chunk), BF16), sds((part, chunk), BF16)),
-            (place, pick, force, held[c]) + halos[c],
-            2.6 / CHUNKS, smem=(0,),
-            scratch=[
-                pltpu.VMEM((dims, 2 * width, chunk), BF16), pltpu.VMEM((dims * slots * elems, chunk), BF16)
-            ],
-            after=(first,),
+            (place, rim, low, high, local), 1.4 / CHUNKS, smem=(0,),
+            scratch=[pltpu.VMEM((4 * dims * width, chunk), BF16)], after=(own[-1] if own else first,),
         )
         own.append(forces)
         far.append(lax.ppermute(sent, "mode", [(i, i ^ 2) for i in range(4)]))

time: 67.7 us -> 66 us (0.975)
  waiting for transfers between devices: 24.1 us -> 19.7 us
  Pallas kernels: 23 us -> 26.1 us
    ppermute x3, waiting for transfers between devices: 11.3 us -> 6.94 us  [combined(): extra = lax.ppermute(stats, 'dom', [(i, i ^ reach) for i in range(parts)])]
    pallas_call x13 -> x15, Pallas kernels: 23 us -> 26.1 us  [call(): pl.pallas_call(body, out_shape=out_shape, in_specs=specs, out_specs=[VMEM...]
    ppermute x3, starting transfers between devices: 8.83 us -> 6.49 us  [combined(): extra = lax.ppermute(stats, 'dom', [(i, i ^ reach) for i in range(parts)])]
    ppermute x1, waiting for transfers between devices: 1.96 us -> 0.01 us  [combined(): lax.ppermute(up, 'dom', ahead)]
    ppermute x1 -> x2, waiting for transfers between devices: 6.59 us -> 8.45 us  [combined(): far.append(lax.ppermute(sent, 'mode', [(i, i ^ 2) for i in range(4)]))]
    ppermute x1 -> x2, starting transfers between devices: 0.57 us -> 2.09 us  [combined(): far.append(lax.ppermute(sent, 'mode', [(i, i ^ 2) for i in range(4)]))]
    unnamed x18 -> x16, local copies, waits for them, and re-layouts: 1.44 us -> 1.44 us
  transfers between devices with their start and end apart: 11 -> 13, of which waited for: 6 -> 5; matrix products, arithmetic and copies ran while one was open for 0% -> 0% of each run, Pallas kernels for 20% -> 29%
where the time goes in v7:
time: 66 us; the launch traced here: 65.6 us
  Pallas kernels  26.1 us (40%)
  waiting for transfers between devices  19.7 us (30%)
  starting transfers between devices  17.5 us (27%)
  local copies, waits for them, and re-layouts  1.52 us (2%)
    pallas_call x15, Pallas kernels, call(): pl.pallas_call(body, out_shape=out_shape, in_specs=specs, out_specs=[VMEM...  26.1 us
    ppermute x2, waiting for transfers between devices, combined(): far.append(lax.ppermute(sent, 'mode', [(i, i ^ 2) for i in range(4)]))  8.45 us
    ppermute x3, waiting for transfers between devices, combined(): extra = lax.ppermute(stats, 'dom', [(i, i ^ reach) for i in range(parts)])  6.94 us
    ppermute x3, starting transfers between devices, combined(): extra = lax.ppermute(stats, 'dom', [(i, i ^ reach) for i in range(parts)])  6.49 us
    ppermute x2, waiting for transfers between devices, combined(): lax.ppermute(value, 'mode', [(i, i ^ reach) for i in range(4)])  4.25 us
    ppermute x1, starting transfers between devices, combined(): lax.ppermute(up, 'dom', ahead)  3.41 us
    ppermute x2, starting transfers between devices, combined(): lax.ppermute(stats, 'mode', [(i, i ^ q) for i in range(4)])  3.06 us
    ppermute x2, starting transfers between devices, combined(): far.append(lax.ppermute(sent, 'mode', [(i, i ^ 2) for i in range(4)]))  2.09 us
  transfers between devices with their start and end apart: 13, of which 5 were waited for; matrix products, arithmetic and copies ran while one was open for 0% of the time, Pallas kernels for 29%

profile of v7, /device:TPU:0, one launch (start us, length us, event | category | flops | bytes accessed | tf_op | source)
XLA Modules:
  0.0 65.6 jit_solution(13151932083343808366)
XLA Ops:
  0.0 2.7 %shard_map.91 = (bf16[192,1024]{1,0:T(8,128)(2,1)}, bf16[192,1024]{1,0:T(8,128)(2,1)}) custom-call(s32[2,64]{1,0:T(2,128)} %refs_0_.1, bf16[3,256,1024]{2,1,0:T(8,128)(2,1)} %refs_3_.2), custom_call_target="tpu_custom_call" | custom-call | flops 2200000000 | tf_op jit(solution)/shard_map/pallas_call | solution.py:27
  2.7 0.0 copy-start.2
  2.7 0.0 copy-start.6
  2.7 0.0 copy-start.7
  2.7 2.9 %shard_map.92.refs_0_ = f32[4,1024]{1,0:T(4,128)} custom-call(f32[1,256]{1,0:T(1,128)} %bitcast.24, bf16[3,256,1024]{2,1,0:T(8,128)(2,1)} %refs_3_.2, bf16[192,1024]{1,0:T(8,128)(2,1)} %get-tuple-element.19.refs_2_), custom_call_target="tpu_custom_call" | custom-call | flops 1650000000 | tf_op jit(solution)/shard_map/pallas_call | solution.py:27
  5.6 3.1 %collective-permute-start.1 = (f32[4,1024]{1,0:T(4,128)}, f32[4,1024]{1,0:T(4,128)S(1)}, u32[]{:S(2)}, u32[]{:S(2)}) collective-permute-start(f32[4,1024]{1,0:T(4,128)} %shard_map.92.refs_0_), channel_id=1, source_target_pairs={{0,2},{1,3},{2,0},{3,1},{4,6},{5,7},{6,4},{7,5},{8,10},{9,11},{10,... | collective-permute-start | bytes 49160 | tf_op jit(solution)/shard_map/ppermute | solution.py:446
  8.7 0.0 collective-permute-start
  8.7 3.4 %collective-permute-start.5 = (bf16[192,1024]{1,0:T(8,128)(2,1)}, bf16[192,1024]{1,0:T(8,128)(2,1)S(1)}, u32[]{:S(2)}, u32[]{:S(2)}) collective-permute-start(bf16[192,1024]{1,0:T(8,128)(2,1)} %get-tuple-element.19.refs_2_), channel_id=1, source_target_pairs={{0,4},{4,8},{8,12},{12,16},{16,20},{20,24},{24,28},{1,5},{5,9},{9,... | collective-permute-start | bytes 1179656 | tf_op jit(solution)/shard_map/ppermute | solution.py:416
  12.1 1.3 %collective-permute-start.6 = (bf16[192,1024]{1,0:T(8,128)(2,1)}, bf16[192,1024]{1,0:T(8,128)(2,1)}, u32[]{:S(2)}, u32[]{:S(2)}) collective-permute-start(bf16[192,1024]{1,0:T(8,128)(2,1)} %get-tuple-element.25), channel_id=1, source_target_pairs={{4,0},{8,4},{12,8},{16,12},{20,16},{24,20},{28,24},{5,1},{9,5},{13... | collective-permute-start | bytes 1179656 | tf_op jit(solution)/shard_map/ppermute | solution.py:416
  13.4 0.0 copy-done.2
  13.4 0.0 copy-done.6
  13.4 0.0 copy-done.7
  13.5 0.0 copy-start
  13.5 1.4 %copy-done = bf16[3,256,1024]{2,1,0:T(8,128)(2,1)S(1)} copy-done((bf16[3,256,1024]{2,1,0:T(8,128)(2,1)S(1)}, bf16[3,256,1024]{2,1,0:T(8,128)(2,1)}, u32[]{:S(2)}) %copy-start) | copy-done | bytes 1572888
  14.9 0.0 copy-start.5
  14.9 0.0 copy-start.3
  14.9 0.0 copy-start.4
  14.9 1.8 %shard_map.94 = (f32[512,1024]{1,0:T(8,128)S(1)}, bf16[512,768]{1,0:T(8,128)(2,1)S(1)}) custom-call(s32[4,64]{1,0:T(4,128)S(1)} %bitcast.22, s32[1,64]{1,0:T(1,128)S(1)} %bitcast.23, bf16[8,3,4,64]{3,2,1,0:T(4,128)(2,1)S(1)} %bitcast.15, bf16[3,256,1024]{2,1,0:T(8,128)(2,1)S(1)} %copy-done), custom_call_target="tpu_custom_call" | custom-call | flops 2529999872 | tf_op jit(solution)/shard_map/pallas_call | solution.py:27
  16.7 0.1 stack.27.refs_0_
  16.7 0.0 collective-permute-done.1.refs_2_
  16.7 0.0 collective-permute-done.refs_1_
  16.8 0.0 copy-done.5
  16.8 3.7 %collective-permute-start.2 = (f32[12,1024]{1,0:T(8,128)S(1)}, f32[12,1024]{1,0:T(8,128)S(1)}, u32[]{:S(2)}, u32[]{:S(2)}) collective-permute-start(f32[12,1024]{1,0:T(8,128)S(1)} %shard_map.93.refs_0_), channel_id=1, source_target_pairs={{0,8},{4,12},{8,0},{12,4},{16,24},{20,28},{24,16},{28,20},{1,9},{5... | collective-permute-start | bytes 147464 | tf_op jit(solution)/shard_map/ppermute | solution.py:460
  20.5 0.0 copy-done.3
  20.5 0.0 copy-done.4
  20.5 3.0 %shard_map.95 = (f32[1024,1024]{1,0:T(8,128)S(1)}, f32[2,512,512]{2,1,0:T(8,128)S(1)}, f32[4,1024,128]{2,1,0:T(8,128)S(1)}) custom-call(s32[6]{0:T(128)S(1)} %stack.27.refs_0_, f32[1,4096]{1,0:T(1,128)S(1)} %bitcast.16, f32[1,4096]{1,0:T(1,128)S(1)} %bitcast.19, bf16[512,768]{1,0:T(8,128)(2,1)S(1)} %get-tuple-element.20.refs_3_.refs_1_), custom_call_target="tpu_custom_call" | custom-call | flops 3300000000 | tf_op jit(solution)/shard_map/pallas_call | solution.py:27
  23.4 4.5 %collective-permute-done.2.refs_1_ = f32[12,1024]{1,0:T(8,128)S(1)} collective-permute-done((f32[12,1024]{1,0:T(8,128)S(1)}, f32[12,1024]{1,0:T(8,128)S(1)}, u32[]{:S(2)}, u32[]{:S(2)}) %collective-permute-start.2) | collective-permute-done | bytes 49184 | tf_op jit(solution)/shard_map/ppermute | solution.py:460
  27.9 2.8 %collective-permute-start.3 = (f32[12,1024]{1,0:T(8,128)S(1)}, f32[12,1024]{1,0:T(8,128)S(1)}, u32[]{:S(2)}, u32[]{:S(2)}) collective-permute-start(f32[12,1024]{1,0:T(8,128)S(1)} %shard_map.96.refs_0_.refs_5_), channel_id=1, source_target_pairs={{0,16},{4,20},{8,24},{12,28},{16,0},{20,4},{24,8},{28,12},{1,17},{... | collective-permute-start | bytes 147464 | tf_op jit(solution)/shard_map/ppermute | solution.py:460
  30.7 2.5 %collective-permute-done.3.refs_1_ = f32[12,1024]{1,0:T(8,128)S(1)} collective-permute-done((f32[12,1024]{1,0:T(8,128)S(1)}, f32[12,1024]{1,0:T(8,128)S(1)}, u32[]{:S(2)}, u32[]{:S(2)}) %collective-permute-start.3) | collective-permute-done | bytes 49184 | tf_op jit(solution)/shard_map/ppermute | solution.py:460
  33.1 0.1 collective-permute-start.4
  33.2 0.0 collective-permute-done.6.refs_3_
  33.2 0.0 collective-permute-done.5.refs_2_
  33.2 1.6 %shard_map.99 = (bf16[512,512]{1,0:T(8,128)(2,1)S(1)}, bf16[256,512]{1,0:T(8,128)(2,1)S(1)}) custom-call(s32[6]{0:T(128)S(1)} %stack.27.refs_0_, bf16[512,768]{1,0:T(8,128)(2,1)S(1)} %get-tuple-element.20.refs_3_.refs_1_, bf16[192,1024]{1,0:T(8,128)(2,1)S(1)} %collective-permute-done.5.refs_2_, bf16[192,1024]{1,0:T(8,128)(2,1)} %collective-permute-done.6.refs_3_, ...), custom_call_target="tpu_custom_call" | custom-call | flops 770000000 | tf_op jit(solution)/shard_map/pallas_call | solution.py:27
  34.9 0.1 collective-permute-start.7
  34.9 1.6 %shard_map.100 = (bf16[512,512]{1,0:T(8,128)(2,1)S(1)}, bf16[256,512]{1,0:T(8,128)(2,1)S(1)}) custom-call(s32[6]{0:T(128)S(1)} %stack.27.refs_0_, bf16[512,768]{1,0:T(8,128)(2,1)S(1)} %get-tuple-element.20.refs_3_.refs_1_, bf16[192,1024]{1,0:T(8,128)(2,1)S(1)} %collective-permute-done.5.refs_2_, bf16[192,1024]{1,0:T(8,128)(2,1)} %collective-permute-done.6.refs_3_, ...), custom_call_target="tpu_custom_call" | custom-call | flops 770000000 | tf_op jit(solution)/shard_map/pallas_call | solution.py:27
  36.5 0.6 collective-permute-start.8
  37.1 0.0 copy-start.1
  37.1 4.4 %shard_map.102.refs_3_ = f32[2048,1024]{1,0:T(8,128)S(1)} custom-call(s32[6]{0:T(128)S(1)} %stack.27.refs_0_, f32[1,4096]{1,0:T(1,128)S(1)} %bitcast.17, f32[1,4096]{1,0:T(1,128)S(1)} %bitcast.20, f32[4,1024,128]{2,1,0:T(8,128)S(1)} %get-tuple-element.30.refs_3_), custom_call_target="tpu_custom_call" | custom-call | flops 4950000128 | tf_op jit(solution)/shard_map/pallas_call | solution.py:27
  41.5 0.0 collective-permute-done.4.refs_2_
  41.5 0.0 copy-done.1
  41.5 0.6 shard_map.98
  42.1 1.4 %shard_map.103.refs_2_ = bf16[2048,1024]{1,0:T(8,128)(2,1)S(1)} custom-call(f32[8,1024]{1,0:T(8,128)S(1)} %get-tuple-element.22.refs_1_.refs_0_, f32[8,1024]{1,0:T(8,128)S(1)} %get-tuple-element.23.refs_2_.refs_1_, f32[8,1024]{1,0:T(8,128)S(1)} %get-tuple-element.29.refs_2_, f32[2048,1024]{1,0:T(8,128)S(1)} %shard_map.102.refs_3_), custom_call_target="tpu_custom_call" | custom-call | flops 3630000128 | tf_op jit(solution)/shard_map/pallas_call | solution.py:27
  43.5 0.6 collective-permute-start.10
  44.1 1.5 %collective-permute-start.9 = (bf16[256,512]{1,0:T(8,128)(2,1)S(1)}, bf16[256,512]{1,0:T(8,128)(2,1)S(1)}, u32[]{:S(2)}, u32[]{:S(2)}) collective-permute-start(bf16[256,512]{1,0:T(8,128)(2,1)S(1)} %get-tuple-element.31), channel_id=1, source_target_pairs={{0,2},{1,3},{2,0},{3,1},{4,6},{5,7},{6,4},{7,5},{8,10},{9,11},{10,... | collective-permute-start | bytes 786440 | tf_op jit(solution)/shard_map/ppermute | solution.py:474
  45.6 0.0 collective-permute-done.8.refs_8_.refs_7_
  45.6 0.0 collective-permute-done.7.refs_7_.refs_6_
  45.6 3.4 %shard_map.101.refs_1_ = f32[512,128]{1,0:T(8,128)S(1)} custom-call(s32[6]{0:T(128)S(1)} %stack.27.refs_0_, f32[8,1024]{1,0:T(8,128)S(1)} %get-tuple-element.22.refs_1_.refs_0_, f32[8,1024]{1,0:T(8,128)S(1)} %get-tuple-element.23.refs_2_.refs_1_, f32[1024,1024]{1,0:T(8,128)S(1)} %get-tuple-element.21.refs_2_.refs_3_, ...), custom_call_target="tpu_custom_call" | custom-call | flops 3740000000 | tf_op jit(solution)/shard_map/pallas_call | solution.py:27
  49.0 8.5 %collective-permute-done.9.refs_3_ = bf16[256,512]{1,0:T(8,128)(2,1)S(1)} collective-permute-done((bf16[256,512]{1,0:T(8,128)(2,1)S(1)}, bf16[256,512]{1,0:T(8,128)(2,1)S(1)}, u32[]{:S(2)}, u32[]{:S(2)}) %collective-permute-start.9) | collective-permute-done | bytes 262176 | tf_op jit(solution)/shard_map/ppermute | solution.py:474
  57.4 1.3 %shard_map.104.refs_1_ = f32[512,128]{1,0:T(8,128)S(1)} custom-call(s32[6]{0:T(128)S(1)} %stack.27.refs_0_, f32[512,128]{1,0:T(8,128)S(1)} %shard_map.101.refs_1_, bf16[2048,1024]{1,0:T(8,128)(2,1)S(1)} %shard_map.103.refs_2_, bf16[256,512]{1,0:T(8,128)(2,1)S(1)} %collective-permute-done.9.refs_3_, bf16[512,512]{1,0:T(8,128)(2,1)S(1)} %get-tuple-element.27.refs_5_.refs_4_, ...), custom_call_target="tpu_custom_call" | custom-call | flops 1155000064 | tf_op jit(solution)/shard_map/pallas_call | solution.py:27
  58.7 0.0 collective-permute-done.10.refs_3_
  58.7 1.6 %shard_map.105 = f32[1,512]{1,0:T(1,128)S(1)} custom-call(s32[6]{0:T(128)S(1)} %stack.27.refs_0_, f32[512,128]{1,0:T(8,128)S(1)} %shard_map.104.refs_1_, bf16[2048,1024]{1,0:T(8,128)(2,1)S(1)} %shard_map.103.refs_2_, bf16[256,512]{1,0:T(8,128)(2,1)S(1)} %collective-permute-done.10.refs_3_, bf16[512,512]{1,0:T(8,128)(2,1)S(1)} %get-tuple-element.27.refs_5_.refs_4_, ...), custom_call_target="tpu_custom_call" | custom-call | flops 1155000064 | tf_op jit(solution)/shard_map/pallas_call | solution.py:27
  60.3 0.0 collective-permute-start.11
  60.3 1.2 %collective-permute-done.11 = f32[512]{0:T(512)S(1)} collective-permute-done((f32[512]{0:T(512)S(1)}, f32[512]{0:T(512)S(1)}, u32[]{:S(2)}, u32[]{:S(2)}) %collective-permute-start.11) | collective-permute-done | bytes 2080 | tf_op jit(solution)/shard_map/ppermute | solution.py:498
  61.5 0.5 collective-permute-start.12
  62.0 3.1 %collective-permute-done.12 = f32[512]{0:T(512)S(1)} collective-permute-done((f32[512]{0:T(512)S(1)}, f32[512]{0:T(512)S(1)}, u32[]{:S(2)}, u32[]{:S(2)}) %collective-permute-start.12) | collective-permute-done | bytes 2080 | tf_op jit(solution)/shard_map/ppermute | solution.py:498
  65.1 0.6 add.7
  (4 shorter events, 0.0 us)
Async XLA Ops:
  2.7 10.7 %copy-start.2 = (bf16[64,8,4,3]{0,2,3,1:T(4,128)(2,1)S(1)}, bf16[64,8,4,3]{0,2,3,1:T(4,128)(2,1)}, u32[]{:S(2)}) copy-start(bf16[64,8,4,3]{0,2,3,1:T(4,128)(2,1)} %param.14) | copy-start | bytes 36868
  2.7 10.7 %copy-start.6 = (s32[64,4]{0,1:T(4,128)S(1)}, s32[64,4]{0,1:T(4,128)}, u32[]{:S(2)}) copy-start(s32[64,4]{0,1:T(4,128)} %param.15) | copy-start | bytes 3076
  2.7 10.7 %copy-start.7 = (s32[64]{0:T(128)S(1)}, s32[64]{0:T(128)}, u32[]{:S(2)}) copy-start(s32[64]{0:T(128)} %param.16) | copy-start | bytes 772
  5.6 11.1 %collective-permute-start.1 = (f32[4,1024]{1,0:T(4,128)}, f32[4,1024]{1,0:T(4,128)S(1)}, u32[]{:S(2)}, u32[]{:S(2)}) collective-permute-start(f32[4,1024]{1,0:T(4,128)} %shard_map.92.refs_0_), channel_id=1, source_target_pairs={{0,2},{1,3},{2,0},{3,1},{4,6},{5,7},{6,4},{7,5},{8,10},{9,11},{10,... | collective-permute-start | bytes 49160 | tf_op jit(solution)/shard_map/ppermute | solution.py:446
  8.7 8.0 %collective-permute-start = (f32[4,1024]{1,0:T(4,128)}, f32[4,1024]{1,0:T(4,128)S(1)}, u32[]{:S(2)}, u32[]{:S(2)}) collective-permute-start(f32[4,1024]{1,0:T(4,128)} %shard_map.92.refs_0_), channel_id=1, source_target_pairs={{0,1},{1,0},{2,3},{3,2},{4,5},{5,4},{6,7},{7,6},{8,9},{9,8},{10,11... | collective-permute-start | bytes 49160 | tf_op jit(solution)/shard_map/ppermute | solution.py:446
  8.7 24.5 %collective-permute-start.5 = (bf16[192,1024]{1,0:T(8,128)(2,1)}, bf16[192,1024]{1,0:T(8,128)(2,1)S(1)}, u32[]{:S(2)}, u32[]{:S(2)}) collective-permute-start(bf16[192,1024]{1,0:T(8,128)(2,1)} %get-tuple-element.19.refs_2_), channel_id=1, source_target_pairs={{0,4},{4,8},{8,12},{12,16},{16,20},{20,24},{24,28},{1,5},{5,9},{9,... | collective-permute-start | bytes 1179656 | tf_op jit(solution)/shard_map/ppermute | solution.py:416
  12.1 21.1 %collective-permute-start.6 = (bf16[192,1024]{1,0:T(8,128)(2,1)}, bf16[192,1024]{1,0:T(8,128)(2,1)}, u32[]{:S(2)}, u32[]{:S(2)}) collective-permute-start(bf16[192,1024]{1,0:T(8,128)(2,1)} %get-tuple-element.25), channel_id=1, source_target_pairs={{4,0},{8,4},{12,8},{16,12},{20,16},{24,20},{28,24},{5,1},{9,5},{13... | collective-permute-start | bytes 1179656 | tf_op jit(solution)/shard_map/ppermute | solution.py:416
  13.5 1.4 %copy-start = (bf16[3,256,1024]{2,1,0:T(8,128)(2,1)S(1)}, bf16[3,256,1024]{2,1,0:T(8,128)(2,1)}, u32[]{:S(2)}) copy-start(bf16[3,256,1024]{2,1,0:T(8,128)(2,1)} %refs_3_.2) | copy-start | bytes 4718596
  14.9 1.9 %copy-start.5 = (f32[4,1024]{1,0:T(4,128)S(1)}, f32[4,1024]{1,0:T(4,128)}, u32[]{:S(2)}) copy-start(f32[4,1024]{1,0:T(4,128)} %shard_map.92.refs_0_) | copy-start | bytes 49156
  14.9 5.6 %copy-start.3 = (f32[4096]{0:T(1024)S(1)}, f32[4096]{0:T(1024)}, u32[]{:S(2)}) copy-start(f32[4096]{0:T(1024)} %param.12) | copy-start | bytes 49156
  14.9 5.6 %copy-start.4 = (f32[4096]{0:T(1024)S(1)}, f32[4096]{0:T(1024)}, u32[]{:S(2)}) copy-start(f32[4096]{0:T(1024)} %param.13) | copy-start | bytes 49156
  16.8 11.1 %collective-permute-start.2 = (f32[12,1024]{1,0:T(8,128)S(1)}, f32[12,1024]{1,0:T(8,128)S(1)}, u32[]{:S(2)}, u32[]{:S(2)}) collective-permute-start(f32[12,1024]{1,0:T(8,128)S(1)} %shard_map.93.refs_0_), channel_id=1, source_target_pairs={{0,8},{4,12},{8,0},{12,4},{16,24},{20,28},{24,16},{28,20},{1,9},{5... | collective-permute-start | bytes 147464 | tf_op jit(solution)/shard_map/ppermute | solution.py:460
  27.9 5.2 %collective-permute-start.3 = (f32[12,1024]{1,0:T(8,128)S(1)}, f32[12,1024]{1,0:T(8,128)S(1)}, u32[]{:S(2)}, u32[]{:S(2)}) collective-permute-start(f32[12,1024]{1,0:T(8,128)S(1)} %shard_map.96.refs_0_.refs_5_), channel_id=1, source_target_pairs={{0,16},{4,20},{8,24},{12,28},{16,0},{20,4},{24,8},{28,12},{1,17},{... | collective-permute-start | bytes 147464 | tf_op jit(solution)/shard_map/ppermute | solution.py:460
  33.1 8.3 %collective-permute-start.4 = (f32[12,1024]{1,0:T(8,128)S(1)}, f32[12,1024]{1,0:T(8,128)S(1)}, u32[]{:S(2)}, u32[]{:S(2)}) collective-permute-start(f32[12,1024]{1,0:T(8,128)S(1)} %shard_map.97.refs_1_), channel_id=1, source_target_pairs={{0,4},{4,0},{8,12},{12,8},{16,20},{20,16},{24,28},{28,24},{1,5},{5... | collective-permute-start | bytes 147464 | tf_op jit(solution)/shard_map/ppermute | solution.py:460
  34.9 10.7 %collective-permute-start.7 = (bf16[512,512]{1,0:T(8,128)(2,1)S(1)}, bf16[512,512]{1,0:T(8,128)(2,1)S(1)}, u32[]{:S(2)}, u32[]{:S(2)}) collective-permute-start(bf16[512,512]{1,0:T(8,128)(2,1)S(1)} %get-tuple-element.27.refs_5_.refs_4_), channel_id=1, source_target_pairs={{0,1},{1,0},{2,3},{3,2},{4,5},{5,4},{6,7},{7,6},{8,9},{9,8},{10,11... | collective-permute-start | bytes 1572872 | tf_op jit(solution)/shard_map/ppermute | solution.py:475
  36.5 9.0 %collective-permute-start.8 = (bf16[512,512]{1,0:T(8,128)(2,1)S(1)}, bf16[512,512]{1,0:T(8,128)(2,1)S(1)}, u32[]{:S(2)}, u32[]{:S(2)}) collective-permute-start(bf16[512,512]{1,0:T(8,128)(2,1)S(1)} %get-tuple-element.28.refs_6_.refs_5_), channel_id=1, source_target_pairs={{0,1},{1,0},{2,3},{3,2},{4,5},{5,4},{6,7},{7,6},{8,9},{9,8},{10,11... | collective-permute-start | bytes 1572872 | tf_op jit(solution)/shard_map/ppermute | solution.py:475
  37.1 4.4 %copy-start.1 = (f32[3,4096]{1,0:T(4,128)S(1)}, f32[3,4096]{1,0:T(4,128)}, u32[]{:S(2)}) copy-start(f32[3,4096]{1,0:T(4,128)} %refs_3_.3) | copy-start | bytes 147460
  43.5 15.2 %collective-permute-start.10 = (bf16[256,512]{1,0:T(8,128)(2,1)S(1)}, bf16[256,512]{1,0:T(8,128)(2,1)S(1)}, u32[]{:S(2)}, u32[]{:S(2)}) collective-permute-start(bf16[256,512]{1,0:T(8,128)(2,1)S(1)} %get-tuple-element.32), channel_id=1, source_target_pairs={{0,2},{1,3},{2,0},{3,1},{4,6},{5,7},{6,4},{7,5},{8,10},{9,11},{10,... | collective-permute-start | bytes 786440 | tf_op jit(solution)/shard_map/ppermute | solution.py:474
  44.1 13.4 %collective-permute-start.9 = (bf16[256,512]{1,0:T(8,128)(2,1)S(1)}, bf16[256,512]{1,0:T(8,128)(2,1)S(1)}, u32[]{:S(2)}, u32[]{:S(2)}) collective-permute-start(bf16[256,512]{1,0:T(8,128)(2,1)S(1)} %get-tuple-element.31), channel_id=1, source_target_pairs={{0,2},{1,3},{2,0},{3,1},{4,6},{5,7},{6,4},{7,5},{8,10},{9,11},{10,... | collective-permute-start | bytes 786440 | tf_op jit(solution)/shard_map/ppermute | solution.py:474
  60.3 1.2 %collective-permute-start.11 = (f32[512]{0:T(512)S(1)}, f32[512]{0:T(512)S(1)}, u32[]{:S(2)}, u32[]{:S(2)}) collective-permute-start(f32[512]{0:T(512)S(1)} %bitcast.13), channel_id=1, source_target_pairs={{0,1},{1,0},{2,3},{3,2},{4,5},{5,4},{6,7},{7,6},{8,9},{9,8},{10,11... | collective-permute-start | bytes 6152 | tf_op jit(solution)/shard_map/ppermute | solution.py:498
  61.5 3.6 %collective-permute-start.12 = (f32[512]{0:T(512)S(1)}, f32[512]{0:T(512)S(1)}, u32[]{:S(2)}, u32[]{:S(2)}) collective-permute-start(f32[512]{0:T(512)S(1)} %add.6), channel_id=1, source_target_pairs={{0,2},{1,3},{2,0},{3,1},{4,6},{5,7},{6,4},{7,5},{8,10},{9,11},{10,... | collective-permute-start | bytes 6152 | tf_op jit(solution)/shard_map/ppermute | solution.py:498

commit v8 on v7

--- a/solution.py
+++ b/solution.py
@@ -39,47 +39,38 @@
     out_ref[...] = left_ref[...] + right_ref[...]
 
 
-def gather_kernel(shared_ref, shapes_ref, up_ref, down_ref, ids, buf, sems):
-    dims, nodes, _ = buf.shape
+def gather_kernel(shared_ref, shapes_ref, up_ref, down_ref, held_ref, sem):
+    dims, nodes, _ = held_ref.shape
     width = shared_ref.shape[1]
-    listed = pltpu.make_async_copy(shared_ref, ids, sems.at[dims])
-    listed.start()
-    loads = [pltpu.make_async_copy(shapes_ref.at[d], buf.at[d], sems.at[d]) for d in range(dims)]
-    for load in loads:
-        load.start()
-    listed.wait()
+    load = pltpu.make_async_copy(shapes_ref, held_ref, sem)
+    load.start()
     node = lax.broadcasted_iota(jnp.int32, (nodes, 2 * width), 0)
-    wanted = jnp.concatenate([ids[1:2, :], ids[0:1, :]], axis=1)
+    wanted = jnp.concatenate([shared_ref[1:2, :], shared_ref[0:1, :]], axis=1)
     pick = jnp.where(node == wanted, 1.0, 0.0).astype(F32).T.astype(BF16)
+    load.wait()
     for d in range(dims):
-        loads[d].wait()
-        got = jnp.dot(pick, buf[d], preferred_element_type=F32).astype(BF16)
+        got = jnp.dot(pick, held_ref[d], preferred_element_type=F32).astype(BF16)
         up_ref[d * width : (d + 1) * width, :] = got[:width]
         down_ref[d * width : (d + 1) * width, :] = got[width:]
 
 
-def stats_kernel(mass_ref, shapes_ref, out_ref, mass_scr, total_scr, buf, sems):
-    dims, nodes, block = buf.shape
-    loads = [pltpu.make_async_copy(shapes_ref.at[d], buf.at[d], sems.at[d]) for d in range(dims)]
-    for load in loads:
-        load.start()
+def stats_kernel(mass_ref, shapes_ref, out_ref, mass_scr):
+    dims, nodes, block = shapes_ref.shape
     column = jnp.broadcast_to(mass_ref[...], (8, nodes)).T
     mass_scr[...] = jnp.broadcast_to(column[:, 0:1], (nodes, 128))
-    for d in range(dims):
-        loads[d].wait()
-        for at in range(0, block, 128):
-            lanes = slice(at, at + 128)
+    for at in range(0, block, 128):
+        lanes = slice(at, at + 128)
+        general = jnp.zeros((8, 128), F32)
+        for d in range(dims):
             lever = jnp.zeros((8, 128), F32)
-            general = jnp.zeros((8, 128), F32) if d == 0 else total_scr[:, lanes]
             for r in range(0, nodes, 16):
-                wide = buf[d, r : r + 16, lanes].astype(F32)
+                wide = shapes_ref[d, r : r + 16, lanes].astype(F32)
                 weighted = wide * mass_scr[r : r + 16, :]
                 square = weighted * wide
                 lever += weighted[:8] + weighted[8:]
                 general += square[:8] + square[8:]
             out_ref[d : d + 1, lanes] = jnp.sum(lever, axis=0, keepdims=True)
-            total_scr[:, lanes] = general
-    out_ref[dims : dims + 1, :] = jnp.sum(total_scr[...], axis=0, keepdims=True)
+        out_ref[dims : dims + 1, lanes] = jnp.sum(general, axis=0, keepdims=True)
 
 
 def local_kernel(codes_ref, count_ref, recovery_ref, shapes_ref, local_ref, rim_ref, pick_ref, force_ref, got_scr):
@@ -145,6 +136,8 @@
         row_scr[which * 8 : which * 8 + 8, :] = rows
         if which == side:
             side_rows.append(rows)
+    if side is None:
+        return
     turned = turn_rows(jnp.concatenate(side_rows, axis=1))
     for t in range(block // 128):
         for q in range(4):
@@ -188,15 +181,20 @@
             fill_rho(row_scr, col_scr, mate_ref.at[i], j * tile, i * half, half, 8, off, tile)
 
 
-def rho_far_kernel(place_ref, freq_ref, rate_ref, own_side_ref, far_ref, col_scr, row_scr):
-    block = far_ref.shape[1]
+def rho_own_kernel(place_ref, freq_ref, rate_ref, side_ref, out_ref, row_scr):
+    block = out_ref.shape[0]
     tile = block // 4
-    mate, far = place_ref[1], place_ref[2]
-    place_modes(freq_ref, rate_ref, row_scr, col_scr, (mate, far), 0, block)
-    for q, side_ref in enumerate((own_side_ref, col_scr)):
-        rows = far_ref.at[q * block : (q + 1) * block, :]
-        for j in range(4):
-            fill_rho(row_scr, side_ref, rows, j * tile, 0, block, 8, j * tile, tile)
+    place_modes(freq_ref, rate_ref, row_scr, None, (place_ref[2],), None, block)
+    for j in range(4):
+        fill_rho(row_scr, side_ref, out_ref, j * tile, 0, block, 0, j * tile, tile)
+
+
+def rho_mate_kernel(place_ref, freq_ref, rate_ref, out_ref, col_scr, row_scr):
+    block = out_ref.shape[0]
+    tile = block // 4
+    place_modes(freq_ref, rate_ref, row_scr, col_scr, (place_ref[1], place_ref[2]), 0, block)
+    for j in range(4):
+        fill_rho(row_scr, col_scr, out_ref, j * tile, 0, block, 8, j * tile, tile)
 
 
 def forces_kernel(at, dims, place_ref, rim_ref, low_ref, high_ref, local_ref, all_ref, part_ref, rim_scr):
@@ -334,17 +332,19 @@
             turn = 1 - turn
 
 
-def weights_kernel(dims, own_amps_ref, mate_amps_ref, far_amps_ref, rho_ref, out_ref, side_scr):
-    block = rho_ref.shape[1]
+def weights_kernel(dims, own_amps_ref, mate_amps_ref, far_amps_ref, own_ref, mate_ref, out_ref, side_scr):
+    block = own_ref.shape[1]
     tile = block // 4
-    side_terms(side_scr, 0, own_amps_ref[...], dims)
-    side_terms(side_scr, block, mate_amps_ref[...], dims)
     cols = col_terms(far_amps_ref[...], dims, 2.0)
-    for at in range(0, 2 * block, tile):
-        rows = slice(at, at + tile)
-        for c in range(0, block, tile):
-            spot = slice(c, c + tile)
-            out_ref[rows, spot] = weigh(rho_ref[rows, spot], side_scr[rows, :], cols[:, spot])
+    for q, (amps_ref, rho_ref) in enumerate(((own_amps_ref, own_ref), (mate_amps_ref, mate_ref))):
+        side_terms(side_scr, q * block, amps_ref[...], dims)
+        for at in range(0, block, tile):
+            base = q * block + at
+            for c in range(0, block, tile):
+                spot = slice(c, c + tile)
+                out_ref[base : base + tile, spot] = weigh(
+                    rho_ref[at : at + tile, spot], side_scr[base : base + tile, :], cols[:, spot]
+                )
 
 
 def far_kernel(at, chunks, per_elem, place_ref, near_ref, w_ref, far_ref, *refs):
@@ -377,7 +377,7 @@
         out_ref[...] = to_row(acc, turned, per_elem)
 
 
-CHUNKS = 2
+CHUNKS = 1
 
 
 def four_groups(*args):
@@ -405,42 +405,37 @@
     freq = frequencies.reshape(1, -1)
     rate = damping.reshape(1, -1)
 
-    up, down = call(
-        gather_kernel, [sds((dims * width, block), BF16)] * 2, (shared, shapes), 2.0, hbm=(0, 1),
-        scratch=[
-            pltpu.VMEM(shared.shape, jnp.int32), pltpu.VMEM(shapes.shape, BF16),
-            pltpu.SemaphoreType.DMA((dims + 1,)),
-        ],
-        vmem=60 << 20,
+    up, down, held = call(
+        gather_kernel, [sds((dims * width, block), BF16)] * 2 + [sds(shapes.shape, BF16)], (shared, shapes),
+        2.0, hbm=(1,), scratch=[pltpu.SemaphoreType.DMA],
     )
     low, high = lax.ppermute(up, "dom", ahead), lax.ppermute(down, "dom", back)
     stats = call(
-        stats_kernel, sds((dims + 1, block), F32), (masses.reshape(1, nodes), shapes), 1.5, hbm=(1,),
-        scratch=[
-            pltpu.VMEM((nodes, 128), F32), pltpu.VMEM((8, block), F32),
-            pltpu.VMEM(shapes.shape, BF16), pltpu.SemaphoreType.DMA((dims,)),
-        ],
-        vmem=60 << 20, after=(up,),
+        stats_kernel, sds((dims + 1, block), F32), (masses.reshape(1, nodes), held), 0.8,
+        scratch=[pltpu.VMEM((nodes, 128), F32)],
+    )
+    rho_diag, rho_mate, sides = call(
+        rho_near_kernel,
+        (sds((block, block), F32), sds((2, block // 2, block // 2), F32), sds((4, block, 128), F32)),
+        (place, freq, rate), 3.0, smem=(0,),
+        scratch=[pltpu.VMEM((16, block), F32)], after=(stats,),
+    )
+    far_own = call(
+        rho_own_kernel, sds((block, block), F32), (place, freq, rate, sides), 1.9, smem=(0,),
+        scratch=[pltpu.VMEM((8, block), F32)],
     )
     taken = slots * elems
     local, rim = call(
         local_kernel, (sds((comps, block), F32), sds((comps, 4 * dims * width), BF16)),
-        (connectivity.T, node_count.reshape(1, elems), recovery.transpose(1, 3, 2, 0), shapes),
-        2.3,
+        (connectivity.T, node_count.reshape(1, elems), recovery.transpose(1, 3, 2, 0), held),
+        1.8, after=(far_own,),
         scratch=[
             pltpu.VMEM((taken, nodes + 2 * width), BF16), pltpu.VMEM((comps, dims * taken), BF16),
             pltpu.VMEM((dims * taken, block), BF16),
         ],
     )
-    rho_diag, rho_mate, sides = call(
-        rho_near_kernel,
-        (sds((block, block), F32), sds((2, block // 2, block // 2), F32), sds((4, block, 128), F32)),
-        (place, freq, rate), 3.0, smem=(0,),
-        scratch=[pltpu.VMEM((16, block), F32)], after=(rim,),
-    )
-    rho_far = call(
-        rho_far_kernel, sds((2 * block, block), F32), (place, freq, rate, sides),
-        4.5, smem=(0,),
+    far_mate = call(
+        rho_mate_kernel, sds((block, block), F32), (place, freq, rate), 2.5, smem=(0,),
         scratch=[pltpu.VMEM((4, block, 128), F32), pltpu.VMEM((16, block), F32)],
     )
     given = [stats] + [lax.ppermute(stats, "mode", [(i, i ^ q) for i in range(4)]) for q in (1, 2)]
@@ -454,7 +449,7 @@
     for q, reach in enumerate(order):
         if q:
             stats = call(
-                add_kernel, sds(stats.shape, F32), (stats, extra), 0.5, after=(rho_diag,) if q == 1 else ()
+                add_kernel, sds(stats.shape, F32), (stats, extra), 0.5, after=(rim,) if q == 1 else ()
             )
             first = stats if q == 1 else first
         extra = lax.ppermute(stats, "dom", [(i, i ^ reach) for i in range(parts)])
@@ -481,7 +476,7 @@
     )
     weights = call(
         functools.partial(weights_kernel, dims), sds((2 * block, block), BF16),
-        (amps, mate_amps, far_amps, rho_far), 3.3,
+        (amps, mate_amps, far_amps, far_own, far_mate), 1.4,
         scratch=[pltpu.VMEM((2 * block, 32), BF16)],
     )
     value = near

time: 66 us -> 60.9 us (0.923)
  Pallas kernels: 26.1 us -> 20.2 us
  local copies, waits for them, and re-layouts: 1.52 us -> 2.21 us
    pallas_call x15 -> x14, Pallas kernels: 26.1 us -> 20.2 us  [call(): pl.pallas_call(body, out_shape=out_shape, in_specs=specs, out_specs=[VMEM...]
    ppermute x2 -> x1, waiting for transfers between devices: 8.45 us -> 5.79 us  [combined(): far.append(lax.ppermute(sent, 'mode', [(i, i ^ 2) for i in range(4)]))]
    ppermute x3, starting transfers between devices: 6.49 us -> 8.92 us  [combined(): extra = lax.ppermute(stats, 'dom', [(i, i ^ reach) for i in range(parts)])]
    ppermute x1, waiting for transfers between devices: 0.01 us -> 1.86 us  [combined(): lax.ppermute(up, 'dom', ahead)]
    ppermute x2 -> x1, starting transfers between devices: 2.09 us -> 0.56 us  [combined(): far.append(lax.ppermute(sent, 'mode', [(i, i ^ 2) for i in range(4)]))]
    unnamed x16 -> x18, local copies, waits for them, and re-layouts: 1.44 us -> 2.13 us
  transfers between devices with their start and end apart: 13 -> 11, of which waited for: 5 -> 7; matrix products, arithmetic and copies ran while one was open for 0% -> 0% of each run, Pallas kernels for 29% -> 25%
where the time goes in v8:
time: 60.9 us; the launch traced here: 60.5 us
  Pallas kernels  20.2 us (33%)
  waiting for transfers between devices  19.4 us (32%)
  starting transfers between devices  17.9 us (29%)
  local copies, waits for them, and re-layouts  2.21 us (4%)
    pallas_call x14, Pallas kernels, call(): pl.pallas_call(body, out_shape=out_shape, in_specs=specs, out_specs=[VMEM...  20.2 us
    ppermute x3, starting transfers between devices, combined(): extra = lax.ppermute(stats, 'dom', [(i, i ^ reach) for i in range(parts)])  8.92 us
    ppermute x3, waiting for transfers between devices, combined(): extra = lax.ppermute(stats, 'dom', [(i, i ^ reach) for i in range(parts)])  7.45 us
    ppermute x1, waiting for transfers between devices, combined(): far.append(lax.ppermute(sent, 'mode', [(i, i ^ 2) for i in range(4)]))  5.79 us
    ppermute x2, waiting for transfers between devices, combined(): lax.ppermute(value, 'mode', [(i, i ^ reach) for i in range(4)])  4.26 us
    ppermute x1, starting transfers between devices, combined(): lax.ppermute(up, 'dom', ahead)  3.4 us
    ppermute x2, starting transfers between devices, combined(): lax.ppermute(stats, 'mode', [(i, i ^ q) for i in range(4)])  3.15 us
    unnamed x18, local copies, waits for them, and re-layouts  2.13 us
  transfers between devices with their start and end apart: 11, of which 7 were waited for; matrix products, arithmetic and copies ran while one was open for 0% of the time, Pallas kernels for 25%

profile of v8, /device:TPU:0, one launch (start us, length us, event | category | flops | bytes accessed | tf_op | source)
XLA Modules:
  0.0 60.5 jit_solution(3533682309248043420)
XLA Ops:
  0.0 0.0 copy-start
  0.0 1.4 %copy-done = bf16[3,256,1024]{2,1,0:T(8,128)(2,1)S(1)} copy-done((bf16[3,256,1024]{2,1,0:T(8,128)(2,1)S(1)}, bf16[3,256,1024]{2,1,0:T(8,128)(2,1)}, u32[]{:S(2)}) %copy-start) | copy-done | bytes 1572888
  1.4 0.0 copy-start.6
  1.4 0.7 %copy-done.6 = s32[2,64]{1,0:T(2,128)S(1)} copy-done((s32[2,64]{1,0:T(2,128)S(1)}, s32[2,64]{1,0:T(2,128)}, u32[]{:S(2)}) %copy-start.6) | copy-done | bytes 536
  2.1 0.0 copy-start.7
  2.1 0.7 %shard_map.91 = (bf16[192,1024]{1,0:T(8,128)(2,1)S(1)}, bf16[192,1024]{1,0:T(8,128)(2,1)S(1)}, bf16[3,256,1024]{2,1,0:T(8,128)(2,1)S(1)}) custom-call(s32[2,64]{1,0:T(2,128)S(1)} %copy-done.6, bf16[3,256,1024]{2,1,0:T(8,128)(2,1)S(1)} %copy-done), custom_call_target="tpu_custom_call" | custom-call | flops 2200000000 | tf_op jit(solution)/shard_map/pallas_call | solution.py:27
  2.8 0.0 copy-start.3
  2.8 0.0 copy-start.4
  2.8 0.0 copy-done.7
  2.8 0.8 %shard_map.92.refs_0_.refs_3_ = f32[4,1024]{1,0:T(4,128)S(1)} custom-call(f32[1,256]{1,0:T(1,128)S(1)} %bitcast.25, bf16[3,256,1024]{2,1,0:T(8,128)(2,1)S(1)} %get-tuple-element.18.refs_1_.refs_3_), custom_call_target="tpu_custom_call" | custom-call | flops 880000000 | tf_op jit(solution)/shard_map/pallas_call | solution.py:27
  3.6 0.6 collective-permute-start
  4.2 2.6 %collective-permute-start.1 = (f32[4,1024]{1,0:T(4,128)S(1)}, f32[4,1024]{1,0:T(4,128)S(1)}, u32[]{:S(2)}, u32[]{:S(2)}) collective-permute-start(f32[4,1024]{1,0:T(4,128)S(1)} %shard_map.92.refs_0_.refs_3_), channel_id=1, source_target_pairs={{0,2},{1,3},{2,0},{3,1},{4,6},{5,7},{6,4},{7,5},{8,10},{9,11},{10,... | collective-permute-start | bytes 49160 | tf_op jit(solution)/shard_map/ppermute | solution.py:441
  6.8 3.4 %collective-permute-start.5 = (bf16[192,1024]{1,0:T(8,128)(2,1)S(1)}, bf16[192,1024]{1,0:T(8,128)(2,1)S(1)}, u32[]{:S(2)}, u32[]{:S(2)}) collective-permute-start(bf16[192,1024]{1,0:T(8,128)(2,1)S(1)} %get-tuple-element.25), channel_id=1, source_target_pairs={{0,4},{4,8},{8,12},{12,16},{16,20},{20,24},{24,28},{1,5},{5,9},{9,... | collective-permute-start | bytes 1179656 | tf_op jit(solution)/shard_map/ppermute | solution.py:412
  10.2 1.3 %collective-permute-start.6 = (bf16[192,1024]{1,0:T(8,128)(2,1)S(1)}, bf16[192,1024]{1,0:T(8,128)(2,1)S(1)}, u32[]{:S(2)}, u32[]{:S(2)}) collective-permute-start(bf16[192,1024]{1,0:T(8,128)(2,1)S(1)} %get-tuple-element.26), channel_id=1, source_target_pairs={{4,0},{8,4},{12,8},{16,12},{20,16},{24,20},{28,24},{5,1},{9,5},{13... | collective-permute-start | bytes 1179656 | tf_op jit(solution)/shard_map/ppermute | solution.py:412
  11.5 0.1 stack.27.refs_0_
  11.6 0.0 copy-done.3
  11.6 0.0 copy-done.4
  11.6 3.0 %shard_map.94 = (f32[1024,1024]{1,0:T(8,128)S(1)}, f32[2,512,512]{2,1,0:T(8,128)S(1)}, f32[4,1024,128]{2,1,0:T(8,128)S(1)}) custom-call(s32[6]{0:T(128)S(1)} %stack.27.refs_0_, f32[1,4096]{1,0:T(1,128)S(1)} %bitcast.16, f32[1,4096]{1,0:T(1,128)S(1)} %bitcast.20, f32[4,1024]{1,0:T(4,128)S(1)} %shard_map.92.refs_0_.refs_3_), custom_call_target="tpu_custom_call" | custom-call | flops 3300000000 | tf_op jit(solution)/shard_map/pallas_call | solution.py:27
  14.6 0.0 copy-start.2
  14.6 0.0 copy-start.5
  14.6 0.0 copy-start.8
  14.6 2.1 %shard_map.95.refs_4_.refs_3_ = f32[1024,1024]{1,0:T(8,128)S(1)} custom-call(s32[6]{0:T(128)S(1)} %stack.27.refs_0_, f32[1,4096]{1,0:T(1,128)S(1)} %bitcast.17, f32[1,4096]{1,0:T(1,128)S(1)} %bitcast.21, f32[4,1024,128]{2,1,0:T(8,128)S(1)} %get-tuple-element.19.refs_3_), custom_call_target="tpu_custom_call" | custom-call | flops 2090000000 | tf_op jit(solution)/shard_map/pallas_call | solution.py:27
  16.7 0.0 collective-permute-done.refs_1_
  16.7 0.0 collective-permute-done.1.refs_2_
  16.7 3.7 %collective-permute-start.2 = (f32[12,1024]{1,0:T(8,128)S(1)}, f32[12,1024]{1,0:T(8,128)S(1)}, u32[]{:S(2)}, u32[]{:S(2)}) collective-permute-start(f32[12,1024]{1,0:T(8,128)S(1)} %shard_map.93.refs_0_), channel_id=1, source_target_pairs={{0,8},{4,12},{8,0},{12,4},{16,24},{20,28},{24,16},{28,20},{1,9},{5... | collective-permute-start | bytes 147464 | tf_op jit(solution)/shard_map/ppermute | solution.py:455
  20.4 0.0 copy-done.2
  20.4 0.0 copy-done.5
  20.4 0.0 copy-done.8
  20.4 1.8 %shard_map.96 = (f32[512,1024]{1,0:T(8,128)S(1)}, bf16[512,768]{1,0:T(8,128)(2,1)S(1)}) custom-call(s32[4,64]{1,0:T(4,128)S(1)} %bitcast.24, s32[1,64]{1,0:T(1,128)S(1)} %bitcast.26, bf16[8,3,4,64]{3,2,1,0:T(4,128)(2,1)S(1)} %bitcast.15, bf16[3,256,1024]{2,1,0:T(8,128)(2,1)S(1)} %get-tuple-element.18.refs_1_.refs_3_, f32[1024,1024]{1,0:T(8,128)S(1)} %shard_map.95.refs_4_.refs_3_), custom_call_target="tpu_custom_call" | custom-call | flops 1980000000 | tf_op jit(solution)/shard_map/pallas_call | solution.py:27
  22.2 3.2 %collective-permute-done.2.refs_1_ = f32[12,1024]{1,0:T(8,128)S(1)} collective-permute-done((f32[12,1024]{1,0:T(8,128)S(1)}, f32[12,1024]{1,0:T(8,128)S(1)}, u32[]{:S(2)}, u32[]{:S(2)}) %collective-permute-start.2) | collective-permute-done | bytes 49184 | tf_op jit(solution)/shard_map/ppermute | solution.py:455
  25.4 1.9 %collective-permute-done.5.refs_2_ = bf16[192,1024]{1,0:T(8,128)(2,1)S(1)} collective-permute-done((bf16[192,1024]{1,0:T(8,128)(2,1)S(1)}, bf16[192,1024]{1,0:T(8,128)(2,1)S(1)}, u32[]{:S(2)}, u32[]{:S(2)}) %collective-permute-start.5) | collective-permute-done | bytes 393248 | tf_op jit(solution)/shard_map/ppermute | solution.py:412
  27.3 0.0 collective-permute-done.6.refs_3_
  27.3 1.6 %shard_map.100 = (bf16[512,1024]{1,0:T(8,128)(2,1)S(1)}, bf16[256,1024]{1,0:T(8,128)(2,1)S(1)}) custom-call(s32[6]{0:T(128)S(1)} %stack.27.refs_0_, bf16[512,768]{1,0:T(8,128)(2,1)S(1)} %get-tuple-element.20.refs_2_.refs_1_, bf16[192,1024]{1,0:T(8,128)(2,1)S(1)} %collective-permute-done.5.refs_2_, bf16[192,1024]{1,0:T(8,128)(2,1)S(1)} %collective-permute-done.6.refs_3_, ...), custom_call_target="tpu_custom_call" | custom-call | flops 1540000000 | tf_op jit(solution)/shard_map/pallas_call | solution.py:27
  28.8 0.1 collective-permute-start.7
  28.9 4.5 %collective-permute-start.3 = (f32[12,1024]{1,0:T(8,128)S(1)}, f32[12,1024]{1,0:T(8,128)S(1)}, u32[]{:S(2)}, u32[]{:S(2)}) collective-permute-start(f32[12,1024]{1,0:T(8,128)S(1)} %shard_map.97.refs_0_.refs_5_), channel_id=1, source_target_pairs={{0,16},{4,20},{8,24},{12,28},{16,0},{20,4},{24,8},{28,12},{1,17},{... | collective-permute-start | bytes 147464 | tf_op jit(solution)/shard_map/ppermute | solution.py:455
  33.5 4.1 %collective-permute-done.3.refs_1_ = f32[12,1024]{1,0:T(8,128)S(1)} collective-permute-done((f32[12,1024]{1,0:T(8,128)S(1)}, f32[12,1024]{1,0:T(8,128)S(1)}, u32[]{:S(2)}, u32[]{:S(2)}) %collective-permute-start.3) | collective-permute-done | bytes 49184 | tf_op jit(solution)/shard_map/ppermute | solution.py:455
  37.6 0.0 copy-start.1
  37.6 0.7 %collective-permute-start.4 = (f32[12,1024]{1,0:T(8,128)S(1)}, f32[12,1024]{1,0:T(8,128)S(1)}, u32[]{:S(2)}, u32[]{:S(2)}) collective-permute-start(f32[12,1024]{1,0:T(8,128)S(1)} %shard_map.98.refs_1_), channel_id=1, source_target_pairs={{0,4},{4,0},{8,12},{12,8},{16,20},{20,16},{24,28},{28,24},{1,5},{5... | collective-permute-start | bytes 147464 | tf_op jit(solution)/shard_map/ppermute | solution.py:455
  38.3 2.9 %shard_map.102.refs_4_ = f32[1024,1024]{1,0:T(8,128)S(1)} custom-call(s32[6]{0:T(128)S(1)} %stack.27.refs_0_, f32[1,4096]{1,0:T(1,128)S(1)} %bitcast.18, f32[1,4096]{1,0:T(1,128)S(1)} %bitcast.22), custom_call_target="tpu_custom_call" | custom-call | flops 2750000128 | tf_op jit(solution)/shard_map/pallas_call | solution.py:27
  41.2 0.6 collective-permute-start.8
  41.7 0.2 collective-permute-done.4.refs_2_
  41.9 0.0 copy-done.1
  41.9 0.6 shard_map.99
  42.5 1.4 %shard_map.103.refs_2_ = bf16[2048,1024]{1,0:T(8,128)(2,1)S(1)} custom-call(f32[8,1024]{1,0:T(8,128)S(1)} %get-tuple-element.21.refs_1_.refs_0_, f32[8,1024]{1,0:T(8,128)S(1)} %get-tuple-element.22.refs_2_.refs_1_, f32[8,1024]{1,0:T(8,128)S(1)} %get-tuple-element.29.refs_2_, f32[1024,1024]{1,0:T(8,128)S(1)} %shard_map.95.refs_4_.refs_3_, ...), custom_call_target="tpu_custom_call" | custom-call | flops 1540000000 | tf_op jit(solution)/shard_map/pallas_call | solution.py:27
  43.9 0.0 collective-permute-done.7.refs_6_.refs_5_
  43.9 3.3 %shard_map.101.refs_1_ = f32[512,128]{1,0:T(8,128)S(1)} custom-call(s32[6]{0:T(128)S(1)} %stack.27.refs_0_, f32[8,1024]{1,0:T(8,128)S(1)} %get-tuple-element.21.refs_1_.refs_0_, f32[8,1024]{1,0:T(8,128)S(1)} %get-tuple-element.22.refs_2_.refs_1_, f32[1024,1024]{1,0:T(8,128)S(1)} %get-tuple-element.23.refs_3_, f32[2,512,512]{2,1,0:T(8,128)S(1)} %get-tuple-element.24.refs_4_, ...), custom_call_target="tpu_custom_call" | custom-call | flops 3740000000 | tf_op jit(solution)/shard_map/pallas_call | solution.py:27
  47.2 5.8 %collective-permute-done.8.refs_3_ = bf16[256,1024]{1,0:T(8,128)(2,1)S(1)} collective-permute-done((bf16[256,1024]{1,0:T(8,128)(2,1)S(1)}, bf16[256,1024]{1,0:T(8,128)(2,1)S(1)}, u32[]{:S(2)}, u32[]{:S(2)}) %collective-permute-start.8) | collective-permute-done | bytes 524320 | tf_op jit(solution)/shard_map/ppermute | solution.py:469
  52.9 2.2 %shard_map.104 = f32[1,512]{1,0:T(1,128)S(1)} custom-call(s32[6]{0:T(128)S(1)} %stack.27.refs_0_, f32[512,128]{1,0:T(8,128)S(1)} %shard_map.101.refs_1_, bf16[2048,1024]{1,0:T(8,128)(2,1)S(1)} %shard_map.103.refs_2_, bf16[256,1024]{1,0:T(8,128)(2,1)S(1)} %collective-permute-done.8.refs_3_, bf16[512,1024]{1,0:T(8,128)(2,1)S(1)} %get-tuple-element.28.refs_5_.refs_4_, ...), custom_call_target="tpu_custom_call" | custom-call | flops 2310000128 | tf_op jit(solution)/shard_map/pallas_call | solution.py:27
  55.1 0.0 collective-permute-start.9
  55.1 1.2 %collective-permute-done.9 = f32[512]{0:T(512)S(1)} collective-permute-done((f32[512]{0:T(512)S(1)}, f32[512]{0:T(512)S(1)}, u32[]{:S(2)}, u32[]{:S(2)}) %collective-permute-start.9) | collective-permute-done | bytes 2080 | tf_op jit(solution)/shard_map/ppermute | solution.py:493
  56.3 0.5 collective-permute-start.10
  56.8 3.1 %collective-permute-done.10 = f32[512]{0:T(512)S(1)} collective-permute-done((f32[512]{0:T(512)S(1)}, f32[512]{0:T(512)S(1)}, u32[]{:S(2)}, u32[]{:S(2)}) %collective-permute-start.10) | collective-permute-done | bytes 2080 | tf_op jit(solution)/shard_map/ppermute | solution.py:493
  59.9 0.6 add.7
  (4 shorter events, 0.0 us)
Async XLA Ops:
  0.0 1.4 %copy-start = (bf16[3,256,1024]{2,1,0:T(8,128)(2,1)S(1)}, bf16[3,256,1024]{2,1,0:T(8,128)(2,1)}, u32[]{:S(2)}) copy-start(bf16[3,256,1024]{2,1,0:T(8,128)(2,1)} %refs_1_.1) | copy-start | bytes 4718596
  1.4 0.7 %copy-start.6 = (s32[2,64]{1,0:T(2,128)S(1)}, s32[2,64]{1,0:T(2,128)}, u32[]{:S(2)}) copy-start(s32[2,64]{1,0:T(2,128)} %refs_0_.1) | copy-start | bytes 1540
  2.1 0.7 %copy-start.7 = (f32[256]{0:T(256)S(1)}, f32[256]{0:T(256)}, u32[]{:S(2)}) copy-start(f32[256]{0:T(256)} %param.10) | copy-start | bytes 3076
  2.8 8.8 %copy-start.3 = (f32[4096]{0:T(1024)S(1)}, f32[4096]{0:T(1024)}, u32[]{:S(2)}) copy-start(f32[4096]{0:T(1024)} %param.12) | copy-start | bytes 49156
  2.8 8.8 %copy-start.4 = (f32[4096]{0:T(1024)S(1)}, f32[4096]{0:T(1024)}, u32[]{:S(2)}) copy-start(f32[4096]{0:T(1024)} %param.13) | copy-start | bytes 49156
  3.6 13.1 %collective-permute-start = (f32[4,1024]{1,0:T(4,128)S(1)}, f32[4,1024]{1,0:T(4,128)S(1)}, u32[]{:S(2)}, u32[]{:S(2)}) collective-permute-start(f32[4,1024]{1,0:T(4,128)S(1)} %shard_map.92.refs_0_.refs_3_), channel_id=1, source_target_pairs={{0,1},{1,0},{2,3},{3,2},{4,5},{5,4},{6,7},{7,6},{8,9},{9,8},{10,11... | collective-permute-start | bytes 49160 | tf_op jit(solution)/shard_map/ppermute | solution.py:441
  4.2 12.5 %collective-permute-start.1 = (f32[4,1024]{1,0:T(4,128)S(1)}, f32[4,1024]{1,0:T(4,128)S(1)}, u32[]{:S(2)}, u32[]{:S(2)}) collective-permute-start(f32[4,1024]{1,0:T(4,128)S(1)} %shard_map.92.refs_0_.refs_3_), channel_id=1, source_target_pairs={{0,2},{1,3},{2,0},{3,1},{4,6},{5,7},{6,4},{7,5},{8,10},{9,11},{10,... | collective-permute-start | bytes 49160 | tf_op jit(solution)/shard_map/ppermute | solution.py:441
  6.8 20.5 %collective-permute-start.5 = (bf16[192,1024]{1,0:T(8,128)(2,1)S(1)}, bf16[192,1024]{1,0:T(8,128)(2,1)S(1)}, u32[]{:S(2)}, u32[]{:S(2)}) collective-permute-start(bf16[192,1024]{1,0:T(8,128)(2,1)S(1)} %get-tuple-element.25), channel_id=1, source_target_pairs={{0,4},{4,8},{8,12},{12,16},{16,20},{20,24},{24,28},{1,5},{5,9},{9,... | collective-permute-start | bytes 1179656 | tf_op jit(solution)/shard_map/ppermute | solution.py:412
  10.2 17.1 %collective-permute-start.6 = (bf16[192,1024]{1,0:T(8,128)(2,1)S(1)}, bf16[192,1024]{1,0:T(8,128)(2,1)S(1)}, u32[]{:S(2)}, u32[]{:S(2)}) collective-permute-start(bf16[192,1024]{1,0:T(8,128)(2,1)S(1)} %get-tuple-element.26), channel_id=1, source_target_pairs={{4,0},{8,4},{12,8},{16,12},{20,16},{24,20},{28,24},{5,1},{9,5},{13... | collective-permute-start | bytes 1179656 | tf_op jit(solution)/shard_map/ppermute | solution.py:412
  14.6 5.8 %copy-start.2 = (bf16[64,8,4,3]{0,2,3,1:T(4,128)(2,1)S(1)}, bf16[64,8,4,3]{0,2,3,1:T(4,128)(2,1)}, u32[]{:S(2)}) copy-start(bf16[64,8,4,3]{0,2,3,1:T(4,128)(2,1)} %param.14) | copy-start | bytes 36868
  14.6 5.8 %copy-start.5 = (s32[64,4]{0,1:T(4,128)S(1)}, s32[64,4]{0,1:T(4,128)}, u32[]{:S(2)}) copy-start(s32[64,4]{0,1:T(4,128)} %param.15) | copy-start | bytes 3076
  14.6 5.8 %copy-start.8 = (s32[64]{0:T(128)S(1)}, s32[64]{0:T(128)}, u32[]{:S(2)}) copy-start(s32[64]{0:T(128)} %param.16) | copy-start | bytes 772
  16.7 8.7 %collective-permute-start.2 = (f32[12,1024]{1,0:T(8,128)S(1)}, f32[12,1024]{1,0:T(8,128)S(1)}, u32[]{:S(2)}, u32[]{:S(2)}) collective-permute-start(f32[12,1024]{1,0:T(8,128)S(1)} %shard_map.93.refs_0_), channel_id=1, source_target_pairs={{0,8},{4,12},{8,0},{12,4},{16,24},{20,28},{24,16},{28,20},{1,9},{5... | collective-permute-start | bytes 147464 | tf_op jit(solution)/shard_map/ppermute | solution.py:455
  28.8 15.0 %collective-permute-start.7 = (bf16[512,1024]{1,0:T(8,128)(2,1)S(1)}, bf16[512,1024]{1,0:T(8,128)(2,1)S(1)}, u32[]{:S(2)}, u32[]{:S(2)}) collective-permute-start(bf16[512,1024]{1,0:T(8,128)(2,1)S(1)} %get-tuple-element.28.refs_5_.refs_4_), channel_id=1, source_target_pairs={{0,1},{1,0},{2,3},{3,2},{4,5},{5,4},{6,7},{7,6},{8,9},{9,8},{10,11... | collective-permute-start | bytes 3145736 | tf_op jit(solution)/shard_map/ppermute | solution.py:470
  28.9 8.6 %collective-permute-start.3 = (f32[12,1024]{1,0:T(8,128)S(1)}, f32[12,1024]{1,0:T(8,128)S(1)}, u32[]{:S(2)}, u32[]{:S(2)}) collective-permute-start(f32[12,1024]{1,0:T(8,128)S(1)} %shard_map.97.refs_0_.refs_5_), channel_id=1, source_target_pairs={{0,16},{4,20},{8,24},{12,28},{16,0},{20,4},{24,8},{28,12},{1,17},{... | collective-permute-start | bytes 147464 | tf_op jit(solution)/shard_map/ppermute | solution.py:455
  37.6 4.3 %copy-start.1 = (f32[3,4096]{1,0:T(4,128)S(1)}, f32[3,4096]{1,0:T(4,128)}, u32[]{:S(2)}) copy-start(f32[3,4096]{1,0:T(4,128)} %refs_3_.1) | copy-start | bytes 147460
  37.6 4.3 %collective-permute-start.4 = (f32[12,1024]{1,0:T(8,128)S(1)}, f32[12,1024]{1,0:T(8,128)S(1)}, u32[]{:S(2)}, u32[]{:S(2)}) collective-permute-start(f32[12,1024]{1,0:T(8,128)S(1)} %shard_map.98.refs_1_), channel_id=1, source_target_pairs={{0,4},{4,0},{8,12},{12,8},{16,20},{20,16},{24,28},{28,24},{1,5},{5... | collective-permute-start | bytes 147464 | tf_op jit(solution)/shard_map/ppermute | solution.py:455
  41.2 11.8 %collective-permute-start.8 = (bf16[256,1024]{1,0:T(8,128)(2,1)S(1)}, bf16[256,1024]{1,0:T(8,128)(2,1)S(1)}, u32[]{:S(2)}, u32[]{:S(2)}) collective-permute-start(bf16[256,1024]{1,0:T(8,128)(2,1)S(1)} %get-tuple-element.30), channel_id=1, source_target_pairs={{0,2},{1,3},{2,0},{3,1},{4,6},{5,7},{6,4},{7,5},{8,10},{9,11},{10,... | collective-permute-start | bytes 1572872 | tf_op jit(solution)/shard_map/ppermute | solution.py:469
  55.1 1.2 %collective-permute-start.9 = (f32[512]{0:T(512)S(1)}, f32[512]{0:T(512)S(1)}, u32[]{:S(2)}, u32[]{:S(2)}) collective-permute-start(f32[512]{0:T(512)S(1)} %bitcast.13), channel_id=1, source_target_pairs={{0,1},{1,0},{2,3},{3,2},{4,5},{5,4},{6,7},{7,6},{8,9},{9,8},{10,11... | collective-permute-start | bytes 6152 | tf_op jit(solution)/shard_map/ppermute | solution.py:493
  56.3 3.6 %collective-permute-start.10 = (f32[512]{0:T(512)S(1)}, f32[512]{0:T(512)S(1)}, u32[]{:S(2)}, u32[]{:S(2)}) collective-permute-start(f32[512]{0:T(512)S(1)} %add.6), channel_id=1, source_target_pairs={{0,2},{1,3},{2,0},{3,1},{4,6},{5,7},{6,4},{7,5},{8,10},{9,11},{10,... | collective-permute-start | bytes 6152 | tf_op jit(solution)/shard_map/ppermute | solution.py:493

commit v9 on v8

--- a/solution.py
+++ b/solution.py
@@ -33,6 +33,11 @@
         cost_estimate=pl.CostEstimate(flops=int(1.1e9 * cost), bytes_accessed=0, transcendentals=0),
         compiler_params=pltpu.CompilerParams(vmem_limit_bytes=vmem),
     )(*args, *after)
+
+
+def place():
+    group = lax.axis_index("mode")
+    return (group, group ^ 1, group ^ 2, group & 1, group >> 1, 1 - (group >> 1))
 
 
 def add_kernel(left_ref, right_ref, out_ref):
@@ -167,11 +172,11 @@
                 out_ref[pl.ds(at, 8), out_col + c : out_col + c + 128] = pair / bottom
 
 
-def rho_near_kernel(place_ref, freq_ref, rate_ref, diag_ref, mate_ref, col_scr, row_scr):
+def rho_near_kernel(freq_ref, rate_ref, diag_ref, mate_ref, col_scr, row_scr):
     block = diag_ref.shape[0]
     half = block // 2
     tile = block // 4
-    own, mate, parity = place_ref[0], place_ref[1], place_ref[3]
+    own, mate, parity = place()[0], place()[1], place()[3]
     place_modes(freq_ref, rate_ref, row_scr, col_scr, (own, mate), 0, block)
     for j in range(4):
         fill_rho(row_scr, col_scr, diag_ref, j * tile, 0, (j + 1) * tile, 0, j * tile, tile)
@@ -181,37 +186,40 @@
             fill_rho(row_scr, col_scr, mate_ref.at[i], j * tile, i * half, half, 8, off, tile)
 
 
-def rho_own_kernel(place_ref, freq_ref, rate_ref, side_ref, out_ref, row_scr):
+def rho_own_kernel(freq_ref, rate_ref, side_ref, out_ref, row_scr):
     block = out_ref.shape[0]
     tile = block // 4
-    place_modes(freq_ref, rate_ref, row_scr, None, (place_ref[2],), None, block)
+    place_modes(freq_ref, rate_ref, row_scr, None, (place()[2],), None, block)
     for j in range(4):
         fill_rho(row_scr, side_ref, out_ref, j * tile, 0, block, 0, j * tile, tile)
 
 
-def rho_mate_kernel(place_ref, freq_ref, rate_ref, out_ref, col_scr, row_scr):
+def rho_mate_kernel(freq_ref, rate_ref, out_ref, col_scr, row_scr):
     block = out_ref.shape[0]
     tile = block // 4
-    place_modes(freq_ref, rate_ref, row_scr, col_scr, (place_ref[1], place_ref[2]), 0, block)
+    place_modes(freq_ref, rate_ref, row_scr, col_scr, (place()[1], place()[2]), 0, block)
     for j in range(4):
         fill_rho(row_scr, col_scr, out_ref, j * tile, 0, block, 8, j * tile, tile)
 
 
-def forces_kernel(at, dims, place_ref, rim_ref, low_ref, high_ref, local_ref, all_ref, part_ref, rim_scr):
-    comps, chunk = all_ref.shape
+def forces_kernel(dims, rim_ref, low_ref, high_ref, local_ref, all_ref, *refs):
+    part_refs, rim_scr = refs[:-1], refs[-1]
+    comps, block = all_ref.shape
     width = low_ref.shape[0] // dims
     part = comps // 2
-    other = place_ref[5]
-    lanes = slice(at, at + chunk)
+    rows = pl.ds(pl.multiple_of(place()[5] * part, part), part)
     for copy in range(2):
         for d in range(dims):
             base = (copy * dims + d) * 2 * width
-            rim_scr[base : base + width, :] = low_ref[d * width : (d + 1) * width, lanes]
-            rim_scr[base + width : base + 2 * width, :] = high_ref[d * width : (d + 1) * width, lanes]
-    for c in range(0, chunk, 256):
+            rim_scr[base : base + width, :] = low_ref[d * width : (d + 1) * width, :]
+            rim_scr[base + width : base + 2 * width, :] = high_ref[d * width : (d + 1) * width, :]
+    for c in range(0, block, 256):
         total = jnp.dot(rim_ref[...], rim_scr[:, c : c + 256], preferred_element_type=F32)
-        all_ref[:, c : c + 256] = (local_ref[:, at + c : at + c + 256] + total).astype(BF16)
-    part_ref[...] = all_ref[pl.ds(pl.multiple_of(other * part, part), part), :]
+        all_ref[:, c : c + 256] = (local_ref[:, c : c + 256] + total).astype(BF16)
+    at = 0
+    for part_ref in part_refs:
+        part_ref[...] = all_ref[rows, at : at + part_ref.shape[1]]
+        at += part_ref.shape[1]
 
 
 def join_kernel(*refs):
@@ -221,10 +229,10 @@
         out_ref[q * size : (q + 1) * size, :] = ref[...]
 
 
-def amps_kernel(place_ref, stats_ref, extra_ref, spectral_ref, freq_ref, rate_ref, *out_refs):
+def amps_kernel(stats_ref, extra_ref, spectral_ref, freq_ref, rate_ref, *out_refs):
     dims, block = spectral_ref.shape[0], stats_ref.shape[1]
     for q, out_ref in enumerate(out_refs):
-        lanes = pl.ds(pl.multiple_of(place_ref[q] * block, block), block)
+        lanes = pl.ds(pl.multiple_of(place()[q] * block, block), block)
         rows = slice(q * (dims + 1), (q + 1) * (dims + 1))
         total = stats_ref[rows, :] + extra_ref[rows, :]
         scale = 2.0 * jnp.sqrt(freq_ref[:, lanes] / rate_ref[:, lanes])
@@ -280,14 +288,14 @@
 
 
 def near_kernel(dims, chunks, *refs):
-    place_ref, own_amps_ref, mate_amps_ref, diag_ref, cross_ref = refs[:5]
-    own_refs, mate_refs = refs[5 : 5 + chunks], refs[5 + chunks : 5 + 2 * chunks]
-    acc, side_scr, w_scr = refs[5 + 2 * chunks :]
+    own_amps_ref, mate_amps_ref, diag_ref, cross_ref = refs[:4]
+    own_refs, mate_refs = refs[4 : 4 + chunks], refs[4 + chunks : 4 + 2 * chunks]
+    acc, side_scr, w_scr = refs[4 + 2 * chunks :]
     _, chunk = own_refs[0].shape
     block = diag_ref.shape[0]
     tile = block // 4
     half = block // 2
-    parity = place_ref[3]
+    parity = place()[3]
 
     def part(parts, at, size):
         return parts[at // chunk][:, at % chunk : at % chunk + size]
@@ -347,37 +355,22 @@
                 )
 
 
-def far_kernel(at, chunks, per_elem, place_ref, near_ref, w_ref, far_ref, *refs):
-    own_refs, mate_refs = refs[:chunks], refs[chunks : 2 * chunks]
-    if len(refs) == 2 * chunks + 1:
-        acc, last = refs[-1], False
-    else:
-        (out_ref, acc, turned), last = refs[2 * chunks :], True
-    comps, chunk = own_refs[0].shape
-    block = w_ref.shape[1]
-    part = comps // 2
+def far_kernel(at, per_elem, near_ref, w_ref, far_ref, own_ref, mate_ref, out_ref, *scratch):
+    _, block = own_ref.shape
+    part, chunk = far_ref.shape
     tile = min(256, chunk)
-    here = pl.multiple_of(place_ref[4] * part, part)
-    rows = pl.ds(here, part)
+    rows = pl.ds(pl.multiple_of(place()[4] * part, part), part)
     total = near_ref[rows, :]
     for c in range(0, chunk, tile):
         spot = slice(at + c, at + c + tile)
-        got = None
-        for which, parts in enumerate((own_refs, mate_refs)):
-            for q in range(chunks):
-                base = which * block + q * chunk
-                piece = jnp.dot(
-                    parts[q][rows, :], w_ref[base : base + chunk, spot], preferred_element_type=F32
-                )
-                got = piece if got is None else got + piece
+        got = jnp.dot(own_ref[rows, :], w_ref[:block, spot], preferred_element_type=F32)
+        got = got + jnp.dot(mate_ref[rows, :], w_ref[block:, spot], preferred_element_type=F32)
         total = total + fold(got * far_ref[:, c : c + tile].astype(F32))
+    acc = scratch[0] if scratch else out_ref
     acc[...] = near_ref[...]
     acc[rows, :] = total
-    if last:
-        out_ref[...] = to_row(acc, turned, per_elem)
-
-
-CHUNKS = 1
+    if scratch:
+        out_ref[...] = to_row(acc, scratch[1], per_elem)
 
 
 def four_groups(*args):
@@ -394,12 +387,7 @@
     part = comps // 2
     width = shared.shape[1]
     parts = lax.axis_size("dom")
-    group = lax.axis_index("mode").astype(jnp.int32)
-    place = jnp.stack(
-        [group, group ^ 1, group ^ 2, group & 1, group >> 1, 1 - (group >> 1)]
-    ).astype(jnp.int32)
     sds = jax.ShapeDtypeStruct
-    chunk = block // CHUNKS
     ahead = [(i, i + 1) for i in range(parts - 1)]
     back = [(i + 1, i) for i in range(parts - 1)]
     freq = frequencies.reshape(1, -1)
@@ -417,11 +405,11 @@
     rho_diag, rho_mate, sides = call(
         rho_near_kernel,
         (sds((block, block), F32), sds((2, block // 2, block // 2), F32), sds((4, block, 128), F32)),
-        (place, freq, rate), 3.0, smem=(0,),
+        (freq, rate), 3.0,
         scratch=[pltpu.VMEM((16, block), F32)], after=(stats,),
     )
     far_own = call(
-        rho_own_kernel, sds((block, block), F32), (place, freq, rate, sides), 1.9, smem=(0,),
+        rho_own_kernel, sds((block, block), F32), (freq, rate, sides), 1.9,
         scratch=[pltpu.VMEM((8, block), F32)],
     )
     taken = slots * elems
@@ -435,7 +423,7 @@
         ],
     )
     far_mate = call(
-        rho_mate_kernel, sds((block, block), F32), (place, freq, rate), 2.5, smem=(0,),
+        rho_mate_kernel, sds((block, block), F32), (freq, rate), 2.5,
         scratch=[pltpu.VMEM((4, block, 128), F32), pltpu.VMEM((16, block), F32)],
     )
     given = [stats] + [lax.ppermute(stats, "mode", [(i, i ^ q) for i in range(4)]) for q in (1, 2)]
@@ -454,24 +442,22 @@
             first = stats if q == 1 else first
         extra = lax.ppermute(stats, "dom", [(i, i ^ reach) for i in range(parts)])
     amps, mate_amps, far_amps = call(
-        amps_kernel, [sds((8, block), F32)] * 3, (place, stats, extra, spectral, freq, rate), 0.8, smem=(0,)
-    )
-
-    own, mate, far = [], [], []
-    for c in range(CHUNKS):
-        forces, sent = call(
-            functools.partial(forces_kernel, c * chunk, dims),
-            (sds((comps, chunk), BF16), sds((part, chunk), BF16)),
-            (place, rim, low, high, local), 1.4 / CHUNKS, smem=(0,),
-            scratch=[pltpu.VMEM((4 * dims * width, chunk), BF16)], after=(own[-1] if own else first,),
-        )
-        own.append(forces)
-        far.append(lax.ppermute(sent, "mode", [(i, i ^ 2) for i in range(4)]))
-        mate.append(lax.ppermute(forces, "mode", [(i, i ^ 1) for i in range(4)]))
+        amps_kernel, [sds((8, block), F32)] * 3, (stats, extra, spectral, freq, rate), 0.8,
+    )
+
+    cuts = [block - block // 4, block // 4]
+    forces, *sent = call(
+        functools.partial(forces_kernel, dims),
+        [sds((comps, block), BF16)] + [sds((part, cut), BF16) for cut in cuts],
+        (rim, low, high, local), 1.4,
+        scratch=[pltpu.VMEM((4 * dims * width, block), BF16)], after=(first,),
+    )
+    far = [lax.ppermute(value, "mode", [(i, i ^ 2) for i in range(4)]) for value in sent]
+    mate = lax.ppermute(forces, "mode", [(i, i ^ 1) for i in range(4)])
     near = call(
-        functools.partial(near_kernel, dims, CHUNKS), sds((comps, 128), F32),
-        (place, amps, mate_amps, rho_diag, rho_mate, *own, *mate),
-        3.4, smem=(0,),
+        functools.partial(near_kernel, dims, 1), sds((comps, 128), F32),
+        (amps, mate_amps, rho_diag, rho_mate, forces, mate),
+        3.4,
         scratch=[pltpu.VMEM((block, 32), BF16), pltpu.VMEM((2, block, block // 4), BF16)],
     )
     weights = call(
@@ -480,14 +466,15 @@
         scratch=[pltpu.VMEM((2 * block, 32), BF16)],
     )
     value = near
-    for c in range(CHUNKS):
-        last = c == CHUNKS - 1
+    at = 0
+    for c, cut in enumerate(cuts):
+        last = c == len(cuts) - 1
         value = call(
-            functools.partial(far_kernel, c * chunk, CHUNKS, per_elem),
-            sds((1, comps) if last else (comps, 128), F32),
-            (place, value, weights, far[c], *own, *mate), 2.1 / CHUNKS,
-            smem=(0,), scratch=[pltpu.VMEM((comps, 128), F32)] * 2 if last else (),
+            functools.partial(far_kernel, at, per_elem), sds((1, comps) if last else (comps, 128), F32),
+            (value, weights, far[c], forces, mate), 2.1 * cut / block,
+            scratch=[pltpu.VMEM((comps, 128), F32)] * 2 if last else (),
         )
+        at += cut
     value = value.reshape(comps)
     for reach in (1, 2):
         value = value + lax.ppermute(value, "mode", [(i, i ^ reach) for i in range(4)])

time: 60.9 us -> 59.5 us (0.977)
  Pallas kernels: 20.2 us -> 17 us
  starting transfers between devices: 17.9 us -> 19.5 us
    pallas_call x14 -> x15, Pallas kernels: 20.2 us -> 17 us  [call(): pl.pallas_call(body, out_shape=out_shape, in_specs=specs, out_specs=[VMEM...]
    ppermute x3, waiting for transfers between devices: 7.45 us -> 9.72 us  [combined(): extra = lax.ppermute(stats, 'dom', [(i, i ^ reach) for i in range(parts)])]
    ppermute x2 -> x3, waiting for transfers between devices: 5.79 us -> 4.01 us  [the longest x2 4.01 us: combined(): lax.ppermute(value, 'mode', [(i, i ^ 2) for i in range(4)])]
    ppermute x2 -> x3, starting transfers between devices: 0.64 us -> 2.23 us  [the longest x2 2.16 us: combined(): lax.ppermute(value, 'mode', [(i, i ^ 2) for i in range(4)])]
  transfers between devices with their start and end apart: 11 -> 12, of which waited for: 7 -> 8; matrix products, arithmetic and copies ran while one was open for 0% -> 0% of each run, Pallas kernels for 25% -> 22%
where the time goes in v9:
time: 59.5 us; the launch traced here: 59.2 us
  waiting for transfers between devices  19.9 us (33%)
  starting transfers between devices  19.5 us (33%)
  Pallas kernels  17 us (29%)
  local copies, waits for them, and re-layouts  2.13 us (4%)
    pallas_call x15, Pallas kernels, call(): pl.pallas_call(body, out_shape=out_shape, in_specs=specs, out_specs=[VMEM...  17 us
    ppermute x3, waiting for transfers between devices, combined(): extra = lax.ppermute(stats, 'dom', [(i, i ^ reach) for i in range(parts)])  9.72 us
    ppermute x3, starting transfers between devices, combined(): extra = lax.ppermute(stats, 'dom', [(i, i ^ reach) for i in range(parts)])  8.91 us
    ppermute x2, waiting for transfers between devices, combined(): lax.ppermute(value, 'mode', [(i, i ^ reach) for i in range(4)])  4.3 us
    ppermute x2, waiting for transfers between devices, combined(): lax.ppermute(value, 'mode', [(i, i ^ 2) for i in range(4)])  4.01 us
    ppermute x1, starting transfers between devices, combined(): lax.ppermute(up, 'dom', ahead)  3.4 us
    ppermute x2, starting transfers between devices, combined(): lax.ppermute(stats, 'mode', [(i, i ^ q) for i in range(4)])  3.15 us
    ppermute x2, starting transfers between devices, combined(): lax.ppermute(value, 'mode', [(i, i ^ 2) for i in range(4)])  2.16 us
  transfers between devices with their start and end apart: 12, of which 8 were waited for; matrix products, arithmetic and copies ran while one was open for 0% of the time, Pallas kernels for 22%

profile of v9, /device:TPU:0, one launch (start us, length us, event | category | flops | bytes accessed | tf_op | source)
XLA Modules:
  0.0 59.2 jit_solution(13365813236216450112)
XLA Ops:
  0.0 0.0 copy-start
  0.0 1.4 %copy-done = bf16[3,256,1024]{2,1,0:T(8,128)(2,1)S(1)} copy-done((bf16[3,256,1024]{2,1,0:T(8,128)(2,1)S(1)}, bf16[3,256,1024]{2,1,0:T(8,128)(2,1)}, u32[]{:S(2)}) %copy-start) | copy-done | bytes 1572888
  1.4 0.0 copy-start.6
  1.4 0.7 %copy-done.6 = s32[2,64]{1,0:T(2,128)S(1)} copy-done((s32[2,64]{1,0:T(2,128)S(1)}, s32[2,64]{1,0:T(2,128)}, u32[]{:S(2)}) %copy-start.6) | copy-done | bytes 536
  2.1 0.0 copy-start.7
  2.1 0.7 %shard_map.91 = (bf16[192,1024]{1,0:T(8,128)(2,1)S(1)}, bf16[192,1024]{1,0:T(8,128)(2,1)S(1)}, bf16[3,256,1024]{2,1,0:T(8,128)(2,1)S(1)}) custom-call(s32[2,64]{1,0:T(2,128)S(1)} %copy-done.6, bf16[3,256,1024]{2,1,0:T(8,128)(2,1)S(1)} %copy-done), custom_call_target="tpu_custom_call" | custom-call | flops 2200000000 | tf_op jit(solution)/shard_map/pallas_call | solution.py:27
  2.8 0.0 copy-start.3
  2.8 0.0 copy-start.4
  2.8 0.0 copy-done.7
  2.8 0.8 %shard_map.92.refs_0_.refs_2_ = f32[4,1024]{1,0:T(4,128)S(1)} custom-call(f32[1,256]{1,0:T(1,128)S(1)} %bitcast.19, bf16[3,256,1024]{2,1,0:T(8,128)(2,1)S(1)} %get-tuple-element.19.refs_1_.refs_3_), custom_call_target="tpu_custom_call" | custom-call | flops 880000000 | tf_op jit(solution)/shard_map/pallas_call | solution.py:27
  3.6 0.6 collective-permute-start
  4.2 2.6 %collective-permute-start.1 = (f32[4,1024]{1,0:T(4,128)S(1)}, f32[4,1024]{1,0:T(4,128)S(1)}, u32[]{:S(2)}, u32[]{:S(2)}) collective-permute-start(f32[4,1024]{1,0:T(4,128)S(1)} %shard_map.92.refs_0_.refs_2_), channel_id=1, source_target_pairs={{0,2},{1,3},{2,0},{3,1},{4,6},{5,7},{6,4},{7,5},{8,10},{9,11},{10,... | collective-permute-start | bytes 49160 | tf_op jit(solution)/shard_map/ppermute | solution.py:429
  6.8 3.4 %collective-permute-start.5 = (bf16[192,1024]{1,0:T(8,128)(2,1)S(1)}, bf16[192,1024]{1,0:T(8,128)(2,1)S(1)}, u32[]{:S(2)}, u32[]{:S(2)}) collective-permute-start(bf16[192,1024]{1,0:T(8,128)(2,1)S(1)} %get-tuple-element.26), channel_id=1, source_target_pairs={{0,4},{4,8},{8,12},{12,16},{16,20},{20,24},{24,28},{1,5},{5,9},{9,... | collective-permute-start | bytes 1179656 | tf_op jit(solution)/shard_map/ppermute | solution.py:400
  10.2 1.3 %collective-permute-start.6 = (bf16[192,1024]{1,0:T(8,128)(2,1)S(1)}, bf16[192,1024]{1,0:T(8,128)(2,1)S(1)}, u32[]{:S(2)}, u32[]{:S(2)}) collective-permute-start(bf16[192,1024]{1,0:T(8,128)(2,1)S(1)} %get-tuple-element.27), channel_id=1, source_target_pairs={{4,0},{8,4},{12,8},{16,12},{20,16},{24,20},{28,24},{5,1},{9,5},{13... | collective-permute-start | bytes 1179656 | tf_op jit(solution)/shard_map/ppermute | solution.py:400
  11.5 0.0 copy-done.3
  11.5 0.0 copy-done.4
  11.5 2.4 %shard_map.94 = (f32[1024,1024]{1,0:T(8,128)S(1)}, f32[2,512,512]{2,1,0:T(8,128)S(1)}, f32[4,1024,128]{2,1,0:T(8,128)S(1)}) custom-call(f32[1,4096]{1,0:T(1,128)S(1)} %bitcast.10, f32[1,4096]{1,0:T(1,128)S(1)} %bitcast.14, f32[4,1024]{1,0:T(4,128)S(1)} %shard_map.92.refs_0_.refs_2_), custom_call_target="tpu_custom_call" | custom-call | flops 3300000000 | tf_op jit(solution)/shard_map/pallas_call | solution.py:27
  13.9 0.0 copy-start.2
  13.9 0.0 copy-start.5
  14.0 0.0 copy-start.8
  14.0 1.6 %shard_map.95.refs_4_.refs_3_ = f32[1024,1024]{1,0:T(8,128)S(1)} custom-call(f32[1,4096]{1,0:T(1,128)S(1)} %bitcast.11, f32[1,4096]{1,0:T(1,128)S(1)} %bitcast.15, f32[4,1024,128]{2,1,0:T(8,128)S(1)} %get-tuple-element.20.refs_2_), custom_call_target="tpu_custom_call" | custom-call | flops 2090000000 | tf_op jit(solution)/shard_map/pallas_call | solution.py:27
  15.5 0.0 collective-permute-done.refs_1_
  15.5 0.0 collective-permute-done.1.refs_2_
  15.6 3.7 %collective-permute-start.2 = (f32[12,1024]{1,0:T(8,128)S(1)}, f32[12,1024]{1,0:T(8,128)S(1)}, u32[]{:S(2)}, u32[]{:S(2)}) collective-permute-start(f32[12,1024]{1,0:T(8,128)S(1)} %shard_map.93.refs_0_), channel_id=1, source_target_pairs={{0,8},{4,12},{8,0},{12,4},{16,24},{20,28},{24,16},{28,20},{1,9},{5... | collective-permute-start | bytes 147464 | tf_op jit(solution)/shard_map/ppermute | solution.py:443
  19.2 0.0 copy-done.2
  19.2 0.0 copy-done.5
  19.2 0.0 copy-done.8
  19.2 1.8 %shard_map.96 = (f32[512,1024]{1,0:T(8,128)S(1)}, bf16[512,768]{1,0:T(8,128)(2,1)S(1)}) custom-call(s32[4,64]{1,0:T(4,128)S(1)} %bitcast.18, s32[1,64]{1,0:T(1,128)S(1)} %bitcast.20, bf16[8,3,4,64]{3,2,1,0:T(4,128)(2,1)S(1)} %bitcast.9, bf16[3,256,1024]{2,1,0:T(8,128)(2,1)S(1)} %get-tuple-element.19.refs_1_.refs_3_, f32[1024,1024]{1,0:T(8,128)S(1)} %shard_map.95.refs_4_.refs_3_), custom_call_target="tpu_custom_call" | custom-call | flops 1980000000 | tf_op jit(solution)/shard_map/pallas_call | solution.py:27
  21.0 4.3 %collective-permute-done.2.refs_1_ = f32[12,1024]{1,0:T(8,128)S(1)} collective-permute-done((f32[12,1024]{1,0:T(8,128)S(1)}, f32[12,1024]{1,0:T(8,128)S(1)}, u32[]{:S(2)}, u32[]{:S(2)}) %collective-permute-start.2) | collective-permute-done | bytes 49184 | tf_op jit(solution)/shard_map/ppermute | solution.py:443
  25.4 1.9 %collective-permute-done.5.refs_1_ = bf16[192,1024]{1,0:T(8,128)(2,1)S(1)} collective-permute-done((bf16[192,1024]{1,0:T(8,128)(2,1)S(1)}, bf16[192,1024]{1,0:T(8,128)(2,1)S(1)}, u32[]{:S(2)}, u32[]{:S(2)}) %collective-permute-start.5) | collective-permute-done | bytes 393248 | tf_op jit(solution)/shard_map/ppermute | solution.py:400
  27.2 0.0 collective-permute-done.6.refs_2_
  27.3 1.1 %shard_map.100 = (bf16[512,1024]{1,0:T(8,128)(2,1)S(1)}, bf16[256,768]{1,0:T(8,128)(2,1)S(1)}, bf16[256,256]{1,0:T(8,128)(2,1)S(1)}) custom-call(bf16[512,768]{1,0:T(8,128)(2,1)S(1)} %get-tuple-element.21.refs_2_.refs_0_, bf16[192,1024]{1,0:T(8,128)(2,1)S(1)} %collective-permute-done.5.refs_1_, bf16[192,1024]{1,0:T(8,128)(2,1)S(1)} %collective-permute-done.6.refs_2_, ...), custom_call_target="tpu_custom_call" | custom-call | flops 1540000000 | tf_op jit(solution)/shard_map/pallas_call | solution.py:27
  28.4 0.1 collective-permute-start.7
  28.5 4.5 %collective-permute-start.3 = (f32[12,1024]{1,0:T(8,128)S(1)}, f32[12,1024]{1,0:T(8,128)S(1)}, u32[]{:S(2)}, u32[]{:S(2)}) collective-permute-start(f32[12,1024]{1,0:T(8,128)S(1)} %shard_map.97.refs_0_.refs_4_), channel_id=1, source_target_pairs={{0,16},{4,20},{8,24},{12,28},{16,0},{20,4},{24,8},{28,12},{1,17},{... | collective-permute-start | bytes 147464 | tf_op jit(solution)/shard_map/ppermute | solution.py:443
  33.0 4.1 %collective-permute-done.3.refs_1_ = f32[12,1024]{1,0:T(8,128)S(1)} collective-permute-done((f32[12,1024]{1,0:T(8,128)S(1)}, f32[12,1024]{1,0:T(8,128)S(1)}, u32[]{:S(2)}, u32[]{:S(2)}) %collective-permute-start.3) | collective-permute-done | bytes 49184 | tf_op jit(solution)/shard_map/ppermute | solution.py:443
  37.1 0.0 copy-start.1
  37.1 0.7 %collective-permute-start.4 = (f32[12,1024]{1,0:T(8,128)S(1)}, f32[12,1024]{1,0:T(8,128)S(1)}, u32[]{:S(2)}, u32[]{:S(2)}) collective-permute-start(f32[12,1024]{1,0:T(8,128)S(1)} %shard_map.98.refs_0_), channel_id=1, source_target_pairs={{0,4},{4,0},{8,12},{12,8},{16,20},{20,16},{24,28},{28,24},{1,5},{5... | collective-permute-start | bytes 147464 | tf_op jit(solution)/shard_map/ppermute | solution.py:443
  37.8 2.3 %shard_map.102.refs_4_ = f32[1024,1024]{1,0:T(8,128)S(1)} custom-call(f32[1,4096]{1,0:T(1,128)S(1)} %bitcast.12, f32[1,4096]{1,0:T(1,128)S(1)} %bitcast.16), custom_call_target="tpu_custom_call" | custom-call | flops 2750000128 | tf_op jit(solution)/shard_map/pallas_call | solution.py:27
  40.1 1.3 %collective-permute-done.4.refs_1_ = f32[12,1024]{1,0:T(8,128)S(1)} collective-permute-done((f32[12,1024]{1,0:T(8,128)S(1)}, f32[12,1024]{1,0:T(8,128)S(1)}, u32[]{:S(2)}, u32[]{:S(2)}) %collective-permute-start.4) | collective-permute-done | bytes 49184 | tf_op jit(solution)/shard_map/ppermute | solution.py:443
  41.4 0.0 copy-done.1
  41.5 0.5 collective-permute-start.8
  42.0 1.4 %shard_map.103.refs_1_ = bf16[2048,1024]{1,0:T(8,128)(2,1)S(1)} custom-call(f32[8,1024]{1,0:T(8,128)S(1)} %get-tuple-element.22.refs_0_, f32[8,1024]{1,0:T(8,128)S(1)} %get-tuple-element.23.refs_1_, f32[8,1024]{1,0:T(8,128)S(1)} %get-tuple-element.30.refs_2_, f32[1024,1024]{1,0:T(8,128)S(1)} %shard_map.95.refs_4_.refs_3_, f32[1024,1024]{1,0:T(8,128)S(1)} %shard_map.102.refs_4_), custom_call_target="tpu_custom_call" | custom-call | flops 1540000000 | tf_op jit(solution)/shard_map/pallas_call | solution.py:27
  43.4 1.6 %collective-permute-start.9 = (bf16[256,256]{1,0:T(8,128)(2,1)S(1)}, bf16[256,256]{1,0:T(8,128)(2,1)S(1)}, u32[]{:S(2)}, u32[]{:S(2)}) collective-permute-start(bf16[256,256]{1,0:T(8,128)(2,1)S(1)} %get-tuple-element.32), channel_id=1, source_target_pairs={{0,2},{1,3},{2,0},{3,1},{4,6},{5,7},{6,4},{7,5},{8,10},{9,11},{10,... | collective-permute-start | bytes 393224 | tf_op jit(solution)/shard_map/ppermute | solution.py:455
  45.0 0.0 collective-permute-done.7.refs_5_.refs_4_
  45.0 2.7 %shard_map.101.refs_0_ = f32[512,128]{1,0:T(8,128)S(1)} custom-call(f32[8,1024]{1,0:T(8,128)S(1)} %get-tuple-element.22.refs_0_, f32[8,1024]{1,0:T(8,128)S(1)} %get-tuple-element.23.refs_1_, f32[1024,1024]{1,0:T(8,128)S(1)} %get-tuple-element.24.refs_2_, f32[2,512,512]{2,1,0:T(8,128)S(1)} %get-tuple-element.25.refs_3_, ...), custom_call_target="tpu_custom_call" | custom-call | flops 3740000000 | tf_op jit(solution)/shard_map/pallas_call | solution.py:27
  47.7 3.6 %collective-permute-done.8.refs_2_ = bf16[256,768]{1,0:T(8,128)(2,1)S(1)} collective-permute-done((bf16[256,768]{1,0:T(8,128)(2,1)S(1)}, bf16[256,768]{1,0:T(8,128)(2,1)S(1)}, u32[]{:S(2)}, u32[]{:S(2)}) %collective-permute-start.8) | collective-permute-done | bytes 393248 | tf_op jit(solution)/shard_map/ppermute | solution.py:455
  51.3 1.0 %shard_map.104.refs_0_ = f32[512,128]{1,0:T(8,128)S(1)} custom-call(f32[512,128]{1,0:T(8,128)S(1)} %shard_map.101.refs_0_, bf16[2048,1024]{1,0:T(8,128)(2,1)S(1)} %shard_map.103.refs_1_, bf16[256,768]{1,0:T(8,128)(2,1)S(1)} %collective-permute-done.8.refs_2_, bf16[512,1024]{1,0:T(8,128)(2,1)S(1)} %get-tuple-element.29.refs_4_.refs_3_, ...), custom_call_target="tpu_custom_call" | custom-call | flops 1732499968 | tf_op jit(solution)/shard_map/pallas_call | solution.py:27
  52.3 0.4 collective-permute-done.9.refs_2_
  52.7 1.2 %shard_map.105 = f32[1,512]{1,0:T(1,128)S(1)} custom-call(f32[512,128]{1,0:T(8,128)S(1)} %shard_map.104.refs_0_, bf16[2048,1024]{1,0:T(8,128)(2,1)S(1)} %shard_map.103.refs_1_, bf16[256,256]{1,0:T(8,128)(2,1)S(1)} %collective-permute-done.9.refs_2_, bf16[512,1024]{1,0:T(8,128)(2,1)S(1)} %get-tuple-element.29.refs_4_.refs_3_, ...), custom_call_target="tpu_custom_call" | custom-call | flops 577500032 | tf_op jit(solution)/shard_map/pallas_call | solution.py:27
  53.9 0.0 collective-permute-start.10
  53.9 1.2 %collective-permute-done.10 = f32[512]{0:T(512)S(1)} collective-permute-done((f32[512]{0:T(512)S(1)}, f32[512]{0:T(512)S(1)}, u32[]{:S(2)}, u32[]{:S(2)}) %collective-permute-start.10) | collective-permute-done | bytes 2080 | tf_op jit(solution)/shard_map/ppermute | solution.py:480
  55.1 0.5 collective-permute-start.11
  55.6 3.1 %collective-permute-done.11 = f32[512]{0:T(512)S(1)} collective-permute-done((f32[512]{0:T(512)S(1)}, f32[512]{0:T(512)S(1)}, u32[]{:S(2)}, u32[]{:S(2)}) %collective-permute-start.11) | collective-permute-done | bytes 2080 | tf_op jit(solution)/shard_map/ppermute | solution.py:480
  58.7 0.6 add.7
  (5 shorter events, 0.1 us)
Async XLA Ops:
  0.0 1.4 %copy-start = (bf16[3,256,1024]{2,1,0:T(8,128)(2,1)S(1)}, bf16[3,256,1024]{2,1,0:T(8,128)(2,1)}, u32[]{:S(2)}) copy-start(bf16[3,256,1024]{2,1,0:T(8,128)(2,1)} %refs_1_.1) | copy-start | bytes 4718596
  1.4 0.7 %copy-start.6 = (s32[2,64]{1,0:T(2,128)S(1)}, s32[2,64]{1,0:T(2,128)}, u32[]{:S(2)}) copy-start(s32[2,64]{1,0:T(2,128)} %refs_0_.1) | copy-start | bytes 1540
  2.1 0.7 %copy-start.7 = (f32[256]{0:T(256)S(1)}, f32[256]{0:T(256)}, u32[]{:S(2)}) copy-start(f32[256]{0:T(256)} %param.10) | copy-start | bytes 3076
  2.8 8.7 %copy-start.3 = (f32[4096]{0:T(1024)S(1)}, f32[4096]{0:T(1024)}, u32[]{:S(2)}) copy-start(f32[4096]{0:T(1024)} %param.12) | copy-start | bytes 49156
  2.8 8.7 %copy-start.4 = (f32[4096]{0:T(1024)S(1)}, f32[4096]{0:T(1024)}, u32[]{:S(2)}) copy-start(f32[4096]{0:T(1024)} %param.13) | copy-start | bytes 49156
  3.6 11.9 %collective-permute-start = (f32[4,1024]{1,0:T(4,128)S(1)}, f32[4,1024]{1,0:T(4,128)S(1)}, u32[]{:S(2)}, u32[]{:S(2)}) collective-permute-start(f32[4,1024]{1,0:T(4,128)S(1)} %shard_map.92.refs_0_.refs_2_), channel_id=1, source_target_pairs={{0,1},{1,0},{2,3},{3,2},{4,5},{5,4},{6,7},{7,6},{8,9},{9,8},{10,11... | collective-permute-start | bytes 49160 | tf_op jit(solution)/shard_map/ppermute | solution.py:429
  4.2 11.4 %collective-permute-start.1 = (f32[4,1024]{1,0:T(4,128)S(1)}, f32[4,1024]{1,0:T(4,128)S(1)}, u32[]{:S(2)}, u32[]{:S(2)}) collective-permute-start(f32[4,1024]{1,0:T(4,128)S(1)} %shard_map.92.refs_0_.refs_2_), channel_id=1, source_target_pairs={{0,2},{1,3},{2,0},{3,1},{4,6},{5,7},{6,4},{7,5},{8,10},{9,11},{10,... | collective-permute-start | bytes 49160 | tf_op jit(solution)/shard_map/ppermute | solution.py:429
  6.8 20.5 %collective-permute-start.5 = (bf16[192,1024]{1,0:T(8,128)(2,1)S(1)}, bf16[192,1024]{1,0:T(8,128)(2,1)S(1)}, u32[]{:S(2)}, u32[]{:S(2)}) collective-permute-start(bf16[192,1024]{1,0:T(8,128)(2,1)S(1)} %get-tuple-element.26), channel_id=1, source_target_pairs={{0,4},{4,8},{8,12},{12,16},{16,20},{20,24},{24,28},{1,5},{5,9},{9,... | collective-permute-start | bytes 1179656 | tf_op jit(solution)/shard_map/ppermute | solution.py:400
  10.2 17.1 %collective-permute-start.6 = (bf16[192,1024]{1,0:T(8,128)(2,1)S(1)}, bf16[192,1024]{1,0:T(8,128)(2,1)S(1)}, u32[]{:S(2)}, u32[]{:S(2)}) collective-permute-start(bf16[192,1024]{1,0:T(8,128)(2,1)S(1)} %get-tuple-element.27), channel_id=1, source_target_pairs={{4,0},{8,4},{12,8},{16,12},{20,16},{24,20},{28,24},{5,1},{9,5},{13... | collective-permute-start | bytes 1179656 | tf_op jit(solution)/shard_map/ppermute | solution.py:400
  13.9 5.3 %copy-start.2 = (bf16[64,8,4,3]{0,2,3,1:T(4,128)(2,1)S(1)}, bf16[64,8,4,3]{0,2,3,1:T(4,128)(2,1)}, u32[]{:S(2)}) copy-start(bf16[64,8,4,3]{0,2,3,1:T(4,128)(2,1)} %param.14) | copy-start | bytes 36868
  13.9 5.3 %copy-start.5 = (s32[64,4]{0,1:T(4,128)S(1)}, s32[64,4]{0,1:T(4,128)}, u32[]{:S(2)}) copy-start(s32[64,4]{0,1:T(4,128)} %param.15) | copy-start | bytes 3076
  14.0 5.3 %copy-start.8 = (s32[64]{0:T(128)S(1)}, s32[64]{0:T(128)}, u32[]{:S(2)}) copy-start(s32[64]{0:T(128)} %param.16) | copy-start | bytes 772
  15.6 9.8 %collective-permute-start.2 = (f32[12,1024]{1,0:T(8,128)S(1)}, f32[12,1024]{1,0:T(8,128)S(1)}, u32[]{:S(2)}, u32[]{:S(2)}) collective-permute-start(f32[12,1024]{1,0:T(8,128)S(1)} %shard_map.93.refs_0_), channel_id=1, source_target_pairs={{0,8},{4,12},{8,0},{12,4},{16,24},{20,28},{24,16},{28,20},{1,9},{5... | collective-permute-start | bytes 147464 | tf_op jit(solution)/shard_map/ppermute | solution.py:443
  28.4 16.6 %collective-permute-start.7 = (bf16[512,1024]{1,0:T(8,128)(2,1)S(1)}, bf16[512,1024]{1,0:T(8,128)(2,1)S(1)}, u32[]{:S(2)}, u32[]{:S(2)}) collective-permute-start(bf16[512,1024]{1,0:T(8,128)(2,1)S(1)} %get-tuple-element.29.refs_4_.refs_3_), channel_id=1, source_target_pairs={{0,1},{1,0},{2,3},{3,2},{4,5},{5,4},{6,7},{7,6},{8,9},{9,8},{10,11... | collective-permute-start | bytes 3145736 | tf_op jit(solution)/shard_map/ppermute | solution.py:456
  28.5 8.6 %collective-permute-start.3 = (f32[12,1024]{1,0:T(8,128)S(1)}, f32[12,1024]{1,0:T(8,128)S(1)}, u32[]{:S(2)}, u32[]{:S(2)}) collective-permute-start(f32[12,1024]{1,0:T(8,128)S(1)} %shard_map.97.refs_0_.refs_4_), channel_id=1, source_target_pairs={{0,16},{4,20},{8,24},{12,28},{16,0},{20,4},{24,8},{28,12},{1,17},{... | collective-permute-start | bytes 147464 | tf_op jit(solution)/shard_map/ppermute | solution.py:443
  37.1 4.3 %copy-start.1 = (f32[3,4096]{1,0:T(4,128)S(1)}, f32[3,4096]{1,0:T(4,128)}, u32[]{:S(2)}) copy-start(f32[3,4096]{1,0:T(4,128)} %refs_2_.1) | copy-start | bytes 147460
  37.1 4.3 %collective-permute-start.4 = (f32[12,1024]{1,0:T(8,128)S(1)}, f32[12,1024]{1,0:T(8,128)S(1)}, u32[]{:S(2)}, u32[]{:S(2)}) collective-permute-start(f32[12,1024]{1,0:T(8,128)S(1)} %shard_map.98.refs_0_), channel_id=1, source_target_pairs={{0,4},{4,0},{8,12},{12,8},{16,20},{20,16},{24,28},{28,24},{1,5},{5... | collective-permute-start | bytes 147464 | tf_op jit(solution)/shard_map/ppermute | solution.py:443
  41.5 9.8 %collective-permute-start.8 = (bf16[256,768]{1,0:T(8,128)(2,1)S(1)}, bf16[256,768]{1,0:T(8,128)(2,1)S(1)}, u32[]{:S(2)}, u32[]{:S(2)}) collective-permute-start(bf16[256,768]{1,0:T(8,128)(2,1)S(1)} %get-tuple-element.31), channel_id=1, source_target_pairs={{0,2},{1,3},{2,0},{3,1},{4,6},{5,7},{6,4},{7,5},{8,10},{9,11},{10,... | collective-permute-start | bytes 1179656 | tf_op jit(solution)/shard_map/ppermute | solution.py:455
  43.4 9.3 %collective-permute-start.9 = (bf16[256,256]{1,0:T(8,128)(2,1)S(1)}, bf16[256,256]{1,0:T(8,128)(2,1)S(1)}, u32[]{:S(2)}, u32[]{:S(2)}) collective-permute-start(bf16[256,256]{1,0:T(8,128)(2,1)S(1)} %get-tuple-element.32), channel_id=1, source_target_pairs={{0,2},{1,3},{2,0},{3,1},{4,6},{5,7},{6,4},{7,5},{8,10},{9,11},{10,... | collective-permute-start | bytes 393224 | tf_op jit(solution)/shard_map/ppermute | solution.py:455
  53.9 1.2 %collective-permute-start.10 = (f32[512]{0:T(512)S(1)}, f32[512]{0:T(512)S(1)}, u32[]{:S(2)}, u32[]{:S(2)}) collective-permute-start(f32[512]{0:T(512)S(1)} %bitcast.7), channel_id=1, source_target_pairs={{0,1},{1,0},{2,3},{3,2},{4,5},{5,4},{6,7},{7,6},{8,9},{9,8},{10,11... | collective-permute-start | bytes 6152 | tf_op jit(solution)/shard_map/ppermute | solution.py:480
  55.1 3.6 %collective-permute-start.11 = (f32[512]{0:T(512)S(1)}, f32[512]{0:T(512)S(1)}, u32[]{:S(2)}, u32[]{:S(2)}) collective-permute-start(f32[512]{0:T(512)S(1)} %add.6), channel_id=1, source_target_pairs={{0,2},{1,3},{2,0},{3,1},{4,6},{5,7},{6,4},{7,5},{8,10},{9,11},{10,... | collective-permute-start | bytes 6152 | tf_op jit(solution)/shard_map/ppermute | solution.py:480

commit v10 on v9

--- a/solution.py
+++ b/solution.py
@@ -44,19 +44,20 @@
     out_ref[...] = left_ref[...] + right_ref[...]
 
 
-def gather_kernel(shared_ref, shapes_ref, up_ref, down_ref, held_ref, sem):
+def gather_kernel(shared_ref, shapes_ref, first_ref, second_ref, held_ref, sem):
     dims, nodes, _ = held_ref.shape
     width = shared_ref.shape[1]
     load = pltpu.make_async_copy(shapes_ref, held_ref, sem)
     load.start()
     node = lax.broadcasted_iota(jnp.int32, (nodes, 2 * width), 0)
-    wanted = jnp.concatenate([shared_ref[1:2, :], shared_ref[0:1, :]], axis=1)
+    odd = lax.axis_index("dom") & 1
+    wanted = jnp.concatenate([shared_ref[pl.ds(1 - odd, 1), :], shared_ref[pl.ds(odd, 1), :]], axis=1)
     pick = jnp.where(node == wanted, 1.0, 0.0).astype(F32).T.astype(BF16)
     load.wait()
     for d in range(dims):
         got = jnp.dot(pick, held_ref[d], preferred_element_type=F32).astype(BF16)
-        up_ref[d * width : (d + 1) * width, :] = got[:width]
-        down_ref[d * width : (d + 1) * width, :] = got[width:]
+        first_ref[d * width : (d + 1) * width, :] = got[:width]
+        second_ref[d * width : (d + 1) * width, :] = got[width:]
 
 
 def stats_kernel(mass_ref, shapes_ref, out_ref, mass_scr):
@@ -85,6 +86,10 @@
     taken = slots * elems
     span = pick_ref.shape[1]
     node = lax.broadcasted_iota(jnp.int32, (span, elems), 0)
+    width = (span - nodes) // 2
+    even = 1 - (lax.axis_index("dom") & 1)
+    swapped = jnp.where(node < nodes + width, node + width, node - width)
+    node = jnp.where((node >= nodes) & (even == 1), swapped, node)
     for s in range(0, slots, 2):
         picks = []
         for q in range(s, min(s + 2, slots)):
@@ -202,17 +207,17 @@
         fill_rho(row_scr, col_scr, out_ref, j * tile, 0, block, 8, j * tile, tile)
 
 
-def forces_kernel(dims, rim_ref, low_ref, high_ref, local_ref, all_ref, *refs):
+def forces_kernel(dims, rim_ref, first_ref, second_ref, local_ref, all_ref, *refs):
     part_refs, rim_scr = refs[:-1], refs[-1]
     comps, block = all_ref.shape
-    width = low_ref.shape[0] // dims
+    width = first_ref.shape[0] // dims
     part = comps // 2
     rows = pl.ds(pl.multiple_of(place()[5] * part, part), part)
     for copy in range(2):
         for d in range(dims):
             base = (copy * dims + d) * 2 * width
-            rim_scr[base : base + width, :] = low_ref[d * width : (d + 1) * width, :]
-            rim_scr[base + width : base + 2 * width, :] = high_ref[d * width : (d + 1) * width, :]
+            rim_scr[base : base + width, :] = first_ref[d * width : (d + 1) * width, :]
+            rim_scr[base + width : base + 2 * width, :] = second_ref[d * width : (d + 1) * width, :]
     for c in range(0, block, 256):
         total = jnp.dot(rim_ref[...], rim_scr[:, c : c + 256], preferred_element_type=F32)
         all_ref[:, c : c + 256] = (local_ref[:, c : c + 256] + total).astype(BF16)
@@ -251,10 +256,9 @@
     elems = acc.shape[0] // per_elem
     for k in range(per_elem):
         turned[pl.ds(k, elems, stride=per_elem), :] = acc[k * elems : (k + 1) * elems, :]
-    ones = jnp.ones((8, acc.shape[1]), F32)
+    pieces = jnp.concatenate([piece.astype(BF16) for piece in split(turned[...])], axis=1)
     return lax.dot_general(
-        ones, turned[...], (((1,), (1,)), ((), ())),
-        precision=lax.Precision.HIGHEST, preferred_element_type=F32,
+        jnp.ones((8, pieces.shape[1]), BF16), pieces, (((1,), (1,)), ((), ())), preferred_element_type=F32
     )[0:1]
 
 
@@ -388,16 +392,17 @@
     width = shared.shape[1]
     parts = lax.axis_size("dom")
     sds = jax.ShapeDtypeStruct
-    ahead = [(i, i + 1) for i in range(parts - 1)]
-    back = [(i + 1, i) for i in range(parts - 1)]
+    halves = [[], []]
+    for i in range(parts - 1):
+        halves[i % 2] += [(i, i + 1), (i + 1, i)]
     freq = frequencies.reshape(1, -1)
     rate = damping.reshape(1, -1)
 
-    up, down, held = call(
+    outgoing, other, held = call(
         gather_kernel, [sds((dims * width, block), BF16)] * 2 + [sds(shapes.shape, BF16)], (shared, shapes),
         2.0, hbm=(1,), scratch=[pltpu.SemaphoreType.DMA],
     )
-    low, high = lax.ppermute(up, "dom", ahead), lax.ppermute(down, "dom", back)
+    rims = (lax.ppermute(outgoing, "dom", halves[0]), lax.ppermute(other, "dom", halves[1]))
     stats = call(
         stats_kernel, sds((dims + 1, block), F32), (masses.reshape(1, nodes), held), 0.8,
         scratch=[pltpu.VMEM((nodes, 128), F32)],
@@ -449,7 +454,7 @@
     forces, *sent = call(
         functools.partial(forces_kernel, dims),
         [sds((comps, block), BF16)] + [sds((part, cut), BF16) for cut in cuts],
-        (rim, low, high, local), 1.4,
+        (rim, *rims, local), 1.4,
         scratch=[pltpu.VMEM((4 * dims * width, block), BF16)], after=(first,),
     )
     far = [lax.ppermute(value, "mode", [(i, i ^ 2) for i in range(4)]) for value in sent]

time: 59.5 us -> 56.5 us (0.950)
  starting transfers between devices: 19.5 us -> 16.5 us
    ppermute x2, starting transfers between devices: 4.7 us -> 2.17 us  [the longest x1 1.5 us: combined(): lax.ppermute(outgoing, 'dom', halves[0])]
    ppermute x2, waiting for transfers between devices: 1.87 us -> 2.92 us  [the longest x1 2.92 us: combined(): lax.ppermute(outgoing, 'dom', halves[0])]
    ppermute x3, waiting for transfers between devices: 9.72 us -> 8.81 us  [combined(): extra = lax.ppermute(stats, 'dom', [(i, i ^ reach) for i in range(parts)])]
  transfers between devices with their start and end apart: 12 -> 12, of which waited for: 8 -> 8; matrix products, arithmetic and copies ran while one was open for 0% -> 0% of each run, Pallas kernels for 22% -> 23%
where the time goes in v10:
time: 56.5 us; the launch traced here: 56.4 us
  waiting for transfers between devices  20.3 us (36%)
  Pallas kernels  16.6 us (29%)
  starting transfers between devices  16.5 us (29%)
  local copies, waits for them, and re-layouts  2.13 us (4%)
  other arithmetic  0.58 us (1%)
    pallas_call x15, Pallas kernels, call(): pl.pallas_call(body, out_shape=out_shape, in_specs=specs, out_specs=[VMEM...  16.6 us
    ppermute x3, waiting for transfers between devices, combined(): extra = lax.ppermute(stats, 'dom', [(i, i ^ reach) for i in range(parts)])  8.81 us
    ppermute x3, starting transfers between devices, combined(): extra = lax.ppermute(stats, 'dom', [(i, i ^ reach) for i in range(parts)])  8.53 us
    ppermute x2, waiting for transfers between devices, combined(): lax.ppermute(value, 'mode', [(i, i ^ reach) for i in range(4)])  4.32 us
    ppermute x2, waiting for transfers between devices, combined(): lax.ppermute(value, 'mode', [(i, i ^ 2) for i in range(4)])  4.23 us
    ppermute x2, starting transfers between devices, combined(): lax.ppermute(stats, 'mode', [(i, i ^ q) for i in range(4)])  3.13 us
    ppermute x1, waiting for transfers between devices, combined(): lax.ppermute(outgoing, 'dom', halves[0])  2.92 us
    ppermute x2, starting transfers between devices, combined(): lax.ppermute(value, 'mode', [(i, i ^ 2) for i in range(4)])  2.16 us
  transfers between devices with their start and end apart: 12, of which 8 were waited for; matrix products, arithmetic and copies ran while one was open for 0% of the time, Pallas kernels for 23%

profile of v10, /device:TPU:0, one launch (start us, length us, event | category | flops | bytes accessed | tf_op | source)
XLA Modules:
  0.0 56.4 jit_solution(108903553811774782)
XLA Ops:
  0.0 0.0 copy-start
  0.0 1.4 %copy-done = bf16[3,256,1024]{2,1,0:T(8,128)(2,1)S(1)} copy-done((bf16[3,256,1024]{2,1,0:T(8,128)(2,1)S(1)}, bf16[3,256,1024]{2,1,0:T(8,128)(2,1)}, u32[]{:S(2)}) %copy-start) | copy-done | bytes 1572888
  1.4 0.0 copy-start.6
  1.4 0.7 %copy-done.6 = s32[2,64]{1,0:T(2,128)S(1)} copy-done((s32[2,64]{1,0:T(2,128)S(1)}, s32[2,64]{1,0:T(2,128)}, u32[]{:S(2)}) %copy-start.6) | copy-done | bytes 536
  2.1 0.0 copy-start.7
  2.1 0.7 %shard_map.91 = (bf16[192,1024]{1,0:T(8,128)(2,1)S(1)}, bf16[192,1024]{1,0:T(8,128)(2,1)S(1)}, bf16[3,256,1024]{2,1,0:T(8,128)(2,1)S(1)}) custom-call(s32[2,64]{1,0:T(2,128)S(1)} %copy-done.6, bf16[3,256,1024]{2,1,0:T(8,128)(2,1)S(1)} %copy-done), custom_call_target="tpu_custom_call" | custom-call | flops 2200000000 | tf_op jit(solution)/shard_map/pallas_call | solution.py:27
  2.8 0.0 copy-start.3
  2.8 0.0 copy-start.4
  2.8 0.0 copy-done.7
  2.8 0.8 %shard_map.92.refs_0_.refs_2_ = f32[4,1024]{1,0:T(4,128)S(1)} custom-call(f32[1,256]{1,0:T(1,128)S(1)} %bitcast.19, bf16[3,256,1024]{2,1,0:T(8,128)(2,1)S(1)} %get-tuple-element.19.refs_1_.refs_3_), custom_call_target="tpu_custom_call" | custom-call | flops 880000000 | tf_op jit(solution)/shard_map/pallas_call | solution.py:27
  3.6 0.6 collective-permute-start
  4.2 2.6 %collective-permute-start.1 = (f32[4,1024]{1,0:T(4,128)S(1)}, f32[4,1024]{1,0:T(4,128)S(1)}, u32[]{:S(2)}, u32[]{:S(2)}) collective-permute-start(f32[4,1024]{1,0:T(4,128)S(1)} %shard_map.92.refs_0_.refs_2_), channel_id=1, source_target_pairs={{0,2},{1,3},{2,0},{3,1},{4,6},{5,7},{6,4},{7,5},{8,10},{9,11},{10,... | collective-permute-start | bytes 49160 | tf_op jit(solution)/shard_map/ppermute | solution.py:434
  6.8 1.5 %collective-permute-start.5 = (bf16[192,1024]{1,0:T(8,128)(2,1)S(1)}, bf16[192,1024]{1,0:T(8,128)(2,1)S(1)}, u32[]{:S(2)}, u32[]{:S(2)}) collective-permute-start(bf16[192,1024]{1,0:T(8,128)(2,1)S(1)} %get-tuple-element.26), channel_id=1, source_target_pairs={{0,4},{4,0},{8,12},{12,8},{16,20},{20,16},{24,28},{28,24},{1,5},{5... | collective-permute-start | bytes 1179656 | tf_op jit(solution)/shard_map/ppermute | solution.py:405
  8.3 0.7 %collective-permute-start.6 = (bf16[192,1024]{1,0:T(8,128)(2,1)S(1)}, bf16[192,1024]{1,0:T(8,128)(2,1)S(1)}, u32[]{:S(2)}, u32[]{:S(2)}) collective-permute-start(bf16[192,1024]{1,0:T(8,128)(2,1)S(1)} %get-tuple-element.27), channel_id=1, source_target_pairs={{4,8},{8,4},{12,16},{16,12},{20,24},{24,20},{5,9},{9,5},{13,17},{1... | collective-permute-start | bytes 1179656 | tf_op jit(solution)/shard_map/ppermute | solution.py:405
  8.9 0.0 copy-done.3
  9.0 0.0 copy-done.4
  9.0 2.4 %shard_map.94 = (f32[1024,1024]{1,0:T(8,128)S(1)}, f32[2,512,512]{2,1,0:T(8,128)S(1)}, f32[4,1024,128]{2,1,0:T(8,128)S(1)}) custom-call(f32[1,4096]{1,0:T(1,128)S(1)} %bitcast.10, f32[1,4096]{1,0:T(1,128)S(1)} %bitcast.14, f32[4,1024]{1,0:T(4,128)S(1)} %shard_map.92.refs_0_.refs_2_), custom_call_target="tpu_custom_call" | custom-call | flops 3300000000 | tf_op jit(solution)/shard_map/pallas_call | solution.py:27
  11.4 0.0 copy-start.2
  11.4 0.0 copy-start.5
  11.4 0.0 copy-start.8
  11.4 1.6 %shard_map.95.refs_4_.refs_3_ = f32[1024,1024]{1,0:T(8,128)S(1)} custom-call(f32[1,4096]{1,0:T(1,128)S(1)} %bitcast.11, f32[1,4096]{1,0:T(1,128)S(1)} %bitcast.15, f32[4,1024,128]{2,1,0:T(8,128)S(1)} %get-tuple-element.20.refs_2_), custom_call_target="tpu_custom_call" | custom-call | flops 2090000000 | tf_op jit(solution)/shard_map/pallas_call | solution.py:27
  13.0 0.0 collective-permute-done.refs_1_
  13.0 0.0 collective-permute-done.1.refs_2_
  13.0 3.3 %collective-permute-start.2 = (f32[12,1024]{1,0:T(8,128)S(1)}, f32[12,1024]{1,0:T(8,128)S(1)}, u32[]{:S(2)}, u32[]{:S(2)}) collective-permute-start(f32[12,1024]{1,0:T(8,128)S(1)} %shard_map.93.refs_0_), channel_id=1, source_target_pairs={{0,8},{4,12},{8,0},{12,4},{16,24},{20,28},{24,16},{28,20},{1,9},{5... | collective-permute-start | bytes 147464 | tf_op jit(solution)/shard_map/ppermute | solution.py:448
  16.3 0.0 copy-done.2
  16.3 0.0 copy-done.5
  16.3 0.0 copy-done.8
  16.3 1.8 %shard_map.96 = (f32[512,1024]{1,0:T(8,128)S(1)}, bf16[512,768]{1,0:T(8,128)(2,1)S(1)}) custom-call(s32[4,64]{1,0:T(4,128)S(1)} %bitcast.18, s32[1,64]{1,0:T(1,128)S(1)} %bitcast.20, bf16[8,3,4,64]{3,2,1,0:T(4,128)(2,1)S(1)} %bitcast.9, bf16[3,256,1024]{2,1,0:T(8,128)(2,1)S(1)} %get-tuple-element.19.refs_1_.refs_3_, f32[1024,1024]{1,0:T(8,128)S(1)} %shard_map.95.refs_4_.refs_3_), custom_call_target="tpu_custom_call" | custom-call | flops 1980000000 | tf_op jit(solution)/shard_map/pallas_call | solution.py:27
  18.1 4.3 %collective-permute-done.2.refs_1_ = f32[12,1024]{1,0:T(8,128)S(1)} collective-permute-done((f32[12,1024]{1,0:T(8,128)S(1)}, f32[12,1024]{1,0:T(8,128)S(1)}, u32[]{:S(2)}, u32[]{:S(2)}) %collective-permute-start.2) | collective-permute-done | bytes 49184 | tf_op jit(solution)/shard_map/ppermute | solution.py:448
  22.5 2.9 %collective-permute-done.5.refs_1_ = bf16[192,1024]{1,0:T(8,128)(2,1)S(1)} collective-permute-done((bf16[192,1024]{1,0:T(8,128)(2,1)S(1)}, bf16[192,1024]{1,0:T(8,128)(2,1)S(1)}, u32[]{:S(2)}, u32[]{:S(2)}) %collective-permute-start.5) | collective-permute-done | bytes 393248 | tf_op jit(solution)/shard_map/ppermute | solution.py:405
  25.4 0.0 collective-permute-done.6.refs_2_
  25.4 1.1 %shard_map.100 = (bf16[512,1024]{1,0:T(8,128)(2,1)S(1)}, bf16[256,768]{1,0:T(8,128)(2,1)S(1)}, bf16[256,256]{1,0:T(8,128)(2,1)S(1)}) custom-call(bf16[512,768]{1,0:T(8,128)(2,1)S(1)} %get-tuple-element.21.refs_2_.refs_0_, bf16[192,1024]{1,0:T(8,128)(2,1)S(1)} %collective-permute-done.5.refs_1_, bf16[192,1024]{1,0:T(8,128)(2,1)S(1)} %collective-permute-done.6.refs_2_, ...), custom_call_target="tpu_custom_call" | custom-call | flops 1540000000 | tf_op jit(solution)/shard_map/pallas_call | solution.py:27
  26.5 0.1 collective-permute-start.7
  26.6 3.6 %collective-permute-start.3 = (f32[12,1024]{1,0:T(8,128)S(1)}, f32[12,1024]{1,0:T(8,128)S(1)}, u32[]{:S(2)}, u32[]{:S(2)}) collective-permute-start(f32[12,1024]{1,0:T(8,128)S(1)} %shard_map.97.refs_0_.refs_4_), channel_id=1, source_target_pairs={{0,16},{4,20},{8,24},{12,28},{16,0},{20,4},{24,8},{28,12},{1,17},{... | collective-permute-start | bytes 147464 | tf_op jit(solution)/shard_map/ppermute | solution.py:448
  30.2 4.1 %collective-permute-done.3.refs_1_ = f32[12,1024]{1,0:T(8,128)S(1)} collective-permute-done((f32[12,1024]{1,0:T(8,128)S(1)}, f32[12,1024]{1,0:T(8,128)S(1)}, u32[]{:S(2)}, u32[]{:S(2)}) %collective-permute-start.3) | collective-permute-done | bytes 49184 | tf_op jit(solution)/shard_map/ppermute | solution.py:448
  34.3 0.0 copy-start.1
  34.3 1.6 %collective-permute-start.4 = (f32[12,1024]{1,0:T(8,128)S(1)}, f32[12,1024]{1,0:T(8,128)S(1)}, u32[]{:S(2)}, u32[]{:S(2)}) collective-permute-start(f32[12,1024]{1,0:T(8,128)S(1)} %shard_map.98.refs_0_), channel_id=1, source_target_pairs={{0,4},{4,0},{8,12},{12,8},{16,20},{20,16},{24,28},{28,24},{1,5},{5... | collective-permute-start | bytes 147464 | tf_op jit(solution)/shard_map/ppermute | solution.py:448
  35.9 2.3 %shard_map.102.refs_4_ = f32[1024,1024]{1,0:T(8,128)S(1)} custom-call(f32[1,4096]{1,0:T(1,128)S(1)} %bitcast.12, f32[1,4096]{1,0:T(1,128)S(1)} %bitcast.16), custom_call_target="tpu_custom_call" | custom-call | flops 2750000128 | tf_op jit(solution)/shard_map/pallas_call | solution.py:27
  38.3 0.4 collective-permute-done.4.refs_1_
  38.7 0.0 copy-done.1
  38.7 0.5 collective-permute-start.8
  39.2 1.4 %shard_map.103.refs_1_ = bf16[2048,1024]{1,0:T(8,128)(2,1)S(1)} custom-call(f32[8,1024]{1,0:T(8,128)S(1)} %get-tuple-element.22.refs_0_, f32[8,1024]{1,0:T(8,128)S(1)} %get-tuple-element.23.refs_1_, f32[8,1024]{1,0:T(8,128)S(1)} %get-tuple-element.30.refs_2_, f32[1024,1024]{1,0:T(8,128)S(1)} %shard_map.95.refs_4_.refs_3_, f32[1024,1024]{1,0:T(8,128)S(1)} %shard_map.102.refs_4_), custom_call_target="tpu_custom_call" | custom-call | flops 1540000000 | tf_op jit(solution)/shard_map/pallas_call | solution.py:27
  40.6 1.6 %collective-permute-start.9 = (bf16[256,256]{1,0:T(8,128)(2,1)S(1)}, bf16[256,256]{1,0:T(8,128)(2,1)S(1)}, u32[]{:S(2)}, u32[]{:S(2)}) collective-permute-start(bf16[256,256]{1,0:T(8,128)(2,1)S(1)} %get-tuple-element.32), channel_id=1, source_target_pairs={{0,2},{1,3},{2,0},{3,1},{4,6},{5,7},{6,4},{7,5},{8,10},{9,11},{10,... | collective-permute-start | bytes 393224 | tf_op jit(solution)/shard_map/ppermute | solution.py:460
  42.2 0.0 collective-permute-done.7.refs_5_.refs_4_
  42.2 2.7 %shard_map.101.refs_0_ = f32[512,128]{1,0:T(8,128)S(1)} custom-call(f32[8,1024]{1,0:T(8,128)S(1)} %get-tuple-element.22.refs_0_, f32[8,1024]{1,0:T(8,128)S(1)} %get-tuple-element.23.refs_1_, f32[1024,1024]{1,0:T(8,128)S(1)} %get-tuple-element.24.refs_2_, f32[2,512,512]{2,1,0:T(8,128)S(1)} %get-tuple-element.25.refs_3_, ...), custom_call_target="tpu_custom_call" | custom-call | flops 3740000000 | tf_op jit(solution)/shard_map/pallas_call | solution.py:27
  44.9 3.8 %collective-permute-done.8.refs_2_ = bf16[256,768]{1,0:T(8,128)(2,1)S(1)} collective-permute-done((bf16[256,768]{1,0:T(8,128)(2,1)S(1)}, bf16[256,768]{1,0:T(8,128)(2,1)S(1)}, u32[]{:S(2)}, u32[]{:S(2)}) %collective-permute-start.8) | collective-permute-done | bytes 393248 | tf_op jit(solution)/shard_map/ppermute | solution.py:460
  48.7 1.0 %shard_map.104.refs_0_ = f32[512,128]{1,0:T(8,128)S(1)} custom-call(f32[512,128]{1,0:T(8,128)S(1)} %shard_map.101.refs_0_, bf16[2048,1024]{1,0:T(8,128)(2,1)S(1)} %shard_map.103.refs_1_, bf16[256,768]{1,0:T(8,128)(2,1)S(1)} %collective-permute-done.8.refs_2_, bf16[512,1024]{1,0:T(8,128)(2,1)S(1)} %get-tuple-element.29.refs_4_.refs_3_, ...), custom_call_target="tpu_custom_call" | custom-call | flops 1732499968 | tf_op jit(solution)/shard_map/pallas_call | solution.py:27
  49.7 0.4 collective-permute-done.9.refs_2_
  50.1 0.9 %shard_map.105 = f32[1,512]{1,0:T(1,128)S(1)} custom-call(f32[512,128]{1,0:T(8,128)S(1)} %shard_map.104.refs_0_, bf16[2048,1024]{1,0:T(8,128)(2,1)S(1)} %shard_map.103.refs_1_, bf16[256,256]{1,0:T(8,128)(2,1)S(1)} %collective-permute-done.9.refs_2_, bf16[512,1024]{1,0:T(8,128)(2,1)S(1)} %get-tuple-element.29.refs_4_.refs_3_, ...), custom_call_target="tpu_custom_call" | custom-call | flops 577500032 | tf_op jit(solution)/shard_map/pallas_call | solution.py:27
  51.0 0.0 collective-permute-start.10
  51.0 1.2 %collective-permute-done.10 = f32[512]{0:T(512)S(1)} collective-permute-done((f32[512]{0:T(512)S(1)}, f32[512]{0:T(512)S(1)}, u32[]{:S(2)}, u32[]{:S(2)}) %collective-permute-start.10) | collective-permute-done | bytes 2080 | tf_op jit(solution)/shard_map/ppermute | solution.py:485
  52.2 0.5 collective-permute-start.11
  52.7 3.1 %collective-permute-done.11 = f32[512]{0:T(512)S(1)} collective-permute-done((f32[512]{0:T(512)S(1)}, f32[512]{0:T(512)S(1)}, u32[]{:S(2)}, u32[]{:S(2)}) %collective-permute-start.11) | collective-permute-done | bytes 2080 | tf_op jit(solution)/shard_map/ppermute | solution.py:485
  55.8 0.6 %add.7 = f32[512]{0:T(512)} add(f32[512]{0:T(512)S(1)} %add.6, f32[512]{0:T(512)S(1)} %collective-permute-done.11) | non-fusion elementwise | flops 512 | bytes 6144 | tf_op jit(solution)/shard_map/add | solution.py:485
  (5 shorter events, 0.1 us)
Async XLA Ops:
  0.0 1.4 %copy-start = (bf16[3,256,1024]{2,1,0:T(8,128)(2,1)S(1)}, bf16[3,256,1024]{2,1,0:T(8,128)(2,1)}, u32[]{:S(2)}) copy-start(bf16[3,256,1024]{2,1,0:T(8,128)(2,1)} %refs_1_.1) | copy-start | bytes 4718596
  1.4 0.7 %copy-start.6 = (s32[2,64]{1,0:T(2,128)S(1)}, s32[2,64]{1,0:T(2,128)}, u32[]{:S(2)}) copy-start(s32[2,64]{1,0:T(2,128)} %refs_0_.1) | copy-start | bytes 1540
  2.1 0.7 %copy-start.7 = (f32[256]{0:T(256)S(1)}, f32[256]{0:T(256)}, u32[]{:S(2)}) copy-start(f32[256]{0:T(256)} %param.10) | copy-start | bytes 3076
  2.8 6.2 %copy-start.3 = (f32[4096]{0:T(1024)S(1)}, f32[4096]{0:T(1024)}, u32[]{:S(2)}) copy-start(f32[4096]{0:T(1024)} %param.12) | copy-start | bytes 49156
  2.8 6.2 %copy-start.4 = (f32[4096]{0:T(1024)S(1)}, f32[4096]{0:T(1024)}, u32[]{:S(2)}) copy-start(f32[4096]{0:T(1024)} %param.13) | copy-start | bytes 49156
  3.6 9.4 %collective-permute-start = (f32[4,1024]{1,0:T(4,128)S(1)}, f32[4,1024]{1,0:T(4,128)S(1)}, u32[]{:S(2)}, u32[]{:S(2)}) collective-permute-start(f32[4,1024]{1,0:T(4,128)S(1)} %shard_map.92.refs_0_.refs_2_), channel_id=1, source_target_pairs={{0,1},{1,0},{2,3},{3,2},{4,5},{5,4},{6,7},{7,6},{8,9},{9,8},{10,11... | collective-permute-start | bytes 49160 | tf_op jit(solution)/shard_map/ppermute | solution.py:434
  4.2 8.8 %collective-permute-start.1 = (f32[4,1024]{1,0:T(4,128)S(1)}, f32[4,1024]{1,0:T(4,128)S(1)}, u32[]{:S(2)}, u32[]{:S(2)}) collective-permute-start(f32[4,1024]{1,0:T(4,128)S(1)} %shard_map.92.refs_0_.refs_2_), channel_id=1, source_target_pairs={{0,2},{1,3},{2,0},{3,1},{4,6},{5,7},{6,4},{7,5},{8,10},{9,11},{10,... | collective-permute-start | bytes 49160 | tf_op jit(solution)/shard_map/ppermute | solution.py:434
  6.8 18.6 %collective-permute-start.5 = (bf16[192,1024]{1,0:T(8,128)(2,1)S(1)}, bf16[192,1024]{1,0:T(8,128)(2,1)S(1)}, u32[]{:S(2)}, u32[]{:S(2)}) collective-permute-start(bf16[192,1024]{1,0:T(8,128)(2,1)S(1)} %get-tuple-element.26), channel_id=1, source_target_pairs={{0,4},{4,0},{8,12},{12,8},{16,20},{20,16},{24,28},{28,24},{1,5},{5... | collective-permute-start | bytes 1179656 | tf_op jit(solution)/shard_map/ppermute | solution.py:405
  8.3 17.1 %collective-permute-start.6 = (bf16[192,1024]{1,0:T(8,128)(2,1)S(1)}, bf16[192,1024]{1,0:T(8,128)(2,1)S(1)}, u32[]{:S(2)}, u32[]{:S(2)}) collective-permute-start(bf16[192,1024]{1,0:T(8,128)(2,1)S(1)} %get-tuple-element.27), channel_id=1, source_target_pairs={{4,8},{8,4},{12,16},{16,12},{20,24},{24,20},{5,9},{9,5},{13,17},{1... | collective-permute-start | bytes 1179656 | tf_op jit(solution)/shard_map/ppermute | solution.py:405
  11.4 4.9 %copy-start.2 = (bf16[64,8,4,3]{0,2,3,1:T(4,128)(2,1)S(1)}, bf16[64,8,4,3]{0,2,3,1:T(4,128)(2,1)}, u32[]{:S(2)}) copy-start(bf16[64,8,4,3]{0,2,3,1:T(4,128)(2,1)} %param.14) | copy-start | bytes 36868
  11.4 4.9 %copy-start.5 = (s32[64,4]{0,1:T(4,128)S(1)}, s32[64,4]{0,1:T(4,128)}, u32[]{:S(2)}) copy-start(s32[64,4]{0,1:T(4,128)} %param.15) | copy-start | bytes 3076
  11.4 4.9 %copy-start.8 = (s32[64]{0:T(128)S(1)}, s32[64]{0:T(128)}, u32[]{:S(2)}) copy-start(s32[64]{0:T(128)} %param.16) | copy-start | bytes 772
  13.0 9.4 %collective-permute-start.2 = (f32[12,1024]{1,0:T(8,128)S(1)}, f32[12,1024]{1,0:T(8,128)S(1)}, u32[]{:S(2)}, u32[]{:S(2)}) collective-permute-start(f32[12,1024]{1,0:T(8,128)S(1)} %shard_map.93.refs_0_), channel_id=1, source_target_pairs={{0,8},{4,12},{8,0},{12,4},{16,24},{20,28},{24,16},{28,20},{1,9},{5... | collective-permute-start | bytes 147464 | tf_op jit(solution)/shard_map/ppermute | solution.py:448
  26.5 15.7 %collective-permute-start.7 = (bf16[512,1024]{1,0:T(8,128)(2,1)S(1)}, bf16[512,1024]{1,0:T(8,128)(2,1)S(1)}, u32[]{:S(2)}, u32[]{:S(2)}) collective-permute-start(bf16[512,1024]{1,0:T(8,128)(2,1)S(1)} %get-tuple-element.29.refs_4_.refs_3_), channel_id=1, source_target_pairs={{0,1},{1,0},{2,3},{3,2},{4,5},{5,4},{6,7},{7,6},{8,9},{9,8},{10,11... | collective-permute-start | bytes 3145736 | tf_op jit(solution)/shard_map/ppermute | solution.py:461
  26.6 7.7 %collective-permute-start.3 = (f32[12,1024]{1,0:T(8,128)S(1)}, f32[12,1024]{1,0:T(8,128)S(1)}, u32[]{:S(2)}, u32[]{:S(2)}) collective-permute-start(f32[12,1024]{1,0:T(8,128)S(1)} %shard_map.97.refs_0_.refs_4_), channel_id=1, source_target_pairs={{0,16},{4,20},{8,24},{12,28},{16,0},{20,4},{24,8},{28,12},{1,17},{... | collective-permute-start | bytes 147464 | tf_op jit(solution)/shard_map/ppermute | solution.py:448
  34.3 4.3 %copy-start.1 = (f32[3,4096]{1,0:T(4,128)S(1)}, f32[3,4096]{1,0:T(4,128)}, u32[]{:S(2)}) copy-start(f32[3,4096]{1,0:T(4,128)} %refs_2_.1) | copy-start | bytes 147460
  34.3 4.3 %collective-permute-start.4 = (f32[12,1024]{1,0:T(8,128)S(1)}, f32[12,1024]{1,0:T(8,128)S(1)}, u32[]{:S(2)}, u32[]{:S(2)}) collective-permute-start(f32[12,1024]{1,0:T(8,128)S(1)} %shard_map.98.refs_0_), channel_id=1, source_target_pairs={{0,4},{4,0},{8,12},{12,8},{16,20},{20,16},{24,28},{28,24},{1,5},{5... | collective-permute-start | bytes 147464 | tf_op jit(solution)/shard_map/ppermute | solution.py:448
  38.7 10.0 %collective-permute-start.8 = (bf16[256,768]{1,0:T(8,128)(2,1)S(1)}, bf16[256,768]{1,0:T(8,128)(2,1)S(1)}, u32[]{:S(2)}, u32[]{:S(2)}) collective-permute-start(bf16[256,768]{1,0:T(8,128)(2,1)S(1)} %get-tuple-element.31), channel_id=1, source_target_pairs={{0,2},{1,3},{2,0},{3,1},{4,6},{5,7},{6,4},{7,5},{8,10},{9,11},{10,... | collective-permute-start | bytes 1179656 | tf_op jit(solution)/shard_map/ppermute | solution.py:460
  40.6 9.5 %collective-permute-start.9 = (bf16[256,256]{1,0:T(8,128)(2,1)S(1)}, bf16[256,256]{1,0:T(8,128)(2,1)S(1)}, u32[]{:S(2)}, u32[]{:S(2)}) collective-permute-start(bf16[256,256]{1,0:T(8,128)(2,1)S(1)} %get-tuple-element.32), channel_id=1, source_target_pairs={{0,2},{1,3},{2,0},{3,1},{4,6},{5,7},{6,4},{7,5},{8,10},{9,11},{10,... | collective-permute-start | bytes 393224 | tf_op jit(solution)/shard_map/ppermute | solution.py:460
  51.0 1.2 %collective-permute-start.10 = (f32[512]{0:T(512)S(1)}, f32[512]{0:T(512)S(1)}, u32[]{:S(2)}, u32[]{:S(2)}) collective-permute-start(f32[512]{0:T(512)S(1)} %bitcast.7), channel_id=1, source_target_pairs={{0,1},{1,0},{2,3},{3,2},{4,5},{5,4},{6,7},{7,6},{8,9},{9,8},{10,11... | collective-permute-start | bytes 6152 | tf_op jit(solution)/shard_map/ppermute | solution.py:485
  52.2 3.6 %collective-permute-start.11 = (f32[512]{0:T(512)S(1)}, f32[512]{0:T(512)S(1)}, u32[]{:S(2)}, u32[]{:S(2)}) collective-permute-start(f32[512]{0:T(512)S(1)} %add.6), channel_id=1, source_target_pairs={{0,2},{1,3},{2,0},{3,1},{4,6},{5,7},{6,4},{7,5},{8,10},{9,11},{10,... | collective-permute-start | bytes 6152 | tf_op jit(solution)/shard_map/ppermute | solution.py:485

commit v11 on v10

--- a/solution.py
+++ b/solution.py
@@ -44,7 +44,8 @@
     out_ref[...] = left_ref[...] + right_ref[...]
 
 
-def gather_kernel(shared_ref, shapes_ref, first_ref, second_ref, held_ref, sem):
+def gather_kernel(shared_ref, shapes_ref, first_ref, *refs):
+    second_refs, (held_ref, sem) = refs[:-2], refs[-2:]
     dims, nodes, _ = held_ref.shape
     width = shared_ref.shape[1]
     load = pltpu.make_async_copy(shapes_ref, held_ref, sem)
@@ -57,7 +58,11 @@
     for d in range(dims):
         got = jnp.dot(pick, held_ref[d], preferred_element_type=F32).astype(BF16)
         first_ref[d * width : (d + 1) * width, :] = got[:width]
-        second_ref[d * width : (d + 1) * width, :] = got[width:]
+        at = 0
+        for second_ref in second_refs:
+            lanes = slice(at, at + second_ref.shape[1])
+            second_ref[d * width : (d + 1) * width, :] = got[width:, lanes]
+            at = lanes.stop
 
 
 def stats_kernel(mass_ref, shapes_ref, out_ref, mass_scr):
@@ -207,24 +212,20 @@
         fill_rho(row_scr, col_scr, out_ref, j * tile, 0, block, 8, j * tile, tile)
 
 
-def forces_kernel(dims, rim_ref, first_ref, second_ref, local_ref, all_ref, *refs):
-    part_refs, rim_scr = refs[:-1], refs[-1]
-    comps, block = all_ref.shape
+def forces_kernel(at, dims, rim_ref, first_ref, second_ref, local_ref, all_ref, part_ref, rim_scr):
+    comps, chunk = all_ref.shape
     width = first_ref.shape[0] // dims
     part = comps // 2
-    rows = pl.ds(pl.multiple_of(place()[5] * part, part), part)
+    lanes = slice(at, at + chunk)
     for copy in range(2):
         for d in range(dims):
             base = (copy * dims + d) * 2 * width
-            rim_scr[base : base + width, :] = first_ref[d * width : (d + 1) * width, :]
+            rim_scr[base : base + width, :] = first_ref[d * width : (d + 1) * width, lanes]
             rim_scr[base + width : base + 2 * width, :] = second_ref[d * width : (d + 1) * width, :]
-    for c in range(0, block, 256):
+    for c in range(0, chunk, 256):
         total = jnp.dot(rim_ref[...], rim_scr[:, c : c + 256], preferred_element_type=F32)
-        all_ref[:, c : c + 256] = (local_ref[:, c : c + 256] + total).astype(BF16)
-    at = 0
-    for part_ref in part_refs:
-        part_ref[...] = all_ref[rows, at : at + part_ref.shape[1]]
-        at += part_ref.shape[1]
+        all_ref[:, c : c + 256] = (local_ref[:, at + c : at + c + 256] + total).astype(BF16)
+    part_ref[...] = all_ref[pl.ds(pl.multiple_of(place()[5] * part, part), part), :]
 
 
 def join_kernel(*refs):
@@ -359,22 +360,29 @@
                 )
 
 
-def far_kernel(at, per_elem, near_ref, w_ref, far_ref, own_ref, mate_ref, out_ref, *scratch):
-    _, block = own_ref.shape
-    part, chunk = far_ref.shape
+def far_kernel(at, per_elem, chunks, near_ref, w_ref, far_ref, *refs):
+    sides, (out_ref, *scratch) = refs[: 2 * chunks], refs[2 * chunks :]
+    _, chunk = sides[0].shape
+    part = far_ref.shape[0]
     tile = min(256, chunk)
     rows = pl.ds(pl.multiple_of(place()[4] * part, part), part)
     total = near_ref[rows, :]
     for c in range(0, chunk, tile):
         spot = slice(at + c, at + c + tile)
-        got = jnp.dot(own_ref[rows, :], w_ref[:block, spot], preferred_element_type=F32)
-        got = got + jnp.dot(mate_ref[rows, :], w_ref[block:, spot], preferred_element_type=F32)
+        got = None
+        for q, side_ref in enumerate(sides):
+            w = w_ref[q * chunk : (q + 1) * chunk, spot]
+            piece = jnp.dot(side_ref[rows, :], w, preferred_element_type=F32)
+            got = piece if got is None else got + piece
         total = total + fold(got * far_ref[:, c : c + tile].astype(F32))
     acc = scratch[0] if scratch else out_ref
     acc[...] = near_ref[...]
     acc[rows, :] = total
     if scratch:
         out_ref[...] = to_row(acc, scratch[1], per_elem)
+
+
+CHUNKS = 2
 
 
 def four_groups(*args):
@@ -398,11 +406,15 @@
     freq = frequencies.reshape(1, -1)
     rate = damping.reshape(1, -1)
 
-    outgoing, other, held = call(
-        gather_kernel, [sds((dims * width, block), BF16)] * 2 + [sds(shapes.shape, BF16)], (shared, shapes),
+    chunk = block // CHUNKS
+    outgoing, *others, held = call(
+        gather_kernel,
+        [sds((dims * width, size), BF16) for size in [block] + [chunk] * CHUNKS] + [sds(shapes.shape, BF16)],
+        (shared, shapes),
         2.0, hbm=(1,), scratch=[pltpu.SemaphoreType.DMA],
     )
-    rims = (lax.ppermute(outgoing, "dom", halves[0]), lax.ppermute(other, "dom", halves[1]))
+    first_rim = lax.ppermute(outgoing, "dom", halves[0])
+    rims = [lax.ppermute(other, "dom", halves[1]) for other in others]
     stats = call(
         stats_kernel, sds((dims + 1, block), F32), (masses.reshape(1, nodes), held), 0.8,
         scratch=[pltpu.VMEM((nodes, 128), F32)],
@@ -433,7 +445,6 @@
     )
     given = [stats] + [lax.ppermute(stats, "mode", [(i, i ^ q) for i in range(4)]) for q in (1, 2)]
     stats = call(join_kernel, sds((3 * (dims + 1), block), F32), given, 0.5)
-    first = stats
     order = [1 << q for q in range(1, parts.bit_length() - 1)] + [1]
     if parts & (parts - 1) or parts == 1:
         stats = lax.psum(stats, "dom")
@@ -444,24 +455,25 @@
             stats = call(
                 add_kernel, sds(stats.shape, F32), (stats, extra), 0.5, after=(rim,) if q == 1 else ()
             )
-            first = stats if q == 1 else first
         extra = lax.ppermute(stats, "dom", [(i, i ^ reach) for i in range(parts)])
     amps, mate_amps, far_amps = call(
         amps_kernel, [sds((8, block), F32)] * 3, (stats, extra, spectral, freq, rate), 0.8,
     )
 
-    cuts = [block - block // 4, block // 4]
-    forces, *sent = call(
-        functools.partial(forces_kernel, dims),
-        [sds((comps, block), BF16)] + [sds((part, cut), BF16) for cut in cuts],
-        (rim, *rims, local), 1.4,
-        scratch=[pltpu.VMEM((4 * dims * width, block), BF16)], after=(first,),
-    )
-    far = [lax.ppermute(value, "mode", [(i, i ^ 2) for i in range(4)]) for value in sent]
-    mate = lax.ppermute(forces, "mode", [(i, i ^ 1) for i in range(4)])
+    own, mate, far = [], [], []
+    for c in range(CHUNKS):
+        forces, sent = call(
+            functools.partial(forces_kernel, c * chunk, dims),
+            [sds((comps, chunk), BF16), sds((part, chunk), BF16)],
+            (rim, first_rim, rims[c], local), 0.8,
+            scratch=[pltpu.VMEM((4 * dims * width, chunk), BF16)],
+        )
+        own.append(forces)
+        far.append(lax.ppermute(sent, "mode", [(i, i ^ 2) for i in range(4)]))
+        mate.append(lax.ppermute(forces, "mode", [(i, i ^ 1) for i in range(4)]))
     near = call(
-        functools.partial(near_kernel, dims, 1), sds((comps, 128), F32),
-        (amps, mate_amps, rho_diag, rho_mate, forces, mate),
+        functools.partial(near_kernel, dims, CHUNKS), sds((comps, 128), F32),
+        (amps, mate_amps, rho_diag, rho_mate, *own, *mate),
         3.4,
         scratch=[pltpu.VMEM((block, 32), BF16), pltpu.VMEM((2, block, block // 4), BF16)],
     )
@@ -471,15 +483,14 @@
         scratch=[pltpu.VMEM((2 * block, 32), BF16)],
     )
     value = near
-    at = 0
-    for c, cut in enumerate(cuts):
-        last = c == len(cuts) - 1
+    for c in range(CHUNKS):
+        last = c == CHUNKS - 1
         value = call(
-            functools.partial(far_kernel, at, per_elem), sds((1, comps) if last else (comps, 128), F32),
-            (value, weights, far[c], forces, mate), 2.1 * cut / block,
+            functools.partial(far_kernel, c * chunk, per_elem, CHUNKS),
+            sds((1, comps) if last else (comps, 128), F32),
+            (value, weights, far[c], *own, *mate), 1.0,
             scratch=[pltpu.VMEM((comps, 128), F32)] * 2 if last else (),
         )
-        at += cut
     value = value.reshape(comps)
     for reach in (1, 2):
         value = value + lax.ppermute(value, "mode", [(i, i ^ reach) for i in range(4)])

time: 56.5 us -> 53.8 us (0.952)
  waiting for transfers between devices: 20.3 us -> 13.2 us
  starting transfers between devices: 16.5 us -> 20.8 us
    ppermute x3, waiting for transfers between devices: 8.81 us -> 1.24 us  [combined(): extra = lax.ppermute(stats, 'dom', [(i, i ^ reach) for i in range(parts)])]
    ppermute x3, starting transfers between devices: 8.53 us -> 11.6 us  [combined(): extra = lax.ppermute(stats, 'dom', [(i, i ^ reach) for i in range(parts)])]
    ppermute x5 -> x7, starting transfers between devices: 4.4 us -> 5.55 us  [the longest x2 2.09 us: combined(): far.append(lax.ppermute(sent, 'mode', [(i, i ^ 2) for i in range(4)]))]
    ppermute x5 -> x7, waiting for transfers between devices: 7.15 us -> 7.6 us  [the longest x2 7.59 us: combined(): far.append(lax.ppermute(sent, 'mode', [(i, i ^ 2) for i in range(4)]))]
    pallas_call x15 -> x16, Pallas kernels: 16.6 us -> 16.8 us  [call(): pl.pallas_call(body, out_shape=out_shape, in_specs=specs, out_specs=[VMEM...]
  transfers between devices with their start and end apart: 12 -> 14, of which waited for: 8 -> 7; matrix products, arithmetic and copies ran while one was open for 0% -> 0% of each run, Pallas kernels for 23% -> 27%
where the time goes in v11:
time: 53.8 us; the launch traced here: 53.6 us
  starting transfers between devices  20.8 us (39%)
  Pallas kernels  16.8 us (31%)
  waiting for transfers between devices  13.2 us (25%)
  local copies, waits for them, and re-layouts  2.13 us (4%)
  other arithmetic  0.58 us (1%)
    pallas_call x16, Pallas kernels, call(): pl.pallas_call(body, out_shape=out_shape, in_specs=specs, out_specs=[VMEM...  16.8 us
    ppermute x3, starting transfers between devices, combined(): extra = lax.ppermute(stats, 'dom', [(i, i ^ reach) for i in range(parts)])  11.6 us
    ppermute x2, waiting for transfers between devices, combined(): far.append(lax.ppermute(sent, 'mode', [(i, i ^ 2) for i in range(4)]))  7.59 us
    ppermute x2, waiting for transfers between devices, combined(): lax.ppermute(value, 'mode', [(i, i ^ reach) for i in range(4)])  4.31 us
    ppermute x2, starting transfers between devices, combined(): lax.ppermute(stats, 'mode', [(i, i ^ q) for i in range(4)])  3.13 us
    unnamed x18, local copies, waits for them, and re-layouts  2.13 us
    ppermute x2, starting transfers between devices, combined(): far.append(lax.ppermute(sent, 'mode', [(i, i ^ 2) for i in range(4)]))  2.09 us
    ppermute x1, starting transfers between devices, combined(): first_rim = lax.ppermute(outgoing, 'dom', halves[0])  1.5 us
  transfers between devices with their start and end apart: 14, of which 7 were waited for; matrix products, arithmetic and copies ran while one was open for 0% of the time, Pallas kernels for 27%

profile of v11, /device:TPU:0, one launch (start us, length us, event | category | flops | bytes accessed | tf_op | source)
XLA Modules:
  0.0 53.6 jit_solution(12184565818156346556)
XLA Ops:
  0.0 0.0 copy-start
  0.0 1.4 %copy-done = bf16[3,256,1024]{2,1,0:T(8,128)(2,1)S(1)} copy-done((bf16[3,256,1024]{2,1,0:T(8,128)(2,1)S(1)}, bf16[3,256,1024]{2,1,0:T(8,128)(2,1)}, u32[]{:S(2)}) %copy-start) | copy-done | bytes 1572888
  1.4 0.0 copy-start.6
  1.4 0.7 %copy-done.6 = s32[2,64]{1,0:T(2,128)S(1)} copy-done((s32[2,64]{1,0:T(2,128)S(1)}, s32[2,64]{1,0:T(2,128)}, u32[]{:S(2)}) %copy-start.6) | copy-done | bytes 536
  2.1 0.0 copy-start.7
  2.1 0.7 %shard_map.91 = (bf16[192,1024]{1,0:T(8,128)(2,1)S(1)}, bf16[192,512]{1,0:T(8,128)(2,1)S(1)}, bf16[192,512]{1,0:T(8,128)(2,1)S(1)}, bf16[3,256,1024]{2,1,0:T(8,128)(2,1)S(1)}) custom-call(s32[2,64]{1,0:T(2,128)S(1)} %copy-done.6, bf16[3,256,1024]{2,1,0:T(8,128)(2,1)S(1)} %copy-done), custom_call_target="tpu_custom_call" | custom-call | flops 2200000000 | tf_op jit(solution)/shard_map/pallas_call | solution.py:27
  2.8 0.0 copy-start.3
  2.8 0.0 copy-start.4
  2.8 0.0 copy-done.7
  2.8 0.8 %shard_map.92.refs_0_.refs_2_ = f32[4,1024]{1,0:T(4,128)S(1)} custom-call(f32[1,256]{1,0:T(1,128)S(1)} %bitcast.19, bf16[3,256,1024]{2,1,0:T(8,128)(2,1)S(1)} %get-tuple-element.21.refs_1_.refs_3_), custom_call_target="tpu_custom_call" | custom-call | flops 880000000 | tf_op jit(solution)/shard_map/pallas_call | solution.py:27
  3.6 0.6 %collective-permute-start = (f32[4,1024]{1,0:T(4,128)S(1)}, f32[4,1024]{1,0:T(4,128)S(1)}, u32[]{:S(2)}, u32[]{:S(2)}) collective-permute-start(f32[4,1024]{1,0:T(4,128)S(1)} %shard_map.92.refs_0_.refs_2_), channel_id=1, source_target_pairs={{0,1},{1,0},{2,3},{3,2},{4,5},{5,4},{6,7},{7,6},{8,9},{9,8},{10,11... | collective-permute-start | bytes 49160 | tf_op jit(solution)/shard_map/ppermute | solution.py:446
  4.2 2.6 %collective-permute-start.1 = (f32[4,1024]{1,0:T(4,128)S(1)}, f32[4,1024]{1,0:T(4,128)S(1)}, u32[]{:S(2)}, u32[]{:S(2)}) collective-permute-start(f32[4,1024]{1,0:T(4,128)S(1)} %shard_map.92.refs_0_.refs_2_), channel_id=1, source_target_pairs={{0,2},{1,3},{2,0},{3,1},{4,6},{5,7},{6,4},{7,5},{8,10},{9,11},{10,... | collective-permute-start | bytes 49160 | tf_op jit(solution)/shard_map/ppermute | solution.py:446
  6.8 1.5 %collective-permute-start.5 = (bf16[192,1024]{1,0:T(8,128)(2,1)S(1)}, bf16[192,1024]{1,0:T(8,128)(2,1)S(1)}, u32[]{:S(2)}, u32[]{:S(2)}) collective-permute-start(bf16[192,1024]{1,0:T(8,128)(2,1)S(1)} %get-tuple-element.28), channel_id=1, source_target_pairs={{0,4},{4,0},{8,12},{12,8},{16,20},{20,16},{24,28},{28,24},{1,5},{5... | collective-permute-start | bytes 1179656 | tf_op jit(solution)/shard_map/ppermute | solution.py:416
  8.3 0.7 %collective-permute-start.6 = (bf16[192,512]{1,0:T(8,128)(2,1)S(1)}, bf16[192,512]{1,0:T(8,128)(2,1)S(1)}, u32[]{:S(2)}, u32[]{:S(2)}) collective-permute-start(bf16[192,512]{1,0:T(8,128)(2,1)S(1)} %get-tuple-element.29), channel_id=1, source_target_pairs={{4,8},{8,4},{12,16},{16,12},{20,24},{24,20},{5,9},{9,5},{13,17},{1... | collective-permute-start | bytes 589832 | tf_op jit(solution)/shard_map/ppermute | solution.py:417
  8.9 0.7 %collective-permute-start.7 = (bf16[192,512]{1,0:T(8,128)(2,1)S(1)}, bf16[192,512]{1,0:T(8,128)(2,1)S(1)}, u32[]{:S(2)}, u32[]{:S(2)}) collective-permute-start(bf16[192,512]{1,0:T(8,128)(2,1)S(1)} %get-tuple-element.32), channel_id=1, source_target_pairs={{4,8},{8,4},{12,16},{16,12},{20,24},{24,20},{5,9},{9,5},{13,17},{1... | collective-permute-start | bytes 589832 | tf_op jit(solution)/shard_map/ppermute | solution.py:417
  9.6 0.0 copy-done.3
  9.6 0.0 copy-done.4
  9.6 2.4 %shard_map.94 = (f32[1024,1024]{1,0:T(8,128)S(1)}, f32[2,512,512]{2,1,0:T(8,128)S(1)}, f32[4,1024,128]{2,1,0:T(8,128)S(1)}) custom-call(f32[1,4096]{1,0:T(1,128)S(1)} %bitcast.10, f32[1,4096]{1,0:T(1,128)S(1)} %bitcast.14, f32[4,1024]{1,0:T(4,128)S(1)} %shard_map.92.refs_0_.refs_2_), custom_call_target="tpu_custom_call" | custom-call | flops 3300000000 | tf_op jit(solution)/shard_map/pallas_call | solution.py:27
  12.1 0.0 copy-start.2
  12.1 0.0 copy-start.5
  12.1 0.0 copy-start.8
  12.1 1.6 %shard_map.95.refs_4_.refs_3_ = f32[1024,1024]{1,0:T(8,128)S(1)} custom-call(f32[1,4096]{1,0:T(1,128)S(1)} %bitcast.11, f32[1,4096]{1,0:T(1,128)S(1)} %bitcast.15, f32[4,1024,128]{2,1,0:T(8,128)S(1)} %get-tuple-element.22.refs_2_), custom_call_target="tpu_custom_call" | custom-call | flops 2090000000 | tf_op jit(solution)/shard_map/pallas_call | solution.py:27
  13.7 0.0 collective-permute-done.refs_1_
  13.7 0.0 collective-permute-done.1.refs_2_
  13.7 7.0 %collective-permute-start.2 = (f32[12,1024]{1,0:T(8,128)S(1)}, f32[12,1024]{1,0:T(8,128)S(1)}, u32[]{:S(2)}, u32[]{:S(2)}) collective-permute-start(f32[12,1024]{1,0:T(8,128)S(1)} %shard_map.93.refs_0_), channel_id=1, source_target_pairs={{0,8},{4,12},{8,0},{12,4},{16,24},{20,28},{24,16},{28,20},{1,9},{5... | collective-permute-start | bytes 147464 | tf_op jit(solution)/shard_map/ppermute | solution.py:458
  20.7 0.0 copy-done.2
  20.7 0.0 copy-done.5
  20.7 0.0 copy-done.8
  20.7 1.8 %shard_map.96 = (f32[512,1024]{1,0:T(8,128)S(1)}, bf16[512,768]{1,0:T(8,128)(2,1)S(1)}) custom-call(s32[4,64]{1,0:T(4,128)S(1)} %bitcast.18, s32[1,64]{1,0:T(1,128)S(1)} %bitcast.20, bf16[8,3,4,64]{3,2,1,0:T(4,128)(2,1)S(1)} %bitcast.9, bf16[3,256,1024]{2,1,0:T(8,128)(2,1)S(1)} %get-tuple-element.21.refs_1_.refs_3_, f32[1024,1024]{1,0:T(8,128)S(1)} %shard_map.95.refs_4_.refs_3_), custom_call_target="tpu_custom_call" | custom-call | flops 1980000000 | tf_op jit(solution)/shard_map/pallas_call | solution.py:27
  22.5 0.4 collective-permute-done.2.refs_1_
  23.0 3.1 %collective-permute-start.3 = (f32[12,1024]{1,0:T(8,128)S(1)}, f32[12,1024]{1,0:T(8,128)S(1)}, u32[]{:S(2)}, u32[]{:S(2)}) collective-permute-start(f32[12,1024]{1,0:T(8,128)S(1)} %shard_map.97.refs_0_), channel_id=1, source_target_pairs={{0,16},{4,20},{8,24},{12,28},{16,0},{20,4},{24,8},{28,12},{1,17},{... | collective-permute-start | bytes 147464 | tf_op jit(solution)/shard_map/ppermute | solution.py:458
  26.1 0.0 collective-permute-done.6.refs_2_
  26.1 0.0 collective-permute-done.5.refs_1_
  26.1 0.6 %shard_map.100 = (bf16[512,512]{1,0:T(8,128)(2,1)S(1)}, bf16[256,512]{1,0:T(8,128)(2,1)S(1)}) custom-call(bf16[512,768]{1,0:T(8,128)(2,1)S(1)} %get-tuple-element.23.refs_2_.refs_0_, bf16[192,1024]{1,0:T(8,128)(2,1)S(1)} %collective-permute-done.5.refs_1_, bf16[192,512]{1,0:T(8,128)(2,1)S(1)} %collective-permute-done.6.refs_2_, ...), custom_call_target="tpu_custom_call" | custom-call | flops 880000000 | tf_op jit(solution)/shard_map/pallas_call | solution.py:27
  26.7 0.1 collective-permute-start.8
  26.8 0.0 collective-permute-done.7.refs_2_
  26.8 0.6 %shard_map.101 = (bf16[512,512]{1,0:T(8,128)(2,1)S(1)}, bf16[256,512]{1,0:T(8,128)(2,1)S(1)}) custom-call(bf16[512,768]{1,0:T(8,128)(2,1)S(1)} %get-tuple-element.23.refs_2_.refs_0_, bf16[192,1024]{1,0:T(8,128)(2,1)S(1)} %collective-permute-done.5.refs_1_, bf16[192,512]{1,0:T(8,128)(2,1)S(1)} %collective-permute-done.7.refs_2_, ...), custom_call_target="tpu_custom_call" | custom-call | flops 880000000 | tf_op jit(solution)/shard_map/pallas_call | solution.py:27
  27.5 0.6 %collective-permute-start.9 = (bf16[512,512]{1,0:T(8,128)(2,1)S(1)}, bf16[512,512]{1,0:T(8,128)(2,1)S(1)}, u32[]{:S(2)}, u32[]{:S(2)}) collective-permute-start(bf16[512,512]{1,0:T(8,128)(2,1)S(1)} %get-tuple-element.33.refs_5_.refs_4_), channel_id=1, source_target_pairs={{0,1},{1,0},{2,3},{3,2},{4,5},{5,4},{6,7},{7,6},{8,9},{9,8},{10,11... | collective-permute-start | bytes 1572872 | tf_op jit(solution)/shard_map/ppermute | solution.py:473
  28.0 0.3 collective-permute-done.3.refs_1_
  28.3 0.0 copy-start.1
  28.4 1.5 %collective-permute-start.4 = (f32[12,1024]{1,0:T(8,128)S(1)}, f32[12,1024]{1,0:T(8,128)S(1)}, u32[]{:S(2)}, u32[]{:S(2)}) collective-permute-start(f32[12,1024]{1,0:T(8,128)S(1)} %shard_map.98.refs_0_), channel_id=1, source_target_pairs={{0,4},{4,0},{8,12},{12,8},{16,20},{20,16},{24,28},{28,24},{1,5},{5... | collective-permute-start | bytes 147464 | tf_op jit(solution)/shard_map/ppermute | solution.py:458
  29.9 2.3 %shard_map.103.refs_4_ = f32[1024,1024]{1,0:T(8,128)S(1)} custom-call(f32[1,4096]{1,0:T(1,128)S(1)} %bitcast.12, f32[1,4096]{1,0:T(1,128)S(1)} %bitcast.16), custom_call_target="tpu_custom_call" | custom-call | flops 2750000128 | tf_op jit(solution)/shard_map/pallas_call | solution.py:27
  32.2 0.5 collective-permute-done.4.refs_1_
  32.7 0.0 copy-done.1
  32.7 1.4 %shard_map.104.refs_1_ = bf16[2048,1024]{1,0:T(8,128)(2,1)S(1)} custom-call(f32[8,1024]{1,0:T(8,128)S(1)} %get-tuple-element.24.refs_0_, f32[8,1024]{1,0:T(8,128)S(1)} %get-tuple-element.25.refs_1_, f32[8,1024]{1,0:T(8,128)S(1)} %get-tuple-element.34.refs_2_, f32[1024,1024]{1,0:T(8,128)S(1)} %shard_map.95.refs_4_.refs_3_, f32[1024,1024]{1,0:T(8,128)S(1)} %shard_map.103.refs_4_), custom_call_target="tpu_custom_call" | custom-call | flops 1540000000 | tf_op jit(solution)/shard_map/pallas_call | solution.py:27
  34.1 0.6 %collective-permute-start.10 = (bf16[256,512]{1,0:T(8,128)(2,1)S(1)}, bf16[256,512]{1,0:T(8,128)(2,1)S(1)}, u32[]{:S(2)}, u32[]{:S(2)}) collective-permute-start(bf16[256,512]{1,0:T(8,128)(2,1)S(1)} %get-tuple-element.35), channel_id=1, source_target_pairs={{0,2},{1,3},{2,0},{3,1},{4,6},{5,7},{6,4},{7,5},{8,10},{9,11},{10,... | collective-permute-start | bytes 786440 | tf_op jit(solution)/shard_map/ppermute | solution.py:472
  34.7 1.5 %collective-permute-start.11 = (bf16[256,512]{1,0:T(8,128)(2,1)S(1)}, bf16[256,512]{1,0:T(8,128)(2,1)S(1)}, u32[]{:S(2)}, u32[]{:S(2)}) collective-permute-start(bf16[256,512]{1,0:T(8,128)(2,1)S(1)} %get-tuple-element.36), channel_id=1, source_target_pairs={{0,2},{1,3},{2,0},{3,1},{4,6},{5,7},{6,4},{7,5},{8,10},{9,11},{10,... | collective-permute-start | bytes 786440 | tf_op jit(solution)/shard_map/ppermute | solution.py:472
  36.2 0.0 collective-permute-done.8.refs_6_.refs_5_
  36.2 0.0 collective-permute-done.9.refs_7_.refs_6_
  36.2 2.8 %shard_map.102.refs_0_ = f32[512,128]{1,0:T(8,128)S(1)} custom-call(f32[8,1024]{1,0:T(8,128)S(1)} %get-tuple-element.24.refs_0_, f32[8,1024]{1,0:T(8,128)S(1)} %get-tuple-element.25.refs_1_, f32[1024,1024]{1,0:T(8,128)S(1)} %get-tuple-element.26.refs_2_, f32[2,512,512]{2,1,0:T(8,128)S(1)} %get-tuple-element.27.refs_3_, ...), custom_call_target="tpu_custom_call" | custom-call | flops 3740000000 | tf_op jit(solution)/shard_map/pallas_call | solution.py:27
  39.0 4.4 %collective-permute-done.10.refs_2_ = bf16[256,512]{1,0:T(8,128)(2,1)S(1)} collective-permute-done((bf16[256,512]{1,0:T(8,128)(2,1)S(1)}, bf16[256,512]{1,0:T(8,128)(2,1)S(1)}, u32[]{:S(2)}, u32[]{:S(2)}) %collective-permute-start.10) | collective-permute-done | bytes 262176 | tf_op jit(solution)/shard_map/ppermute | solution.py:472
  43.4 0.7 %shard_map.105.refs_0_ = f32[512,128]{1,0:T(8,128)S(1)} custom-call(f32[512,128]{1,0:T(8,128)S(1)} %shard_map.102.refs_0_, bf16[2048,1024]{1,0:T(8,128)(2,1)S(1)} %shard_map.104.refs_1_, bf16[256,512]{1,0:T(8,128)(2,1)S(1)} %collective-permute-done.10.refs_2_, bf16[512,512]{1,0:T(8,128)(2,1)S(1)} %get-tuple-element.31.refs_4_.refs_3_, ...), custom_call_target="tpu_custom_call" | custom-call | flops 1100000000 | tf_op jit(solution)/shard_map/pallas_call | solution.py:27
  44.1 3.2 %collective-permute-done.11.refs_2_ = bf16[256,512]{1,0:T(8,128)(2,1)S(1)} collective-permute-done((bf16[256,512]{1,0:T(8,128)(2,1)S(1)}, bf16[256,512]{1,0:T(8,128)(2,1)S(1)}, u32[]{:S(2)}, u32[]{:S(2)}) %collective-permute-start.11) | collective-permute-done | bytes 262176 | tf_op jit(solution)/shard_map/ppermute | solution.py:472
  47.3 1.0 %shard_map.106 = f32[1,512]{1,0:T(1,128)S(1)} custom-call(f32[512,128]{1,0:T(8,128)S(1)} %shard_map.105.refs_0_, bf16[2048,1024]{1,0:T(8,128)(2,1)S(1)} %shard_map.104.refs_1_, bf16[256,512]{1,0:T(8,128)(2,1)S(1)} %collective-permute-done.11.refs_2_, bf16[512,512]{1,0:T(8,128)(2,1)S(1)} %get-tuple-element.31.refs_4_.refs_3_, ...), custom_call_target="tpu_custom_call" | custom-call | flops 1100000000 | tf_op jit(solution)/shard_map/pallas_call | solution.py:27
  48.3 0.0 collective-permute-start.12
  48.3 1.2 %collective-permute-done.12 = f32[512]{0:T(512)S(1)} collective-permute-done((f32[512]{0:T(512)S(1)}, f32[512]{0:T(512)S(1)}, u32[]{:S(2)}, u32[]{:S(2)}) %collective-permute-start.12) | collective-permute-done | bytes 2080 | tf_op jit(solution)/shard_map/ppermute | solution.py:496
  49.5 0.4 collective-permute-start.13
  49.9 3.1 %collective-permute-done.13 = f32[512]{0:T(512)S(1)} collective-permute-done((f32[512]{0:T(512)S(1)}, f32[512]{0:T(512)S(1)}, u32[]{:S(2)}, u32[]{:S(2)}) %collective-permute-start.13) | collective-permute-done | bytes 2080 | tf_op jit(solution)/shard_map/ppermute | solution.py:496
  53.1 0.6 %add.7 = f32[512]{0:T(512)} add(f32[512]{0:T(512)S(1)} %add.6, f32[512]{0:T(512)S(1)} %collective-permute-done.13) | non-fusion elementwise | flops 512 | bytes 6144 | tf_op jit(solution)/shard_map/add | solution.py:496
  (5 shorter events, 0.1 us)
Async XLA Ops:
  0.0 1.4 %copy-start = (bf16[3,256,1024]{2,1,0:T(8,128)(2,1)S(1)}, bf16[3,256,1024]{2,1,0:T(8,128)(2,1)}, u32[]{:S(2)}) copy-start(bf16[3,256,1024]{2,1,0:T(8,128)(2,1)} %refs_1_.1) | copy-start | bytes 4718596
  1.4 0.7 %copy-start.6 = (s32[2,64]{1,0:T(2,128)S(1)}, s32[2,64]{1,0:T(2,128)}, u32[]{:S(2)}) copy-start(s32[2,64]{1,0:T(2,128)} %refs_0_.1) | copy-start | bytes 1540
  2.1 0.7 %copy-start.7 = (f32[256]{0:T(256)S(1)}, f32[256]{0:T(256)}, u32[]{:S(2)}) copy-start(f32[256]{0:T(256)} %param.10) | copy-start | bytes 3076
  2.8 6.8 %copy-start.3 = (f32[4096]{0:T(1024)S(1)}, f32[4096]{0:T(1024)}, u32[]{:S(2)}) copy-start(f32[4096]{0:T(1024)} %param.12) | copy-start | bytes 49156
  2.8 6.8 %copy-start.4 = (f32[4096]{0:T(1024)S(1)}, f32[4096]{0:T(1024)}, u32[]{:S(2)}) copy-start(f32[4096]{0:T(1024)} %param.13) | copy-start | bytes 49156
  3.6 10.0 %collective-permute-start = (f32[4,1024]{1,0:T(4,128)S(1)}, f32[4,1024]{1,0:T(4,128)S(1)}, u32[]{:S(2)}, u32[]{:S(2)}) collective-permute-start(f32[4,1024]{1,0:T(4,128)S(1)} %shard_map.92.refs_0_.refs_2_), channel_id=1, source_target_pairs={{0,1},{1,0},{2,3},{3,2},{4,5},{5,4},{6,7},{7,6},{8,9},{9,8},{10,11... | collective-permute-start | bytes 49160 | tf_op jit(solution)/shard_map/ppermute | solution.py:446
  4.2 9.5 %collective-permute-start.1 = (f32[4,1024]{1,0:T(4,128)S(1)}, f32[4,1024]{1,0:T(4,128)S(1)}, u32[]{:S(2)}, u32[]{:S(2)}) collective-permute-start(f32[4,1024]{1,0:T(4,128)S(1)} %shard_map.92.refs_0_.refs_2_), channel_id=1, source_target_pairs={{0,2},{1,3},{2,0},{3,1},{4,6},{5,7},{6,4},{7,5},{8,10},{9,11},{10,... | collective-permute-start | bytes 49160 | tf_op jit(solution)/shard_map/ppermute | solution.py:446
  6.8 19.3 %collective-permute-start.5 = (bf16[192,1024]{1,0:T(8,128)(2,1)S(1)}, bf16[192,1024]{1,0:T(8,128)(2,1)S(1)}, u32[]{:S(2)}, u32[]{:S(2)}) collective-permute-start(bf16[192,1024]{1,0:T(8,128)(2,1)S(1)} %get-tuple-element.28), channel_id=1, source_target_pairs={{0,4},{4,0},{8,12},{12,8},{16,20},{20,16},{24,28},{28,24},{1,5},{5... | collective-permute-start | bytes 1179656 | tf_op jit(solution)/shard_map/ppermute | solution.py:416
  8.3 17.8 %collective-permute-start.6 = (bf16[192,512]{1,0:T(8,128)(2,1)S(1)}, bf16[192,512]{1,0:T(8,128)(2,1)S(1)}, u32[]{:S(2)}, u32[]{:S(2)}) collective-permute-start(bf16[192,512]{1,0:T(8,128)(2,1)S(1)} %get-tuple-element.29), channel_id=1, source_target_pairs={{4,8},{8,4},{12,16},{16,12},{20,24},{24,20},{5,9},{9,5},{13,17},{1... | collective-permute-start | bytes 589832 | tf_op jit(solution)/shard_map/ppermute | solution.py:417
  8.9 17.9 %collective-permute-start.7 = (bf16[192,512]{1,0:T(8,128)(2,1)S(1)}, bf16[192,512]{1,0:T(8,128)(2,1)S(1)}, u32[]{:S(2)}, u32[]{:S(2)}) collective-permute-start(bf16[192,512]{1,0:T(8,128)(2,1)S(1)} %get-tuple-element.32), channel_id=1, source_target_pairs={{4,8},{8,4},{12,16},{16,12},{20,24},{24,20},{5,9},{9,5},{13,17},{1... | collective-permute-start | bytes 589832 | tf_op jit(solution)/shard_map/ppermute | solution.py:417
  12.1 8.7 %copy-start.2 = (bf16[64,8,4,3]{0,2,3,1:T(4,128)(2,1)S(1)}, bf16[64,8,4,3]{0,2,3,1:T(4,128)(2,1)}, u32[]{:S(2)}) copy-start(bf16[64,8,4,3]{0,2,3,1:T(4,128)(2,1)} %param.14) | copy-start | bytes 36868
  12.1 8.7 %copy-start.5 = (s32[64,4]{0,1:T(4,128)S(1)}, s32[64,4]{0,1:T(4,128)}, u32[]{:S(2)}) copy-start(s32[64,4]{0,1:T(4,128)} %param.15) | copy-start | bytes 3076
  12.1 8.6 %copy-start.8 = (s32[64]{0:T(128)S(1)}, s32[64]{0:T(128)}, u32[]{:S(2)}) copy-start(s32[64]{0:T(128)} %param.16) | copy-start | bytes 772
  13.7 9.3 %collective-permute-start.2 = (f32[12,1024]{1,0:T(8,128)S(1)}, f32[12,1024]{1,0:T(8,128)S(1)}, u32[]{:S(2)}, u32[]{:S(2)}) collective-permute-start(f32[12,1024]{1,0:T(8,128)S(1)} %shard_map.93.refs_0_), channel_id=1, source_target_pairs={{0,8},{4,12},{8,0},{12,4},{16,24},{20,28},{24,16},{28,20},{1,9},{5... | collective-permute-start | bytes 147464 | tf_op jit(solution)/shard_map/ppermute | solution.py:458
  23.0 5.3 %collective-permute-start.3 = (f32[12,1024]{1,0:T(8,128)S(1)}, f32[12,1024]{1,0:T(8,128)S(1)}, u32[]{:S(2)}, u32[]{:S(2)}) collective-permute-start(f32[12,1024]{1,0:T(8,128)S(1)} %shard_map.97.refs_0_), channel_id=1, source_target_pairs={{0,16},{4,20},{8,24},{12,28},{16,0},{20,4},{24,8},{28,12},{1,17},{... | collective-permute-start | bytes 147464 | tf_op jit(solution)/shard_map/ppermute | solution.py:458
  26.7 9.5 %collective-permute-start.8 = (bf16[512,512]{1,0:T(8,128)(2,1)S(1)}, bf16[512,512]{1,0:T(8,128)(2,1)S(1)}, u32[]{:S(2)}, u32[]{:S(2)}) collective-permute-start(bf16[512,512]{1,0:T(8,128)(2,1)S(1)} %get-tuple-element.31.refs_4_.refs_3_), channel_id=1, source_target_pairs={{0,1},{1,0},{2,3},{3,2},{4,5},{5,4},{6,7},{7,6},{8,9},{9,8},{10,11... | collective-permute-start | bytes 1572872 | tf_op jit(solution)/shard_map/ppermute | solution.py:473
  27.5 8.7 %collective-permute-start.9 = (bf16[512,512]{1,0:T(8,128)(2,1)S(1)}, bf16[512,512]{1,0:T(8,128)(2,1)S(1)}, u32[]{:S(2)}, u32[]{:S(2)}) collective-permute-start(bf16[512,512]{1,0:T(8,128)(2,1)S(1)} %get-tuple-element.33.refs_5_.refs_4_), channel_id=1, source_target_pairs={{0,1},{1,0},{2,3},{3,2},{4,5},{5,4},{6,7},{7,6},{8,9},{9,8},{10,11... | collective-permute-start | bytes 1572872 | tf_op jit(solution)/shard_map/ppermute | solution.py:473
  28.3 4.3 %copy-start.1 = (f32[3,4096]{1,0:T(4,128)S(1)}, f32[3,4096]{1,0:T(4,128)}, u32[]{:S(2)}) copy-start(f32[3,4096]{1,0:T(4,128)} %refs_2_.1) | copy-start | bytes 147460
  28.4 4.3 %collective-permute-start.4 = (f32[12,1024]{1,0:T(8,128)S(1)}, f32[12,1024]{1,0:T(8,128)S(1)}, u32[]{:S(2)}, u32[]{:S(2)}) collective-permute-start(f32[12,1024]{1,0:T(8,128)S(1)} %shard_map.98.refs_0_), channel_id=1, source_target_pairs={{0,4},{4,0},{8,12},{12,8},{16,20},{20,16},{24,28},{28,24},{1,5},{5... | collective-permute-start | bytes 147464 | tf_op jit(solution)/shard_map/ppermute | solution.py:458
  34.1 9.2 %collective-permute-start.10 = (bf16[256,512]{1,0:T(8,128)(2,1)S(1)}, bf16[256,512]{1,0:T(8,128)(2,1)S(1)}, u32[]{:S(2)}, u32[]{:S(2)}) collective-permute-start(bf16[256,512]{1,0:T(8,128)(2,1)S(1)} %get-tuple-element.35), channel_id=1, source_target_pairs={{0,2},{1,3},{2,0},{3,1},{4,6},{5,7},{6,4},{7,5},{8,10},{9,11},{10,... | collective-permute-start | bytes 786440 | tf_op jit(solution)/shard_map/ppermute | solution.py:472
  34.7 12.6 %collective-permute-start.11 = (bf16[256,512]{1,0:T(8,128)(2,1)S(1)}, bf16[256,512]{1,0:T(8,128)(2,1)S(1)}, u32[]{:S(2)}, u32[]{:S(2)}) collective-permute-start(bf16[256,512]{1,0:T(8,128)(2,1)S(1)} %get-tuple-element.36), channel_id=1, source_target_pairs={{0,2},{1,3},{2,0},{3,1},{4,6},{5,7},{6,4},{7,5},{8,10},{9,11},{10,... | collective-permute-start | bytes 786440 | tf_op jit(solution)/shard_map/ppermute | solution.py:472
  48.3 1.2 %collective-permute-start.12 = (f32[512]{0:T(512)S(1)}, f32[512]{0:T(512)S(1)}, u32[]{:S(2)}, u32[]{:S(2)}) collective-permute-start(f32[512]{0:T(512)S(1)} %bitcast.7), channel_id=1, source_target_pairs={{0,1},{1,0},{2,3},{3,2},{4,5},{5,4},{6,7},{7,6},{8,9},{9,8},{10,11... | collective-permute-start | bytes 6152 | tf_op jit(solution)/shard_map/ppermute | solution.py:496
  49.5 3.6 %collective-permute-start.13 = (f32[512]{0:T(512)S(1)}, f32[512]{0:T(512)S(1)}, u32[]{:S(2)}, u32[]{:S(2)}) collective-permute-start(f32[512]{0:T(512)S(1)} %add.6), channel_id=1, source_target_pairs={{0,2},{1,3},{2,0},{3,1},{4,6},{5,7},{6,4},{7,5},{8,10},{9,11},{10,... | collective-permute-start | bytes 6152 | tf_op jit(solution)/shard_map/ppermute | solution.py:496

commit v12 on v10

--- a/solution.py
+++ b/solution.py
@@ -44,20 +44,31 @@
     out_ref[...] = left_ref[...] + right_ref[...]
 
 
-def gather_kernel(shared_ref, shapes_ref, first_ref, second_ref, held_ref, sem):
-    dims, nodes, _ = held_ref.shape
-    width = shared_ref.shape[1]
+def pick_kernel(shared_ref, pick_ref):
+    nodes = pick_ref.shape[1]
+    odd = lax.axis_index("dom") & 1
+    wanted = jnp.concatenate([shared_ref[pl.ds(1 - odd, 1), :], shared_ref[pl.ds(odd, 1), :]], axis=1)
+    node = lax.broadcasted_iota(jnp.int32, (nodes, wanted.shape[1]), 0)
+    pick_ref[...] = jnp.where(node == wanted, 1.0, 0.0).astype(F32).T.astype(BF16)
+
+
+def pair_rows_kernel(pick_ref, shapes_ref, out_ref):
+    dims = shapes_ref.shape[0]
+    width = out_ref.shape[0] // dims
+    for d in range(dims):
+        got = jnp.dot(pick_ref[:width, :], shapes_ref[d], preferred_element_type=F32)
+        out_ref[d * width : (d + 1) * width, :] = got.astype(BF16)
+
+
+def next_rows_kernel(pick_ref, shapes_ref, out_ref, held_ref, sem):
+    dims = held_ref.shape[0]
+    width = out_ref.shape[0] // dims
     load = pltpu.make_async_copy(shapes_ref, held_ref, sem)
     load.start()
-    node = lax.broadcasted_iota(jnp.int32, (nodes, 2 * width), 0)
-    odd = lax.axis_index("dom") & 1
-    wanted = jnp.concatenate([shared_ref[pl.ds(1 - odd, 1), :], shared_ref[pl.ds(odd, 1), :]], axis=1)
-    pick = jnp.where(node == wanted, 1.0, 0.0).astype(F32).T.astype(BF16)
     load.wait()
     for d in range(dims):
-        got = jnp.dot(pick, held_ref[d], preferred_element_type=F32).astype(BF16)
-        first_ref[d * width : (d + 1) * width, :] = got[:width]
-        second_ref[d * width : (d + 1) * width, :] = got[width:]
+        got = jnp.dot(pick_ref[width:, :], held_ref[d], preferred_element_type=F32)
+        out_ref[d * width : (d + 1) * width, :] = got.astype(BF16)
 
 
 def stats_kernel(mass_ref, shapes_ref, out_ref, mass_scr):
@@ -398,9 +409,12 @@
     freq = frequencies.reshape(1, -1)
     rate = damping.reshape(1, -1)
 
-    outgoing, other, held = call(
-        gather_kernel, [sds((dims * width, block), BF16)] * 2 + [sds(shapes.shape, BF16)], (shared, shapes),
-        2.0, hbm=(1,), scratch=[pltpu.SemaphoreType.DMA],
+    picked = call(pick_kernel, sds((2 * width, nodes), BF16), (shared,), 2.0)
+    rows = sds((dims * width, block), BF16)
+    outgoing = call(pair_rows_kernel, rows, (picked, shapes), 0.4)
+    other, held = call(
+        next_rows_kernel, [rows, sds(shapes.shape, BF16)], (picked, shapes), 0.7, hbm=(1,),
+        scratch=[pltpu.SemaphoreType.DMA],
     )
     rims = (lax.ppermute(outgoing, "dom", halves[0]), lax.ppermute(other, "dom", halves[1]))
     stats = call(
@@ -433,7 +447,6 @@
     )
     given = [stats] + [lax.ppermute(stats, "mode", [(i, i ^ q) for i in range(4)]) for q in (1, 2)]
     stats = call(join_kernel, sds((3 * (dims + 1), block), F32), given, 0.5)
-    first = stats
     order = [1 << q for q in range(1, parts.bit_length() - 1)] + [1]
     if parts & (parts - 1) or parts == 1:
         stats = lax.psum(stats, "dom")
@@ -444,7 +457,6 @@
             stats = call(
                 add_kernel, sds(stats.shape, F32), (stats, extra), 0.5, after=(rim,) if q == 1 else ()
             )
-            first = stats if q == 1 else first
         extra = lax.ppermute(stats, "dom", [(i, i ^ reach) for i in range(parts)])
     amps, mate_amps, far_amps = call(
         amps_kernel, [sds((8, block), F32)] * 3, (stats, extra, spectral, freq, rate), 0.8,
@@ -455,7 +467,7 @@
         functools.partial(forces_kernel, dims),
         [sds((comps, block), BF16)] + [sds((part, cut), BF16) for cut in cuts],
         (rim, *rims, local), 1.4,
-        scratch=[pltpu.VMEM((4 * dims * width, block), BF16)], after=(first,),
+        scratch=[pltpu.VMEM((4 * dims * width, block), BF16)],
     )
     far = [lax.ppermute(value, "mode", [(i, i ^ 2) for i in range(4)]) for value in sent]
     mate = lax.ppermute(forces, "mode", [(i, i ^ 1) for i in range(4)])

time: 56.5 us -> 58.3 us (1.032)
  waiting for transfers between devices: 20.3 us -> 22 us
  local copies, waits for them, and re-layouts: 2.13 us -> 1.29 us
    ppermute x1, waiting for transfers between devices: 2.92 us -> 8.85 us  [combined(): lax.ppermute(outgoing, 'dom', halves[0])]
    ppermute x3, waiting for transfers between devices: 8.81 us -> 4.6 us  [combined(): extra = lax.ppermute(stats, 'dom', [(i, i ^ reach) for i in range(parts)])]
    ppermute x2, waiting for transfers between devices: 0.01 us -> 2.25 us  [combined(): lax.ppermute(stats, 'mode', [(i, i ^ q) for i in range(4)])]
    ppermute x1, starting transfers between devices: 1.5 us -> 3.03 us  [combined(): lax.ppermute(outgoing, 'dom', halves[0])]
    ppermute x2, waiting for transfers between devices: 4.23 us -> 2.95 us  [combined(): lax.ppermute(value, 'mode', [(i, i ^ 2) for i in range(4)])]
    ppermute x2, starting transfers between devices: 3.13 us -> 1.98 us  [combined(): lax.ppermute(stats, 'mode', [(i, i ^ q) for i in range(4)])]
    ppermute x2, starting transfers between devices: 0.47 us -> 1.48 us  [combined(): lax.ppermute(value, 'mode', [(i, i ^ reach) for i in range(4)])]
    ppermute x2, waiting for transfers between devices: 4.32 us -> 3.3 us  [combined(): lax.ppermute(value, 'mode', [(i, i ^ reach) for i in range(4)])]
  transfers between devices with their start and end apart: 12 -> 12, of which waited for: 8 -> 10; matrix products, arithmetic and copies ran while one was open for 0% -> 0% of each run, Pallas kernels for 23% -> 25%
where the time goes in v12:
time: 58.3 us; the launch traced here: 58.1 us
  waiting for transfers between devices  22 us (38%)
  Pallas kernels  17 us (29%)
  starting transfers between devices  17 us (29%)
  local copies, waits for them, and re-layouts  1.29 us (2%)
    pallas_call x17, Pallas kernels, call(): pl.pallas_call(body, out_shape=out_shape, in_specs=specs, out_specs=[VMEM...  17 us
    ppermute x1, waiting for transfers between devices, combined(): lax.ppermute(outgoing, 'dom', halves[0])  8.85 us
    ppermute x3, starting transfers between devices, combined(): extra = lax.ppermute(stats, 'dom', [(i, i ^ reach) for i in range(parts)])  7.62 us
    ppermute x3, waiting for transfers between devices, combined(): extra = lax.ppermute(stats, 'dom', [(i, i ^ reach) for i in range(parts)])  4.6 us
    ppermute x2, waiting for transfers between devices, combined(): lax.ppermute(value, 'mode', [(i, i ^ reach) for i in range(4)])  3.3 us
    ppermute x1, starting transfers between devices, combined(): lax.ppermute(outgoing, 'dom', halves[0])  3.03 us
    ppermute x2, waiting for transfers between devices, combined(): lax.ppermute(value, 'mode', [(i, i ^ 2) for i in range(4)])  2.95 us
    ppermute x2, waiting for transfers between devices, combined(): lax.ppermute(stats, 'mode', [(i, i ^ q) for i in range(4)])  2.25 us
  transfers between devices with their start and end apart: 12, of which 10 were waited for; matrix products, arithmetic and copies ran while one was open for 0% of the time, Pallas kernels for 25%

profile of v12, /device:TPU:0, one launch (start us, length us, event | category | flops | bytes accessed | tf_op | source)
XLA Modules:
  0.0 58.1 jit_solution(11826006516910418960)
XLA Ops:
  0.0 0.0 copy-start
  0.0 0.0 copy-start.6
  0.0 0.8 %copy-done.6 = s32[2,64]{1,0:T(2,128)S(1)} copy-done((s32[2,64]{1,0:T(2,128)S(1)}, s32[2,64]{1,0:T(2,128)}, u32[]{:S(2)}) %copy-start.6) | copy-done | bytes 536
  0.8 0.2 shard_map.91.refs_0_
  1.0 0.4 copy-done
  1.4 0.0 copy-start.7
  1.4 0.4 shard_map.101
  1.8 3.0 %collective-permute-start.5 = (bf16[192,1024]{1,0:T(8,128)(2,1)S(1)}, bf16[192,1024]{1,0:T(8,128)(2,1)S(1)}, u32[]{:S(2)}, u32[]{:S(2)}) collective-permute-start(bf16[192,1024]{1,0:T(8,128)(2,1)S(1)} %shard_map.101), channel_id=1, source_target_pairs={{0,4},{4,0},{8,12},{12,8},{16,20},{20,16},{24,28},{28,24},{1,5},{5... | collective-permute-start | bytes 1179656 | tf_op jit(solution)/shard_map/ppermute | solution.py:419
  4.9 0.5 shard_map.92
  5.4 0.0 copy-start.3
  5.4 0.0 copy-start.4
  5.4 0.7 %collective-permute-start.6 = (bf16[192,1024]{1,0:T(8,128)(2,1)S(1)}, bf16[192,1024]{1,0:T(8,128)(2,1)S(1)}, u32[]{:S(2)}, u32[]{:S(2)}) collective-permute-start(bf16[192,1024]{1,0:T(8,128)(2,1)S(1)} %get-tuple-element.25), channel_id=1, source_target_pairs={{4,8},{8,4},{12,16},{16,12},{20,24},{24,20},{5,9},{9,5},{13,17},{1... | collective-permute-start | bytes 1179656 | tf_op jit(solution)/shard_map/ppermute | solution.py:419
  6.1 0.0 copy-done.7
  6.1 0.8 %shard_map.93.refs_0_.refs_2_ = f32[4,1024]{1,0:T(4,128)S(1)} custom-call(f32[1,256]{1,0:T(1,128)S(1)} %bitcast.19, bf16[3,256,1024]{2,1,0:T(8,128)(2,1)S(1)} %get-tuple-element.18.refs_1_.refs_3_), custom_call_target="tpu_custom_call" | custom-call | flops 880000000 | tf_op jit(solution)/shard_map/pallas_call | solution.py:27
  6.9 0.0 copy-done.3
  6.9 0.0 copy-done.4
  6.9 2.4 %shard_map.95 = (f32[1024,1024]{1,0:T(8,128)S(1)}, f32[2,512,512]{2,1,0:T(8,128)S(1)}, f32[4,1024,128]{2,1,0:T(8,128)S(1)}) custom-call(f32[1,4096]{1,0:T(1,128)S(1)} %bitcast.10, f32[1,4096]{1,0:T(1,128)S(1)} %bitcast.14, f32[4,1024]{1,0:T(4,128)S(1)} %shard_map.93.refs_0_.refs_2_), custom_call_target="tpu_custom_call" | custom-call | flops 3300000000 | tf_op jit(solution)/shard_map/pallas_call | solution.py:27
  9.4 0.0 copy-start.2
  9.4 0.0 copy-start.5
  9.4 0.0 copy-start.8
  9.4 1.6 %shard_map.96.refs_4_.refs_3_ = f32[1024,1024]{1,0:T(8,128)S(1)} custom-call(f32[1,4096]{1,0:T(1,128)S(1)} %bitcast.11, f32[1,4096]{1,0:T(1,128)S(1)} %bitcast.15, f32[4,1024,128]{2,1,0:T(8,128)S(1)} %get-tuple-element.19.refs_2_), custom_call_target="tpu_custom_call" | custom-call | flops 2090000000 | tf_op jit(solution)/shard_map/pallas_call | solution.py:27
  11.0 0.0 copy-done.2
  11.0 0.0 copy-done.5
  11.0 0.0 copy-done.8
  11.0 1.8 %shard_map.97 = (f32[512,1024]{1,0:T(8,128)S(1)}, bf16[512,768]{1,0:T(8,128)(2,1)S(1)}) custom-call(s32[4,64]{1,0:T(4,128)S(1)} %bitcast.18, s32[1,64]{1,0:T(1,128)S(1)} %bitcast.20, bf16[8,3,4,64]{3,2,1,0:T(4,128)(2,1)S(1)} %bitcast.9, bf16[3,256,1024]{2,1,0:T(8,128)(2,1)S(1)} %get-tuple-element.18.refs_1_.refs_3_, f32[1024,1024]{1,0:T(8,128)S(1)} %shard_map.96.refs_4_.refs_3_), custom_call_target="tpu_custom_call" | custom-call | flops 1980000000 | tf_op jit(solution)/shard_map/pallas_call | solution.py:27
  12.8 8.9 %collective-permute-done.5.refs_1_ = bf16[192,1024]{1,0:T(8,128)(2,1)S(1)} collective-permute-done((bf16[192,1024]{1,0:T(8,128)(2,1)S(1)}, bf16[192,1024]{1,0:T(8,128)(2,1)S(1)}, u32[]{:S(2)}, u32[]{:S(2)}) %collective-permute-start.5) | collective-permute-done | bytes 393248 | tf_op jit(solution)/shard_map/ppermute | solution.py:419
  21.7 0.0 collective-permute-done.6.refs_2_
  21.7 1.1 %shard_map.102 = (bf16[512,1024]{1,0:T(8,128)(2,1)S(1)}, bf16[256,768]{1,0:T(8,128)(2,1)S(1)}, bf16[256,256]{1,0:T(8,128)(2,1)S(1)}) custom-call(bf16[512,768]{1,0:T(8,128)(2,1)S(1)} %get-tuple-element.20.refs_2_.refs_0_, bf16[192,1024]{1,0:T(8,128)(2,1)S(1)} %collective-permute-done.5.refs_1_, bf16[192,1024]{1,0:T(8,128)(2,1)S(1)} %collective-permute-done.6.refs_2_, ...), custom_call_target="tpu_custom_call" | custom-call | flops 1540000000 | tf_op jit(solution)/shard_map/pallas_call | solution.py:27
  22.8 0.1 collective-permute-start.7
  22.8 0.5 collective-permute-start
  23.3 1.5 %collective-permute-start.1 = (f32[4,1024]{1,0:T(4,128)S(1)}, f32[4,1024]{1,0:T(4,128)S(1)}, u32[]{:S(2)}, u32[]{:S(2)}) collective-permute-start(f32[4,1024]{1,0:T(4,128)S(1)} %shard_map.93.refs_0_.refs_2_), channel_id=1, source_target_pairs={{0,2},{1,3},{2,0},{3,1},{4,6},{5,7},{6,4},{7,5},{8,10},{9,11},{10,... | collective-permute-start | bytes 49160 | tf_op jit(solution)/shard_map/ppermute | solution.py:448
  24.8 0.7 %collective-permute-done.refs_1_ = f32[4,1024]{1,0:T(4,128)S(1)} collective-permute-done((f32[4,1024]{1,0:T(4,128)S(1)}, f32[4,1024]{1,0:T(4,128)S(1)}, u32[]{:S(2)}, u32[]{:S(2)}) %collective-permute-start) | collective-permute-done | bytes 16416 | tf_op jit(solution)/shard_map/ppermute | solution.py:448
  25.5 1.6 %collective-permute-done.1.refs_2_ = f32[4,1024]{1,0:T(4,128)S(1)} collective-permute-done((f32[4,1024]{1,0:T(4,128)S(1)}, f32[4,1024]{1,0:T(4,128)S(1)}, u32[]{:S(2)}, u32[]{:S(2)}) %collective-permute-start.1) | collective-permute-done | bytes 16416 | tf_op jit(solution)/shard_map/ppermute | solution.py:448
  27.1 2.6 %collective-permute-start.2 = (f32[12,1024]{1,0:T(8,128)S(1)}, f32[12,1024]{1,0:T(8,128)S(1)}, u32[]{:S(2)}, u32[]{:S(2)}) collective-permute-start(f32[12,1024]{1,0:T(8,128)S(1)} %shard_map.94.refs_0_), channel_id=1, source_target_pairs={{0,8},{4,12},{8,0},{12,4},{16,24},{20,28},{24,16},{28,20},{1,9},{5... | collective-permute-start | bytes 147464 | tf_op jit(solution)/shard_map/ppermute | solution.py:460
  29.7 2.2 %collective-permute-done.2.refs_1_ = f32[12,1024]{1,0:T(8,128)S(1)} collective-permute-done((f32[12,1024]{1,0:T(8,128)S(1)}, f32[12,1024]{1,0:T(8,128)S(1)}, u32[]{:S(2)}, u32[]{:S(2)}) %collective-permute-start.2) | collective-permute-done | bytes 49184 | tf_op jit(solution)/shard_map/ppermute | solution.py:460
  32.0 3.1 %collective-permute-start.3 = (f32[12,1024]{1,0:T(8,128)S(1)}, f32[12,1024]{1,0:T(8,128)S(1)}, u32[]{:S(2)}, u32[]{:S(2)}) collective-permute-start(f32[12,1024]{1,0:T(8,128)S(1)} %shard_map.98.refs_0_), channel_id=1, source_target_pairs={{0,16},{4,20},{8,24},{12,28},{16,0},{20,4},{24,8},{28,12},{1,17},{... | collective-permute-start | bytes 147464 | tf_op jit(solution)/shard_map/ppermute | solution.py:460
  35.1 2.2 %collective-permute-done.3.refs_1_ = f32[12,1024]{1,0:T(8,128)S(1)} collective-permute-done((f32[12,1024]{1,0:T(8,128)S(1)}, f32[12,1024]{1,0:T(8,128)S(1)}, u32[]{:S(2)}, u32[]{:S(2)}) %collective-permute-start.3) | collective-permute-done | bytes 49184 | tf_op jit(solution)/shard_map/ppermute | solution.py:460
  37.3 0.0 copy-start.1
  37.4 1.9 %collective-permute-start.4 = (f32[12,1024]{1,0:T(8,128)S(1)}, f32[12,1024]{1,0:T(8,128)S(1)}, u32[]{:S(2)}, u32[]{:S(2)}) collective-permute-start(f32[12,1024]{1,0:T(8,128)S(1)} %shard_map.99.refs_0_), channel_id=1, source_target_pairs={{0,4},{4,0},{8,12},{12,8},{16,20},{20,16},{24,28},{28,24},{1,5},{5... | collective-permute-start | bytes 147464 | tf_op jit(solution)/shard_map/ppermute | solution.py:460
  39.2 2.3 %shard_map.104.refs_4_ = f32[1024,1024]{1,0:T(8,128)S(1)} custom-call(f32[1,4096]{1,0:T(1,128)S(1)} %bitcast.12, f32[1,4096]{1,0:T(1,128)S(1)} %bitcast.16), custom_call_target="tpu_custom_call" | custom-call | flops 2750000128 | tf_op jit(solution)/shard_map/pallas_call | solution.py:27
  41.6 0.1 collective-permute-done.4.refs_1_
  41.7 0.0 copy-done.1
  41.7 1.6 %collective-permute-start.8 = (bf16[256,768]{1,0:T(8,128)(2,1)S(1)}, bf16[256,768]{1,0:T(8,128)(2,1)S(1)}, u32[]{:S(2)}, u32[]{:S(2)}) collective-permute-start(bf16[256,768]{1,0:T(8,128)(2,1)S(1)} %get-tuple-element.29), channel_id=1, source_target_pairs={{0,2},{1,3},{2,0},{3,1},{4,6},{5,7},{6,4},{7,5},{8,10},{9,11},{10,... | collective-permute-start | bytes 1179656 | tf_op jit(solution)/shard_map/ppermute | solution.py:472
  43.3 1.4 %shard_map.105.refs_1_ = bf16[2048,1024]{1,0:T(8,128)(2,1)S(1)} custom-call(f32[8,1024]{1,0:T(8,128)S(1)} %get-tuple-element.21.refs_0_, f32[8,1024]{1,0:T(8,128)S(1)} %get-tuple-element.22.refs_1_, f32[8,1024]{1,0:T(8,128)S(1)} %get-tuple-element.28.refs_2_, f32[1024,1024]{1,0:T(8,128)S(1)} %shard_map.96.refs_4_.refs_3_, f32[1024,1024]{1,0:T(8,128)S(1)} %shard_map.104.refs_4_), custom_call_target="tpu_custom_call" | custom-call | flops 1540000000 | tf_op jit(solution)/shard_map/pallas_call | solution.py:27
  44.7 0.6 %collective-permute-start.9 = (bf16[256,256]{1,0:T(8,128)(2,1)S(1)}, bf16[256,256]{1,0:T(8,128)(2,1)S(1)}, u32[]{:S(2)}, u32[]{:S(2)}) collective-permute-start(bf16[256,256]{1,0:T(8,128)(2,1)S(1)} %get-tuple-element.30), channel_id=1, source_target_pairs={{0,2},{1,3},{2,0},{3,1},{4,6},{5,7},{6,4},{7,5},{8,10},{9,11},{10,... | collective-permute-start | bytes 393224 | tf_op jit(solution)/shard_map/ppermute | solution.py:472
  45.3 0.0 collective-permute-done.7.refs_5_.refs_4_
  45.3 2.7 %shard_map.103.refs_0_ = f32[512,128]{1,0:T(8,128)S(1)} custom-call(f32[8,1024]{1,0:T(8,128)S(1)} %get-tuple-element.21.refs_0_, f32[8,1024]{1,0:T(8,128)S(1)} %get-tuple-element.22.refs_1_, f32[1024,1024]{1,0:T(8,128)S(1)} %get-tuple-element.23.refs_2_, f32[2,512,512]{2,1,0:T(8,128)S(1)} %get-tuple-element.24.refs_3_, ...), custom_call_target="tpu_custom_call" | custom-call | flops 3740000000 | tf_op jit(solution)/shard_map/pallas_call | solution.py:27
  47.9 2.6 %collective-permute-done.8.refs_2_ = bf16[256,768]{1,0:T(8,128)(2,1)S(1)} collective-permute-done((bf16[256,768]{1,0:T(8,128)(2,1)S(1)}, bf16[256,768]{1,0:T(8,128)(2,1)S(1)}, u32[]{:S(2)}, u32[]{:S(2)}) %collective-permute-start.8) | collective-permute-done | bytes 393248 | tf_op jit(solution)/shard_map/ppermute | solution.py:472
  50.5 1.0 %shard_map.106.refs_0_ = f32[512,128]{1,0:T(8,128)S(1)} custom-call(f32[512,128]{1,0:T(8,128)S(1)} %shard_map.103.refs_0_, bf16[2048,1024]{1,0:T(8,128)(2,1)S(1)} %shard_map.105.refs_1_, bf16[256,768]{1,0:T(8,128)(2,1)S(1)} %collective-permute-done.8.refs_2_, bf16[512,1024]{1,0:T(8,128)(2,1)S(1)} %get-tuple-element.27.refs_4_.refs_3_, ...), custom_call_target="tpu_custom_call" | custom-call | flops 1732499968 | tf_op jit(solution)/shard_map/pallas_call | solution.py:27
  51.5 0.4 collective-permute-done.9.refs_2_
  51.9 0.9 %shard_map.107 = f32[1,512]{1,0:T(1,128)S(1)} custom-call(f32[512,128]{1,0:T(8,128)S(1)} %shard_map.106.refs_0_, bf16[2048,1024]{1,0:T(8,128)(2,1)S(1)} %shard_map.105.refs_1_, bf16[256,256]{1,0:T(8,128)(2,1)S(1)} %collective-permute-done.9.refs_2_, bf16[512,1024]{1,0:T(8,128)(2,1)S(1)} %get-tuple-element.27.refs_4_.refs_3_, ...), custom_call_target="tpu_custom_call" | custom-call | flops 577500032 | tf_op jit(solution)/shard_map/pallas_call | solution.py:27
  52.8 0.0 collective-permute-start.10
  52.8 1.2 %collective-permute-done.10 = f32[512]{0:T(512)S(1)} collective-permute-done((f32[512]{0:T(512)S(1)}, f32[512]{0:T(512)S(1)}, u32[]{:S(2)}, u32[]{:S(2)}) %collective-permute-start.10) | collective-permute-done | bytes 2080 | tf_op jit(solution)/shard_map/ppermute | solution.py:497
  54.0 1.5 %collective-permute-start.11 = (f32[512]{0:T(512)S(1)}, f32[512]{0:T(512)S(1)}, u32[]{:S(2)}, u32[]{:S(2)}) collective-permute-start(f32[512]{0:T(512)S(1)} %add.6), channel_id=1, source_target_pairs={{0,2},{1,3},{2,0},{3,1},{4,6},{5,7},{6,4},{7,5},{8,10},{9,11},{10,... | collective-permute-start | bytes 6152 | tf_op jit(solution)/shard_map/ppermute | solution.py:497
  55.4 2.1 %collective-permute-done.11 = f32[512]{0:T(512)S(1)} collective-permute-done((f32[512]{0:T(512)S(1)}, f32[512]{0:T(512)S(1)}, u32[]{:S(2)}, u32[]{:S(2)}) %collective-permute-start.11) | collective-permute-done | bytes 2080 | tf_op jit(solution)/shard_map/ppermute | solution.py:497
  57.5 0.6 add.7
  (5 shorter events, 0.1 us)
Async XLA Ops:
  0.0 1.4 %copy-start = (bf16[3,256,1024]{2,1,0:T(8,128)(2,1)S(1)}, bf16[3,256,1024]{2,1,0:T(8,128)(2,1)}, u32[]{:S(2)}) copy-start(bf16[3,256,1024]{2,1,0:T(8,128)(2,1)} %refs_1_.3) | copy-start | bytes 4718596
  0.0 0.8 %copy-start.6 = (s32[2,64]{1,0:T(2,128)S(1)}, s32[2,64]{1,0:T(2,128)}, u32[]{:S(2)}) copy-start(s32[2,64]{1,0:T(2,128)} %refs_0_.1) | copy-start | bytes 1540
  1.4 4.7 %copy-start.7 = (f32[256]{0:T(256)S(1)}, f32[256]{0:T(256)}, u32[]{:S(2)}) copy-start(f32[256]{0:T(256)} %param.10) | copy-start | bytes 3076
  1.8 19.8 %collective-permute-start.5 = (bf16[192,1024]{1,0:T(8,128)(2,1)S(1)}, bf16[192,1024]{1,0:T(8,128)(2,1)S(1)}, u32[]{:S(2)}, u32[]{:S(2)}) collective-permute-start(bf16[192,1024]{1,0:T(8,128)(2,1)S(1)} %shard_map.101), channel_id=1, source_target_pairs={{0,4},{4,0},{8,12},{12,8},{16,20},{20,16},{24,28},{28,24},{1,5},{5... | collective-permute-start | bytes 1179656 | tf_op jit(solution)/shard_map/ppermute | solution.py:419
  5.4 1.5 %copy-start.3 = (f32[4096]{0:T(1024)S(1)}, f32[4096]{0:T(1024)}, u32[]{:S(2)}) copy-start(f32[4096]{0:T(1024)} %param.12) | copy-start | bytes 49156
  5.4 1.5 %copy-start.4 = (f32[4096]{0:T(1024)S(1)}, f32[4096]{0:T(1024)}, u32[]{:S(2)}) copy-start(f32[4096]{0:T(1024)} %param.13) | copy-start | bytes 49156
  5.4 16.3 %collective-permute-start.6 = (bf16[192,1024]{1,0:T(8,128)(2,1)S(1)}, bf16[192,1024]{1,0:T(8,128)(2,1)S(1)}, u32[]{:S(2)}, u32[]{:S(2)}) collective-permute-start(bf16[192,1024]{1,0:T(8,128)(2,1)S(1)} %get-tuple-element.25), channel_id=1, source_target_pairs={{4,8},{8,4},{12,16},{16,12},{20,24},{24,20},{5,9},{9,5},{13,17},{1... | collective-permute-start | bytes 1179656 | tf_op jit(solution)/shard_map/ppermute | solution.py:419
  9.4 1.6 %copy-start.2 = (bf16[64,8,4,3]{0,2,3,1:T(4,128)(2,1)S(1)}, bf16[64,8,4,3]{0,2,3,1:T(4,128)(2,1)}, u32[]{:S(2)}) copy-start(bf16[64,8,4,3]{0,2,3,1:T(4,128)(2,1)} %param.14) | copy-start | bytes 36868
  9.4 1.6 %copy-start.5 = (s32[64,4]{0,1:T(4,128)S(1)}, s32[64,4]{0,1:T(4,128)}, u32[]{:S(2)}) copy-start(s32[64,4]{0,1:T(4,128)} %param.15) | copy-start | bytes 3076
  9.4 1.6 %copy-start.8 = (s32[64]{0:T(128)S(1)}, s32[64]{0:T(128)}, u32[]{:S(2)}) copy-start(s32[64]{0:T(128)} %param.16) | copy-start | bytes 772
  22.8 22.5 %collective-permute-start.7 = (bf16[512,1024]{1,0:T(8,128)(2,1)S(1)}, bf16[512,1024]{1,0:T(8,128)(2,1)S(1)}, u32[]{:S(2)}, u32[]{:S(2)}) collective-permute-start(bf16[512,1024]{1,0:T(8,128)(2,1)S(1)} %get-tuple-element.27.refs_4_.refs_3_), channel_id=1, source_target_pairs={{0,1},{1,0},{2,3},{3,2},{4,5},{5,4},{6,7},{7,6},{8,9},{9,8},{10,11... | collective-permute-start | bytes 3145736 | tf_op jit(solution)/shard_map/ppermute | solution.py:473
  22.8 2.7 %collective-permute-start = (f32[4,1024]{1,0:T(4,128)S(1)}, f32[4,1024]{1,0:T(4,128)S(1)}, u32[]{:S(2)}, u32[]{:S(2)}) collective-permute-start(f32[4,1024]{1,0:T(4,128)S(1)} %shard_map.93.refs_0_.refs_2_), channel_id=1, source_target_pairs={{0,1},{1,0},{2,3},{3,2},{4,5},{5,4},{6,7},{7,6},{8,9},{9,8},{10,11... | collective-permute-start | bytes 49160 | tf_op jit(solution)/shard_map/ppermute | solution.py:448
  23.3 3.7 %collective-permute-start.1 = (f32[4,1024]{1,0:T(4,128)S(1)}, f32[4,1024]{1,0:T(4,128)S(1)}, u32[]{:S(2)}, u32[]{:S(2)}) collective-permute-start(f32[4,1024]{1,0:T(4,128)S(1)} %shard_map.93.refs_0_.refs_2_), channel_id=1, source_target_pairs={{0,2},{1,3},{2,0},{3,1},{4,6},{5,7},{6,4},{7,5},{8,10},{9,11},{10,... | collective-permute-start | bytes 49160 | tf_op jit(solution)/shard_map/ppermute | solution.py:448
  27.1 4.9 %collective-permute-start.2 = (f32[12,1024]{1,0:T(8,128)S(1)}, f32[12,1024]{1,0:T(8,128)S(1)}, u32[]{:S(2)}, u32[]{:S(2)}) collective-permute-start(f32[12,1024]{1,0:T(8,128)S(1)} %shard_map.94.refs_0_), channel_id=1, source_target_pairs={{0,8},{4,12},{8,0},{12,4},{16,24},{20,28},{24,16},{28,20},{1,9},{5... | collective-permute-start | bytes 147464 | tf_op jit(solution)/shard_map/ppermute | solution.py:460
  32.0 5.3 %collective-permute-start.3 = (f32[12,1024]{1,0:T(8,128)S(1)}, f32[12,1024]{1,0:T(8,128)S(1)}, u32[]{:S(2)}, u32[]{:S(2)}) collective-permute-start(f32[12,1024]{1,0:T(8,128)S(1)} %shard_map.98.refs_0_), channel_id=1, source_target_pairs={{0,16},{4,20},{8,24},{12,28},{16,0},{20,4},{24,8},{28,12},{1,17},{... | collective-permute-start | bytes 147464 | tf_op jit(solution)/shard_map/ppermute | solution.py:460
  37.3 4.3 %copy-start.1 = (f32[3,4096]{1,0:T(4,128)S(1)}, f32[3,4096]{1,0:T(4,128)}, u32[]{:S(2)}) copy-start(f32[3,4096]{1,0:T(4,128)} %refs_2_.1) | copy-start | bytes 147460
  37.4 4.3 %collective-permute-start.4 = (f32[12,1024]{1,0:T(8,128)S(1)}, f32[12,1024]{1,0:T(8,128)S(1)}, u32[]{:S(2)}, u32[]{:S(2)}) collective-permute-start(f32[12,1024]{1,0:T(8,128)S(1)} %shard_map.99.refs_0_), channel_id=1, source_target_pairs={{0,4},{4,0},{8,12},{12,8},{16,20},{20,16},{24,28},{28,24},{1,5},{5... | collective-permute-start | bytes 147464 | tf_op jit(solution)/shard_map/ppermute | solution.py:460
  41.7 8.7 %collective-permute-start.8 = (bf16[256,768]{1,0:T(8,128)(2,1)S(1)}, bf16[256,768]{1,0:T(8,128)(2,1)S(1)}, u32[]{:S(2)}, u32[]{:S(2)}) collective-permute-start(bf16[256,768]{1,0:T(8,128)(2,1)S(1)} %get-tuple-element.29), channel_id=1, source_target_pairs={{0,2},{1,3},{2,0},{3,1},{4,6},{5,7},{6,4},{7,5},{8,10},{9,11},{10,... | collective-permute-start | bytes 1179656 | tf_op jit(solution)/shard_map/ppermute | solution.py:472
  44.7 7.2 %collective-permute-start.9 = (bf16[256,256]{1,0:T(8,128)(2,1)S(1)}, bf16[256,256]{1,0:T(8,128)(2,1)S(1)}, u32[]{:S(2)}, u32[]{:S(2)}) collective-permute-start(bf16[256,256]{1,0:T(8,128)(2,1)S(1)} %get-tuple-element.30), channel_id=1, source_target_pairs={{0,2},{1,3},{2,0},{3,1},{4,6},{5,7},{6,4},{7,5},{8,10},{9,11},{10,... | collective-permute-start | bytes 393224 | tf_op jit(solution)/shard_map/ppermute | solution.py:472
  52.8 1.2 %collective-permute-start.10 = (f32[512]{0:T(512)S(1)}, f32[512]{0:T(512)S(1)}, u32[]{:S(2)}, u32[]{:S(2)}) collective-permute-start(f32[512]{0:T(512)S(1)} %bitcast.7), channel_id=1, source_target_pairs={{0,1},{1,0},{2,3},{3,2},{4,5},{5,4},{6,7},{7,6},{8,9},{9,8},{10,11... | collective-permute-start | bytes 6152 | tf_op jit(solution)/shard_map/ppermute | solution.py:497
  54.0 3.6 %collective-permute-start.11 = (f32[512]{0:T(512)S(1)}, f32[512]{0:T(512)S(1)}, u32[]{:S(2)}, u32[]{:S(2)}) collective-permute-start(f32[512]{0:T(512)S(1)} %add.6), channel_id=1, source_target_pairs={{0,2},{1,3},{2,0},{3,1},{4,6},{5,7},{6,4},{7,5},{8,10},{9,11},{10,... | collective-permute-start | bytes 6152 | tf_op jit(solution)/shard_map/ppermute | solution.py:497

commit v13 on v11

--- a/solution.py
+++ b/solution.py
@@ -44,25 +44,31 @@
     out_ref[...] = left_ref[...] + right_ref[...]
 
 
-def gather_kernel(shared_ref, shapes_ref, first_ref, *refs):
-    second_refs, (held_ref, sem) = refs[:-2], refs[-2:]
-    dims, nodes, _ = held_ref.shape
-    width = shared_ref.shape[1]
+def pick_kernel(shared_ref, pick_ref):
+    nodes = pick_ref.shape[1]
+    odd = lax.axis_index("dom") & 1
+    wanted = jnp.concatenate([shared_ref[pl.ds(1 - odd, 1), :], shared_ref[pl.ds(odd, 1), :]], axis=1)
+    node = lax.broadcasted_iota(jnp.int32, (nodes, wanted.shape[1]), 0)
+    pick_ref[...] = jnp.where(node == wanted, 1.0, 0.0).astype(F32).T.astype(BF16)
+
+
+def pair_rows_kernel(pick_ref, shapes_ref, out_ref):
+    dims = shapes_ref.shape[0]
+    width = out_ref.shape[0] // dims
+    for d in range(dims):
+        got = jnp.dot(pick_ref[:width, :], shapes_ref[d], preferred_element_type=F32)
+        out_ref[d * width : (d + 1) * width, :] = got.astype(BF16)
+
+
+def next_rows_kernel(pick_ref, shapes_ref, out_ref, held_ref, sem):
+    dims = held_ref.shape[0]
+    width = out_ref.shape[0] // dims
     load = pltpu.make_async_copy(shapes_ref, held_ref, sem)
     load.start()
-    node = lax.broadcasted_iota(jnp.int32, (nodes, 2 * width), 0)
-    odd = lax.axis_index("dom") & 1
-    wanted = jnp.concatenate([shared_ref[pl.ds(1 - odd, 1), :], shared_ref[pl.ds(odd, 1), :]], axis=1)
-    pick = jnp.where(node == wanted, 1.0, 0.0).astype(F32).T.astype(BF16)
     load.wait()
     for d in range(dims):
-        got = jnp.dot(pick, held_ref[d], preferred_element_type=F32).astype(BF16)
-        first_ref[d * width : (d + 1) * width, :] = got[:width]
-        at = 0
-        for second_ref in second_refs:
-            lanes = slice(at, at + second_ref.shape[1])
-            second_ref[d * width : (d + 1) * width, :] = got[width:, lanes]
-            at = lanes.stop
+        got = jnp.dot(pick_ref[width:, :], held_ref[d], preferred_element_type=F32)
+        out_ref[d * width : (d + 1) * width, :] = got.astype(BF16)
 
 
 def stats_kernel(mass_ref, shapes_ref, out_ref, mass_scr):
@@ -221,7 +227,7 @@
         for d in range(dims):
             base = (copy * dims + d) * 2 * width
             rim_scr[base : base + width, :] = first_ref[d * width : (d + 1) * width, lanes]
-            rim_scr[base + width : base + 2 * width, :] = second_ref[d * width : (d + 1) * width, :]
+            rim_scr[base + width : base + 2 * width, :] = second_ref[d * width : (d + 1) * width, lanes]
     for c in range(0, chunk, 256):
         total = jnp.dot(rim_ref[...], rim_scr[:, c : c + 256], preferred_element_type=F32)
         all_ref[:, c : c + 256] = (local_ref[:, at + c : at + c + 256] + total).astype(BF16)
@@ -406,15 +412,14 @@
     freq = frequencies.reshape(1, -1)
     rate = damping.reshape(1, -1)
 
-    chunk = block // CHUNKS
-    outgoing, *others, held = call(
-        gather_kernel,
-        [sds((dims * width, size), BF16) for size in [block] + [chunk] * CHUNKS] + [sds(shapes.shape, BF16)],
-        (shared, shapes),
-        2.0, hbm=(1,), scratch=[pltpu.SemaphoreType.DMA],
-    )
-    first_rim = lax.ppermute(outgoing, "dom", halves[0])
-    rims = [lax.ppermute(other, "dom", halves[1]) for other in others]
+    picked = call(pick_kernel, sds((2 * width, nodes), BF16), (shared,), 2.0)
+    rows = sds((dims * width, block), BF16)
+    outgoing = call(pair_rows_kernel, rows, (picked, shapes), 0.4)
+    other, held = call(
+        next_rows_kernel, [rows, sds(shapes.shape, BF16)], (picked, shapes), 0.7, hbm=(1,),
+        scratch=[pltpu.SemaphoreType.DMA],
+    )
+    rims = (lax.ppermute(outgoing, "dom", halves[0]), lax.ppermute(other, "dom", halves[1]))
     stats = call(
         stats_kernel, sds((dims + 1, block), F32), (masses.reshape(1, nodes), held), 0.8,
         scratch=[pltpu.VMEM((nodes, 128), F32)],
@@ -460,12 +465,13 @@
         amps_kernel, [sds((8, block), F32)] * 3, (stats, extra, spectral, freq, rate), 0.8,
     )
 
+    chunk = block // CHUNKS
     own, mate, far = [], [], []
     for c in range(CHUNKS):
         forces, sent = call(
             functools.partial(forces_kernel, c * chunk, dims),
             [sds((comps, chunk), BF16), sds((part, chunk), BF16)],
-            (rim, first_rim, rims[c], local), 0.8,
+            (rim, *rims, local), 0.6,
             scratch=[pltpu.VMEM((4 * dims * width, chunk), BF16)],
         )
         own.append(forces)

time: 53.8 us -> 53.6 us (level)
  starting transfers between devices: 20.8 us -> 17 us
  waiting for transfers between devices: 13.2 us -> 17 us
  local copies, waits for them, and re-layouts: 2.13 us -> 1.44 us
    ppermute x3, waiting for transfers between devices: 1.24 us -> 4.66 us  [combined(): extra = lax.ppermute(stats, 'dom', [(i, i ^ reach) for i in range(parts)])]
    ppermute x3, starting transfers between devices: 11.6 us -> 8.42 us  [combined(): extra = lax.ppermute(stats, 'dom', [(i, i ^ reach) for i in range(parts)])]
    unnamed x18, local copies, waits for them, and re-layouts: 2.13 us -> 1.44 us
    ppermute x3 -> x2, starting transfers between devices: 2.83 us -> 2.23 us  [the longest x1 1.56 us: combined(): lax.ppermute(outgoing, 'dom', halves[0])]
    pallas_call x16 -> x18, Pallas kernels: 16.8 us -> 17.2 us  [call(): pl.pallas_call(body, out_shape=out_shape, in_specs=specs, out_specs=[VMEM...]
  transfers between devices with their start and end apart: 14 -> 13, of which waited for: 7 -> 6; matrix products, arithmetic and copies ran while one was open for 0% -> 0% of each run, Pallas kernels for 27% -> 27%
where the time goes in v13:
time: 53.6 us; the launch traced here: 53.4 us
  Pallas kernels  17.2 us (32%)
  starting transfers between devices  17 us (32%)
  waiting for transfers between devices  17 us (32%)
  local copies, waits for them, and re-layouts  1.44 us (3%)
  other arithmetic  0.58 us (1%)
    pallas_call x18, Pallas kernels, call(): pl.pallas_call(body, out_shape=out_shape, in_specs=specs, out_specs=[VMEM...  17.2 us
    ppermute x3, starting transfers between devices, combined(): extra = lax.ppermute(stats, 'dom', [(i, i ^ reach) for i in range(parts)])  8.42 us
    ppermute x2, waiting for transfers between devices, combined(): far.append(lax.ppermute(sent, 'mode', [(i, i ^ 2) for i in range(4)]))  8.04 us
    ppermute x3, waiting for transfers between devices, combined(): extra = lax.ppermute(stats, 'dom', [(i, i ^ reach) for i in range(parts)])  4.66 us
    ppermute x2, waiting for transfers between devices, combined(): lax.ppermute(value, 'mode', [(i, i ^ reach) for i in range(4)])  4.3 us
    ppermute x2, starting transfers between devices, combined(): lax.ppermute(stats, 'mode', [(i, i ^ q) for i in range(4)])  3.14 us
    ppermute x2, starting transfers between devices, combined(): far.append(lax.ppermute(sent, 'mode', [(i, i ^ 2) for i in range(4)]))  2.09 us
    ppermute x1, starting transfers between devices, combined(): lax.ppermute(outgoing, 'dom', halves[0])  1.56 us
  transfers between devices with their start and end apart: 13, of which 6 were waited for; matrix products, arithmetic and copies ran while one was open for 0% of the time, Pallas kernels for 27%

profile of v13, /device:TPU:0, one launch (start us, length us, event | category | flops | bytes accessed | tf_op | source)
XLA Modules:
  0.0 53.4 jit_solution(9629079752907939222)
XLA Ops:
  0.0 0.0 copy-start
  0.0 0.0 copy-start.6
  0.0 0.8 %copy-done.6 = s32[2,64]{1,0:T(2,128)S(1)} copy-done((s32[2,64]{1,0:T(2,128)S(1)}, s32[2,64]{1,0:T(2,128)}, u32[]{:S(2)}) %copy-start.6) | copy-done | bytes 536
  0.8 0.2 shard_map.91.refs_0_
  1.0 0.4 copy-done
  1.4 0.0 copy-start.7
  1.4 0.5 shard_map.92
  1.9 0.2 copy-done.7
  2.1 0.0 copy-start.3
  2.1 0.0 copy-start.4
  2.1 0.8 %shard_map.93.refs_0_.refs_2_ = f32[4,1024]{1,0:T(4,128)S(1)} custom-call(f32[1,256]{1,0:T(1,128)S(1)} %bitcast.19, bf16[3,256,1024]{2,1,0:T(8,128)(2,1)S(1)} %get-tuple-element.19.refs_1_.refs_3_), custom_call_target="tpu_custom_call" | custom-call | flops 880000000 | tf_op jit(solution)/shard_map/pallas_call | solution.py:27
  2.9 0.6 %collective-permute-start = (f32[4,1024]{1,0:T(4,128)S(1)}, f32[4,1024]{1,0:T(4,128)S(1)}, u32[]{:S(2)}, u32[]{:S(2)}) collective-permute-start(f32[4,1024]{1,0:T(4,128)S(1)} %shard_map.93.refs_0_.refs_2_), channel_id=1, source_target_pairs={{0,1},{1,0},{2,3},{3,2},{4,5},{5,4},{6,7},{7,6},{8,9},{9,8},{10,11... | collective-permute-start | bytes 49160 | tf_op jit(solution)/shard_map/ppermute | solution.py:451
  3.5 2.6 %collective-permute-start.1 = (f32[4,1024]{1,0:T(4,128)S(1)}, f32[4,1024]{1,0:T(4,128)S(1)}, u32[]{:S(2)}, u32[]{:S(2)}) collective-permute-start(f32[4,1024]{1,0:T(4,128)S(1)} %shard_map.93.refs_0_.refs_2_), channel_id=1, source_target_pairs={{0,2},{1,3},{2,0},{3,1},{4,6},{5,7},{6,4},{7,5},{8,10},{9,11},{10,... | collective-permute-start | bytes 49160 | tf_op jit(solution)/shard_map/ppermute | solution.py:451
  6.1 0.4 shard_map.101
  6.5 1.6 %collective-permute-start.5 = (bf16[192,1024]{1,0:T(8,128)(2,1)S(1)}, bf16[192,1024]{1,0:T(8,128)(2,1)S(1)}, u32[]{:S(2)}, u32[]{:S(2)}) collective-permute-start(bf16[192,1024]{1,0:T(8,128)(2,1)S(1)} %shard_map.101), channel_id=1, source_target_pairs={{0,4},{4,0},{8,12},{12,8},{16,20},{20,16},{24,28},{28,24},{1,5},{5... | collective-permute-start | bytes 1179656 | tf_op jit(solution)/shard_map/ppermute | solution.py:422
  8.0 0.7 %collective-permute-start.6 = (bf16[192,1024]{1,0:T(8,128)(2,1)S(1)}, bf16[192,1024]{1,0:T(8,128)(2,1)S(1)}, u32[]{:S(2)}, u32[]{:S(2)}) collective-permute-start(bf16[192,1024]{1,0:T(8,128)(2,1)S(1)} %get-tuple-element.26), channel_id=1, source_target_pairs={{4,8},{8,4},{12,16},{16,12},{20,24},{24,20},{5,9},{9,5},{13,17},{1... | collective-permute-start | bytes 1179656 | tf_op jit(solution)/shard_map/ppermute | solution.py:422
  8.7 0.0 copy-done.3
  8.7 0.0 copy-done.4
  8.7 2.4 %shard_map.95 = (f32[1024,1024]{1,0:T(8,128)S(1)}, f32[2,512,512]{2,1,0:T(8,128)S(1)}, f32[4,1024,128]{2,1,0:T(8,128)S(1)}) custom-call(f32[1,4096]{1,0:T(1,128)S(1)} %bitcast.10, f32[1,4096]{1,0:T(1,128)S(1)} %bitcast.14, f32[4,1024]{1,0:T(4,128)S(1)} %shard_map.93.refs_0_.refs_2_), custom_call_target="tpu_custom_call" | custom-call | flops 3300000000 | tf_op jit(solution)/shard_map/pallas_call | solution.py:27
  11.1 0.0 copy-start.2
  11.2 0.0 copy-start.5
  11.2 0.0 copy-start.8
  11.2 1.6 %shard_map.96.refs_4_.refs_3_ = f32[1024,1024]{1,0:T(8,128)S(1)} custom-call(f32[1,4096]{1,0:T(1,128)S(1)} %bitcast.11, f32[1,4096]{1,0:T(1,128)S(1)} %bitcast.15, f32[4,1024,128]{2,1,0:T(8,128)S(1)} %get-tuple-element.20.refs_2_), custom_call_target="tpu_custom_call" | custom-call | flops 2090000000 | tf_op jit(solution)/shard_map/pallas_call | solution.py:27
  12.7 0.0 collective-permute-done.refs_1_
  12.8 0.0 collective-permute-done.1.refs_2_
  12.8 3.3 %collective-permute-start.2 = (f32[12,1024]{1,0:T(8,128)S(1)}, f32[12,1024]{1,0:T(8,128)S(1)}, u32[]{:S(2)}, u32[]{:S(2)}) collective-permute-start(f32[12,1024]{1,0:T(8,128)S(1)} %shard_map.94.refs_0_), channel_id=1, source_target_pairs={{0,8},{4,12},{8,0},{12,4},{16,24},{20,28},{24,16},{28,20},{1,9},{5... | collective-permute-start | bytes 147464 | tf_op jit(solution)/shard_map/ppermute | solution.py:463
  16.1 0.0 copy-done.2
  16.1 0.0 copy-done.5
  16.1 0.0 copy-done.8
  16.1 1.8 %shard_map.97 = (f32[512,1024]{1,0:T(8,128)S(1)}, bf16[512,768]{1,0:T(8,128)(2,1)S(1)}) custom-call(s32[4,64]{1,0:T(4,128)S(1)} %bitcast.18, s32[1,64]{1,0:T(1,128)S(1)} %bitcast.20, bf16[8,3,4,64]{3,2,1,0:T(4,128)(2,1)S(1)} %bitcast.9, bf16[3,256,1024]{2,1,0:T(8,128)(2,1)S(1)} %get-tuple-element.19.refs_1_.refs_3_, f32[1024,1024]{1,0:T(8,128)S(1)} %shard_map.96.refs_4_.refs_3_), custom_call_target="tpu_custom_call" | custom-call | flops 1980000000 | tf_op jit(solution)/shard_map/pallas_call | solution.py:27
  17.9 4.3 %collective-permute-done.2.refs_1_ = f32[12,1024]{1,0:T(8,128)S(1)} collective-permute-done((f32[12,1024]{1,0:T(8,128)S(1)}, f32[12,1024]{1,0:T(8,128)S(1)}, u32[]{:S(2)}, u32[]{:S(2)}) %collective-permute-start.2) | collective-permute-done | bytes 49184 | tf_op jit(solution)/shard_map/ppermute | solution.py:463
  22.2 3.1 %collective-permute-start.3 = (f32[12,1024]{1,0:T(8,128)S(1)}, f32[12,1024]{1,0:T(8,128)S(1)}, u32[]{:S(2)}, u32[]{:S(2)}) collective-permute-start(f32[12,1024]{1,0:T(8,128)S(1)} %shard_map.98.refs_0_), channel_id=1, source_target_pairs={{0,16},{4,20},{8,24},{12,28},{16,0},{20,4},{24,8},{28,12},{1,17},{... | collective-permute-start | bytes 147464 | tf_op jit(solution)/shard_map/ppermute | solution.py:463
  25.3 0.0 collective-permute-done.5.refs_1_
  25.3 0.0 collective-permute-done.6.refs_2_
  25.3 0.6 %shard_map.102 = (bf16[512,512]{1,0:T(8,128)(2,1)S(1)}, bf16[256,512]{1,0:T(8,128)(2,1)S(1)}) custom-call(bf16[512,768]{1,0:T(8,128)(2,1)S(1)} %get-tuple-element.21.refs_2_.refs_0_, bf16[192,1024]{1,0:T(8,128)(2,1)S(1)} %collective-permute-done.5.refs_1_, bf16[192,1024]{1,0:T(8,128)(2,1)S(1)} %collective-permute-done.6.refs_2_, ...), custom_call_target="tpu_custom_call" | custom-call | flops 660000000 | tf_op jit(solution)/shard_map/pallas_call | solution.py:27
  25.9 0.1 collective-permute-start.7
  26.0 0.6 %shard_map.103 = (bf16[512,512]{1,0:T(8,128)(2,1)S(1)}, bf16[256,512]{1,0:T(8,128)(2,1)S(1)}) custom-call(bf16[512,768]{1,0:T(8,128)(2,1)S(1)} %get-tuple-element.21.refs_2_.refs_0_, bf16[192,1024]{1,0:T(8,128)(2,1)S(1)} %collective-permute-done.5.refs_1_, bf16[192,1024]{1,0:T(8,128)(2,1)S(1)} %collective-permute-done.6.refs_2_, ...), custom_call_target="tpu_custom_call" | custom-call | flops 660000000 | tf_op jit(solution)/shard_map/pallas_call | solution.py:27
  26.6 0.6 %collective-permute-start.8 = (bf16[512,512]{1,0:T(8,128)(2,1)S(1)}, bf16[512,512]{1,0:T(8,128)(2,1)S(1)}, u32[]{:S(2)}, u32[]{:S(2)}) collective-permute-start(bf16[512,512]{1,0:T(8,128)(2,1)S(1)} %get-tuple-element.29.refs_5_.refs_4_), channel_id=1, source_target_pairs={{0,1},{1,0},{2,3},{3,2},{4,5},{5,4},{6,7},{7,6},{8,9},{9,8},{10,11... | collective-permute-start | bytes 1572872 | tf_op jit(solution)/shard_map/ppermute | solution.py:479
  27.2 0.3 collective-permute-done.3.refs_1_
  27.5 0.0 copy-start.1
  27.6 2.1 %collective-permute-start.4 = (f32[12,1024]{1,0:T(8,128)S(1)}, f32[12,1024]{1,0:T(8,128)S(1)}, u32[]{:S(2)}, u32[]{:S(2)}) collective-permute-start(f32[12,1024]{1,0:T(8,128)S(1)} %shard_map.99.refs_0_), channel_id=1, source_target_pairs={{0,4},{4,0},{8,12},{12,8},{16,20},{20,16},{24,28},{28,24},{1,5},{5... | collective-permute-start | bytes 147464 | tf_op jit(solution)/shard_map/ppermute | solution.py:463
  29.6 2.3 %shard_map.105.refs_4_ = f32[1024,1024]{1,0:T(8,128)S(1)} custom-call(f32[1,4096]{1,0:T(1,128)S(1)} %bitcast.12, f32[1,4096]{1,0:T(1,128)S(1)} %bitcast.16), custom_call_target="tpu_custom_call" | custom-call | flops 2750000128 | tf_op jit(solution)/shard_map/pallas_call | solution.py:27
  32.0 0.0 collective-permute-done.4.refs_1_
  32.0 0.0 copy-done.1
  32.0 1.4 %shard_map.106.refs_1_ = bf16[2048,1024]{1,0:T(8,128)(2,1)S(1)} custom-call(f32[8,1024]{1,0:T(8,128)S(1)} %get-tuple-element.22.refs_0_, f32[8,1024]{1,0:T(8,128)S(1)} %get-tuple-element.23.refs_1_, f32[8,1024]{1,0:T(8,128)S(1)} %get-tuple-element.30.refs_2_, f32[1024,1024]{1,0:T(8,128)S(1)} %shard_map.96.refs_4_.refs_3_, f32[1024,1024]{1,0:T(8,128)S(1)} %shard_map.105.refs_4_), custom_call_target="tpu_custom_call" | custom-call | flops 1540000000 | tf_op jit(solution)/shard_map/pallas_call | solution.py:27
  33.4 0.5 collective-permute-start.9
  33.9 1.6 %collective-permute-start.10 = (bf16[256,512]{1,0:T(8,128)(2,1)S(1)}, bf16[256,512]{1,0:T(8,128)(2,1)S(1)}, u32[]{:S(2)}, u32[]{:S(2)}) collective-permute-start(bf16[256,512]{1,0:T(8,128)(2,1)S(1)} %get-tuple-element.32), channel_id=1, source_target_pairs={{0,2},{1,3},{2,0},{3,1},{4,6},{5,7},{6,4},{7,5},{8,10},{9,11},{10,... | collective-permute-start | bytes 786440 | tf_op jit(solution)/shard_map/ppermute | solution.py:478
  35.5 0.0 collective-permute-done.7.refs_6_.refs_5_
  35.5 0.0 collective-permute-done.8.refs_7_.refs_6_
  35.5 2.8 %shard_map.104.refs_0_ = f32[512,128]{1,0:T(8,128)S(1)} custom-call(f32[8,1024]{1,0:T(8,128)S(1)} %get-tuple-element.22.refs_0_, f32[8,1024]{1,0:T(8,128)S(1)} %get-tuple-element.23.refs_1_, f32[1024,1024]{1,0:T(8,128)S(1)} %get-tuple-element.24.refs_2_, f32[2,512,512]{2,1,0:T(8,128)S(1)} %get-tuple-element.25.refs_3_, ...), custom_call_target="tpu_custom_call" | custom-call | flops 3740000000 | tf_op jit(solution)/shard_map/pallas_call | solution.py:27
  38.3 4.4 %collective-permute-done.9.refs_2_ = bf16[256,512]{1,0:T(8,128)(2,1)S(1)} collective-permute-done((bf16[256,512]{1,0:T(8,128)(2,1)S(1)}, bf16[256,512]{1,0:T(8,128)(2,1)S(1)}, u32[]{:S(2)}, u32[]{:S(2)}) %collective-permute-start.9) | collective-permute-done | bytes 262176 | tf_op jit(solution)/shard_map/ppermute | solution.py:478
  42.6 0.7 %shard_map.107.refs_0_ = f32[512,128]{1,0:T(8,128)S(1)} custom-call(f32[512,128]{1,0:T(8,128)S(1)} %shard_map.104.refs_0_, bf16[2048,1024]{1,0:T(8,128)(2,1)S(1)} %shard_map.106.refs_1_, bf16[256,512]{1,0:T(8,128)(2,1)S(1)} %collective-permute-done.9.refs_2_, bf16[512,512]{1,0:T(8,128)(2,1)S(1)} %get-tuple-element.28.refs_4_.refs_3_, ...), custom_call_target="tpu_custom_call" | custom-call | flops 1100000000 | tf_op jit(solution)/shard_map/pallas_call | solution.py:27
  43.4 3.7 %collective-permute-done.10.refs_2_ = bf16[256,512]{1,0:T(8,128)(2,1)S(1)} collective-permute-done((bf16[256,512]{1,0:T(8,128)(2,1)S(1)}, bf16[256,512]{1,0:T(8,128)(2,1)S(1)}, u32[]{:S(2)}, u32[]{:S(2)}) %collective-permute-start.10) | collective-permute-done | bytes 262176 | tf_op jit(solution)/shard_map/ppermute | solution.py:478
  47.0 1.0 %shard_map.108 = f32[1,512]{1,0:T(1,128)S(1)} custom-call(f32[512,128]{1,0:T(8,128)S(1)} %shard_map.107.refs_0_, bf16[2048,1024]{1,0:T(8,128)(2,1)S(1)} %shard_map.106.refs_1_, bf16[256,512]{1,0:T(8,128)(2,1)S(1)} %collective-permute-done.10.refs_2_, bf16[512,512]{1,0:T(8,128)(2,1)S(1)} %get-tuple-element.28.refs_4_.refs_3_, ...), custom_call_target="tpu_custom_call" | custom-call | flops 1100000000 | tf_op jit(solution)/shard_map/pallas_call | solution.py:27
  48.0 0.0 collective-permute-start.11
  48.1 1.2 %collective-permute-done.11 = f32[512]{0:T(512)S(1)} collective-permute-done((f32[512]{0:T(512)S(1)}, f32[512]{0:T(512)S(1)}, u32[]{:S(2)}, u32[]{:S(2)}) %collective-permute-start.11) | collective-permute-done | bytes 2080 | tf_op jit(solution)/shard_map/ppermute | solution.py:502
  49.2 0.4 collective-permute-start.12
  49.7 3.1 %collective-permute-done.12 = f32[512]{0:T(512)S(1)} collective-permute-done((f32[512]{0:T(512)S(1)}, f32[512]{0:T(512)S(1)}, u32[]{:S(2)}, u32[]{:S(2)}) %collective-permute-start.12) | collective-permute-done | bytes 2080 | tf_op jit(solution)/shard_map/ppermute | solution.py:502
  52.8 0.6 %add.7 = f32[512]{0:T(512)} add(f32[512]{0:T(512)S(1)} %add.6, f32[512]{0:T(512)S(1)} %collective-permute-done.12) | non-fusion elementwise | flops 512 | bytes 6144 | tf_op jit(solution)/shard_map/add | solution.py:502
  (5 shorter events, 0.1 us)
Async XLA Ops:
  0.0 1.4 %copy-start = (bf16[3,256,1024]{2,1,0:T(8,128)(2,1)S(1)}, bf16[3,256,1024]{2,1,0:T(8,128)(2,1)}, u32[]{:S(2)}) copy-start(bf16[3,256,1024]{2,1,0:T(8,128)(2,1)} %refs_1_.3) | copy-start | bytes 4718596
  0.0 0.8 %copy-start.6 = (s32[2,64]{1,0:T(2,128)S(1)}, s32[2,64]{1,0:T(2,128)}, u32[]{:S(2)}) copy-start(s32[2,64]{1,0:T(2,128)} %refs_0_.1) | copy-start | bytes 1540
  1.4 0.7 %copy-start.7 = (f32[256]{0:T(256)S(1)}, f32[256]{0:T(256)}, u32[]{:S(2)}) copy-start(f32[256]{0:T(256)} %param.10) | copy-start | bytes 3076
  2.1 6.6 %copy-start.3 = (f32[4096]{0:T(1024)S(1)}, f32[4096]{0:T(1024)}, u32[]{:S(2)}) copy-start(f32[4096]{0:T(1024)} %param.12) | copy-start | bytes 49156
  2.1 6.6 %copy-start.4 = (f32[4096]{0:T(1024)S(1)}, f32[4096]{0:T(1024)}, u32[]{:S(2)}) copy-start(f32[4096]{0:T(1024)} %param.13) | copy-start | bytes 49156
  2.9 9.8 %collective-permute-start = (f32[4,1024]{1,0:T(4,128)S(1)}, f32[4,1024]{1,0:T(4,128)S(1)}, u32[]{:S(2)}, u32[]{:S(2)}) collective-permute-start(f32[4,1024]{1,0:T(4,128)S(1)} %shard_map.93.refs_0_.refs_2_), channel_id=1, source_target_pairs={{0,1},{1,0},{2,3},{3,2},{4,5},{5,4},{6,7},{7,6},{8,9},{9,8},{10,11... | collective-permute-start | bytes 49160 | tf_op jit(solution)/shard_map/ppermute | solution.py:451
  3.5 9.3 %collective-permute-start.1 = (f32[4,1024]{1,0:T(4,128)S(1)}, f32[4,1024]{1,0:T(4,128)S(1)}, u32[]{:S(2)}, u32[]{:S(2)}) collective-permute-start(f32[4,1024]{1,0:T(4,128)S(1)} %shard_map.93.refs_0_.refs_2_), channel_id=1, source_target_pairs={{0,2},{1,3},{2,0},{3,1},{4,6},{5,7},{6,4},{7,5},{8,10},{9,11},{10,... | collective-permute-start | bytes 49160 | tf_op jit(solution)/shard_map/ppermute | solution.py:451
  6.5 18.8 %collective-permute-start.5 = (bf16[192,1024]{1,0:T(8,128)(2,1)S(1)}, bf16[192,1024]{1,0:T(8,128)(2,1)S(1)}, u32[]{:S(2)}, u32[]{:S(2)}) collective-permute-start(bf16[192,1024]{1,0:T(8,128)(2,1)S(1)} %shard_map.101), channel_id=1, source_target_pairs={{0,4},{4,0},{8,12},{12,8},{16,20},{20,16},{24,28},{28,24},{1,5},{5... | collective-permute-start | bytes 1179656 | tf_op jit(solution)/shard_map/ppermute | solution.py:422
  8.0 17.3 %collective-permute-start.6 = (bf16[192,1024]{1,0:T(8,128)(2,1)S(1)}, bf16[192,1024]{1,0:T(8,128)(2,1)S(1)}, u32[]{:S(2)}, u32[]{:S(2)}) collective-permute-start(bf16[192,1024]{1,0:T(8,128)(2,1)S(1)} %get-tuple-element.26), channel_id=1, source_target_pairs={{4,8},{8,4},{12,16},{16,12},{20,24},{24,20},{5,9},{9,5},{13,17},{1... | collective-permute-start | bytes 1179656 | tf_op jit(solution)/shard_map/ppermute | solution.py:422
  11.1 4.9 %copy-start.2 = (bf16[64,8,4,3]{0,2,3,1:T(4,128)(2,1)S(1)}, bf16[64,8,4,3]{0,2,3,1:T(4,128)(2,1)}, u32[]{:S(2)}) copy-start(bf16[64,8,4,3]{0,2,3,1:T(4,128)(2,1)} %param.14) | copy-start | bytes 36868
  11.2 4.9 %copy-start.5 = (s32[64,4]{0,1:T(4,128)S(1)}, s32[64,4]{0,1:T(4,128)}, u32[]{:S(2)}) copy-start(s32[64,4]{0,1:T(4,128)} %param.15) | copy-start | bytes 3076
  11.2 4.9 %copy-start.8 = (s32[64]{0:T(128)S(1)}, s32[64]{0:T(128)}, u32[]{:S(2)}) copy-start(s32[64]{0:T(128)} %param.16) | copy-start | bytes 772
  12.8 9.4 %collective-permute-start.2 = (f32[12,1024]{1,0:T(8,128)S(1)}, f32[12,1024]{1,0:T(8,128)S(1)}, u32[]{:S(2)}, u32[]{:S(2)}) collective-permute-start(f32[12,1024]{1,0:T(8,128)S(1)} %shard_map.94.refs_0_), channel_id=1, source_target_pairs={{0,8},{4,12},{8,0},{12,4},{16,24},{20,28},{24,16},{28,20},{1,9},{5... | collective-permute-start | bytes 147464 | tf_op jit(solution)/shard_map/ppermute | solution.py:463
  22.2 5.3 %collective-permute-start.3 = (f32[12,1024]{1,0:T(8,128)S(1)}, f32[12,1024]{1,0:T(8,128)S(1)}, u32[]{:S(2)}, u32[]{:S(2)}) collective-permute-start(f32[12,1024]{1,0:T(8,128)S(1)} %shard_map.98.refs_0_), channel_id=1, source_target_pairs={{0,16},{4,20},{8,24},{12,28},{16,0},{20,4},{24,8},{28,12},{1,17},{... | collective-permute-start | bytes 147464 | tf_op jit(solution)/shard_map/ppermute | solution.py:463
  25.9 9.6 %collective-permute-start.7 = (bf16[512,512]{1,0:T(8,128)(2,1)S(1)}, bf16[512,512]{1,0:T(8,128)(2,1)S(1)}, u32[]{:S(2)}, u32[]{:S(2)}) collective-permute-start(bf16[512,512]{1,0:T(8,128)(2,1)S(1)} %get-tuple-element.28.refs_4_.refs_3_), channel_id=1, source_target_pairs={{0,1},{1,0},{2,3},{3,2},{4,5},{5,4},{6,7},{7,6},{8,9},{9,8},{10,11... | collective-permute-start | bytes 1572872 | tf_op jit(solution)/shard_map/ppermute | solution.py:479
  26.6 8.8 %collective-permute-start.8 = (bf16[512,512]{1,0:T(8,128)(2,1)S(1)}, bf16[512,512]{1,0:T(8,128)(2,1)S(1)}, u32[]{:S(2)}, u32[]{:S(2)}) collective-permute-start(bf16[512,512]{1,0:T(8,128)(2,1)S(1)} %get-tuple-element.29.refs_5_.refs_4_), channel_id=1, source_target_pairs={{0,1},{1,0},{2,3},{3,2},{4,5},{5,4},{6,7},{7,6},{8,9},{9,8},{10,11... | collective-permute-start | bytes 1572872 | tf_op jit(solution)/shard_map/ppermute | solution.py:479
  27.5 4.4 %copy-start.1 = (f32[3,4096]{1,0:T(4,128)S(1)}, f32[3,4096]{1,0:T(4,128)}, u32[]{:S(2)}) copy-start(f32[3,4096]{1,0:T(4,128)} %refs_2_.1) | copy-start | bytes 147460
  27.6 4.4 %collective-permute-start.4 = (f32[12,1024]{1,0:T(8,128)S(1)}, f32[12,1024]{1,0:T(8,128)S(1)}, u32[]{:S(2)}, u32[]{:S(2)}) collective-permute-start(f32[12,1024]{1,0:T(8,128)S(1)} %shard_map.99.refs_0_), channel_id=1, source_target_pairs={{0,4},{4,0},{8,12},{12,8},{16,20},{20,16},{24,28},{28,24},{1,5},{5... | collective-permute-start | bytes 147464 | tf_op jit(solution)/shard_map/ppermute | solution.py:463
  33.4 9.2 %collective-permute-start.9 = (bf16[256,512]{1,0:T(8,128)(2,1)S(1)}, bf16[256,512]{1,0:T(8,128)(2,1)S(1)}, u32[]{:S(2)}, u32[]{:S(2)}) collective-permute-start(bf16[256,512]{1,0:T(8,128)(2,1)S(1)} %get-tuple-element.31), channel_id=1, source_target_pairs={{0,2},{1,3},{2,0},{3,1},{4,6},{5,7},{6,4},{7,5},{8,10},{9,11},{10,... | collective-permute-start | bytes 786440 | tf_op jit(solution)/shard_map/ppermute | solution.py:478
  33.9 13.1 %collective-permute-start.10 = (bf16[256,512]{1,0:T(8,128)(2,1)S(1)}, bf16[256,512]{1,0:T(8,128)(2,1)S(1)}, u32[]{:S(2)}, u32[]{:S(2)}) collective-permute-start(bf16[256,512]{1,0:T(8,128)(2,1)S(1)} %get-tuple-element.32), channel_id=1, source_target_pairs={{0,2},{1,3},{2,0},{3,1},{4,6},{5,7},{6,4},{7,5},{8,10},{9,11},{10,... | collective-permute-start | bytes 786440 | tf_op jit(solution)/shard_map/ppermute | solution.py:478
  48.0 1.2 %collective-permute-start.11 = (f32[512]{0:T(512)S(1)}, f32[512]{0:T(512)S(1)}, u32[]{:S(2)}, u32[]{:S(2)}) collective-permute-start(f32[512]{0:T(512)S(1)} %bitcast.7), channel_id=1, source_target_pairs={{0,1},{1,0},{2,3},{3,2},{4,5},{5,4},{6,7},{7,6},{8,9},{9,8},{10,11... | collective-permute-start | bytes 6152 | tf_op jit(solution)/shard_map/ppermute | solution.py:502
  49.2 3.6 %collective-permute-start.12 = (f32[512]{0:T(512)S(1)}, f32[512]{0:T(512)S(1)}, u32[]{:S(2)}, u32[]{:S(2)}) collective-permute-start(f32[512]{0:T(512)S(1)} %add.6), channel_id=1, source_target_pairs={{0,2},{1,3},{2,0},{3,1},{4,6},{5,7},{6,4},{7,5},{8,10},{9,11},{10,... | collective-permute-start | bytes 6152 | tf_op jit(solution)/shard_map/ppermute | solution.py:502

commit v14 on v13

--- a/solution.py
+++ b/solution.py
@@ -218,8 +218,9 @@
         fill_rho(row_scr, col_scr, out_ref, j * tile, 0, block, 8, j * tile, tile)
 
 
-def forces_kernel(at, dims, rim_ref, first_ref, second_ref, local_ref, all_ref, part_ref, rim_scr):
-    comps, chunk = all_ref.shape
+def forces_kernel(at, dims, rim_ref, first_ref, second_ref, local_ref, *refs):
+    all_ref, part_ref, rim_scr = refs[-3:]
+    comps, chunk = all_ref.shape[0], part_ref.shape[1]
     width = first_ref.shape[0] // dims
     part = comps // 2
     lanes = slice(at, at + chunk)
@@ -230,8 +231,10 @@
             rim_scr[base + width : base + 2 * width, :] = second_ref[d * width : (d + 1) * width, lanes]
     for c in range(0, chunk, 256):
         total = jnp.dot(rim_ref[...], rim_scr[:, c : c + 256], preferred_element_type=F32)
-        all_ref[:, c : c + 256] = (local_ref[:, at + c : at + c + 256] + total).astype(BF16)
-    part_ref[...] = all_ref[pl.ds(pl.multiple_of(place()[5] * part, part), part), :]
+        all_ref[:, at + c : at + c + 256] = (local_ref[:, at + c : at + c + 256] + total).astype(BF16)
+    part_ref[...] = all_ref[pl.ds(pl.multiple_of(place()[5] * part, part), part), lanes]
+    if at:
+        all_ref[:, :at] = refs[0][...]
 
 
 def join_kernel(*refs):
@@ -369,11 +372,11 @@
 def far_kernel(at, per_elem, chunks, near_ref, w_ref, far_ref, *refs):
     sides, (out_ref, *scratch) = refs[: 2 * chunks], refs[2 * chunks :]
     _, chunk = sides[0].shape
-    part = far_ref.shape[0]
-    tile = min(256, chunk)
+    part, size = far_ref.shape
+    tile = min(256, size)
     rows = pl.ds(pl.multiple_of(place()[4] * part, part), part)
     total = near_ref[rows, :]
-    for c in range(0, chunk, tile):
+    for c in range(0, size, tile):
         spot = slice(at + c, at + c + tile)
         got = None
         for q, side_ref in enumerate(sides):
@@ -466,20 +469,20 @@
     )
 
     chunk = block // CHUNKS
-    own, mate, far = [], [], []
+    far, forces = [], ()
     for c in range(CHUNKS):
-        forces, sent = call(
+        *forces, sent = call(
             functools.partial(forces_kernel, c * chunk, dims),
-            [sds((comps, chunk), BF16), sds((part, chunk), BF16)],
-            (rim, *rims, local), 0.6,
+            [sds((comps, (c + 1) * chunk), BF16), sds((part, chunk), BF16)],
+            (rim, *rims, local, *forces), 0.6,
             scratch=[pltpu.VMEM((4 * dims * width, chunk), BF16)],
         )
-        own.append(forces)
         far.append(lax.ppermute(sent, "mode", [(i, i ^ 2) for i in range(4)]))
-        mate.append(lax.ppermute(forces, "mode", [(i, i ^ 1) for i in range(4)]))
+    forces = forces[0]
+    mate = lax.ppermute(forces, "mode", [(i, i ^ 1) for i in range(4)])
     near = call(
-        functools.partial(near_kernel, dims, CHUNKS), sds((comps, 128), F32),
-        (amps, mate_amps, rho_diag, rho_mate, *own, *mate),
+        functools.partial(near_kernel, dims, 1), sds((comps, 128), F32),
+        (amps, mate_amps, rho_diag, rho_mate, forces, mate),
         3.4,
         scratch=[pltpu.VMEM((block, 32), BF16), pltpu.VMEM((2, block, block // 4), BF16)],
     )
@@ -492,9 +495,9 @@
     for c in range(CHUNKS):
         last = c == CHUNKS - 1
         value = call(
-            functools.partial(far_kernel, c * chunk, per_elem, CHUNKS),
+            functools.partial(far_kernel, c * chunk, per_elem, 1),
             sds((1, comps) if last else (comps, 128), F32),
-            (value, weights, far[c], *own, *mate), 1.0,
+            (value, weights, far[c], forces, mate), 1.0,
             scratch=[pltpu.VMEM((comps, 128), F32)] * 2 if last else (),
         )
     value = value.reshape(comps)

time: 53.6 us -> 60 us (1.12)
  waiting for transfers between devices: 17 us -> 23.7 us
    ppermute x1, waiting for transfers between devices: 0.01 us -> 8.85 us  [combined(): lax.ppermute(outgoing, 'dom', halves[0])]
    ppermute x2, waiting for transfers between devices: 8.04 us -> 4.68 us  [combined(): far.append(lax.ppermute(sent, 'mode', [(i, i ^ 2) for i in range(4)]))]
    ppermute x2, waiting for transfers between devices: 0.01 us -> 2.27 us  [combined(): lax.ppermute(stats, 'mode', [(i, i ^ q) for i in range(4)])]
    ppermute x1, starting transfers between devices: 1.56 us -> 3.03 us  [combined(): lax.ppermute(outgoing, 'dom', halves[0])]
    ppermute x2, starting transfers between devices: 3.14 us -> 1.97 us  [combined(): lax.ppermute(stats, 'mode', [(i, i ^ q) for i in range(4)])]
    ppermute x2, starting transfers between devices: 0.46 us -> 1.48 us  [combined(): lax.ppermute(value, 'mode', [(i, i ^ reach) for i in range(4)])]
    ppermute x2, waiting for transfers between devices: 4.3 us -> 3.28 us  [combined(): lax.ppermute(value, 'mode', [(i, i ^ reach) for i in range(4)])]
    ppermute x3, starting transfers between devices: 8.42 us -> 7.62 us  [combined(): extra = lax.ppermute(stats, 'dom', [(i, i ^ reach) for i in range(parts)])]
  transfers between devices with their start and end apart: 13 -> 12, of which waited for: 6 -> 10; matrix products, arithmetic and copies ran while one was open for 0% -> 0% of each run, Pallas kernels for 27% -> 24%
where the time goes in v14:
time: 60 us; the launch traced here: 59.8 us
  waiting for transfers between devices  23.7 us (40%)
  Pallas kernels  17.1 us (29%)
  starting transfers between devices  16.9 us (28%)
  local copies, waits for them, and re-layouts  1.29 us (2%)
    pallas_call x18, Pallas kernels, call(): pl.pallas_call(body, out_shape=out_shape, in_specs=specs, out_specs=[VMEM...  17.1 us
    ppermute x1, waiting for transfers between devices, combined(): lax.ppermute(outgoing, 'dom', halves[0])  8.85 us
    ppermute x3, starting transfers between devices, combined(): extra = lax.ppermute(stats, 'dom', [(i, i ^ reach) for i in range(parts)])  7.62 us
    ppermute x2, waiting for transfers between devices, combined(): far.append(lax.ppermute(sent, 'mode', [(i, i ^ 2) for i in range(4)]))  4.68 us
    ppermute x3, waiting for transfers between devices, combined(): extra = lax.ppermute(stats, 'dom', [(i, i ^ reach) for i in range(parts)])  4.61 us
    ppermute x2, waiting for transfers between devices, combined(): lax.ppermute(value, 'mode', [(i, i ^ reach) for i in range(4)])  3.28 us
    ppermute x1, starting transfers between devices, combined(): lax.ppermute(outgoing, 'dom', halves[0])  3.03 us
    ppermute x2, waiting for transfers between devices, combined(): lax.ppermute(stats, 'mode', [(i, i ^ q) for i in range(4)])  2.27 us
  transfers between devices with their start and end apart: 12, of which 10 were waited for; matrix products, arithmetic and copies ran while one was open for 0% of the time, Pallas kernels for 24%

profile of v14, /device:TPU:0, one launch (start us, length us, event | category | flops | bytes accessed | tf_op | source)
XLA Modules:
  0.0 59.8 jit_solution(11045794727928951048)
XLA Ops:
  0.0 0.0 copy-start
  0.0 0.0 copy-start.6
  0.0 0.8 %copy-done.6 = s32[2,64]{1,0:T(2,128)S(1)} copy-done((s32[2,64]{1,0:T(2,128)S(1)}, s32[2,64]{1,0:T(2,128)}, u32[]{:S(2)}) %copy-start.6) | copy-done | bytes 536
  0.8 0.2 shard_map.91.refs_0_
  1.0 0.4 copy-done
  1.4 0.0 copy-start.7
  1.4 0.4 shard_map.101
  1.8 3.0 %collective-permute-start.5 = (bf16[192,1024]{1,0:T(8,128)(2,1)S(1)}, bf16[192,1024]{1,0:T(8,128)(2,1)S(1)}, u32[]{:S(2)}, u32[]{:S(2)}) collective-permute-start(bf16[192,1024]{1,0:T(8,128)(2,1)S(1)} %shard_map.101), channel_id=1, source_target_pairs={{0,4},{4,0},{8,12},{12,8},{16,20},{20,16},{24,28},{28,24},{1,5},{5... | collective-permute-start | bytes 1179656 | tf_op jit(solution)/shard_map/ppermute | solution.py:425
  4.9 0.5 shard_map.92
  5.4 0.0 copy-start.3
  5.4 0.0 copy-start.4
  5.4 0.7 %collective-permute-start.6 = (bf16[192,1024]{1,0:T(8,128)(2,1)S(1)}, bf16[192,1024]{1,0:T(8,128)(2,1)S(1)}, u32[]{:S(2)}, u32[]{:S(2)}) collective-permute-start(bf16[192,1024]{1,0:T(8,128)(2,1)S(1)} %get-tuple-element.26), channel_id=1, source_target_pairs={{4,8},{8,4},{12,16},{16,12},{20,24},{24,20},{5,9},{9,5},{13,17},{1... | collective-permute-start | bytes 1179656 | tf_op jit(solution)/shard_map/ppermute | solution.py:425
  6.1 0.0 copy-done.7
  6.1 0.8 %shard_map.93.refs_0_.refs_2_ = f32[4,1024]{1,0:T(4,128)S(1)} custom-call(f32[1,256]{1,0:T(1,128)S(1)} %bitcast.19, bf16[3,256,1024]{2,1,0:T(8,128)(2,1)S(1)} %get-tuple-element.19.refs_1_.refs_3_), custom_call_target="tpu_custom_call" | custom-call | flops 880000000 | tf_op jit(solution)/shard_map/pallas_call | solution.py:27
  6.9 0.0 copy-done.3
  6.9 0.0 copy-done.4
  6.9 2.4 %shard_map.95 = (f32[1024,1024]{1,0:T(8,128)S(1)}, f32[2,512,512]{2,1,0:T(8,128)S(1)}, f32[4,1024,128]{2,1,0:T(8,128)S(1)}) custom-call(f32[1,4096]{1,0:T(1,128)S(1)} %bitcast.10, f32[1,4096]{1,0:T(1,128)S(1)} %bitcast.14, f32[4,1024]{1,0:T(4,128)S(1)} %shard_map.93.refs_0_.refs_2_), custom_call_target="tpu_custom_call" | custom-call | flops 3300000000 | tf_op jit(solution)/shard_map/pallas_call | solution.py:27
  9.4 0.0 copy-start.2
  9.4 0.0 copy-start.5
  9.4 0.0 copy-start.8
  9.4 1.6 %shard_map.96.refs_4_.refs_3_ = f32[1024,1024]{1,0:T(8,128)S(1)} custom-call(f32[1,4096]{1,0:T(1,128)S(1)} %bitcast.11, f32[1,4096]{1,0:T(1,128)S(1)} %bitcast.15, f32[4,1024,128]{2,1,0:T(8,128)S(1)} %get-tuple-element.20.refs_2_), custom_call_target="tpu_custom_call" | custom-call | flops 2090000000 | tf_op jit(solution)/shard_map/pallas_call | solution.py:27
  11.0 0.0 copy-done.2
  11.0 0.0 copy-done.5
  11.0 0.0 copy-done.8
  11.0 1.8 %shard_map.97 = (f32[512,1024]{1,0:T(8,128)S(1)}, bf16[512,768]{1,0:T(8,128)(2,1)S(1)}) custom-call(s32[4,64]{1,0:T(4,128)S(1)} %bitcast.18, s32[1,64]{1,0:T(1,128)S(1)} %bitcast.20, bf16[8,3,4,64]{3,2,1,0:T(4,128)(2,1)S(1)} %bitcast.9, bf16[3,256,1024]{2,1,0:T(8,128)(2,1)S(1)} %get-tuple-element.19.refs_1_.refs_3_, f32[1024,1024]{1,0:T(8,128)S(1)} %shard_map.96.refs_4_.refs_3_), custom_call_target="tpu_custom_call" | custom-call | flops 1980000000 | tf_op jit(solution)/shard_map/pallas_call | solution.py:27
  12.8 8.9 %collective-permute-done.5.refs_1_ = bf16[192,1024]{1,0:T(8,128)(2,1)S(1)} collective-permute-done((bf16[192,1024]{1,0:T(8,128)(2,1)S(1)}, bf16[192,1024]{1,0:T(8,128)(2,1)S(1)}, u32[]{:S(2)}, u32[]{:S(2)}) %collective-permute-start.5) | collective-permute-done | bytes 393248 | tf_op jit(solution)/shard_map/ppermute | solution.py:425
  21.7 0.0 collective-permute-done.6.refs_2_
  21.7 0.6 %shard_map.102 = (bf16[512,512]{1,0:T(8,128)(2,1)S(1)}, bf16[256,512]{1,0:T(8,128)(2,1)S(1)}) custom-call(bf16[512,768]{1,0:T(8,128)(2,1)S(1)} %get-tuple-element.21.refs_2_.refs_0_, bf16[192,1024]{1,0:T(8,128)(2,1)S(1)} %collective-permute-done.5.refs_1_, bf16[192,1024]{1,0:T(8,128)(2,1)S(1)} %collective-permute-done.6.refs_2_, ...), custom_call_target="tpu_custom_call" | custom-call | flops 660000000 | tf_op jit(solution)/shard_map/pallas_call | solution.py:27
  22.3 0.7 %shard_map.103 = (bf16[512,1024]{1,0:T(8,128)(2,1)S(1)}, bf16[256,512]{1,0:T(8,128)(2,1)S(1)}) custom-call(bf16[512,768]{1,0:T(8,128)(2,1)S(1)} %get-tuple-element.21.refs_2_.refs_0_, bf16[192,1024]{1,0:T(8,128)(2,1)S(1)} %collective-permute-done.5.refs_1_, bf16[192,1024]{1,0:T(8,128)(2,1)S(1)} %collective-permute-done.6.refs_2_, ...), custom_call_target="tpu_custom_call" | custom-call | flops 660000000 | tf_op jit(solution)/shard_map/pallas_call | solution.py:27
  23.0 0.1 collective-permute-start.7
  23.0 0.5 collective-permute-start
  23.5 1.5 %collective-permute-start.1 = (f32[4,1024]{1,0:T(4,128)S(1)}, f32[4,1024]{1,0:T(4,128)S(1)}, u32[]{:S(2)}, u32[]{:S(2)}) collective-permute-start(f32[4,1024]{1,0:T(4,128)S(1)} %shard_map.93.refs_0_.refs_2_), channel_id=1, source_target_pairs={{0,2},{1,3},{2,0},{3,1},{4,6},{5,7},{6,4},{7,5},{8,10},{9,11},{10,... | collective-permute-start | bytes 49160 | tf_op jit(solution)/shard_map/ppermute | solution.py:454
  25.0 0.7 %collective-permute-done.refs_1_ = f32[4,1024]{1,0:T(4,128)S(1)} collective-permute-done((f32[4,1024]{1,0:T(4,128)S(1)}, f32[4,1024]{1,0:T(4,128)S(1)}, u32[]{:S(2)}, u32[]{:S(2)}) %collective-permute-start) | collective-permute-done | bytes 16416 | tf_op jit(solution)/shard_map/ppermute | solution.py:454
  25.7 1.6 %collective-permute-done.1.refs_2_ = f32[4,1024]{1,0:T(4,128)S(1)} collective-permute-done((f32[4,1024]{1,0:T(4,128)S(1)}, f32[4,1024]{1,0:T(4,128)S(1)}, u32[]{:S(2)}, u32[]{:S(2)}) %collective-permute-start.1) | collective-permute-done | bytes 16416 | tf_op jit(solution)/shard_map/ppermute | solution.py:454
  27.3 2.6 %collective-permute-start.2 = (f32[12,1024]{1,0:T(8,128)S(1)}, f32[12,1024]{1,0:T(8,128)S(1)}, u32[]{:S(2)}, u32[]{:S(2)}) collective-permute-start(f32[12,1024]{1,0:T(8,128)S(1)} %shard_map.94.refs_0_), channel_id=1, source_target_pairs={{0,8},{4,12},{8,0},{12,4},{16,24},{20,28},{24,16},{28,20},{1,9},{5... | collective-permute-start | bytes 147464 | tf_op jit(solution)/shard_map/ppermute | solution.py:466
  29.9 2.2 %collective-permute-done.2.refs_1_ = f32[12,1024]{1,0:T(8,128)S(1)} collective-permute-done((f32[12,1024]{1,0:T(8,128)S(1)}, f32[12,1024]{1,0:T(8,128)S(1)}, u32[]{:S(2)}, u32[]{:S(2)}) %collective-permute-start.2) | collective-permute-done | bytes 49184 | tf_op jit(solution)/shard_map/ppermute | solution.py:466
  32.2 3.1 %collective-permute-start.3 = (f32[12,1024]{1,0:T(8,128)S(1)}, f32[12,1024]{1,0:T(8,128)S(1)}, u32[]{:S(2)}, u32[]{:S(2)}) collective-permute-start(f32[12,1024]{1,0:T(8,128)S(1)} %shard_map.98.refs_0_), channel_id=1, source_target_pairs={{0,16},{4,20},{8,24},{12,28},{16,0},{20,4},{24,8},{28,12},{1,17},{... | collective-permute-start | bytes 147464 | tf_op jit(solution)/shard_map/ppermute | solution.py:466
  35.3 2.2 %collective-permute-done.3.refs_1_ = f32[12,1024]{1,0:T(8,128)S(1)} collective-permute-done((f32[12,1024]{1,0:T(8,128)S(1)}, f32[12,1024]{1,0:T(8,128)S(1)}, u32[]{:S(2)}, u32[]{:S(2)}) %collective-permute-start.3) | collective-permute-done | bytes 49184 | tf_op jit(solution)/shard_map/ppermute | solution.py:466
  37.5 0.0 copy-start.1
  37.5 1.9 %collective-permute-start.4 = (f32[12,1024]{1,0:T(8,128)S(1)}, f32[12,1024]{1,0:T(8,128)S(1)}, u32[]{:S(2)}, u32[]{:S(2)}) collective-permute-start(f32[12,1024]{1,0:T(8,128)S(1)} %shard_map.99.refs_0_), channel_id=1, source_target_pairs={{0,4},{4,0},{8,12},{12,8},{16,20},{20,16},{24,28},{28,24},{1,5},{5... | collective-permute-start | bytes 147464 | tf_op jit(solution)/shard_map/ppermute | solution.py:466
  39.4 2.3 %shard_map.105.refs_4_ = f32[1024,1024]{1,0:T(8,128)S(1)} custom-call(f32[1,4096]{1,0:T(1,128)S(1)} %bitcast.12, f32[1,4096]{1,0:T(1,128)S(1)} %bitcast.16), custom_call_target="tpu_custom_call" | custom-call | flops 2750000128 | tf_op jit(solution)/shard_map/pallas_call | solution.py:27
  41.8 0.1 collective-permute-done.4.refs_1_
  41.9 0.0 copy-done.1
  41.9 1.4 %shard_map.106.refs_1_ = bf16[2048,1024]{1,0:T(8,128)(2,1)S(1)} custom-call(f32[8,1024]{1,0:T(8,128)S(1)} %get-tuple-element.22.refs_0_, f32[8,1024]{1,0:T(8,128)S(1)} %get-tuple-element.23.refs_1_, f32[8,1024]{1,0:T(8,128)S(1)} %get-tuple-element.30.refs_2_, f32[1024,1024]{1,0:T(8,128)S(1)} %shard_map.96.refs_4_.refs_3_, f32[1024,1024]{1,0:T(8,128)S(1)} %shard_map.105.refs_4_), custom_call_target="tpu_custom_call" | custom-call | flops 1540000000 | tf_op jit(solution)/shard_map/pallas_call | solution.py:27
  43.3 1.5 %collective-permute-start.8 = (bf16[256,512]{1,0:T(8,128)(2,1)S(1)}, bf16[256,512]{1,0:T(8,128)(2,1)S(1)}, u32[]{:S(2)}, u32[]{:S(2)}) collective-permute-start(bf16[256,512]{1,0:T(8,128)(2,1)S(1)} %get-tuple-element.31), channel_id=1, source_target_pairs={{0,2},{1,3},{2,0},{3,1},{4,6},{5,7},{6,4},{7,5},{8,10},{9,11},{10,... | collective-permute-start | bytes 786440 | tf_op jit(solution)/shard_map/ppermute | solution.py:480
  44.8 0.6 collective-permute-start.9
  45.4 0.0 collective-permute-done.7.refs_5_.refs_4_
  45.4 2.7 %shard_map.104.refs_0_ = f32[512,128]{1,0:T(8,128)S(1)} custom-call(f32[8,1024]{1,0:T(8,128)S(1)} %get-tuple-element.22.refs_0_, f32[8,1024]{1,0:T(8,128)S(1)} %get-tuple-element.23.refs_1_, f32[1024,1024]{1,0:T(8,128)S(1)} %get-tuple-element.24.refs_2_, f32[2,512,512]{2,1,0:T(8,128)S(1)} %get-tuple-element.25.refs_3_, ...), custom_call_target="tpu_custom_call" | custom-call | flops 3740000000 | tf_op jit(solution)/shard_map/pallas_call | solution.py:27
  48.0 2.6 %collective-permute-done.8.refs_2_ = bf16[256,512]{1,0:T(8,128)(2,1)S(1)} collective-permute-done((bf16[256,512]{1,0:T(8,128)(2,1)S(1)}, bf16[256,512]{1,0:T(8,128)(2,1)S(1)}, u32[]{:S(2)}, u32[]{:S(2)}) %collective-permute-start.8) | collective-permute-done | bytes 262176 | tf_op jit(solution)/shard_map/ppermute | solution.py:480
  50.6 0.7 %shard_map.107.refs_0_ = f32[512,128]{1,0:T(8,128)S(1)} custom-call(f32[512,128]{1,0:T(8,128)S(1)} %shard_map.104.refs_0_, bf16[2048,1024]{1,0:T(8,128)(2,1)S(1)} %shard_map.106.refs_1_, bf16[256,512]{1,0:T(8,128)(2,1)S(1)} %collective-permute-done.8.refs_2_, bf16[512,1024]{1,0:T(8,128)(2,1)S(1)} %get-tuple-element.29.refs_4_.refs_3_, ...), custom_call_target="tpu_custom_call" | custom-call | flops 1100000000 | tf_op jit(solution)/shard_map/pallas_call | solution.py:27
  51.4 2.1 %collective-permute-done.9.refs_2_ = bf16[256,512]{1,0:T(8,128)(2,1)S(1)} collective-permute-done((bf16[256,512]{1,0:T(8,128)(2,1)S(1)}, bf16[256,512]{1,0:T(8,128)(2,1)S(1)}, u32[]{:S(2)}, u32[]{:S(2)}) %collective-permute-start.9) | collective-permute-done | bytes 262176 | tf_op jit(solution)/shard_map/ppermute | solution.py:480
  53.4 1.0 %shard_map.108 = f32[1,512]{1,0:T(1,128)S(1)} custom-call(f32[512,128]{1,0:T(8,128)S(1)} %shard_map.107.refs_0_, bf16[2048,1024]{1,0:T(8,128)(2,1)S(1)} %shard_map.106.refs_1_, bf16[256,512]{1,0:T(8,128)(2,1)S(1)} %collective-permute-done.9.refs_2_, bf16[512,1024]{1,0:T(8,128)(2,1)S(1)} %get-tuple-element.29.refs_4_.refs_3_, ...), custom_call_target="tpu_custom_call" | custom-call | flops 1100000000 | tf_op jit(solution)/shard_map/pallas_call | solution.py:27
  54.4 0.0 collective-permute-start.10
  54.5 1.2 %collective-permute-done.10 = f32[512]{0:T(512)S(1)} collective-permute-done((f32[512]{0:T(512)S(1)}, f32[512]{0:T(512)S(1)}, u32[]{:S(2)}, u32[]{:S(2)}) %collective-permute-start.10) | collective-permute-done | bytes 2080 | tf_op jit(solution)/shard_map/ppermute | solution.py:505
  55.6 1.5 %collective-permute-start.11 = (f32[512]{0:T(512)S(1)}, f32[512]{0:T(512)S(1)}, u32[]{:S(2)}, u32[]{:S(2)}) collective-permute-start(f32[512]{0:T(512)S(1)} %add.6), channel_id=1, source_target_pairs={{0,2},{1,3},{2,0},{3,1},{4,6},{5,7},{6,4},{7,5},{8,10},{9,11},{10,... | collective-permute-start | bytes 6152 | tf_op jit(solution)/shard_map/ppermute | solution.py:505
  57.1 2.1 %collective-permute-done.11 = f32[512]{0:T(512)S(1)} collective-permute-done((f32[512]{0:T(512)S(1)}, f32[512]{0:T(512)S(1)}, u32[]{:S(2)}, u32[]{:S(2)}) %collective-permute-start.11) | collective-permute-done | bytes 2080 | tf_op jit(solution)/shard_map/ppermute | solution.py:505
  59.2 0.6 add.7
  (5 shorter events, 0.1 us)
Async XLA Ops:
  0.0 1.4 %copy-start = (bf16[3,256,1024]{2,1,0:T(8,128)(2,1)S(1)}, bf16[3,256,1024]{2,1,0:T(8,128)(2,1)}, u32[]{:S(2)}) copy-start(bf16[3,256,1024]{2,1,0:T(8,128)(2,1)} %refs_1_.3) | copy-start | bytes 4718596
  0.0 0.8 %copy-start.6 = (s32[2,64]{1,0:T(2,128)S(1)}, s32[2,64]{1,0:T(2,128)}, u32[]{:S(2)}) copy-start(s32[2,64]{1,0:T(2,128)} %refs_0_.1) | copy-start | bytes 1540
  1.4 4.7 %copy-start.7 = (f32[256]{0:T(256)S(1)}, f32[256]{0:T(256)}, u32[]{:S(2)}) copy-start(f32[256]{0:T(256)} %param.10) | copy-start | bytes 3076
  1.8 19.8 %collective-permute-start.5 = (bf16[192,1024]{1,0:T(8,128)(2,1)S(1)}, bf16[192,1024]{1,0:T(8,128)(2,1)S(1)}, u32[]{:S(2)}, u32[]{:S(2)}) collective-permute-start(bf16[192,1024]{1,0:T(8,128)(2,1)S(1)} %shard_map.101), channel_id=1, source_target_pairs={{0,4},{4,0},{8,12},{12,8},{16,20},{20,16},{24,28},{28,24},{1,5},{5... | collective-permute-start | bytes 1179656 | tf_op jit(solution)/shard_map/ppermute | solution.py:425
  5.4 1.5 %copy-start.3 = (f32[4096]{0:T(1024)S(1)}, f32[4096]{0:T(1024)}, u32[]{:S(2)}) copy-start(f32[4096]{0:T(1024)} %param.12) | copy-start | bytes 49156
  5.4 1.5 %copy-start.4 = (f32[4096]{0:T(1024)S(1)}, f32[4096]{0:T(1024)}, u32[]{:S(2)}) copy-start(f32[4096]{0:T(1024)} %param.13) | copy-start | bytes 49156
  5.4 16.3 %collective-permute-start.6 = (bf16[192,1024]{1,0:T(8,128)(2,1)S(1)}, bf16[192,1024]{1,0:T(8,128)(2,1)S(1)}, u32[]{:S(2)}, u32[]{:S(2)}) collective-permute-start(bf16[192,1024]{1,0:T(8,128)(2,1)S(1)} %get-tuple-element.26), channel_id=1, source_target_pairs={{4,8},{8,4},{12,16},{16,12},{20,24},{24,20},{5,9},{9,5},{13,17},{1... | collective-permute-start | bytes 1179656 | tf_op jit(solution)/shard_map/ppermute | solution.py:425
  9.4 1.6 %copy-start.2 = (bf16[64,8,4,3]{0,2,3,1:T(4,128)(2,1)S(1)}, bf16[64,8,4,3]{0,2,3,1:T(4,128)(2,1)}, u32[]{:S(2)}) copy-start(bf16[64,8,4,3]{0,2,3,1:T(4,128)(2,1)} %param.14) | copy-start | bytes 36868
  9.4 1.6 %copy-start.5 = (s32[64,4]{0,1:T(4,128)S(1)}, s32[64,4]{0,1:T(4,128)}, u32[]{:S(2)}) copy-start(s32[64,4]{0,1:T(4,128)} %param.15) | copy-start | bytes 3076
  9.4 1.6 %copy-start.8 = (s32[64]{0:T(128)S(1)}, s32[64]{0:T(128)}, u32[]{:S(2)}) copy-start(s32[64]{0:T(128)} %param.16) | copy-start | bytes 772
  23.0 22.4 %collective-permute-start.7 = (bf16[512,1024]{1,0:T(8,128)(2,1)S(1)}, bf16[512,1024]{1,0:T(8,128)(2,1)S(1)}, u32[]{:S(2)}, u32[]{:S(2)}) collective-permute-start(bf16[512,1024]{1,0:T(8,128)(2,1)S(1)} %get-tuple-element.29.refs_4_.refs_3_), channel_id=1, source_target_pairs={{0,1},{1,0},{2,3},{3,2},{4,5},{5,4},{6,7},{7,6},{8,9},{9,8},{10,11... | collective-permute-start | bytes 3145736 | tf_op jit(solution)/shard_map/ppermute | solution.py:482
  23.0 2.7 %collective-permute-start = (f32[4,1024]{1,0:T(4,128)S(1)}, f32[4,1024]{1,0:T(4,128)S(1)}, u32[]{:S(2)}, u32[]{:S(2)}) collective-permute-start(f32[4,1024]{1,0:T(4,128)S(1)} %shard_map.93.refs_0_.refs_2_), channel_id=1, source_target_pairs={{0,1},{1,0},{2,3},{3,2},{4,5},{5,4},{6,7},{7,6},{8,9},{9,8},{10,11... | collective-permute-start | bytes 49160 | tf_op jit(solution)/shard_map/ppermute | solution.py:454
  23.5 3.7 %collective-permute-start.1 = (f32[4,1024]{1,0:T(4,128)S(1)}, f32[4,1024]{1,0:T(4,128)S(1)}, u32[]{:S(2)}, u32[]{:S(2)}) collective-permute-start(f32[4,1024]{1,0:T(4,128)S(1)} %shard_map.93.refs_0_.refs_2_), channel_id=1, source_target_pairs={{0,2},{1,3},{2,0},{3,1},{4,6},{5,7},{6,4},{7,5},{8,10},{9,11},{10,... | collective-permute-start | bytes 49160 | tf_op jit(solution)/shard_map/ppermute | solution.py:454
  27.3 4.9 %collective-permute-start.2 = (f32[12,1024]{1,0:T(8,128)S(1)}, f32[12,1024]{1,0:T(8,128)S(1)}, u32[]{:S(2)}, u32[]{:S(2)}) collective-permute-start(f32[12,1024]{1,0:T(8,128)S(1)} %shard_map.94.refs_0_), channel_id=1, source_target_pairs={{0,8},{4,12},{8,0},{12,4},{16,24},{20,28},{24,16},{28,20},{1,9},{5... | collective-permute-start | bytes 147464 | tf_op jit(solution)/shard_map/ppermute | solution.py:466
  32.2 5.3 %collective-permute-start.3 = (f32[12,1024]{1,0:T(8,128)S(1)}, f32[12,1024]{1,0:T(8,128)S(1)}, u32[]{:S(2)}, u32[]{:S(2)}) collective-permute-start(f32[12,1024]{1,0:T(8,128)S(1)} %shard_map.98.refs_0_), channel_id=1, source_target_pairs={{0,16},{4,20},{8,24},{12,28},{16,0},{20,4},{24,8},{28,12},{1,17},{... | collective-permute-start | bytes 147464 | tf_op jit(solution)/shard_map/ppermute | solution.py:466
  37.5 4.3 %copy-start.1 = (f32[3,4096]{1,0:T(4,128)S(1)}, f32[3,4096]{1,0:T(4,128)}, u32[]{:S(2)}) copy-start(f32[3,4096]{1,0:T(4,128)} %refs_2_.1) | copy-start | bytes 147460
  37.5 4.3 %collective-permute-start.4 = (f32[12,1024]{1,0:T(8,128)S(1)}, f32[12,1024]{1,0:T(8,128)S(1)}, u32[]{:S(2)}, u32[]{:S(2)}) collective-permute-start(f32[12,1024]{1,0:T(8,128)S(1)} %shard_map.99.refs_0_), channel_id=1, source_target_pairs={{0,4},{4,0},{8,12},{12,8},{16,20},{20,16},{24,28},{28,24},{1,5},{5... | collective-permute-start | bytes 147464 | tf_op jit(solution)/shard_map/ppermute | solution.py:466
  43.3 7.3 %collective-permute-start.8 = (bf16[256,512]{1,0:T(8,128)(2,1)S(1)}, bf16[256,512]{1,0:T(8,128)(2,1)S(1)}, u32[]{:S(2)}, u32[]{:S(2)}) collective-permute-start(bf16[256,512]{1,0:T(8,128)(2,1)S(1)} %get-tuple-element.31), channel_id=1, source_target_pairs={{0,2},{1,3},{2,0},{3,1},{4,6},{5,7},{6,4},{7,5},{8,10},{9,11},{10,... | collective-permute-start | bytes 786440 | tf_op jit(solution)/shard_map/ppermute | solution.py:480
  44.8 8.6 %collective-permute-start.9 = (bf16[256,512]{1,0:T(8,128)(2,1)S(1)}, bf16[256,512]{1,0:T(8,128)(2,1)S(1)}, u32[]{:S(2)}, u32[]{:S(2)}) collective-permute-start(bf16[256,512]{1,0:T(8,128)(2,1)S(1)} %get-tuple-element.32), channel_id=1, source_target_pairs={{0,2},{1,3},{2,0},{3,1},{4,6},{5,7},{6,4},{7,5},{8,10},{9,11},{10,... | collective-permute-start | bytes 786440 | tf_op jit(solution)/shard_map/ppermute | solution.py:480
  54.4 1.2 %collective-permute-start.10 = (f32[512]{0:T(512)S(1)}, f32[512]{0:T(512)S(1)}, u32[]{:S(2)}, u32[]{:S(2)}) collective-permute-start(f32[512]{0:T(512)S(1)} %bitcast.7), channel_id=1, source_target_pairs={{0,1},{1,0},{2,3},{3,2},{4,5},{5,4},{6,7},{7,6},{8,9},{9,8},{10,11... | collective-permute-start | bytes 6152 | tf_op jit(solution)/shard_map/ppermute | solution.py:505
  55.6 3.6 %collective-permute-start.11 = (f32[512]{0:T(512)S(1)}, f32[512]{0:T(512)S(1)}, u32[]{:S(2)}, u32[]{:S(2)}) collective-permute-start(f32[512]{0:T(512)S(1)} %add.6), channel_id=1, source_target_pairs={{0,2},{1,3},{2,0},{3,1},{4,6},{5,7},{6,4},{7,5},{8,10},{9,11},{10,... | collective-permute-start | bytes 6152 | tf_op jit(solution)/shard_map/ppermute | solution.py:505

commit v15 on v14

--- a/solution.py
+++ b/solution.py
@@ -453,7 +453,7 @@
     )
     given = [stats] + [lax.ppermute(stats, "mode", [(i, i ^ q) for i in range(4)]) for q in (1, 2)]
     stats = call(join_kernel, sds((3 * (dims + 1), block), F32), given, 0.5)
-    order = [1 << q for q in range(1, parts.bit_length() - 1)] + [1]
+    order = [1 << q for q in reversed(range(1, parts.bit_length() - 1))] + [1]
     if parts & (parts - 1) or parts == 1:
         stats = lax.psum(stats, "dom")
         order = []
@@ -501,9 +501,10 @@
             scratch=[pltpu.VMEM((comps, 128), F32)] * 2 if last else (),
         )
     value = value.reshape(comps)
-    for reach in (1, 2):
-        value = value + lax.ppermute(value, "mode", [(i, i ^ reach) for i in range(4)])
-    return value
+    far, diagonal, mate = (
+        lax.ppermute(value, "mode", [(i, i ^ reach) for i in range(4)]) for reach in (2, 3, 1)
+    )
+    return (value + mate) + (far + diagonal)
 
 
 def extended_2(block, sides, width):

time: 60 us -> 59.7 us (level)
  waiting for transfers between devices: 23.7 us -> 22.9 us
  starting transfers between devices: 16.9 us -> 17.5 us
    ppermute x2 -> x3, waiting for transfers between devices: 3.28 us -> 2.34 us  [combined(): lax.ppermute(value, 'mode', [(i, i ^ reach) for i in range(4)])]
    ppermute x2 -> x3, starting transfers between devices: 1.48 us -> 2.16 us  [combined(): lax.ppermute(value, 'mode', [(i, i ^ reach) for i in range(4)])]
  transfers between devices with their start and end apart: 12 -> 13, of which waited for: 10 -> 10; matrix products, arithmetic and copies ran while one was open for 0% -> 0% of each run, Pallas kernels for 24% -> 24%
where the time goes in v15:
time: 59.7 us; the launch traced here: 59.6 us
  waiting for transfers between devices  22.9 us (38%)
  starting transfers between devices  17.5 us (29%)
  Pallas kernels  17.1 us (29%)
  local copies, waits for them, and re-layouts  1.29 us (2%)
    pallas_call x18, Pallas kernels, call(): pl.pallas_call(body, out_shape=out_shape, in_specs=specs, out_specs=[VMEM...  17.1 us
    ppermute x1, waiting for transfers between devices, combined(): lax.ppermute(outgoing, 'dom', halves[0])  8.85 us
    ppermute x3, starting transfers between devices, combined(): extra = lax.ppermute(stats, 'dom', [(i, i ^ reach) for i in range(parts)])  7.5 us
    ppermute x3, waiting for transfers between devices, combined(): extra = lax.ppermute(stats, 'dom', [(i, i ^ reach) for i in range(parts)])  4.73 us
    ppermute x2, waiting for transfers between devices, combined(): far.append(lax.ppermute(sent, 'mode', [(i, i ^ 2) for i in range(4)]))  4.7 us
    ppermute x1, starting transfers between devices, combined(): lax.ppermute(outgoing, 'dom', halves[0])  3.03 us
    ppermute x3, waiting for transfers between devices, combined(): lax.ppermute(value, 'mode', [(i, i ^ reach) for i in range(4)])  2.34 us
    ppermute x2, waiting for transfers between devices, combined(): lax.ppermute(stats, 'mode', [(i, i ^ q) for i in range(4)])  2.27 us
  transfers between devices with their start and end apart: 13, of which 10 were waited for; matrix products, arithmetic and copies ran while one was open for 0% of the time, Pallas kernels for 24%

profile of v15, /device:TPU:0, one launch (start us, length us, event | category | flops | bytes accessed | tf_op | source)
XLA Modules:
  0.0 59.6 jit_solution(11374514614348857010)
XLA Ops:
  0.0 0.0 copy-start
  0.0 0.0 copy-start.6
  0.0 0.8 %copy-done.6 = s32[2,64]{1,0:T(2,128)S(1)} copy-done((s32[2,64]{1,0:T(2,128)S(1)}, s32[2,64]{1,0:T(2,128)}, u32[]{:S(2)}) %copy-start.6) | copy-done | bytes 536
  0.8 0.2 shard_map.91.refs_0_
  1.0 0.4 copy-done
  1.4 0.0 copy-start.7
  1.4 0.4 shard_map.101
  1.8 3.0 %collective-permute-start.5 = (bf16[192,1024]{1,0:T(8,128)(2,1)S(1)}, bf16[192,1024]{1,0:T(8,128)(2,1)S(1)}, u32[]{:S(2)}, u32[]{:S(2)}) collective-permute-start(bf16[192,1024]{1,0:T(8,128)(2,1)S(1)} %shard_map.101), channel_id=1, source_target_pairs={{0,4},{4,0},{8,12},{12,8},{16,20},{20,16},{24,28},{28,24},{1,5},{5... | collective-permute-start | bytes 1179656 | tf_op jit(solution)/shard_map/ppermute | solution.py:425
  4.9 0.5 shard_map.92
  5.4 0.0 copy-start.3
  5.4 0.0 copy-start.4
  5.4 0.7 %collective-permute-start.6 = (bf16[192,1024]{1,0:T(8,128)(2,1)S(1)}, bf16[192,1024]{1,0:T(8,128)(2,1)S(1)}, u32[]{:S(2)}, u32[]{:S(2)}) collective-permute-start(bf16[192,1024]{1,0:T(8,128)(2,1)S(1)} %get-tuple-element.26), channel_id=1, source_target_pairs={{4,8},{8,4},{12,16},{16,12},{20,24},{24,20},{5,9},{9,5},{13,17},{1... | collective-permute-start | bytes 1179656 | tf_op jit(solution)/shard_map/ppermute | solution.py:425
  6.1 0.0 copy-done.7
  6.1 0.8 %shard_map.93.refs_0_.refs_2_ = f32[4,1024]{1,0:T(4,128)S(1)} custom-call(f32[1,256]{1,0:T(1,128)S(1)} %bitcast.21, bf16[3,256,1024]{2,1,0:T(8,128)(2,1)S(1)} %get-tuple-element.19.refs_1_.refs_3_), custom_call_target="tpu_custom_call" | custom-call | flops 880000000 | tf_op jit(solution)/shard_map/pallas_call | solution.py:27
  6.9 0.0 copy-done.3
  6.9 0.0 copy-done.4
  6.9 2.4 %shard_map.95 = (f32[1024,1024]{1,0:T(8,128)S(1)}, f32[2,512,512]{2,1,0:T(8,128)S(1)}, f32[4,1024,128]{2,1,0:T(8,128)S(1)}) custom-call(f32[1,4096]{1,0:T(1,128)S(1)} %bitcast.12, f32[1,4096]{1,0:T(1,128)S(1)} %bitcast.16, f32[4,1024]{1,0:T(4,128)S(1)} %shard_map.93.refs_0_.refs_2_), custom_call_target="tpu_custom_call" | custom-call | flops 3300000000 | tf_op jit(solution)/shard_map/pallas_call | solution.py:27
  9.4 0.0 copy-start.2
  9.4 0.0 copy-start.5
  9.4 0.0 copy-start.8
  9.4 1.6 %shard_map.96.refs_4_.refs_3_ = f32[1024,1024]{1,0:T(8,128)S(1)} custom-call(f32[1,4096]{1,0:T(1,128)S(1)} %bitcast.13, f32[1,4096]{1,0:T(1,128)S(1)} %bitcast.17, f32[4,1024,128]{2,1,0:T(8,128)S(1)} %get-tuple-element.20.refs_2_), custom_call_target="tpu_custom_call" | custom-call | flops 2090000000 | tf_op jit(solution)/shard_map/pallas_call | solution.py:27
  11.0 0.0 copy-done.2
  11.0 0.0 copy-done.5
  11.0 0.0 copy-done.8
  11.0 1.8 %shard_map.97 = (f32[512,1024]{1,0:T(8,128)S(1)}, bf16[512,768]{1,0:T(8,128)(2,1)S(1)}) custom-call(s32[4,64]{1,0:T(4,128)S(1)} %bitcast.20, s32[1,64]{1,0:T(1,128)S(1)} %bitcast.22, bf16[8,3,4,64]{3,2,1,0:T(4,128)(2,1)S(1)} %bitcast.11, bf16[3,256,1024]{2,1,0:T(8,128)(2,1)S(1)} %get-tuple-element.19.refs_1_.refs_3_, f32[1024,1024]{1,0:T(8,128)S(1)} %shard_map.96.refs_4_.refs_3_), custom_call_target="tpu_custom_call" | custom-call | flops 1980000000 | tf_op jit(solution)/shard_map/pallas_call | solution.py:27
  12.8 8.9 %collective-permute-done.5.refs_1_ = bf16[192,1024]{1,0:T(8,128)(2,1)S(1)} collective-permute-done((bf16[192,1024]{1,0:T(8,128)(2,1)S(1)}, bf16[192,1024]{1,0:T(8,128)(2,1)S(1)}, u32[]{:S(2)}, u32[]{:S(2)}) %collective-permute-start.5) | collective-permute-done | bytes 393248 | tf_op jit(solution)/shard_map/ppermute | solution.py:425
  21.7 0.0 collective-permute-done.6.refs_2_
  21.7 0.6 %shard_map.102 = (bf16[512,512]{1,0:T(8,128)(2,1)S(1)}, bf16[256,512]{1,0:T(8,128)(2,1)S(1)}) custom-call(bf16[512,768]{1,0:T(8,128)(2,1)S(1)} %get-tuple-element.21.refs_2_.refs_0_, bf16[192,1024]{1,0:T(8,128)(2,1)S(1)} %collective-permute-done.5.refs_1_, bf16[192,1024]{1,0:T(8,128)(2,1)S(1)} %collective-permute-done.6.refs_2_, ...), custom_call_target="tpu_custom_call" | custom-call | flops 660000000 | tf_op jit(solution)/shard_map/pallas_call | solution.py:27
  22.3 0.7 %shard_map.103 = (bf16[512,1024]{1,0:T(8,128)(2,1)S(1)}, bf16[256,512]{1,0:T(8,128)(2,1)S(1)}) custom-call(bf16[512,768]{1,0:T(8,128)(2,1)S(1)} %get-tuple-element.21.refs_2_.refs_0_, bf16[192,1024]{1,0:T(8,128)(2,1)S(1)} %collective-permute-done.5.refs_1_, bf16[192,1024]{1,0:T(8,128)(2,1)S(1)} %collective-permute-done.6.refs_2_, ...), custom_call_target="tpu_custom_call" | custom-call | flops 660000000 | tf_op jit(solution)/shard_map/pallas_call | solution.py:27
  23.0 0.1 collective-permute-start.7
  23.0 0.5 collective-permute-start
  23.5 1.5 %collective-permute-start.1 = (f32[4,1024]{1,0:T(4,128)S(1)}, f32[4,1024]{1,0:T(4,128)S(1)}, u32[]{:S(2)}, u32[]{:S(2)}) collective-permute-start(f32[4,1024]{1,0:T(4,128)S(1)} %shard_map.93.refs_0_.refs_2_), channel_id=1, source_target_pairs={{0,2},{1,3},{2,0},{3,1},{4,6},{5,7},{6,4},{7,5},{8,10},{9,11},{10,... | collective-permute-start | bytes 49160 | tf_op jit(solution)/shard_map/ppermute | solution.py:454
  25.0 0.7 %collective-permute-done.refs_1_ = f32[4,1024]{1,0:T(4,128)S(1)} collective-permute-done((f32[4,1024]{1,0:T(4,128)S(1)}, f32[4,1024]{1,0:T(4,128)S(1)}, u32[]{:S(2)}, u32[]{:S(2)}) %collective-permute-start) | collective-permute-done | bytes 16416 | tf_op jit(solution)/shard_map/ppermute | solution.py:454
  25.7 1.6 %collective-permute-done.1.refs_2_ = f32[4,1024]{1,0:T(4,128)S(1)} collective-permute-done((f32[4,1024]{1,0:T(4,128)S(1)}, f32[4,1024]{1,0:T(4,128)S(1)}, u32[]{:S(2)}, u32[]{:S(2)}) %collective-permute-start.1) | collective-permute-done | bytes 16416 | tf_op jit(solution)/shard_map/ppermute | solution.py:454
  27.3 3.6 %collective-permute-start.2 = (f32[12,1024]{1,0:T(8,128)S(1)}, f32[12,1024]{1,0:T(8,128)S(1)}, u32[]{:S(2)}, u32[]{:S(2)}) collective-permute-start(f32[12,1024]{1,0:T(8,128)S(1)} %shard_map.94.refs_0_), channel_id=1, source_target_pairs={{0,16},{4,20},{8,24},{12,28},{16,0},{20,4},{24,8},{28,12},{1,17},{... | collective-permute-start | bytes 147464 | tf_op jit(solution)/shard_map/ppermute | solution.py:466
  30.9 2.2 %collective-permute-done.2.refs_1_ = f32[12,1024]{1,0:T(8,128)S(1)} collective-permute-done((f32[12,1024]{1,0:T(8,128)S(1)}, f32[12,1024]{1,0:T(8,128)S(1)}, u32[]{:S(2)}, u32[]{:S(2)}) %collective-permute-start.2) | collective-permute-done | bytes 49184 | tf_op jit(solution)/shard_map/ppermute | solution.py:466
  33.2 2.0 %collective-permute-start.3 = (f32[12,1024]{1,0:T(8,128)S(1)}, f32[12,1024]{1,0:T(8,128)S(1)}, u32[]{:S(2)}, u32[]{:S(2)}) collective-permute-start(f32[12,1024]{1,0:T(8,128)S(1)} %shard_map.98.refs_0_), channel_id=1, source_target_pairs={{0,8},{4,12},{8,0},{12,4},{16,24},{20,28},{24,16},{28,20},{1,9},{5... | collective-permute-start | bytes 147464 | tf_op jit(solution)/shard_map/ppermute | solution.py:466
  35.2 2.4 %collective-permute-done.3.refs_1_ = f32[12,1024]{1,0:T(8,128)S(1)} collective-permute-done((f32[12,1024]{1,0:T(8,128)S(1)}, f32[12,1024]{1,0:T(8,128)S(1)}, u32[]{:S(2)}, u32[]{:S(2)}) %collective-permute-start.3) | collective-permute-done | bytes 49184 | tf_op jit(solution)/shard_map/ppermute | solution.py:466
  37.5 0.0 copy-start.1
  37.5 1.9 %collective-permute-start.4 = (f32[12,1024]{1,0:T(8,128)S(1)}, f32[12,1024]{1,0:T(8,128)S(1)}, u32[]{:S(2)}, u32[]{:S(2)}) collective-permute-start(f32[12,1024]{1,0:T(8,128)S(1)} %shard_map.99.refs_0_), channel_id=1, source_target_pairs={{0,4},{4,0},{8,12},{12,8},{16,20},{20,16},{24,28},{28,24},{1,5},{5... | collective-permute-start | bytes 147464 | tf_op jit(solution)/shard_map/ppermute | solution.py:466
  39.4 2.3 %shard_map.105.refs_4_ = f32[1024,1024]{1,0:T(8,128)S(1)} custom-call(f32[1,4096]{1,0:T(1,128)S(1)} %bitcast.14, f32[1,4096]{1,0:T(1,128)S(1)} %bitcast.18), custom_call_target="tpu_custom_call" | custom-call | flops 2750000128 | tf_op jit(solution)/shard_map/pallas_call | solution.py:27
  41.8 0.1 collective-permute-done.4.refs_1_
  41.9 0.0 copy-done.1
  41.9 1.4 %shard_map.106.refs_1_ = bf16[2048,1024]{1,0:T(8,128)(2,1)S(1)} custom-call(f32[8,1024]{1,0:T(8,128)S(1)} %get-tuple-element.22.refs_0_, f32[8,1024]{1,0:T(8,128)S(1)} %get-tuple-element.23.refs_1_, f32[8,1024]{1,0:T(8,128)S(1)} %get-tuple-element.30.refs_2_, f32[1024,1024]{1,0:T(8,128)S(1)} %shard_map.96.refs_4_.refs_3_, f32[1024,1024]{1,0:T(8,128)S(1)} %shard_map.105.refs_4_), custom_call_target="tpu_custom_call" | custom-call | flops 1540000000 | tf_op jit(solution)/shard_map/pallas_call | solution.py:27
  43.3 1.5 %collective-permute-start.8 = (bf16[256,512]{1,0:T(8,128)(2,1)S(1)}, bf16[256,512]{1,0:T(8,128)(2,1)S(1)}, u32[]{:S(2)}, u32[]{:S(2)}) collective-permute-start(bf16[256,512]{1,0:T(8,128)(2,1)S(1)} %get-tuple-element.31), channel_id=1, source_target_pairs={{0,2},{1,3},{2,0},{3,1},{4,6},{5,7},{6,4},{7,5},{8,10},{9,11},{10,... | collective-permute-start | bytes 786440 | tf_op jit(solution)/shard_map/ppermute | solution.py:480
  44.8 0.6 collective-permute-start.9
  45.4 0.0 collective-permute-done.7.refs_5_.refs_4_
  45.4 2.7 %shard_map.104.refs_0_ = f32[512,128]{1,0:T(8,128)S(1)} custom-call(f32[8,1024]{1,0:T(8,128)S(1)} %get-tuple-element.22.refs_0_, f32[8,1024]{1,0:T(8,128)S(1)} %get-tuple-element.23.refs_1_, f32[1024,1024]{1,0:T(8,128)S(1)} %get-tuple-element.24.refs_2_, f32[2,512,512]{2,1,0:T(8,128)S(1)} %get-tuple-element.25.refs_3_, ...), custom_call_target="tpu_custom_call" | custom-call | flops 3740000000 | tf_op jit(solution)/shard_map/pallas_call | solution.py:27
  48.0 2.6 %collective-permute-done.8.refs_2_ = bf16[256,512]{1,0:T(8,128)(2,1)S(1)} collective-permute-done((bf16[256,512]{1,0:T(8,128)(2,1)S(1)}, bf16[256,512]{1,0:T(8,128)(2,1)S(1)}, u32[]{:S(2)}, u32[]{:S(2)}) %collective-permute-start.8) | collective-permute-done | bytes 262176 | tf_op jit(solution)/shard_map/ppermute | solution.py:480
  50.6 0.7 %shard_map.107.refs_0_ = f32[512,128]{1,0:T(8,128)S(1)} custom-call(f32[512,128]{1,0:T(8,128)S(1)} %shard_map.104.refs_0_, bf16[2048,1024]{1,0:T(8,128)(2,1)S(1)} %shard_map.106.refs_1_, bf16[256,512]{1,0:T(8,128)(2,1)S(1)} %collective-permute-done.8.refs_2_, bf16[512,1024]{1,0:T(8,128)(2,1)S(1)} %get-tuple-element.29.refs_4_.refs_3_, ...), custom_call_target="tpu_custom_call" | custom-call | flops 1100000000 | tf_op jit(solution)/shard_map/pallas_call | solution.py:27
  51.4 2.1 %collective-permute-done.9.refs_2_ = bf16[256,512]{1,0:T(8,128)(2,1)S(1)} collective-permute-done((bf16[256,512]{1,0:T(8,128)(2,1)S(1)}, bf16[256,512]{1,0:T(8,128)(2,1)S(1)}, u32[]{:S(2)}, u32[]{:S(2)}) %collective-permute-start.9) | collective-permute-done | bytes 262176 | tf_op jit(solution)/shard_map/ppermute | solution.py:480
  53.5 1.0 %shard_map.108 = f32[1,512]{1,0:T(1,128)S(1)} custom-call(f32[512,128]{1,0:T(8,128)S(1)} %shard_map.107.refs_0_, bf16[2048,1024]{1,0:T(8,128)(2,1)S(1)} %shard_map.106.refs_1_, bf16[256,512]{1,0:T(8,128)(2,1)S(1)} %collective-permute-done.9.refs_2_, bf16[512,1024]{1,0:T(8,128)(2,1)S(1)} %get-tuple-element.29.refs_4_.refs_3_, ...), custom_call_target="tpu_custom_call" | custom-call | flops 1100000000 | tf_op jit(solution)/shard_map/pallas_call | solution.py:27
  54.5 1.5 %collective-permute-start.11 = (f32[512]{0:T(512)S(1)}, f32[512]{0:T(512)S(1)}, u32[]{:S(2)}, u32[]{:S(2)}) collective-permute-start(f32[512]{0:T(512)S(1)} %bitcast.7), channel_id=1, source_target_pairs={{0,2},{1,3},{2,0},{3,1},{4,6},{5,7},{6,4},{7,5},{8,10},{9,11},{10,... | collective-permute-start | bytes 6152 | tf_op jit(solution)/shard_map/ppermute | solution.py:505
  56.0 0.0 collective-permute-start.12
  56.0 0.7 %collective-permute-start.10 = (f32[512]{0:T(512)S(1)}, f32[512]{0:T(512)S(1)}, u32[]{:S(2)}, u32[]{:S(2)}) collective-permute-start(f32[512]{0:T(512)S(1)} %bitcast.9), channel_id=1, source_target_pairs={{0,1},{1,0},{2,3},{3,2},{4,5},{5,4},{6,7},{7,6},{8,9},{9,8},{10,11... | collective-permute-start | bytes 6152 | tf_op jit(solution)/shard_map/ppermute | solution.py:505
  56.6 1.4 %collective-permute-done.11 = f32[512]{0:T(512)S(1)} collective-permute-done((f32[512]{0:T(512)S(1)}, f32[512]{0:T(512)S(1)}, u32[]{:S(2)}, u32[]{:S(2)}) %collective-permute-start.11) | collective-permute-done | bytes 2080 | tf_op jit(solution)/shard_map/ppermute | solution.py:505
  58.1 0.9 %collective-permute-done.12 = f32[512]{0:T(512)S(1)} collective-permute-done((f32[512]{0:T(512)S(1)}, f32[512]{0:T(512)S(1)}, u32[]{:S(2)}, u32[]{:S(2)}) %collective-permute-start.12) | collective-permute-done | bytes 2080 | tf_op jit(solution)/shard_map/ppermute | solution.py:505
  59.0 0.0 collective-permute-done.10
  59.0 0.6 add_add_fusion
  (4 shorter events, 0.1 us)
Async XLA Ops:
  0.0 1.4 %copy-start = (bf16[3,256,1024]{2,1,0:T(8,128)(2,1)S(1)}, bf16[3,256,1024]{2,1,0:T(8,128)(2,1)}, u32[]{:S(2)}) copy-start(bf16[3,256,1024]{2,1,0:T(8,128)(2,1)} %refs_1_.3) | copy-start | bytes 4718596
  0.0 0.8 %copy-start.6 = (s32[2,64]{1,0:T(2,128)S(1)}, s32[2,64]{1,0:T(2,128)}, u32[]{:S(2)}) copy-start(s32[2,64]{1,0:T(2,128)} %refs_0_.1) | copy-start | bytes 1540
  1.4 4.7 %copy-start.7 = (f32[256]{0:T(256)S(1)}, f32[256]{0:T(256)}, u32[]{:S(2)}) copy-start(f32[256]{0:T(256)} %param.10) | copy-start | bytes 3076
  1.8 19.8 %collective-permute-start.5 = (bf16[192,1024]{1,0:T(8,128)(2,1)S(1)}, bf16[192,1024]{1,0:T(8,128)(2,1)S(1)}, u32[]{:S(2)}, u32[]{:S(2)}) collective-permute-start(bf16[192,1024]{1,0:T(8,128)(2,1)S(1)} %shard_map.101), channel_id=1, source_target_pairs={{0,4},{4,0},{8,12},{12,8},{16,20},{20,16},{24,28},{28,24},{1,5},{5... | collective-permute-start | bytes 1179656 | tf_op jit(solution)/shard_map/ppermute | solution.py:425
  5.4 1.5 %copy-start.3 = (f32[4096]{0:T(1024)S(1)}, f32[4096]{0:T(1024)}, u32[]{:S(2)}) copy-start(f32[4096]{0:T(1024)} %param.12) | copy-start | bytes 49156
  5.4 1.5 %copy-start.4 = (f32[4096]{0:T(1024)S(1)}, f32[4096]{0:T(1024)}, u32[]{:S(2)}) copy-start(f32[4096]{0:T(1024)} %param.13) | copy-start | bytes 49156
  5.4 16.3 %collective-permute-start.6 = (bf16[192,1024]{1,0:T(8,128)(2,1)S(1)}, bf16[192,1024]{1,0:T(8,128)(2,1)S(1)}, u32[]{:S(2)}, u32[]{:S(2)}) collective-permute-start(bf16[192,1024]{1,0:T(8,128)(2,1)S(1)} %get-tuple-element.26), channel_id=1, source_target_pairs={{4,8},{8,4},{12,16},{16,12},{20,24},{24,20},{5,9},{9,5},{13,17},{1... | collective-permute-start | bytes 1179656 | tf_op jit(solution)/shard_map/ppermute | solution.py:425
  9.4 1.6 %copy-start.2 = (bf16[64,8,4,3]{0,2,3,1:T(4,128)(2,1)S(1)}, bf16[64,8,4,3]{0,2,3,1:T(4,128)(2,1)}, u32[]{:S(2)}) copy-start(bf16[64,8,4,3]{0,2,3,1:T(4,128)(2,1)} %param.14) | copy-start | bytes 36868
  9.4 1.6 %copy-start.5 = (s32[64,4]{0,1:T(4,128)S(1)}, s32[64,4]{0,1:T(4,128)}, u32[]{:S(2)}) copy-start(s32[64,4]{0,1:T(4,128)} %param.15) | copy-start | bytes 3076
  9.4 1.6 %copy-start.8 = (s32[64]{0:T(128)S(1)}, s32[64]{0:T(128)}, u32[]{:S(2)}) copy-start(s32[64]{0:T(128)} %param.16) | copy-start | bytes 772
  23.0 22.4 %collective-permute-start.7 = (bf16[512,1024]{1,0:T(8,128)(2,1)S(1)}, bf16[512,1024]{1,0:T(8,128)(2,1)S(1)}, u32[]{:S(2)}, u32[]{:S(2)}) collective-permute-start(bf16[512,1024]{1,0:T(8,128)(2,1)S(1)} %get-tuple-element.29.refs_4_.refs_3_), channel_id=1, source_target_pairs={{0,1},{1,0},{2,3},{3,2},{4,5},{5,4},{6,7},{7,6},{8,9},{9,8},{10,11... | collective-permute-start | bytes 3145736 | tf_op jit(solution)/shard_map/ppermute | solution.py:482
  23.0 2.7 %collective-permute-start = (f32[4,1024]{1,0:T(4,128)S(1)}, f32[4,1024]{1,0:T(4,128)S(1)}, u32[]{:S(2)}, u32[]{:S(2)}) collective-permute-start(f32[4,1024]{1,0:T(4,128)S(1)} %shard_map.93.refs_0_.refs_2_), channel_id=1, source_target_pairs={{0,1},{1,0},{2,3},{3,2},{4,5},{5,4},{6,7},{7,6},{8,9},{9,8},{10,11... | collective-permute-start | bytes 49160 | tf_op jit(solution)/shard_map/ppermute | solution.py:454
  23.5 3.7 %collective-permute-start.1 = (f32[4,1024]{1,0:T(4,128)S(1)}, f32[4,1024]{1,0:T(4,128)S(1)}, u32[]{:S(2)}, u32[]{:S(2)}) collective-permute-start(f32[4,1024]{1,0:T(4,128)S(1)} %shard_map.93.refs_0_.refs_2_), channel_id=1, source_target_pairs={{0,2},{1,3},{2,0},{3,1},{4,6},{5,7},{6,4},{7,5},{8,10},{9,11},{10,... | collective-permute-start | bytes 49160 | tf_op jit(solution)/shard_map/ppermute | solution.py:454
  27.3 5.9 %collective-permute-start.2 = (f32[12,1024]{1,0:T(8,128)S(1)}, f32[12,1024]{1,0:T(8,128)S(1)}, u32[]{:S(2)}, u32[]{:S(2)}) collective-permute-start(f32[12,1024]{1,0:T(8,128)S(1)} %shard_map.94.refs_0_), channel_id=1, source_target_pairs={{0,16},{4,20},{8,24},{12,28},{16,0},{20,4},{24,8},{28,12},{1,17},{... | collective-permute-start | bytes 147464 | tf_op jit(solution)/shard_map/ppermute | solution.py:466
  33.2 4.3 %collective-permute-start.3 = (f32[12,1024]{1,0:T(8,128)S(1)}, f32[12,1024]{1,0:T(8,128)S(1)}, u32[]{:S(2)}, u32[]{:S(2)}) collective-permute-start(f32[12,1024]{1,0:T(8,128)S(1)} %shard_map.98.refs_0_), channel_id=1, source_target_pairs={{0,8},{4,12},{8,0},{12,4},{16,24},{20,28},{24,16},{28,20},{1,9},{5... | collective-permute-start | bytes 147464 | tf_op jit(solution)/shard_map/ppermute | solution.py:466
  37.5 4.3 %copy-start.1 = (f32[3,4096]{1,0:T(4,128)S(1)}, f32[3,4096]{1,0:T(4,128)}, u32[]{:S(2)}) copy-start(f32[3,4096]{1,0:T(4,128)} %refs_2_.1) | copy-start | bytes 147460
  37.5 4.3 %collective-permute-start.4 = (f32[12,1024]{1,0:T(8,128)S(1)}, f32[12,1024]{1,0:T(8,128)S(1)}, u32[]{:S(2)}, u32[]{:S(2)}) collective-permute-start(f32[12,1024]{1,0:T(8,128)S(1)} %shard_map.99.refs_0_), channel_id=1, source_target_pairs={{0,4},{4,0},{8,12},{12,8},{16,20},{20,16},{24,28},{28,24},{1,5},{5... | collective-permute-start | bytes 147464 | tf_op jit(solution)/shard_map/ppermute | solution.py:466
  43.3 7.3 %collective-permute-start.8 = (bf16[256,512]{1,0:T(8,128)(2,1)S(1)}, bf16[256,512]{1,0:T(8,128)(2,1)S(1)}, u32[]{:S(2)}, u32[]{:S(2)}) collective-permute-start(bf16[256,512]{1,0:T(8,128)(2,1)S(1)} %get-tuple-element.31), channel_id=1, source_target_pairs={{0,2},{1,3},{2,0},{3,1},{4,6},{5,7},{6,4},{7,5},{8,10},{9,11},{10,... | collective-permute-start | bytes 786440 | tf_op jit(solution)/shard_map/ppermute | solution.py:480
  44.8 8.6 %collective-permute-start.9 = (bf16[256,512]{1,0:T(8,128)(2,1)S(1)}, bf16[256,512]{1,0:T(8,128)(2,1)S(1)}, u32[]{:S(2)}, u32[]{:S(2)}) collective-permute-start(bf16[256,512]{1,0:T(8,128)(2,1)S(1)} %get-tuple-element.32), channel_id=1, source_target_pairs={{0,2},{1,3},{2,0},{3,1},{4,6},{5,7},{6,4},{7,5},{8,10},{9,11},{10,... | collective-permute-start | bytes 786440 | tf_op jit(solution)/shard_map/ppermute | solution.py:480
  54.5 3.6 %collective-permute-start.11 = (f32[512]{0:T(512)S(1)}, f32[512]{0:T(512)S(1)}, u32[]{:S(2)}, u32[]{:S(2)}) collective-permute-start(f32[512]{0:T(512)S(1)} %bitcast.7), channel_id=1, source_target_pairs={{0,2},{1,3},{2,0},{3,1},{4,6},{5,7},{6,4},{7,5},{8,10},{9,11},{10,... | collective-permute-start | bytes 6152 | tf_op jit(solution)/shard_map/ppermute | solution.py:505
  56.0 3.0 %collective-permute-start.12 = (f32[512]{0:T(512)S(1)}, f32[512]{0:T(512)S(1)}, u32[]{:S(2)}, u32[]{:S(2)}) collective-permute-start(f32[512]{0:T(512)S(1)} %bitcast.8), channel_id=1, source_target_pairs={{0,3},{1,2},{2,1},{3,0},{4,7},{5,6},{6,5},{7,4},{8,11},{9,10},{10,... | collective-permute-start | bytes 6152 | tf_op jit(solution)/shard_map/ppermute | solution.py:505
  56.0 3.0 %collective-permute-start.10 = (f32[512]{0:T(512)S(1)}, f32[512]{0:T(512)S(1)}, u32[]{:S(2)}, u32[]{:S(2)}) collective-permute-start(f32[512]{0:T(512)S(1)} %bitcast.9), channel_id=1, source_target_pairs={{0,1},{1,0},{2,3},{3,2},{4,5},{5,4},{6,7},{7,6},{8,9},{9,8},{10,11... | collective-permute-start | bytes 6152 | tf_op jit(solution)/shard_map/ppermute | solution.py:505
